TPU v7x, 32 devices: a whole 2x2x4 slice. The times are simulated.
32 devices in a mesh: fsdp: 8 (over y, x, core), tensor: 4 (over z).
Axes of the slice: x: 2, y: 2, z: 4, core: 2. Of those that a mesh axis runs over, the one named last changes fastest.
Arguments:
- hidden: bfloat16 [4096, 2048], P(('fsdp', 'tensor')), may hold values from -6 to 6
- cotangent: bfloat16 [4096, 2048], P(('fsdp', 'tensor')), may hold values from -6 to 6
- seq_lengths: int32 [8, 3], P('fsdp'), may hold values from 1 to 256, 512 in all within a row
- pack_order: int32 [8, 3], P('fsdp'), may hold values from 0 to 2, each once within a row
- norm_gain: bfloat16 [2048], P(('fsdp', 'tensor')), may hold values from 0.099609375 to 1.8984375
- w_in: bfloat16 [2, 4096, 2048], P(None, ('fsdp', 'tensor')), may hold values from -0.125 to 0.125
- conv_weight: bfloat16 [4096, 4], P(('fsdp', 'tensor')), may hold values from -3 to 3
- conv_bias: bfloat16 [4096], P(('fsdp', 'tensor')), may hold values from -3 to 3
- w_xproj: bfloat16 [4096, 160], P(('fsdp', 'tensor')), may hold values from -0.1875 to 0.1875
- w_dt: bfloat16 [4096, 128], P(('fsdp', 'tensor')), may hold values from -0.5 to 0.5
- dt_bias: bfloat16 [4096], P(('fsdp', 'tensor')), may hold values from -7 to -2
- a_log: bfloat16 [4096, 16], P(('fsdp', 'tensor')), may hold values from -1 to 2.6875
- d_skip: bfloat16 [4096], P(('fsdp', 'tensor')), may hold values from 0.099609375 to 1.8984375
- w_out: bfloat16 [4096, 2048], P(('fsdp', 'tensor')), may hold values from -0.1875 to 0.1875
Outputs:
- output: bfloat16 [4096, 2048], P(('fsdp', 'tensor'))
- grad_hidden: float32 [4096, 2048], P(('fsdp', 'tensor'))
- grad_norm_gain: float32 [2048], P(('fsdp', 'tensor'))
- grad_w_in: float32 [2, 4096, 2048], P(None, ('fsdp', 'tensor'))
- grad_conv_weight: float32 [4096, 4], P(('fsdp', 'tensor'))
- grad_conv_bias: float32 [4096], P(('fsdp', 'tensor'))
- grad_w_xproj: float32 [4096, 160], P(('fsdp', 'tensor'))
- grad_w_dt: float32 [4096, 128], P(('fsdp', 'tensor'))
- grad_dt_bias: float32 [4096], P(('fsdp', 'tensor'))
- grad_a_log: float32 [4096, 16], P(('fsdp', 'tensor'))
- grad_d_skip: float32 [4096], P(('fsdp', 'tensor'))
- grad_w_out: float32 [4096, 2048], P(('fsdp', 'tensor'))
Inputs may be any that keep to these rules, and one draw needn't show every extreme that they name: `seq_lengths`: each row holds the lengths of the 3 sequences of one token group; they sum to 512 and the largest of each row is exactly 256. `pack_order`: each row is a permutation of 0 to 2: the sequence packed into each slot.
All inputs are finite; a program needn't handle non-finite values.
Results may differ from a plain program's by a relative error of at most 0.012.
Values may be sent and summed in bfloat16 or wider, within the bound.
No kernel may reach another device: no remote copies, remote signals or barrier semaphores. Data moves between devices by JAX's collectives and lax.ppermute only.
A program may use at most 320 MiB of HBM per device.

v0:
```python
import math

import jax
import jax.numpy as jnp
from jax import lax
from jax.sharding import PartitionSpec as P

EPSILON = 1e-05


def normalize(values, scales):
    factor = lax.rsqrt(jnp.mean(values * values, axis=1, keepdims=True) + EPSILON)
    return values * factor * scales[None, :]


def distances(lengths, pack_rows, row_count):
    slot_count = lengths.shape[0]
    picks = pack_rows[:, None] == jnp.arange(slot_count, dtype=jnp.int32)[None, :]
    packed = jnp.sum(jnp.where(picks, lengths[None, :], 0), axis=1)
    starts = jnp.cumsum(packed) - packed
    positions = jnp.arange(row_count, dtype=jnp.int32)
    latest = jnp.max(jnp.where(starts[None, :] <= positions[:, None], starts[None, :], 0), axis=1)
    return positions - latest


def convolve(signal, weights, biases, offsets):
    kernel_taps = weights.shape[1]
    result = biases[None, :] + weights[:, kernel_taps - 1][None, :] * signal
    for lag_index in range(1, kernel_taps):
        shifted = jnp.concatenate(
            [jnp.zeros((lag_index, signal.shape[1]), jnp.float32), signal[:-lag_index]], axis=0
        )
        in_sequence = (offsets >= lag_index).astype(jnp.float32)[:, None]
        result = result + weights[:, kernel_taps - 1 - lag_index][None, :] * shifted * in_sequence
    return result


def block_scan(carried, step_sizes, inputs, b_in, c_out, decays, keep_mask):
    row_count = step_sizes.shape[0]
    stretch_len = math.gcd(row_count, 16)
    stretches = row_count // stretch_len
    channels = step_sizes.shape[1]
    state_cols = decays.shape[1]
    factors = jnp.exp(step_sizes[:, :, None] * decays[None, :, :]) * keep_mask[:, None, None]
    drives = (step_sizes * inputs)[:, :, None] * b_in[:, None, :]
    factors = factors.reshape(stretches, stretch_len, channels, state_cols)
    drives = drives.reshape(stretches, stretch_len, channels, state_cols)
    running = drives[:, 0]
    product = factors[:, 0]
    running_list = [running]
    product_list = [product]
    for offset in range(1, stretch_len):
        running = factors[:, offset] * running + drives[:, offset]
        product = factors[:, offset] * product
        running_list.append(running)
        product_list.append(product)
    running_all = jnp.stack(running_list, axis=1)
    product_all = jnp.stack(product_list, axis=1)

    def carry_step(current, members):
        return (members[0] * current + members[1], current)

    closing, entering = lax.scan(carry_step, carried, (product_all[:, -1], running_all[:, -1]))
    states = running_all + product_all * entering[:, None]
    states = states.reshape(row_count, channels, state_cols)
    return (closing, jnp.sum(states * c_out[:, None, :], axis=2))


def selective(step_sizes, inputs, b_in, c_out, decays, keep_mask, block_len):
    row_count = step_sizes.shape[0]
    blocks = row_count // block_len

    def block_step(carried, pieces):
        return block_scan(carried, pieces[0], pieces[1], pieces[2], pieces[3], decays, pieces[4])

    pieces = (
        step_sizes.reshape(blocks, block_len, -1),
        inputs.reshape(blocks, block_len, -1),
        b_in.reshape(blocks, block_len, -1),
        c_out.reshape(blocks, block_len, -1),
        keep_mask.reshape(blocks, block_len),
    )
    initial = jnp.zeros((step_sizes.shape[1], decays.shape[1]), jnp.float32)
    _, outputs = lax.scan(jax.checkpoint(block_step), initial, pieces)
    return outputs.reshape(row_count, -1)


def mix_states(
    proj, b_in, c_out, inner, gate_in, step_bias, log_rates, skip_scale, keep_mask, block_len
):
    step_sizes = jax.nn.softplus(proj + step_bias[None, :])
    decays = -jnp.exp(log_rates)
    scanned = selective(step_sizes, inner, b_in, c_out, decays, keep_mask, block_len)
    return (scanned + skip_scale[None, :] * inner) * jax.nn.silu(gate_in)


def shards(
    hidden,
    cotangent,
    seq_lengths,
    pack_order,
    norm_gain,
    w_in,
    conv_weight,
    conv_bias,
    w_xproj,
    w_dt,
    dt_bias,
    a_log,
    d_skip,
    w_out,
):
    f32 = jnp.float32
    bf16 = jnp.bfloat16
    n_fsdp = lax.axis_size("fsdp")
    n_tensor = lax.axis_size("tensor")
    tok_rows = hidden.shape[0]
    group_rows = tok_rows * n_tensor
    rank_cols = w_dt.shape[1]
    state_cols = a_log.shape[1]
    block_len = math.gcd(group_rows, 256)
    gathered = (
        lax.all_gather(w_in, "fsdp", axis=1, tiled=True),
        lax.all_gather(conv_weight, "fsdp", axis=0, tiled=True),
        lax.all_gather(conv_bias, "fsdp", axis=0, tiled=True),
        lax.all_gather(w_xproj, "fsdp", axis=0, tiled=True),
        lax.all_gather(w_dt, "fsdp", axis=0, tiled=True),
        lax.all_gather(dt_bias, "fsdp", axis=0, tiled=True),
        lax.all_gather(a_log, "fsdp", axis=0, tiled=True),
        lax.all_gather(d_skip, "fsdp", axis=0, tiled=True),
        lax.all_gather(w_out, "fsdp", axis=0, tiled=True),
        lax.all_gather(norm_gain, "fsdp", axis=0, tiled=True),
    )
    w_in_t, conv_w_t, conv_b_t, w_x_t, w_dt_t, dt_b_t, a_log_t, d_skip_t, w_out_t, gain_fsdp = (
        gathered
    )
    rows_all, gain_tensor = (
        lax.all_gather(hidden, "tensor", axis=0, tiled=True),
        lax.all_gather(gain_fsdp, "tensor", axis=0, tiled=True),
    )
    gain_full = gain_tensor.reshape(n_tensor, n_fsdp, -1).transpose(1, 0, 2).reshape(-1).astype(f32)
    offsets = distances(seq_lengths[0], pack_order[0], group_rows)
    keep_mask = (offsets > 0).astype(f32)
    row_values = rows_all.astype(f32)
    normed = normalize(row_values, gain_full).astype(bf16)
    xz_all = jnp.einsum("gd,hcd->ghc", normed, w_in_t, preferred_element_type=f32)
    signal = xz_all[:, 0]
    gate_in = xz_all[:, 1]
    inner, front_back = jax.vjp(
        lambda signal_in, taps_in, biases_in: jax.nn.silu(
            convolve(signal_in, taps_in, biases_in, offsets)
        ),
        signal,
        conv_w_t.astype(f32),
        conv_b_t.astype(f32),
    )
    inner_low = inner.astype(bf16)
    pieces_x = jnp.dot(inner_low, w_x_t, preferred_element_type=f32)
    mixed = lax.psum(pieces_x, "tensor")
    step_in = mixed[:, :rank_cols].astype(bf16)
    b_in = mixed[:, rank_cols : rank_cols + state_cols]
    c_out = mixed[:, rank_cols + state_cols :]
    proj = jnp.einsum("gr,cr->gc", step_in, w_dt_t, preferred_element_type=f32)
    gated, mixer_back = jax.vjp(
        lambda proj_in, b_part, c_part, inner_in, gate_part, bias_part, rates_part, skip_part: mix_states(
            proj_in,
            b_part,
            c_part,
            inner_in,
            gate_part,
            bias_part,
            rates_part,
            skip_part,
            keep_mask,
            block_len,
        ),
        proj,
        b_in,
        c_out,
        inner_low.astype(f32),
        gate_in,
        dt_b_t.astype(f32),
        a_log_t.astype(f32),
        d_skip_t.astype(f32),
    )
    gated_low = gated.astype(bf16)
    branch = lax.psum_scatter(
        jnp.dot(gated_low, w_out_t, preferred_element_type=f32),
        "tensor",
        scatter_dimension=0,
        tiled=True,
    )
    output = (hidden.astype(f32) + branch).astype(bf16)
    cot_all = lax.all_gather(cotangent, "tensor", axis=0, tiled=True)
    grad_gated = (
        jnp.einsum("gd,cd->gc", cot_all, w_out_t, preferred_element_type=f32)
        .astype(bf16)
        .astype(f32)
    )
    out_grad = jnp.einsum("gc,gd->cd", gated_low, cot_all, preferred_element_type=f32)
    g_proj, g_b, g_c, g_inner_scan, g_gate, g_dt_bias, g_a_log, g_d_skip = mixer_back(grad_gated)
    g_proj_low = g_proj.astype(bf16)
    g_step = jnp.dot(g_proj_low, w_dt_t, preferred_element_type=f32)
    w_dt_grad = jnp.einsum("gc,gr->cr", g_proj_low, step_in, preferred_element_type=f32)
    mixed_grad = lax.psum(jnp.concatenate([g_step, g_b, g_c], axis=1), "tensor")
    mixed_low = mixed_grad.astype(bf16)
    g_inner = g_inner_scan + jnp.einsum("gk,ck->gc", mixed_low, w_x_t, preferred_element_type=f32)
    w_x_grad = jnp.einsum("gc,gk->ck", inner_low, mixed_low, preferred_element_type=f32)
    g_signal, g_conv_w, g_conv_b = front_back(g_inner)
    g_xz = jnp.stack([g_signal, g_gate], axis=1).astype(bf16)
    w_in_grad = jnp.einsum("ghc,gd->hcd", g_xz, normed, preferred_element_type=f32)
    g_normed = jnp.einsum("ghc,hcd->gd", g_xz, w_in_t, preferred_element_type=f32)
    gain_term = jax.vjp(lambda scales: normalize(row_values, scales), gain_full)[1](g_normed)[0]
    gain_term = gain_term.reshape(n_fsdp, n_tensor, -1).transpose(1, 0, 2).reshape(-1)
    g_norm_own, gain_part = (
        lax.psum_scatter(g_normed, "tensor", scatter_dimension=0, tiled=True),
        lax.psum_scatter(gain_term, "tensor", scatter_dimension=0, tiled=True),
    )
    norm_back = jax.vjp(lambda own_values: normalize(own_values, gain_full), hidden.astype(f32))[1]
    grad_hidden = cotangent.astype(f32) + norm_back(g_norm_own)[0]
    results = (
        lax.psum_scatter(w_in_grad, "fsdp", scatter_dimension=1, tiled=True),
        lax.psum_scatter(g_conv_w, "fsdp", scatter_dimension=0, tiled=True),
        lax.psum_scatter(g_conv_b, "fsdp", scatter_dimension=0, tiled=True),
        lax.psum_scatter(w_x_grad, "fsdp", scatter_dimension=0, tiled=True),
        lax.psum_scatter(w_dt_grad, "fsdp", scatter_dimension=0, tiled=True),
        lax.psum_scatter(g_dt_bias, "fsdp", scatter_dimension=0, tiled=True),
        lax.psum_scatter(g_a_log, "fsdp", scatter_dimension=0, tiled=True),
        lax.psum_scatter(g_d_skip, "fsdp", scatter_dimension=0, tiled=True),
        lax.psum_scatter(out_grad, "fsdp", scatter_dimension=0, tiled=True),
        lax.psum_scatter(gain_part, "fsdp", scatter_dimension=0, tiled=True),
    )
    return (
        output,
        grad_hidden,
        results[9],
        results[0],
        results[1],
        results[2],
        results[3],
        results[4],
        results[5],
        results[6],
        results[7],
        results[8],
    )


def solution(mesh):
    placed = (
        P(("fsdp", "tensor"), None),
        P(("fsdp", "tensor"), None),
        P("fsdp", None),
        P("fsdp", None),
        P(("fsdp", "tensor")),
        P(None, ("fsdp", "tensor"), None),
        P(("fsdp", "tensor"), None),
        P(("fsdp", "tensor")),
        P(("fsdp", "tensor"), None),
        P(("fsdp", "tensor"), None),
        P(("fsdp", "tensor")),
        P(("fsdp", "tensor"), None),
        P(("fsdp", "tensor")),
        P(("fsdp", "tensor"), None),
    )
    return jax.shard_map(
        shards,
        mesh=mesh,
        in_specs=placed,
        out_specs=(
            P(("fsdp", "tensor"), None),
            P(("fsdp", "tensor"), None),
            P(("fsdp", "tensor")),
            P(None, ("fsdp", "tensor"), None),
            P(("fsdp", "tensor"), None),
            P(("fsdp", "tensor")),
            P(("fsdp", "tensor"), None),
            P(("fsdp", "tensor"), None),
            P(("fsdp", "tensor")),
            P(("fsdp", "tensor"), None),
            P(("fsdp", "tensor")),
            P(("fsdp", "tensor"), None),
        ),
        check_vma=False,
    )
```

profile of v0, /device:TPU:8, one launch (start us, length us, event | category | flops | bytes accessed | tf_op | source)
XLA Modules:
  0.0 1660.6 jit_solution(14647917128028557112)
XLA Ops:
  12.9 14.1 all-reduce.59
  26.9 12.3 all-gather.1
  39.5 7.8 all-gather
  48.4 8.8 all_gather.40
  57.2 8.8 all_gather.45
  68.5 43.3 %all-gather.11.cloned.1.call-done = bf16[2,1024,2048]{2,1,0:T(8,128)(2,1)} async-done(((bf16[2,128,2048]{2,1,0:T(8,128)(2,1)}), bf16[2,1024,2048]{2,1,0:T(8,128)(2,1)}) %all-gather.11.cloned.1.call-update) | async-done | bytes 8388624 | tf_op jit(solution)/shard_map/all_gather | solution.py:123
  111.9 7.7 fusion.64
  123.6 34.2 %all-gather.15.cloned.1.call-done = bf16[512,2048]{1,0:T(8,128)(2,1)} async-done(((bf16[128,2048]{1,0:T(8,128)(2,1)}), bf16[512,2048]{1,0:T(8,128)(2,1)}) %all-gather.15.cloned.1.call-update) | async-done | bytes 2097168 | tf_op jit(solution)/shard_map/all_gather | solution.py:194
  157.8 38.8 %all-gather.13.cloned.1.call-done = bf16[1024,2048]{1,0:T(8,128)(2,1)} async-done(((bf16[128,2048]{1,0:T(8,128)(2,1)}), bf16[1024,2048]{1,0:T(8,128)(2,1)}) %all-gather.13.cloned.1.call-update) | async-done | bytes 4194320 | tf_op jit(solution)/shard_map/all_gather | solution.py:131
  196.7 12.5 multiply_reduce_fusion.6
  211.0 8.7 all-gather.2
  219.7 7.8 all-gather.3
  228.1 8.8 all_gather.48
  237.0 9.3 all_gather.46
  253.9 242.1 %while.116 = (s32[]{:T(128)}, f32[1024,16]{0,1:T(8,128)S(1)}, f32[2,256,1024]{2,1,0:T(8,128)}, f32[2,1024,16]{1,2,0:T(8,128)}, f32[2,256,1024]{2,1,0:T(8,128)}, ...) while((s32[]{:T(128)}, f32[1024,16]{0,1:T(8,128)S(1)}, ...), condition=%wide.region_9.10_spmd, body=%wide.region_5.9_spmd.sunk | while | flops 52199424 | bytes 568369280 | solution.py:84
  280.6 5.8 copy-done.3
  288.5 8.5 broadcast_multiply_fusion.10
  333.0 6.3 bitcast_add_fusion.23
  341.2 24.7 %while.120 = (s32[]{:T(128)}, f32[1024,16]{0,1:T(8,128)S(1)}, f32[16,1024,16]{1,2,0:T(8,128)}, f32[16,1024,16]{1,2,0:T(8,128)}, f32[16,1024,16]{1,2,0:T(8,128)}, /*index=5*/s32[]{:T(128)}) while((s32[]{:T(128)}, f32[1024,16]{0,1:T(8,128)S(1)}, f32[16,1024,16]{1,2,0:T(8,128)}, f32[16,1024,16]{1,2,0:T(8,128)}, f32[16,1024,16]{1,2,0:T(8,128)}, ...), condition=%wide.region_7.7_spmd, body=%wide.region_6.6_spmd.sunk | while | flops 32770 | bytes 393801 | solution.py:63
  366.2 12.8 multiply_reduce_fusion.15
  394.9 5.8 copy-done.3
  402.7 8.5 broadcast_multiply_fusion.10
  447.2 6.3 bitcast_add_fusion.23
  455.5 24.7 %while.120 = (s32[]{:T(128)}, f32[1024,16]{0,1:T(8,128)S(1)}, f32[16,1024,16]{1,2,0:T(8,128)}, f32[16,1024,16]{1,2,0:T(8,128)}, f32[16,1024,16]{1,2,0:T(8,128)}, /*index=5*/s32[]{:T(128)}) while((s32[]{:T(128)}, f32[1024,16]{0,1:T(8,128)S(1)}, f32[16,1024,16]{1,2,0:T(8,128)}, f32[16,1024,16]{1,2,0:T(8,128)}, f32[16,1024,16]{1,2,0:T(8,128)}, ...), condition=%wide.region_7.7_spmd, body=%wide.region_6.6_spmd.sunk | while | flops 32770 | bytes 393801 | solution.py:63
  480.4 12.8 multiply_reduce_fusion.15
  500.4 609.0 %while.119 = (s32[]{:T(128)}, f32[1024,16]{0,1:T(8,128)}, f32[1024,16]{0,1:T(8,128)S(1)}, f32[2,256,1024]{2,1,0:T(8,128)}, f32[2,256,1024]{2,1,0:T(8,128)}, /*in...) while((s32[]{:T(128)}, f32[1024,16]{0,1:T(8,128)}, ...), condition=%wide.region_22.23_spmd.clone, body=%wide.region_11.22_spmd.clone.sunk | while | flops 338518016 | bytes 1045472448 | solution.py:84
  531.9 7.0 broadcast_multiply_fusion.11
  539.7 6.5 fusion.145
  546.3 13.2 bitcast_add_fusion.24
  576.9 9.7 fusion.146
  632.9 15.0 while.121
  650.1 13.3 multiply_reduce_fusion.16
  664.6 24.8 %while.122 = (s32[]{:T(128)}, f32[1024,16]{0,1:T(8,128)S(1)}, f32[16,1024,16]{1,2,0:T(8,128)S(1)}, f32[16,1024,16]{1,2,0:T(8,128)}, f32[16,1024,16]{1,2,0:T(8,12...) while((s32[]{:T(128)}, f32[1024,16]{0,1:T(8,128)S(1)}, ...), condition=%wide.region_16.16_spmd, body=%wide.region_15.15_spmd.sunk | while | flops 49155 | bytes 524401 | solution.py:63
  689.4 7.5 multiply_add_fusion.26
  696.9 5.7 copy-done.2
  704.2 15.5 slice_add_fusion.81
  719.8 11.0 multiply_reduce_fusion.18
  792.3 14.9 multiply_reduce_fusion.17
  821.0 7.0 broadcast_multiply_fusion.11
  828.8 6.5 fusion.145
  835.4 13.2 bitcast_add_fusion.24
  865.9 9.7 fusion.146
  922.0 15.0 while.121
  939.1 13.3 multiply_reduce_fusion.16
  953.7 24.8 %while.122 = (s32[]{:T(128)}, f32[1024,16]{0,1:T(8,128)S(1)}, f32[16,1024,16]{1,2,0:T(8,128)S(1)}, f32[16,1024,16]{1,2,0:T(8,128)}, f32[16,1024,16]{1,2,0:T(8,12...) while((s32[]{:T(128)}, f32[1024,16]{0,1:T(8,128)S(1)}, ...), condition=%wide.region_16.16_spmd, body=%wide.region_15.15_spmd.sunk | while | flops 49155 | bytes 524401 | solution.py:63
  978.5 7.5 multiply_add_fusion.26
  993.2 15.5 slice_add_fusion.81
  1008.9 11.0 multiply_reduce_fusion.18
  1081.3 14.9 multiply_reduce_fusion.17
  1116.5 21.9 %all-reduce.70 = bf16[512,160]{0,1:T(8,128)(2,1)S(1)} all-reduce(f32[512,160]{0,1:T(8,128)S(1)} %pad_maximum_fusion.3), channel_id=1, replica_groups=mesh['fsdp'=8,'tensor'=4] {'tensor'}, use_global_device_ids=true, to_apply=%region_23.24 | all-reduce | flops 81920 | bytes 491520 | tf_op jit(solution)/shard_map/psum | solution.py:205
  1138.5 6.2 multiply_reduce_fusion.10
  1151.4 11.2 fusion.49
  1162.7 6.9 fusion.95
  1173.3 7.8 fusion.96
  1181.2 9.5 fusion.62
  1194.0 13.1 all-reduce.60
  1207.2 22.4 %all-reduce.65 = (f32[512]{0:T(512)S(1)}, f32[1024]{0:T(1024)S(1)}, f32[1024]{0:T(1024)S(1)}, f32[1024]{0:T(1024)S(1)}) all-reduce(f32[512]{0:T(512)S(1)} %dynamic-slice.2, f32[1024]{0:T(1024)S(1)} %get-tuple-element.866, f32[1024]{0:T(1024)S(1)} %get-tuple-element.1057, ...), channel_id=5, replica_groups=mesh['fsdp'=8,'tensor'=4] {'fsdp'}, use_global_device_ids=true, to_apply=%region_29.30.clone | all-reduce | flops 3584 | bytes 28672
  1233.4 33.0 %reduce-scatter.13.cloned.1.call-done = f32[128,2048]{1,0:T(8,128)} async-done(((f32[512,2048]{1,0:T(8,128)}), f32[128,2048]{1,0:T(8,128)}) %reduce-scatter.13.cloned.1.call-update) | async-done | bytes 1048592 | tf_op jit(solution)/shard_map/reduce_scatter | solution.py:216
  1268.0 78.0 %reduce-scatter.11.cloned.1.call-done = f32[128,2048]{1,0:T(8,128)} async-done(((f32[512,2048]{1,0:T(8,128)}), f32[128,2048]{1,0:T(8,128)}) %reduce-scatter.11.cloned.1.call-update) | async-done | bytes 1048592 | tf_op jit(solution)/shard_map/reduce_scatter | solution.py:187
  1349.0 32.8 %reduce-scatter.21.cloned.1.call-done = f32[128,16]{0,1:T(8,128)} async-done(((f32[1024,16]{0,1:T(8,128)}), f32[128,16]{0,1:T(8,128)}) %reduce-scatter.21.cloned.1.call-update) | async-done | bytes 8208 | tf_op jit(solution)/shard_map/reduce_scatter | solution.py:228
  1381.8 37.6 %reduce-scatter.19.cloned.1.call-done = f32[128,128]{1,0:T(8,128)} async-done(((f32[1024,128]{1,0:T(8,128)}), f32[128,128]{1,0:T(8,128)}) %reduce-scatter.19.cloned.1.call-update) | async-done | bytes 65552 | tf_op jit(solution)/shard_map/reduce_scatter | solution.py:226
  1419.5 38.6 %reduce-scatter.17.cloned.1.call-done = f32[128,160]{0,1:T(8,128)} async-done(((f32[1024,160]{0,1:T(8,128)}), f32[128,160]{0,1:T(8,128)}) %reduce-scatter.17.cloned.1.call-update) | async-done | bytes 81936 | tf_op jit(solution)/shard_map/reduce_scatter | solution.py:225
  1458.1 75.6 %reduce-scatter.23.cloned.1.call-done = f32[128,2048]{1,0:T(8,128)} async-done(((f32[1024,2048]{1,0:T(8,128)}), f32[128,2048]{1,0:T(8,128)}) %reduce-scatter.23.cloned.1.call-update) | async-done | bytes 1048592 | tf_op jit(solution)/shard_map/reduce_scatter | solution.py:230
  1533.7 120.1 %reduce-scatter.15.cloned.1.call-done = f32[2,128,2048]{2,1,0:T(8,128)} async-done(((f32[2,1024,2048]{2,1,0:T(8,128)}), f32[2,128,2048]{2,1,0:T(8,128)}) %reduce-scatter.15.cloned.1.call-update) | async-done | bytes 2097168 | tf_op jit(solution)/shard_map/reduce_scatter | solution.py:222
  (1036 shorter events, 587.1 us)
Async XLA Ops:
  7.2 58.9 %all-gather.9.cloned.1.call-start = ((), (), s32[]{:S(2)}) async-start(), calls=%async_computation.8 | async-start | bytes 2621440 | tf_op jit(solution)/shard_map/all_gather | solution.py:138
  7.9 103.9 %all-gather.11.cloned.1.call-start = ((), (), s32[]{:S(2)}) async-start(), calls=%async_computation.9 | async-start | bytes 9437184 | tf_op jit(solution)/shard_map/all_gather | solution.py:123
  8.7 149.1 %all-gather.15.cloned.1.call-start = ((), (), s32[]{:S(2)}) async-start(), calls=%async_computation.13 | async-start | bytes 2621440 | tf_op jit(solution)/shard_map/all_gather | solution.py:194
  9.4 187.2 %all-gather.13.cloned.1.call-start = ((), (), s32[]{:S(2)}) async-start(), calls=%async_computation.11 | async-start | bytes 4718592 | tf_op jit(solution)/shard_map/all_gather | solution.py:131
  10.0 237.2 %all-reduce.69.cloned.1.call-start = ((), (), s32[]{:S(2)}) async-start(), calls=%async_computation.10 | async-start | bytes 655360 | tf_op jit(solution)/shard_map/psum | solution.py:159
  39.5 80.1 %copy-start.102 = (f32[2048]{0:T(1024)}, f32[2048]{0:T(1024)S(1)}, u32[]{:S(2)}) copy-start(f32[2048]{0:T(1024)S(1)} %reshape.379) | copy-start | bytes 24580
  66.0 143.2 %copy-start.83 = (bf16[1024,160]{0,1:T(8,128)(2,1)}, bf16[1024,160]{0,1:T(8,128)(2,1)S(1)}, u32[]{:S(2)}) copy-start(bf16[1024,160]{0,1:T(8,128)(2,1)S(1)} %all_gather.45) | copy-start | bytes 983044
  66.0 130.6 %copy-start.115 = (f32[512]{0:T(512)}, f32[512]{0:T(512)S(1)}, u32[]{:S(2)}) copy-start(f32[512]{0:T(512)S(1)} %get-tuple-element.1111) | copy-start | bytes 6148
  66.0 130.6 %copy-start.116 = (f32[512]{0:T(512)}, f32[512]{0:T(512)S(1)}, u32[]{:S(2)}) copy-start(f32[512]{0:T(512)S(1)} %get-tuple-element.1112) | copy-start | bytes 6148
  66.0 130.6 %copy-start.117 = (f32[512]{0:T(512)}, f32[512]{0:T(512)S(1)}, u32[]{:S(2)}) copy-start(f32[512]{0:T(512)S(1)} %get-tuple-element.1113) | copy-start | bytes 6148
  66.1 130.6 %copy-start.107 = (f32[1024,1]{0,1:T(1,128)}, f32[1024,1]{0,1:T(1,128)S(1)}, u32[]{:S(2)}) copy-start(f32[1024,1]{0,1:T(1,128)S(1)} %get-tuple-element.1108) | copy-start | bytes 12292
  66.1 130.6 %copy-start.109 = (f32[1024,1]{0,1:T(1,128)}, f32[1024,1]{0,1:T(1,128)S(1)}, u32[]{:S(2)}) copy-start(f32[1024,1]{0,1:T(1,128)S(1)} %get-tuple-element.1110) | copy-start | bytes 12292
  66.1 130.6 %copy-start.111 = (f32[1024,1]{0,1:T(1,128)}, f32[1024,1]{0,1:T(1,128)S(1)}, u32[]{:S(2)}) copy-start(f32[1024,1]{0,1:T(1,128)S(1)} %get-tuple-element.1109) | copy-start | bytes 12292
  66.1 130.6 %copy-start.113 = (f32[1024,1]{0,1:T(1,128)}, f32[1024,1]{0,1:T(1,128)S(1)}, u32[]{:S(2)}) copy-start(f32[1024,1]{0,1:T(1,128)S(1)} %get-tuple-element.1107) | copy-start | bytes 12292
  68.5 51.0 %copy-start.120 = (f32[512]{0:T(512)}, f32[512]{0:T(512)S(1)}, u32[]{:S(2)}) copy-start(f32[512]{0:T(512)S(1)} %add_rsqrt_fusion) | copy-start | bytes 6148
  119.8 89.4 %copy-start.75 = (f32[509,1024]{1,0:T(8,128)}, f32[509,1024]{1,0:T(8,128)S(1)}, u32[]{:S(2)}) copy-start(f32[509,1024]{1,0:T(8,128)S(1)} %slice_bitcast_fusion.1) | copy-start | bytes 6254596
  196.7 23.1 %copy-start.123 = (bf16[128]{0:T(256)(128)(2,1)S(1)}, bf16[128]{0:T(256)(128)(2,1)}, u32[]{:S(2)}) copy-start(bf16[128]{0:T(256)(128)(2,1)} %param.36) | copy-start | bytes 772
  196.7 31.5 %copy-start.118 = (bf16[128,16]{0,1:T(8,128)(2,1)S(1)}, bf16[128,16]{0,1:T(8,128)(2,1)}, u32[]{:S(2)}) copy-start(bf16[128,16]{0,1:T(8,128)(2,1)} %param.35) | copy-start | bytes 12292
  196.7 40.3 %copy-start.105 = (bf16[128,128]{1,0:T(8,128)(2,1)S(1)}, bf16[128,128]{1,0:T(8,128)(2,1)}, u32[]{:S(2)}) copy-start(bf16[128,128]{1,0:T(8,128)(2,1)} %param.33) | copy-start | bytes 98308
  209.2 44.7 %copy-start.69 = (bf16[512,1024]{1,0:T(8,128)(2,1)}, bf16[512,1024]{1,0:T(8,128)(2,1)S(1)}, u32[]{:S(2)}) copy-start(bf16[512,1024]{1,0:T(8,128)(2,1)S(1)} %get-tuple-element.1055) | copy-start | bytes 3145732
  210.4 1021.5 %reduce-scatter.25.cloned.1.call-start = ((), (), s32[]{:S(2)}) async-start(), calls=%async_computation.20 | async-start | bytes 589824
  219.7 34.2 %copy-start.106 = (f32[8,1,128]{2,1,0:T(1,128)}, f32[8,1,128]{2,1,0:T(1,128)S(1)}, u32[]{:S(2)}) copy-start(f32[8,1,128]{2,1,0:T(1,128)S(1)} %convert_element_type.124) | copy-start | bytes 12292
  253.9 246.5 %copy-start.81 = (f32[1024,16]{0,1:T(8,128)S(1)}, f32[1024,16]{0,1:T(8,128)}, u32[]{:S(2)}) copy-start(f32[1024,16]{0,1:T(8,128)} %get-tuple-element.1815) | copy-start | bytes 196612
  576.9 28.0 %slice-start = ((s8[16777216]{0:T(1024)(128)(4,1)}), s8[4194304]{0:T(1024)(128)(4,1)S(1)}, s32[]{:S(2)}) async-start(s8[16777216]{0:T(1024)(128)(4,1)} %bitcast.492), calls=%async_computation.21 | async-start | bytes 8388608 | tf_op jit(solution)/shard_map/transpose(jvp())/while
  576.9 28.0 %slice-start.1 = ((s8[16777216]{0:T(1024)(128)(4,1)}), s8[4194304]{0:T(1024)(128)(4,1)S(1)}, s32[]{:S(2)}) async-start(s8[16777216]{0:T(1024)(128)(4,1)} %bitcast.492), calls=%async_computation.22 | async-start | bytes 8388608 | tf_op jit(solution)/shard_map/transpose(jvp())/while
  576.9 28.0 %slice-start.2 = ((s8[16777216]{0:T(1024)(128)(4,1)}), s8[4194304]{0:T(1024)(128)(4,1)S(1)}, s32[]{:S(2)}) async-start(s8[16777216]{0:T(1024)(128)(4,1)} %bitcast.492), calls=%async_computation.23 | async-start | bytes 8388608 | tf_op jit(solution)/shard_map/transpose(jvp())/while
  586.5 23.3 %copy-start.5 = (f32[16,1,1024,16]{2,3,0,1:T(8,128)S(1)}, f32[16,1,1024,16]{2,3,0,1:T(8,128)}, u32[]{:S(2)}) copy-start(f32[16,1,1024,16]{2,3,0,1:T(8,128)} %copy-done.4) | copy-start | bytes 3145732 | tf_op jit(solution)/shard_map/transpose(jvp())/while
  719.7 24.1 %copy-start.30 = (f32[16,1,1024,16]{2,3,0,1:T(8,128)}, f32[16,1,1024,16]{2,3,0,1:T(8,128)S(1)}, u32[]{:S(2)}) copy-start(f32[16,1,1024,16]{2,3,0,1:T(8,128)S(1)} %get-tuple-element.1646) | copy-start | bytes 3145732 | tf_op jit(solution)/shard_map/transpose(jvp())/while
  719.7 24.1 %copy-start.31 = (f32[16,1,1024,16]{2,3,0,1:T(8,128)}, f32[16,1,1024,16]{2,3,0,1:T(8,128)S(1)}, u32[]{:S(2)}) copy-start(f32[16,1,1024,16]{2,3,0,1:T(8,128)S(1)} %get-tuple-element.1648) | copy-start | bytes 3145732 | tf_op jit(solution)/shard_map/transpose(jvp())/while
  719.8 24.0 %copy-start.17 = (f32[16,1,1024,16]{2,3,0,1:T(8,128)S(1)}, f32[16,1,1024,16]{2,3,0,1:T(8,128)}, u32[]{:S(2)}) copy-start(f32[16,1,1024,16]{2,3,0,1:T(8,128)} %copy-done.16) | copy-start | bytes 3145732 | tf_op jit(solution)/shard_map/transpose(jvp())/while
  719.8 24.0 %copy-start.34 = (f32[16,1,1024,16]{2,3,0,1:T(8,128)S(1)}, f32[16,1,1024,16]{2,3,0,1:T(8,128)}, u32[]{:S(2)}) copy-start(f32[16,1,1024,16]{2,3,0,1:T(8,128)} %get-tuple-element.1656) | copy-start | bytes 3145732 | tf_op jit(solution)/shard_map/transpose(jvp())/while
  719.8 25.1 %copy-start.6 = (f32[16,1,1024,16]{2,3,0,1:T(8,128)S(1)}, f32[16,1,1024,16]{2,3,0,1:T(8,128)}, u32[]{:S(2)}) copy-start(f32[16,1,1024,16]{2,3,0,1:T(8,128)} %copy-done.4) | copy-start | bytes 3145732 | tf_op jit(solution)/shard_map/transpose(jvp())/while
  719.8 25.1 %copy-start.33 = (f32[16,1,1024,16]{2,3,0,1:T(8,128)S(1)}, f32[16,1,1024,16]{2,3,0,1:T(8,128)}, u32[]{:S(2)}) copy-start(f32[16,1,1024,16]{2,3,0,1:T(8,128)} %get-tuple-element.1654) | copy-start | bytes 3145732 | tf_op jit(solution)/shard_map/transpose(jvp())/while
  719.8 26.3 %copy-start.32 = (f32[16,1,1024,16]{2,3,0,1:T(8,128)S(1)}, f32[16,1,1024,16]{2,3,0,1:T(8,128)}, u32[]{:S(2)}) copy-start(f32[16,1,1024,16]{2,3,0,1:T(8,128)} %get-tuple-element.1652) | copy-start | bytes 3145732 | tf_op jit(solution)/shard_map/transpose(jvp())/while
  719.8 41.9 %slice-start.12 = ((s8[16777216]{0:T(1024)(128)(4,1)}), s8[4194304]{0:T(1024)(128)(4,1)S(1)}, s32[]{:S(2)}) async-start(s8[16777216]{0:T(1024)(128)(4,1)} %bitcast.498), calls=%async_computation.33 | async-start | bytes 8388608 | tf_op jit(solution)/shard_map/transpose(jvp())/while
  719.8 41.9 %slice-start.13 = ((s8[16777216]{0:T(1024)(128)(4,1)}), s8[4194304]{0:T(1024)(128)(4,1)S(1)}, s32[]{:S(2)}) async-start(s8[16777216]{0:T(1024)(128)(4,1)} %bitcast.498), calls=%async_computation.34 | async-start | bytes 8388608 | tf_op jit(solution)/shard_map/transpose(jvp())/while
  730.9 22.0 %copy-start.45 = (f32[16,1,1024,16]{2,3,0,1:T(8,128)S(1)}, f32[16,1,1024,16]{2,3,0,1:T(8,128)}, u32[]{:S(2)}) copy-start(f32[16,1,1024,16]{2,3,0,1:T(8,128)} %copy-done.44) | copy-start | bytes 3145732 | tf_op jit(solution)/shard_map/transpose(jvp())/while
  865.9 28.0 %slice-start = ((s8[16777216]{0:T(1024)(128)(4,1)}), s8[4194304]{0:T(1024)(128)(4,1)S(1)}, s32[]{:S(2)}) async-start(s8[16777216]{0:T(1024)(128)(4,1)} %bitcast.492), calls=%async_computation.21 | async-start | bytes 8388608 | tf_op jit(solution)/shard_map/transpose(jvp())/while
  865.9 28.0 %slice-start.1 = ((s8[16777216]{0:T(1024)(128)(4,1)}), s8[4194304]{0:T(1024)(128)(4,1)S(1)}, s32[]{:S(2)}) async-start(s8[16777216]{0:T(1024)(128)(4,1)} %bitcast.492), calls=%async_computation.22 | async-start | bytes 8388608 | tf_op jit(solution)/shard_map/transpose(jvp())/while
  865.9 28.0 %slice-start.2 = ((s8[16777216]{0:T(1024)(128)(4,1)}), s8[4194304]{0:T(1024)(128)(4,1)S(1)}, s32[]{:S(2)}) async-start(s8[16777216]{0:T(1024)(128)(4,1)} %bitcast.492), calls=%async_computation.23 | async-start | bytes 8388608 | tf_op jit(solution)/shard_map/transpose(jvp())/while
  875.6 23.3 %copy-start.5 = (f32[16,1,1024,16]{2,3,0,1:T(8,128)S(1)}, f32[16,1,1024,16]{2,3,0,1:T(8,128)}, u32[]{:S(2)}) copy-start(f32[16,1,1024,16]{2,3,0,1:T(8,128)} %copy-done.4) | copy-start | bytes 3145732 | tf_op jit(solution)/shard_map/transpose(jvp())/while
  1008.8 24.1 %copy-start.30 = (f32[16,1,1024,16]{2,3,0,1:T(8,128)}, f32[16,1,1024,16]{2,3,0,1:T(8,128)S(1)}, u32[]{:S(2)}) copy-start(f32[16,1,1024,16]{2,3,0,1:T(8,128)S(1)} %get-tuple-element.1646) | copy-start | bytes 3145732 | tf_op jit(solution)/shard_map/transpose(jvp())/while
  1008.8 24.1 %copy-start.31 = (f32[16,1,1024,16]{2,3,0,1:T(8,128)}, f32[16,1,1024,16]{2,3,0,1:T(8,128)S(1)}, u32[]{:S(2)}) copy-start(f32[16,1,1024,16]{2,3,0,1:T(8,128)S(1)} %get-tuple-element.1648) | copy-start | bytes 3145732 | tf_op jit(solution)/shard_map/transpose(jvp())/while
  1008.8 24.0 %copy-start.17 = (f32[16,1,1024,16]{2,3,0,1:T(8,128)S(1)}, f32[16,1,1024,16]{2,3,0,1:T(8,128)}, u32[]{:S(2)}) copy-start(f32[16,1,1024,16]{2,3,0,1:T(8,128)} %copy-done.16) | copy-start | bytes 3145732 | tf_op jit(solution)/shard_map/transpose(jvp())/while
  1008.8 24.0 %copy-start.34 = (f32[16,1,1024,16]{2,3,0,1:T(8,128)S(1)}, f32[16,1,1024,16]{2,3,0,1:T(8,128)}, u32[]{:S(2)}) copy-start(f32[16,1,1024,16]{2,3,0,1:T(8,128)} %get-tuple-element.1656) | copy-start | bytes 3145732 | tf_op jit(solution)/shard_map/transpose(jvp())/while
  1008.8 25.1 %copy-start.6 = (f32[16,1,1024,16]{2,3,0,1:T(8,128)S(1)}, f32[16,1,1024,16]{2,3,0,1:T(8,128)}, u32[]{:S(2)}) copy-start(f32[16,1,1024,16]{2,3,0,1:T(8,128)} %copy-done.4) | copy-start | bytes 3145732 | tf_op jit(solution)/shard_map/transpose(jvp())/while
  1008.9 25.1 %copy-start.33 = (f32[16,1,1024,16]{2,3,0,1:T(8,128)S(1)}, f32[16,1,1024,16]{2,3,0,1:T(8,128)}, u32[]{:S(2)}) copy-start(f32[16,1,1024,16]{2,3,0,1:T(8,128)} %get-tuple-element.1654) | copy-start | bytes 3145732 | tf_op jit(solution)/shard_map/transpose(jvp())/while
  1008.9 26.3 %copy-start.32 = (f32[16,1,1024,16]{2,3,0,1:T(8,128)S(1)}, f32[16,1,1024,16]{2,3,0,1:T(8,128)}, u32[]{:S(2)}) copy-start(f32[16,1,1024,16]{2,3,0,1:T(8,128)} %get-tuple-element.1652) | copy-start | bytes 3145732 | tf_op jit(solution)/shard_map/transpose(jvp())/while
  1008.9 41.9 %slice-start.12 = ((s8[16777216]{0:T(1024)(128)(4,1)}), s8[4194304]{0:T(1024)(128)(4,1)S(1)}, s32[]{:S(2)}) async-start(s8[16777216]{0:T(1024)(128)(4,1)} %bitcast.498), calls=%async_computation.33 | async-start | bytes 8388608 | tf_op jit(solution)/shard_map/transpose(jvp())/while
  1008.9 41.9 %slice-start.13 = ((s8[16777216]{0:T(1024)(128)(4,1)}), s8[4194304]{0:T(1024)(128)(4,1)S(1)}, s32[]{:S(2)}) async-start(s8[16777216]{0:T(1024)(128)(4,1)} %bitcast.498), calls=%async_computation.34 | async-start | bytes 8388608 | tf_op jit(solution)/shard_map/transpose(jvp())/while
  1019.9 22.0 %copy-start.45 = (f32[16,1,1024,16]{2,3,0,1:T(8,128)S(1)}, f32[16,1,1024,16]{2,3,0,1:T(8,128)}, u32[]{:S(2)}) copy-start(f32[16,1,1024,16]{2,3,0,1:T(8,128)} %copy-done.44) | copy-start | bytes 3145732 | tf_op jit(solution)/shard_map/transpose(jvp())/while
  1025.2 22.0 %copy-start.39 = (f32[16,1,1024,16]{2,3,0,1:T(8,128)S(1)}, f32[16,1,1024,16]{2,3,0,1:T(8,128)}, u32[]{:S(2)}) copy-start(f32[16,1,1024,16]{2,3,0,1:T(8,128)} %copy-done.38) | copy-start | bytes 3145732 | tf_op jit(solution)/shard_map/transpose(jvp())/while
  1109.4 35.3 %copy-start.112 = (f32[1024,1]{0,1:T(1,128)S(1)}, f32[1024,1]{0,1:T(1,128)}, u32[]{:S(2)}) copy-start(f32[1024,1]{0,1:T(1,128)} %copy-done.111) | copy-start | bytes 12292
  1109.4 35.8 %copy-start.110 = (f32[1024,1]{0,1:T(1,128)S(1)}, f32[1024,1]{0,1:T(1,128)}, u32[]{:S(2)}) copy-start(f32[1024,1]{0,1:T(1,128)} %copy-done.109) | copy-start | bytes 12292
  1113.5 32.1 %copy-start.108 = (f32[1024,1]{0,1:T(1,128)S(1)}, f32[1024,1]{0,1:T(1,128)}, u32[]{:S(2)}) copy-start(f32[1024,1]{0,1:T(1,128)} %copy-done.107) | copy-start | bytes 12292
  1151.4 115.1 %reduce-scatter.13.cloned.1.call-start = ((), (), s32[]{:S(2)}) async-start(), calls=%async_computation.14 | async-start | bytes 5242880 | tf_op jit(solution)/shard_map/reduce_scatter | solution.py:216
  1162.7 183.3 %reduce-scatter.11.cloned.1.call-start = ((), (), s32[]{:S(2)}) async-start(), calls=%async_computation.12 | async-start | bytes 5242880 | tf_op jit(solution)/shard_map/reduce_scatter | solution.py:187
  1169.7 212.2 %reduce-scatter.21.cloned.1.call-start = ((), (), s32[]{:S(2)}) async-start(), calls=%async_computation.18 | async-start | bytes 73728 | tf_op jit(solution)/shard_map/reduce_scatter | solution.py:228
  1170.4 249.1 %reduce-scatter.19.cloned.1.call-start = ((), (), s32[]{:S(2)}) async-start(), calls=%async_computation.17 | async-start | bytes 589824 | tf_op jit(solution)/shard_map/reduce_scatter | solution.py:226
  1171.8 286.3 %reduce-scatter.17.cloned.1.call-start = ((), (), s32[]{:S(2)}) async-start(), calls=%async_computation.16 | async-start | bytes 737280 | tf_op jit(solution)/shard_map/reduce_scatter | solution.py:225
  1173.2 360.5 %reduce-scatter.23.cloned.1.call-start = ((), (), s32[]{:S(2)}) async-start(), calls=%async_computation.19 | async-start | bytes 9437184 | tf_op jit(solution)/shard_map/reduce_scatter | solution.py:230
  1181.1 472.7 %reduce-scatter.15.cloned.1.call-start = ((), (), s32[]{:S(2)}) async-start(), calls=%async_computation.15 | async-start | bytes 18874368 | tf_op jit(solution)/shard_map/reduce_scatter | solution.py:222
  1190.6 75.8 %copy-start.82 = (bf16[128,2048]{1,0:T(8,128)(2,1)S(1)}, bf16[128,2048]{1,0:T(8,128)(2,1)}, u32[]{:S(2)}) copy-start(bf16[128,2048]{1,0:T(8,128)(2,1)} %param.24) | copy-start | bytes 1572868
  1190.6 155.3 %copy-start.88 = (bf16[128,2048]{1,0:T(8,128)(2,1)S(1)}, bf16[128,2048]{1,0:T(8,128)(2,1)}, u32[]{:S(2)}) copy-start(bf16[128,2048]{1,0:T(8,128)(2,1)} %param.25) | copy-start | bytes 1572868
  (189 other events, 2353.5 us)
Sparse Core Ops, SparseCore 0:
  9.6 45.6 all-gather.8
  57.1 54.6 all-gather.10
  113.4 44.3 all-gather.14
  159.5 37.0 all-gather.12
  210.6 36.1 all-reduce.68
  1151.5 35.3 reduce-scatter.24
  1189.2 77.1 reduce-scatter.12
  1268.7 77.1 reduce-scatter.10
  1349.8 31.9 reduce-scatter.20
  1385.3 34.1 reduce-scatter.18
  1423.5 34.5 reduce-scatter.16
  1462.4 71.2 reduce-scatter.22
  1537.8 115.9 reduce-scatter.14
where the time goes:
time: 1680 us; the launch traced here: 1660 us
  other arithmetic  657 us (39%)
  waiting for transfers between devices  535 us (32%)
  local copies, waits for them, and re-layouts  187 us (11%)
  blocking collectives  144 us (9%)
  matrix products  71.2 us (4%)
  loops' own time  48.6 us (3%)
  between operations  17.3 us (1%)
    while x86, other arithmetic  135 us
    reduce_scatter x1, waiting for transfers between devices, shards(): lax.psum_scatter(w_in_grad, 'fsdp', scatter_dimension=1, tiled=True)  120 us
    while x432, local copies, waits for them, and re-layouts  96.3 us
    mul x20, other arithmetic, block_scan(): product = factors[:, offset] * product  84 us
    reduce_scatter x1, waiting for transfers between devices, shards(): lax.psum_scatter(jnp.dot(gated_low, w_out_t, preferred_element_type=f32),...  78 us
    reduce_scatter x1, waiting for transfers between devices, shards(): lax.psum_scatter(out_grad, 'fsdp', scatter_dimension=0, tiled=True)  75.6 us
    add x64, other arithmetic, carry_step(): return (members[0] * current + members[1], current)  57.8 us
    mul x28, other arithmetic, block_scan(): running = factors[:, offset] * running + drives[:, offset]  55.4 us
  transfers between devices with their start and end apart: 13, of which 10 were waited for; matrix products, arithmetic and copies ran while one was open for 4% of the time, Pallas kernels for 0%

commit v1 on v0

--- a/solution.py
+++ b/solution.py
@@ -1,8 +1,11 @@
+import functools
 import math
 
 import jax
 import jax.numpy as jnp
 from jax import lax
+from jax.experimental import pallas as pl
+from jax.experimental.pallas import tpu as pltpu
 from jax.sharding import PartitionSpec as P
 
 EPSILON = 1e-05
@@ -35,63 +38,209 @@
     return result
 
 
-def block_scan(carried, step_sizes, inputs, b_in, c_out, decays, keep_mask):
-    row_count = step_sizes.shape[0]
-    stretch_len = math.gcd(row_count, 16)
-    stretches = row_count // stretch_len
-    channels = step_sizes.shape[1]
-    state_cols = decays.shape[1]
-    factors = jnp.exp(step_sizes[:, :, None] * decays[None, :, :]) * keep_mask[:, None, None]
-    drives = (step_sizes * inputs)[:, :, None] * b_in[:, None, :]
-    factors = factors.reshape(stretches, stretch_len, channels, state_cols)
-    drives = drives.reshape(stretches, stretch_len, channels, state_cols)
-    running = drives[:, 0]
-    product = factors[:, 0]
-    running_list = [running]
-    product_list = [product]
-    for offset in range(1, stretch_len):
-        running = factors[:, offset] * running + drives[:, offset]
-        product = factors[:, offset] * product
-        running_list.append(running)
-        product_list.append(product)
-    running_all = jnp.stack(running_list, axis=1)
-    product_all = jnp.stack(product_list, axis=1)
-
-    def carry_step(current, members):
-        return (members[0] * current + members[1], current)
-
-    closing, entering = lax.scan(carry_step, carried, (product_all[:, -1], running_all[:, -1]))
-    states = running_all + product_all * entering[:, None]
-    states = states.reshape(row_count, channels, state_cols)
-    return (closing, jnp.sum(states * c_out[:, None, :], axis=2))
-
-
-def selective(step_sizes, inputs, b_in, c_out, decays, keep_mask, block_len):
-    row_count = step_sizes.shape[0]
-    blocks = row_count // block_len
-
-    def block_step(carried, pieces):
-        return block_scan(carried, pieces[0], pieces[1], pieces[2], pieces[3], decays, pieces[4])
-
-    pieces = (
-        step_sizes.reshape(blocks, block_len, -1),
-        inputs.reshape(blocks, block_len, -1),
-        b_in.reshape(blocks, block_len, -1),
-        c_out.reshape(blocks, block_len, -1),
-        keep_mask.reshape(blocks, block_len),
-    )
-    initial = jnp.zeros((step_sizes.shape[1], decays.shape[1]), jnp.float32)
-    _, outputs = lax.scan(jax.checkpoint(block_step), initial, pieces)
-    return outputs.reshape(row_count, -1)
-
-
-def mix_states(
-    proj, b_in, c_out, inner, gate_in, step_bias, log_rates, skip_scale, keep_mask, block_len
-):
-    step_sizes = jax.nn.softplus(proj + step_bias[None, :])
-    decays = -jnp.exp(log_rates)
-    scanned = selective(step_sizes, inner, b_in, c_out, decays, keep_mask, block_len)
-    return (scanned + skip_scale[None, :] * inner) * jax.nn.silu(gate_in)
+f32 = jnp.float32
+bf16 = jnp.bfloat16
+BIG = 1e30
+LANES=128
+SUB=8
+
+def tile_rows(ti, j, subs):
+    return pl.ds((ti * subs + j) * SUB, SUB)
+
+def put_tiles(ref, value, subs):
+    for ti in range(value.shape[0] // SUB):
+        for j in range(subs):
+            ref[tile_rows(ti, j, subs), :] = value[ti*SUB:(ti+1)*SUB, j*LANES:(j+1)*LANES]
+
+def get_tiles(ref, rows, subs):
+    return jnp.concatenate([jnp.concatenate([ref[tile_rows(ti, j, subs), :] for j in range(subs)], axis=1) for ti in range(rows // SUB)], axis=0)
+
+def put_spread(ref, value, count):
+    for ti in range(value.shape[0] // SUB):
+        for n in range(count):
+            ref[pl.ds((ti*count+n)*SUB, SUB), :] = jnp.broadcast_to(value[ti*SUB:(ti+1)*SUB, n:n+1], (SUB, LANES))
+
+def fwd_body(states, subs, keep_ref, step_ref, bc_ref, wdt_ref, db_ref, ds_ref, dec_ref, inner_ref, gate_ref,
+             hs_ref, dl_ref, ys_ref, gated_ref, h_sc, du_sc, bb_sc, y_sc):
+    chunk = pl.program_id(0)
+    rows = step_ref.shape[0]
+    span = states * subs
+    @pl.when(chunk == 0)
+    def _():
+        h_sc[...] = jnp.zeros_like(h_sc)
+    raw = jnp.dot(step_ref[...], wdt_ref[...], preferred_element_type=f32) + db_ref[...]
+    delta = jnp.maximum(raw, 0.0) + jnp.log1p(jnp.exp(-jnp.abs(raw)))
+    inner = inner_ref[...].astype(f32)
+    put_tiles(dl_ref, delta, subs)
+    put_tiles(du_sc, delta * inner, subs)
+    put_spread(bb_sc, bc_ref[...], 2 * states)
+    hs_ref[pl.ds(0, span), :] = h_sc[...]
+    decs = [dec_ref[pl.ds(n*subs, subs), :] for n in range(states)]
+    def step(ti, hs):
+        hs = list(hs)
+        for s in range(SUB):
+            t = ti * SUB + s
+            row = ti * (subs * SUB) + s
+            d = dl_ref[pl.ds(row, subs, stride=SUB), :]
+            u = du_sc[pl.ds(row, subs, stride=SUB), :]
+            d = jnp.where(keep_ref[chunk*rows + t] > 0, d, BIG)
+            y = None
+            for n in range(states):
+                b = bb_sc[pl.ds((ti*2*states + n)*SUB + s, subs, stride=0), :]
+                c = bb_sc[pl.ds((ti*2*states + states + n)*SUB + s, subs, stride=0), :]
+                hs[n] = jnp.exp2(d * decs[n]) * hs[n] + u * b
+                hs_ref[pl.ds(pl.multiple_of((t + 1) * span + n*subs, subs), subs), :] = hs[n]
+                y = c * hs[n] if y is None else y + c * hs[n]
+            y_sc[pl.ds(row, subs, stride=SUB), :] = y
+        return tuple(hs)
+    hs = lax.fori_loop(0, rows // SUB, step, tuple(h_sc[pl.ds(n*subs, subs), :] for n in range(states)))
+    for n in range(states):
+        h_sc[pl.ds(n*subs, subs), :] = hs[n]
+    total = get_tiles(y_sc, rows, subs) + ds_ref[...] * inner
+    ys_ref[...] = total
+    gate = gate_ref[...]
+    gated_ref[...] = (total * gate / (1.0 + jnp.exp(-gate))).astype(bf16)
+
+def scan_forward(keep, step_in, bc, wdt, dt_bias, d_skip, dec, inner, gate, chunk_rows=64):
+    rows, channels = inner.shape
+    subs = channels // LANES
+    states = bc.shape[1] // 2
+    rank = step_in.shape[1]
+    nch = rows // chunk_rows
+    span = states * subs
+    row_block = lambda w: pl.BlockSpec((chunk_rows, w), lambda i, *_: (i, 0))
+    whole = lambda a: pl.BlockSpec(a.shape, lambda i, *_: (0,) * a.ndim)
+    grid_spec = pltpu.PrefetchScalarGridSpec(
+        num_scalar_prefetch=1, grid=(nch,),
+        in_specs=[row_block(rank), row_block(2*states), whole(wdt), whole(dt_bias), whole(d_skip), whole(dec), row_block(channels), row_block(channels)],
+        out_specs=[pl.BlockSpec(((chunk_rows+1)*span, LANES), lambda i, *_: (i, 0)),
+                   pl.BlockSpec((chunk_rows*subs, LANES), lambda i, *_: (i, 0)), row_block(channels), row_block(channels)],
+        scratch_shapes=[pltpu.VMEM((span, LANES), f32), pltpu.VMEM((chunk_rows*subs, LANES), f32),
+                        pltpu.VMEM((chunk_rows*2*states, LANES), f32), pltpu.VMEM((chunk_rows*subs, LANES), f32)])
+    return pl.pallas_call(
+        functools.partial(fwd_body, states, subs), grid_spec=grid_spec,
+        out_shape=[jax.ShapeDtypeStruct((nch*(chunk_rows+1)*span, LANES), f32), jax.ShapeDtypeStruct((rows*subs, LANES), f32),
+                   jax.ShapeDtypeStruct((rows, channels), f32), jax.ShapeDtypeStruct((rows, channels), bf16)],
+        compiler_params=pltpu.CompilerParams(vmem_limit_bytes=48 << 20), name="scan_forward",
+    )(keep, step_in, bc, wdt, dt_bias, d_skip, dec, inner, gate)
+
+def fold_rows(parts, sub_iota):
+    if parts[0].shape[0] != SUB:
+        return jnp.concatenate([jnp.sum(p, axis=0, keepdims=True) for p in parts], axis=0)
+    up = sub_iota < 4
+    xs = [jnp.where(up, parts[n], parts[n+4]) + pltpu.roll(jnp.where(up, parts[n+4], parts[n]), 4, 0) for n in range(4)]
+    pair = (sub_iota & 3) < 2
+    ys = [jnp.where(pair, xs[n] + pltpu.roll(xs[n], 6, 0), xs[n+2] + pltpu.roll(xs[n+2], 2, 0)) for n in range(2)]
+    even = (sub_iota & 1) == 0
+    return jnp.where(even, ys[0] + pltpu.roll(ys[0], 7, 0), ys[1] + pltpu.roll(ys[1], 1, 0))
+
+def bwd_body(states, subs, keep_ref, bc_ref, wdt_ref, ds_ref, dst_ref, dec_ref, inner_ref, gate_ref, gg_ref, ys_ref, hs_ref, dl_ref,
+             gi_ref, gx_ref, gp_ref, gstep_ref, gbc_ref, red_ref, acc_ref, gh_sc, in_sc, gy_sc, bb_sc, gd_sc, go_sc, r_sc):
+    i = pl.program_id(0)
+    last = pl.num_programs(0) - 1
+    chunk = last - i
+    rows = inner_ref.shape[0]
+    all_rows = r_sc.shape[0] // (2 * states)
+    span = states * subs
+    @pl.when(i == 0)
+    def _():
+        gh_sc[...] = jnp.zeros_like(gh_sc)
+        acc_ref[...] = jnp.zeros_like(acc_ref)
+        red_ref[...] = jnp.zeros_like(red_ref)
+    gate = gate_ref[...]
+    sig = 1.0 / (1.0 + jnp.exp(-gate))
+    gg = gg_ref[...].astype(f32)
+    gy_all = gg * (gate * sig)
+    gx_ref[...] = (gg * ys_ref[...] * (sig * (1.0 + gate * (1.0 - sig)))).astype(bf16)
+    inner_all = inner_ref[...].astype(f32)
+    red_ref[pl.ds(0, 1), :] += jnp.sum(gy_all * inner_all, axis=0, keepdims=True)
+    put_tiles(gy_sc, gy_all, subs)
+    put_tiles(in_sc, inner_all, subs)
+    put_spread(bb_sc, bc_ref[...], 2 * states)
+    sub_iota = lax.broadcasted_iota(jnp.int32, (SUB, LANES), 0)
+    skip = dst_ref[...]
+    order = (0, 4, 2, 6, 1, 5, 3, 7)
+    def step(k, carried):
+        ghs = list(carried[:states]); accs = list(carried[states:])
+        ti = rows // SUB - 1 - k
+        for s in reversed(range(SUB)):
+            t = ti * SUB + s
+            row = ti * (subs * SUB) + s
+            d = dl_ref[pl.ds(row, subs, stride=SUB), :]
+            v = in_sc[pl.ds(row, subs, stride=SUB), :]
+            gy = gy_sc[pl.ds(row, subs, stride=SUB), :]
+            u = d * v
+            da = jnp.where(keep_ref[chunk*rows + t] > 0, d, BIG)
+            gd = gs = None
+            for g in range(states // SUB):
+                pb = [None]*SUB; pc = [None]*SUB
+                for o in order:
+                    n = g*SUB + o
+                    b = bb_sc[pl.ds((ti*2*states + n)*SUB + s, subs, stride=0), :]
+                    c = bb_sc[pl.ds((ti*2*states + states + n)*SUB + s, subs, stride=0), :]
+                    dec = dec_ref[pl.ds(n*subs, subs), :]
+                    before = hs_ref[pl.ds(pl.multiple_of(t*span + n*subs, subs), subs), :]
+                    after = hs_ref[pl.ds(pl.multiple_of((t+1)*span + n*subs, subs), subs), :]
+                    gh = c * gy + ghs[n]
+                    ghs[n] = jnp.exp2(da * dec) * gh
+                    q = ghs[n] * before
+                    gd = dec * q if gd is None else gd + dec * q
+                    accs[n] = accs[n] + q * d
+                    gs = gh * b if gs is None else gs + gh * b
+                    pb[o] = gh * u
+                    pc[o] = after * gy
+                r_sc[pl.ds(g*SUB*all_rows + chunk*rows + t, SUB, stride=all_rows), :] = fold_rows(pb, sub_iota)
+                r_sc[pl.ds((states + g*SUB)*all_rows + chunk*rows + t, SUB, stride=all_rows), :] = fold_rows(pc, sub_iota)
+            gd_sc[pl.ds(row, subs, stride=SUB), :] = gd * math.log(2.0) + gs * v
+            go_sc[pl.ds(row, subs, stride=SUB), :] = gy * skip + gs * d
+        return tuple(ghs + accs)
+    init = tuple(gh_sc[pl.ds(n*subs, subs), :] for n in range(states)) + tuple(acc_ref[pl.ds(n*subs, subs), :] for n in range(states))
+    out = lax.fori_loop(0, rows // SUB, step, init)
+    for n in range(states):
+        gh_sc[pl.ds(n*subs, subs), :] = out[n]
+        acc_ref[pl.ds(n*subs, subs), :] = out[states+n]
+    gi_ref[...] = get_tiles(go_sc, rows, subs)
+    d_all = get_tiles(dl_ref, rows, subs)
+    small = d_all * (1.0 - d_all * (0.5 - d_all * (1.0/6 - d_all * (1.0/24))))
+    slope = jnp.where(d_all < 0.03125, small, 1.0 - jnp.exp(-d_all))
+    gp = get_tiles(gd_sc, rows, subs) * slope
+    red_ref[pl.ds(1, 1), :] += jnp.sum(gp, axis=0, keepdims=True)
+    low = gp.astype(bf16)
+    gp_ref[...] = low
+    gstep_ref[...] = lax.dot_general(low, wdt_ref[...], (((1,), (1,)), ((), ())), preferred_element_type=f32)
+    @pl.when(i == last)
+    def _():
+        lane = lax.broadcasted_iota(jnp.int32, (LANES, LANES), 1)
+        total = jnp.zeros((all_rows, LANES), f32)
+        for n in range(2 * states):
+            pick = jnp.where(lane == n, 1.0, 0.0).astype(bf16)
+            total = total + jnp.dot(r_sc[pl.ds(n*all_rows, all_rows), :].astype(bf16), pick, preferred_element_type=f32)
+        gbc_ref[...] = total
+
+def scan_backward(keep, bc, wdt, d_skip, d_skip_tm, dec, inner, gate, gg, ysum, hs, delta_tm, chunk_rows=64):
+    rows, channels = inner.shape
+    subs = channels // LANES
+    states = bc.shape[1] // 2
+    rank = wdt.shape[0]
+    nch = rows // chunk_rows
+    span = states * subs
+    rev = lambda i, *_: (nch - 1 - i, 0)
+    row_block = lambda w: pl.BlockSpec((chunk_rows, w), rev)
+    whole = lambda a: pl.BlockSpec(a.shape, lambda i, *_: (0,) * a.ndim)
+    fixed = lambda shape: pl.BlockSpec(shape, lambda i, *_: (0, 0))
+    tm = pltpu.VMEM((chunk_rows*subs, LANES), f32)
+    grid_spec = pltpu.PrefetchScalarGridSpec(
+        num_scalar_prefetch=1, grid=(nch,),
+        in_specs=[row_block(2*states), whole(wdt), whole(d_skip), whole(d_skip_tm), whole(dec), row_block(channels), row_block(channels), row_block(channels), row_block(channels),
+                  pl.BlockSpec(((chunk_rows+1)*span, LANES), rev), pl.BlockSpec((chunk_rows*subs, LANES), rev)],
+        out_specs=[row_block(channels), row_block(channels), row_block(channels), row_block(rank), fixed((rows, LANES)), fixed((8, channels)), fixed((span, LANES))],
+        scratch_shapes=[pltpu.VMEM((span, LANES), f32), tm, tm, pltpu.VMEM((chunk_rows*2*states, LANES), f32), tm, tm, pltpu.VMEM((2*states*rows, LANES), f32)])
+    S = jax.ShapeDtypeStruct
+    return pl.pallas_call(
+        functools.partial(bwd_body, states, subs), grid_spec=grid_spec,
+        out_shape=[S((rows, channels), f32), S((rows, channels), bf16), S((rows, channels), bf16), S((rows, rank), f32), S((rows, LANES), f32), S((8, channels), f32), S((span, LANES), f32)],
+        compiler_params=pltpu.CompilerParams(vmem_limit_bytes=56 << 20), name="scan_backward",
+    )(keep, bc, wdt, d_skip, d_skip_tm, dec, inner, gate, gg, ysum, hs, delta_tm)
 
 
 def shards(
@@ -110,15 +259,12 @@
     d_skip,
     w_out,
 ):
-    f32 = jnp.float32
-    bf16 = jnp.bfloat16
     n_fsdp = lax.axis_size("fsdp")
     n_tensor = lax.axis_size("tensor")
     tok_rows = hidden.shape[0]
     group_rows = tok_rows * n_tensor
     rank_cols = w_dt.shape[1]
     state_cols = a_log.shape[1]
-    block_len = math.gcd(group_rows, 256)
     gathered = (
         lax.all_gather(w_in, "fsdp", axis=1, tiled=True),
         lax.all_gather(conv_weight, "fsdp", axis=0, tiled=True),
@@ -140,7 +286,6 @@
     )
     gain_full = gain_tensor.reshape(n_tensor, n_fsdp, -1).transpose(1, 0, 2).reshape(-1).astype(f32)
     offsets = distances(seq_lengths[0], pack_order[0], group_rows)
-    keep_mask = (offsets > 0).astype(f32)
     row_values = rows_all.astype(f32)
     normed = normalize(row_values, gain_full).astype(bf16)
     xz_all = jnp.einsum("gd,hcd->ghc", normed, w_in_t, preferred_element_type=f32)
@@ -160,30 +305,16 @@
     step_in = mixed[:, :rank_cols].astype(bf16)
     b_in = mixed[:, rank_cols : rank_cols + state_cols]
     c_out = mixed[:, rank_cols + state_cols :]
-    proj = jnp.einsum("gr,cr->gc", step_in, w_dt_t, preferred_element_type=f32)
-    gated, mixer_back = jax.vjp(
-        lambda proj_in, b_part, c_part, inner_in, gate_part, bias_part, rates_part, skip_part: mix_states(
-            proj_in,
-            b_part,
-            c_part,
-            inner_in,
-            gate_part,
-            bias_part,
-            rates_part,
-            skip_part,
-            keep_mask,
-            block_len,
-        ),
-        proj,
-        b_in,
-        c_out,
-        inner_low.astype(f32),
-        gate_in,
-        dt_b_t.astype(f32),
-        a_log_t.astype(f32),
-        d_skip_t.astype(f32),
-    )
-    gated_low = gated.astype(bf16)
+    keep = (offsets > 0).astype(jnp.int32)
+    bc = mixed[:, rank_cols:]
+    channels = inner_low.shape[1]
+    decays = -jnp.exp(a_log_t.astype(f32)).T
+    rates = (decays * math.log2(math.e)).reshape(-1, LANES)
+    w_dt_rows = w_dt_t.T
+    skip_row = d_skip_t.astype(f32)[None, :]
+    states, deltas, sums, gated_low = scan_forward(
+        keep, step_in, bc, w_dt_rows, dt_b_t.astype(f32)[None, :], skip_row, rates, inner_low, gate_in
+    )
     branch = lax.psum_scatter(
         jnp.dot(gated_low, w_out_t, preferred_element_type=f32),
         "tensor",
@@ -192,22 +323,21 @@
     )
     output = (hidden.astype(f32) + branch).astype(bf16)
     cot_all = lax.all_gather(cotangent, "tensor", axis=0, tiled=True)
-    grad_gated = (
-        jnp.einsum("gd,cd->gc", cot_all, w_out_t, preferred_element_type=f32)
-        .astype(bf16)
-        .astype(f32)
-    )
+    grad_gated = jnp.einsum("gd,cd->gc", cot_all, w_out_t, preferred_element_type=f32).astype(bf16)
     out_grad = jnp.einsum("gc,gd->cd", gated_low, cot_all, preferred_element_type=f32)
-    g_proj, g_b, g_c, g_inner_scan, g_gate, g_dt_bias, g_a_log, g_d_skip = mixer_back(grad_gated)
-    g_proj_low = g_proj.astype(bf16)
-    g_step = jnp.dot(g_proj_low, w_dt_t, preferred_element_type=f32)
+    g_inner_scan, g_gate, g_proj_low, g_step, g_bc, sums_c, acc_a = scan_backward(
+        keep, bc, w_dt_rows, skip_row, skip_row.reshape(-1, LANES), rates, inner_low, gate_in, grad_gated, sums, states, deltas
+    )
+    g_d_skip = sums_c[0]
+    g_dt_bias = sums_c[1]
+    g_a_log = (acc_a.reshape(state_cols, channels) * decays).T
     w_dt_grad = jnp.einsum("gc,gr->cr", g_proj_low, step_in, preferred_element_type=f32)
-    mixed_grad = lax.psum(jnp.concatenate([g_step, g_b, g_c], axis=1), "tensor")
+    mixed_grad = lax.psum(jnp.concatenate([g_step, g_bc[:, : 2 * state_cols]], axis=1), "tensor")
     mixed_low = mixed_grad.astype(bf16)
     g_inner = g_inner_scan + jnp.einsum("gk,ck->gc", mixed_low, w_x_t, preferred_element_type=f32)
     w_x_grad = jnp.einsum("gc,gk->ck", inner_low, mixed_low, preferred_element_type=f32)
     g_signal, g_conv_w, g_conv_b = front_back(g_inner)
-    g_xz = jnp.stack([g_signal, g_gate], axis=1).astype(bf16)
+    g_xz = jnp.stack([g_signal.astype(bf16), g_gate], axis=1)
     w_in_grad = jnp.einsum("ghc,gd->hcd", g_xz, normed, preferred_element_type=f32)
     g_normed = jnp.einsum("ghc,hcd->gd", g_xz, w_in_t, preferred_element_type=f32)
     gain_term = jax.vjp(lambda scales: normalize(row_values, scales), gain_full)[1](g_normed)[0]

time: 1680 us -> 868 us (0.52); the launches traced: 1660 us -> 866 us
  other arithmetic: 657 us -> 16.5 us
  local copies, waits for them, and re-layouts: 187 us -> 23.1 us
  Pallas kernels: 0 us -> 63.7 us
  loops' own time: 48.6 us -> 0 us
    mul x63 -> x1, other arithmetic: 190 us -> 0.02 us  [shards(): rates = (decays * math.log2(math.e)).reshape(-1, LANES)]
    while x86 -> x0, other arithmetic: 135 us -> none
    reduce_sum x9 -> x0, other arithmetic: 108 us -> none  [the longest x4 52.2 us: block_scan(): return (closing, jnp.sum(states * c_out[:, None, :], axis=2))]
    add x68 -> x0, other arithmetic: 96.9 us -> none  [the longest x64 57.8 us: carry_step(): return (members[0] * current + members[1], current)]
    while x433 -> x0, local copies, waits for them, and re-layouts: 96.4 us -> none
    add_any x38 -> x0, other arithmetic: 74.9 us -> none  [the longest x2 31 us: block_scan(): running = factors[:, offset] * running + drives[:, offset]]
    pallas_call x0 -> x2, Pallas kernels: none -> 63.7 us  [the longest x1 45.2 us: scan_backward(): pl.pallas_call(functools.partial(bwd_body, states, subs), grid_spec=grid_...]
    another operation x8 -> x0, loops' own time: 48.6 us -> none  [the longest x2 46.9 us: selective(): _, outputs = lax.scan(jax.checkpoint(block_step), initial, pieces)]
  transfers between devices with their start and end apart: 13 -> 13, of which waited for: 10 -> 11; matrix products, arithmetic and copies ran while one was open for 4% -> 7% of each run, Pallas kernels for 0% -> 0%
where the time goes in v1:
time: 868 us; the launch traced here: 866 us
  waiting for transfers between devices  542 us (62%)
  blocking collectives  146 us (17%)
  Pallas kernels  63.7 us (7%)
  matrix products  56.9 us (7%)
  local copies, waits for them, and re-layouts  23.1 us (3%)
  between operations  17 us (2%)
  other arithmetic  16.5 us (2%)
    reduce_scatter x1, waiting for transfers between devices, shards(): lax.psum_scatter(w_in_grad, 'fsdp', scatter_dimension=1, tiled=True)  120 us
    reduce_scatter x1, waiting for transfers between devices, shards(): lax.psum_scatter(jnp.dot(gated_low, w_out_t, preferred_element_type=f32),...  77.8 us
    reduce_scatter x1, waiting for transfers between devices, shards(): lax.psum_scatter(out_grad, 'fsdp', scatter_dimension=0, tiled=True)  75.6 us
    all_gather x1, waiting for transfers between devices, shards(): lax.all_gather(w_in, 'fsdp', axis=1, tiled=True)  50 us
    unnamed x3, blocking collectives  48.7 us
    pallas_call x1, Pallas kernels, scan_backward(): pl.pallas_call(functools.partial(bwd_body, states, subs), grid_spec=grid_...  45.2 us
    all_gather x1, waiting for transfers between devices, shards(): lax.all_gather(w_out, 'fsdp', axis=0, tiled=True)  39 us
    reduce_scatter x1, waiting for transfers between devices, shards(): lax.psum_scatter(w_x_grad, 'fsdp', scatter_dimension=0, tiled=True)  38.6 us
  transfers between devices with their start and end apart: 13, of which 11 were waited for; matrix products, arithmetic and copies ran while one was open for 7% of the time, Pallas kernels for 0%

profile of v1, /device:TPU:8, one launch (start us, length us, event | category | flops | bytes accessed | tf_op | source)
XLA Modules:
  0.0 865.6 jit_solution(18413654532077000123)
XLA Ops:
  7.3 0.7 all-gather.9.cloned.1.call-update
  8.1 0.7 all-gather.15.cloned.1.call-update
  8.8 0.7 all-gather.13.cloned.1.call-update
  10.2 0.6 fusion.28
  11.7 13.7 %all-reduce.10 = bf16[512]{0:T(512)(128)(2,1)S(1)} all-reduce(bf16[512]{0:T(512)(128)(2,1)S(1)} %dynamic-update-slice), channel_id=1, replica_groups=mesh['fsdp'=8,'tensor'=4] {'fsdp'}, use_global_device_ids=true, to_apply=%add.10 | all-reduce | flops 512 | bytes 2048
  25.3 12.7 %all-gather.1 = bf16[4,1,512]{2,1,0:T(2,128)(2,1)S(1)} all-gather(bf16[1,1,512]{2,1,0:T(2,128)(2,1)S(1)} %reshape.166), channel_id=1, replica_groups=mesh['fsdp'=8,'tensor'=4] {'tensor'}, dimensions={0}, use_global_device_ids=true | all-gather | bytes 5120 | tf_op jit(solution)/shard_map/all_gather | solution.py:285
  38.2 7.6 all-gather
  45.8 9.0 %all_gather.49 = bf16[1024,16]{0,1:T(8,128)(2,1)S(1)} all-gather(bf16[128,16]{0,1:T(8,128)(2,1)S(1)} %copy-done.24), channel_id=1, replica_groups=mesh['fsdp'=8,'tensor'=4] {'fsdp'}, dimensions={0}, use_global_device_ids=true | all-gather | bytes 36864 | tf_op jit(solution)/shard_map/all_gather | solution.py:275
  55.4 7.6 all-gather.3
  63.0 8.9 %all-gather.2 = bf16[8,1,128]{2,1,0:T(2,128)(2,1)S(1)} all-gather(bf16[1,1,128]{2,1,0:T(2,128)(2,1)S(1)} %bitcast.103), channel_id=1, replica_groups=mesh['fsdp'=8,'tensor'=4] {'fsdp'}, dimensions={0}, use_global_device_ids=true | all-gather | bytes 2304 | tf_op jit(solution)/shard_map/all_gather | solution.py:274
  71.9 7.7 all_gather.40
  79.6 9.5 %all_gather.46 = bf16[1024,128]{0,1:T(8,128)(2,1)S(1)} all-gather(bf16[128,128]{0,1:T(8,128)(2,1)S(1)} %copy.48), channel_id=1, replica_groups=mesh['fsdp'=8,'tensor'=4] {'fsdp'}, dimensions={0}, use_global_device_ids=true | all-gather | bytes 294912 | tf_op jit(solution)/shard_map/all_gather | solution.py:273
  89.1 8.4 all_gather.45
  97.6 0.6 fusion.24
  98.3 2.1 fusion.4
  100.4 1.3 all-gather.15.cloned.1.call-done
  101.6 39.0 %all-gather.13.cloned.1.call-done = bf16[1024,2048]{1,0:T(8,128)(2,1)} async-done(((bf16[128,2048]{1,0:T(8,128)(2,1)}), bf16[1024,2048]{1,0:T(8,128)(2,1)}) %all-gather.13.cloned.1.call-update) | async-done | bytes 4194320 | tf_op jit(solution)/shard_map/all_gather | solution.py:277
  140.6 6.2 convolution_convert_fusion.gg_ref
  146.8 50.0 %all-gather.11.cloned.1.call-done = bf16[2,1024,2048]{2,1,0:T(8,128)(2,1)} async-done(((bf16[2,128,2048]{2,1,0:T(8,128)(2,1)}), bf16[2,1024,2048]{2,1,0:T(8,128)(2,1)}) %all-gather.11.cloned.1.call-update) | async-done | bytes 8388624 | tf_op jit(solution)/shard_map/all_gather | solution.py:269
  196.8 7.7 fusion.10
  205.2 1.2 copy-done.8
  206.5 0.6 copy-done.10
  207.1 0.8 copy-done.12
  207.9 3.2 multiply_convert_fusion
  211.1 1.2 fusion.31
  212.6 3.2 slice_bitcast_fusion.gate_ref
  215.8 34.8 %all-reduce.20.cloned.1.call-done = f32[512,160]{1,0:T(8,128)} async-done(((f32[512,160]{1,0:T(8,128)}), f32[512,160]{1,0:T(8,128)}) %all-reduce.20.cloned.1.call-update) | async-done | bytes 327696 | tf_op jit(solution)/shard_map/psum | solution.py:304
  250.6 1.0 slice.81.bc_ref
  251.6 1.1 slice.93.step_ref
  252.7 18.5 %scan_forward.1 = (f32[66560,128]{1,0:T(8,128)}, f32[4096,128]{1,0:T(8,128)S(1)}, f32[512,1024]{1,0:T(8,128)}, bf16[512,1024]{1,0:T(8,128)(2,1)S(1)}) custom-call(s32[512]{0:T(512)S(1)} %get-tuple-element.68.keep_ref, bf16[512,128]{1,0:T(8,128)(2,1)S(1)} %slice.93.step_ref, f32[512,32]{1,0:T(8,128)S(1)} %slice.81.bc_ref, bf16[128,1024]{1,0:T(8,128)(2,1)S(1)} %bitcast.79, ...), custom_call_target="tpu_custom_call" | custom-call | tf_op jit(solution)/shard_map/scan_forward/pallas_call | solution.py:120
  271.2 1.4 copy-done.4
  272.6 45.2 %scan_backward.1 = (f32[512,1024]{1,0:T(8,128)}, bf16[512,1024]{1,0:T(8,128)(2,1)}, bf16[512,1024]{1,0:T(8,128)(2,1)}, f32[512,128]{1,0:T(8,128)}, f32[512,128]{...) custom-call(s32[512]{0:T(512)} %copy-done.7, f32[512,32]{1,0:T(8,128)} %copy-done.3, bf16[128,1024]{1,0:T(8,128)(2,1)} %bitcast.80, ...), custom_call_target="tpu_custom_call" | custom-call | tf_op jit(solution)/shard_map/scan_backward/pallas_call | solution.py:239
  317.7 1.9 pad_maximum_fusion.3
  319.6 25.8 %all-reduce.21 = bf16[512,160]{1,0:T(8,128)(2,1)} all-reduce(f32[512,160]{1,0:T(8,128)} %pad_maximum_fusion.3), channel_id=1, replica_groups=mesh['fsdp'=8,'tensor'=4] {'tensor'}, use_global_device_ids=true, to_apply=%region_6.7 | all-reduce | flops 81920 | bytes 491520 | tf_op jit(solution)/shard_map/psum | solution.py:335
  345.4 4.6 multiply_reduce_fusion.3
  350.9 1.9 copy-done.9
  352.8 2.3 fusion.25
  355.1 1.0 copy.54
  356.3 10.5 %fusion.3 = (f32[2048]{0:T(1024)S(1)}, f32[512,2048]{1,0:T(8,128)}) fusion(bf16[512,2048]{1,0:T(8,128)(2,1)S(1)} %copy-done.17, f32[512]{0:T(512)S(1)} %add_rsqrt_fusion, bf16[2,1024,2048]{2,1,0:T(8,128)(2,1)} %all-gather.11.cloned.1.call-done, bf16[512,1,1024]{2,0,1:T(8,128)(2,1)} %bitcast.104, bf16[512,1,1024]{2,0,1:T(8,128)(2,1)} %get-tuple-element.50), kind=kOutput, calls=%fused_computation.5 | convolution fusion | flops 4300208128 | bytes 16787456 | tf_op jit(solution)/shard_map/ghc,hcd->gd/dot_general | solution.py:342
  367.1 6.5 fusion.32
  373.7 1.0 reshape.157
  374.7 0.7 fusion.20
  375.4 2.2 fusion.29
  377.7 1.2 fusion.34
  379.1 7.2 fusion.33
  386.3 1.5 copy-done.18
  388.1 9.6 %fusion.8 = f32[2,1024,2048]{2,1,0:T(8,128)} fusion(bf16[512,1,1024]{2,0,1:T(8,128)(2,1)} %bitcast.105, bf16[512,1,1024]{2,0,1:T(8,128)(2,1)S(1)} %copy-done.20, bf16[512,2048]{1,0:T(8,128)(2,1)S(1)} %copy-done.18, f32[2048]{0:T(1024)S(1)} %reshape.158, f32[512]{0:T(512)S(1)} %add_rsqrt_fusion), kind=kOutput, calls=%fused_computation.35 | convolution fusion | flops 4300210176 | bytes 20981760 | tf_op jit(solution)/shard_map/ghc,gd->hcd/dot_general | solution.py:341
  397.7 0.6 copy-done.33
  398.3 0.6 dynamic-slice.1
  401.0 12.6 %all-reduce.11 = f32[2048]{0:T(1024)S(1)} all-reduce(f32[2048]{0:T(1024)S(1)} %reshape.156), channel_id=4, replica_groups=mesh['fsdp'=8,'tensor'=4] {'tensor'}, use_global_device_ids=true, to_apply=%region_11.12.clone | all-reduce | flops 2048 | bytes 16384
  413.7 0.8 fusion.26
  414.6 22.4 %all-reduce.16 = (f32[512]{0:T(512)S(1)}, f32[1024]{0:T(1024)S(1)}, f32[1024]{0:T(1024)S(1)}, f32[1024]{0:T(1024)S(1)}) all-reduce(f32[512]{0:T(512)S(1)} %dynamic-slice.2, f32[1024]{0:T(1024)S(1)} %get-tuple-element.34, f32[1024]{0:T(1024)S(1)} %bitcast.100, f32[1024]{0:T(1024)S(1)} %bitcast.99), channel_id=5, replica_groups=mesh['fsdp'=8,'tensor'=4] {'fsdp'}, use_global_device_ids=true, to_apply=%region_12.13.clone | all-reduce | flops 3584 | bytes 28672
  437.0 0.6 dynamic-slice.10
  437.6 0.6 dynamic-slice.6
  439.3 1.5 copy.55
  440.8 30.9 %reduce-scatter.13.cloned.1.call-done = f32[128,2048]{1,0:T(8,128)} async-done(((f32[512,2048]{1,0:T(8,128)}), f32[128,2048]{1,0:T(8,128)}) %reduce-scatter.13.cloned.1.call-update) | async-done | bytes 1048592 | tf_op jit(solution)/shard_map/reduce_scatter | solution.py:346
  471.8 1.6 fusion.14
  473.4 77.8 %reduce-scatter.11.cloned.1.call-done = f32[128,2048]{1,0:T(8,128)} async-done(((f32[512,2048]{1,0:T(8,128)}), f32[128,2048]{1,0:T(8,128)}) %reduce-scatter.11.cloned.1.call-update) | async-done | bytes 1048592 | tf_op jit(solution)/shard_map/reduce_scatter | solution.py:318
  551.2 2.8 fusion.12
  553.9 33.0 %reduce-scatter.21.cloned.1.call-done = f32[128,16]{0,1:T(8,128)} async-done(((f32[1024,16]{0,1:T(8,128)}), f32[128,16]{0,1:T(8,128)}) %reduce-scatter.21.cloned.1.call-update) | async-done | bytes 8208 | tf_op jit(solution)/shard_map/reduce_scatter | solution.py:358
  587.0 37.7 %reduce-scatter.19.cloned.1.call-done = f32[128,128]{1,0:T(8,128)} async-done(((f32[1024,128]{1,0:T(8,128)}), f32[128,128]{1,0:T(8,128)}) %reduce-scatter.19.cloned.1.call-update) | async-done | bytes 65552 | tf_op jit(solution)/shard_map/reduce_scatter | solution.py:356
  624.7 38.6 %reduce-scatter.17.cloned.1.call-done = f32[128,160]{0,1:T(8,128)} async-done(((f32[1024,160]{0,1:T(8,128)}), f32[128,160]{0,1:T(8,128)}) %reduce-scatter.17.cloned.1.call-update) | async-done | bytes 81936 | tf_op jit(solution)/shard_map/reduce_scatter | solution.py:355
  663.3 75.6 %reduce-scatter.23.cloned.1.call-done = f32[128,2048]{1,0:T(8,128)} async-done(((f32[1024,2048]{1,0:T(8,128)}), f32[128,2048]{1,0:T(8,128)}) %reduce-scatter.23.cloned.1.call-update) | async-done | bytes 1048592 | tf_op jit(solution)/shard_map/reduce_scatter | solution.py:360
  738.9 120.1 %reduce-scatter.15.cloned.1.call-done = f32[2,128,2048]{2,1,0:T(8,128)} async-done(((f32[2,1024,2048]{2,1,0:T(8,128)}), f32[2,128,2048]{2,1,0:T(8,128)}) %reduce-scatter.15.cloned.1.call-update) | async-done | bytes 2097168 | tf_op jit(solution)/shard_map/reduce_scatter | solution.py:352
  (119 shorter events, 6.1 us)
Async XLA Ops:
  7.2 3.0 copy-start.25
  7.2 4.2 copy-start.30
  7.2 31.0 %copy-start.27 = (bf16[128]{0:T(256)(128)(2,1)S(1)}, bf16[128]{0:T(256)(128)(2,1)}, u32[]{:S(2)}) copy-start(bf16[128]{0:T(256)(128)(2,1)} %param.21) | copy-start | bytes 772
  7.2 38.6 %copy-start.24 = (bf16[128,16]{0,1:T(8,128)(2,1)S(1)}, bf16[128,16]{0,1:T(8,128)(2,1)}, u32[]{:S(2)}) copy-start(bf16[128,16]{0,1:T(8,128)(2,1)} %param.25) | copy-start | bytes 12292
  7.2 47.7 %copy-start.23 = (bf16[128,128]{1,0:T(8,128)(2,1)S(1)}, bf16[128,128]{1,0:T(8,128)(2,1)}, u32[]{:S(2)}) copy-start(bf16[128,128]{1,0:T(8,128)(2,1)} %param.23) | copy-start | bytes 98308
  7.2 47.8 %copy-start.32 = (s32[1,3]{1,0:T(1,128)S(1)}, s32[1,3]{1,0:T(1,128)}, u32[]{:S(2)}) copy-start(s32[1,3]{1,0:T(1,128)} %param.17) | copy-start | bytes 40
  7.2 47.8 %copy-start.31 = (s32[1,3]{1,0:T(1,128)S(1)}, s32[1,3]{1,0:T(1,128)}, u32[]{:S(2)}) copy-start(s32[1,3]{1,0:T(1,128)} %param.16) | copy-start | bytes 40
  7.3 48.2 %copy-start.28 = (bf16[128]{0:T(256)(128)(2,1)S(1)}, bf16[128]{0:T(256)(128)(2,1)}, u32[]{:S(2)}) copy-start(bf16[128]{0:T(256)(128)(2,1)} %param.26) | copy-start | bytes 772
  7.3 55.8 %copy-start.29 = (bf16[128]{0:T(256)(128)(2,1)S(1)}, bf16[128]{0:T(256)(128)(2,1)}, u32[]{:S(2)}) copy-start(bf16[128]{0:T(256)(128)(2,1)} %param.24) | copy-start | bytes 772
  7.3 64.6 %copy-start.26 = (bf16[128,4]{0,1:T(4,128)(2,1)S(1)}, bf16[128,4]{0,1:T(4,128)(2,1)}, u32[]{:S(2)}) copy-start(bf16[128,4]{0,1:T(4,128)(2,1)} %param.20) | copy-start | bytes 3076
  7.3 81.9 %copy-start.22 = (bf16[128,160]{0,1:T(8,128)(2,1)S(1)}, bf16[128,160]{0,1:T(8,128)(2,1)}, u32[]{:S(2)}) copy-start(bf16[128,160]{0,1:T(8,128)(2,1)} %param.22) | copy-start | bytes 122884
  7.3 91.0 %all-gather.9.cloned.1.call-start = ((), (), s32[]{:S(2)}) async-start(), calls=%async_computation.8 | async-start | bytes 2621440 | tf_op jit(solution)/shard_map/all_gather | solution.py:284
  8.0 93.6 %all-gather.15.cloned.1.call-start = ((), (), s32[]{:S(2)}) async-start(), calls=%async_computation.13 | async-start | bytes 2621440 | tf_op jit(solution)/shard_map/all_gather | solution.py:325
  8.8 131.8 %all-gather.13.cloned.1.call-start = ((), (), s32[]{:S(2)}) async-start(), calls=%async_computation.11 | async-start | bytes 4718592 | tf_op jit(solution)/shard_map/all_gather | solution.py:277
  9.5 187.3 %all-gather.11.cloned.1.call-start = ((), (), s32[]{:S(2)}) async-start(), calls=%async_computation.9 | async-start | bytes 9437184 | tf_op jit(solution)/shard_map/all_gather | solution.py:269
  10.1 240.5 %all-reduce.20.cloned.1.call-start = ((), (), s32[]{:S(2)}) async-start(), calls=%async_computation.10 | async-start | bytes 1048576 | tf_op jit(solution)/shard_map/psum | solution.py:304
  54.9 197.7 %copy-start.5 = (f32[128,128]{1,0:T(8,128)}, f32[128,128]{1,0:T(8,128)S(1)}, u32[]{:S(2)}) copy-start(f32[128,128]{1,0:T(8,128)S(1)} %reshape.154.dec_ref) | copy-start | bytes 196612
  89.1 163.5 %copy-start.2 = (bf16[1024,128]{0,1:T(8,128)(2,1)}, bf16[1024,128]{0,1:T(8,128)(2,1)S(1)}, u32[]{:S(2)}) copy-start(bf16[1024,128]{0,1:T(8,128)(2,1)S(1)} %all_gather.46) | copy-start | bytes 786436
  98.2 154.5 %copy-start.6 = (f32[8,1,128]{2,0,1:T(8,128)}, f32[8,1,128]{2,0,1:T(8,128)S(1)}, u32[]{:S(2)}) copy-start(f32[8,1,128]{2,0,1:T(8,128)S(1)} %get-tuple-element.64) | copy-start | bytes 12292
  98.2 154.5 %copy-start.7 = (s32[512]{0:T(512)}, s32[512]{0:T(512)S(1)}, u32[]{:S(2)}) copy-start(s32[512]{0:T(512)S(1)} %get-tuple-element.68.keep_ref) | copy-start | bytes 6148
  204.5 2.0 copy-start.8
  204.7 2.4 copy-start.10
  205.0 2.9 copy-start.12
  205.2 5.9 copy-start.13
  211.1 41.6 %copy-start = (bf16[512,1024]{1,0:T(8,128)(2,1)}, bf16[512,1024]{1,0:T(8,128)(2,1)S(1)}, u32[]{:S(2)}) copy-start(bf16[512,1024]{1,0:T(8,128)(2,1)S(1)} %get-tuple-element.48.inner_ref) | copy-start | bytes 3145732
  212.4 227.0 %reduce-scatter.25.cloned.1.call-start = ((), (), s32[]{:S(2)}) async-start(), calls=%async_computation.20 | async-start | bytes 589824
  251.6 21.0 %copy-start.3 = (f32[512,32]{1,0:T(8,128)}, f32[512,32]{1,0:T(8,128)S(1)}, u32[]{:S(2)}) copy-start(f32[512,32]{1,0:T(8,128)S(1)} %slice.81.bc_ref) | copy-start | bytes 196612
  271.2 1.4 copy-start.4
  272.6 72.9 %copy-start.11 = (f32[509,1024]{1,0:T(8,128)S(1)}, f32[509,1024]{1,0:T(8,128)}, u32[]{:S(2)}) copy-start(f32[509,1024]{1,0:T(8,128)} %copy-done.10) | copy-start | bytes 6254596
  350.6 2.2 copy-start.9
  352.8 3.5 copy-start.17
  356.2 115.6 %reduce-scatter.13.cloned.1.call-start = ((), (), s32[]{:S(2)}) async-start(), calls=%async_computation.14 | async-start | bytes 5242880 | tf_op jit(solution)/shard_map/reduce_scatter | solution.py:346
  366.8 184.4 %reduce-scatter.11.cloned.1.call-start = ((), (), s32[]{:S(2)}) async-start(), calls=%async_computation.12 | async-start | bytes 5242880 | tf_op jit(solution)/shard_map/reduce_scatter | solution.py:318
  373.6 1.8 copy-start.21
  373.6 4.1 copy-start.1
  373.6 4.1 copy-start.16
  373.6 213.4 %reduce-scatter.21.cloned.1.call-start = ((), (), s32[]{:S(2)}) async-start(), calls=%async_computation.18 | async-start | bytes 73728 | tf_op jit(solution)/shard_map/reduce_scatter | solution.py:358
  375.4 249.3 %reduce-scatter.19.cloned.1.call-start = ((), (), s32[]{:S(2)}) async-start(), calls=%async_computation.17 | async-start | bytes 589824 | tf_op jit(solution)/shard_map/reduce_scatter | solution.py:356
  377.7 285.6 %reduce-scatter.17.cloned.1.call-start = ((), (), s32[]{:S(2)}) async-start(), calls=%async_computation.16 | async-start | bytes 737280 | tf_op jit(solution)/shard_map/reduce_scatter | solution.py:355
  379.0 359.9 %reduce-scatter.23.cloned.1.call-start = ((), (), s32[]{:S(2)}) async-start(), calls=%async_computation.19 | async-start | bytes 9437184 | tf_op jit(solution)/shard_map/reduce_scatter | solution.py:360
  386.3 1.6 copy-start.18
  386.3 1.9 copy-start.20
  386.3 472.7 %reduce-scatter.15.cloned.1.call-start = ((), (), s32[]{:S(2)}) async-start(), calls=%async_computation.15 | async-start | bytes 18874368 | tf_op jit(solution)/shard_map/reduce_scatter | solution.py:352
  397.7 0.7 copy-start.33
  397.7 74.1 %copy-start.14 = (bf16[128,2048]{1,0:T(8,128)(2,1)S(1)}, bf16[128,2048]{1,0:T(8,128)(2,1)}, u32[]{:S(2)}) copy-start(bf16[128,2048]{1,0:T(8,128)(2,1)} %param.14) | copy-start | bytes 1572868
  398.3 152.9 %copy-start.19 = (bf16[128,2048]{1,0:T(8,128)(2,1)S(1)}, bf16[128,2048]{1,0:T(8,128)(2,1)}, u32[]{:S(2)}) copy-start(bf16[128,2048]{1,0:T(8,128)(2,1)} %param.15) | copy-start | bytes 1572868
  471.8 79.4 %copy-start.15 = (f32[128,2048]{1,0:T(8,128)S(1)}, f32[128,2048]{1,0:T(8,128)}, u32[]{:S(2)}) copy-start(f32[128,2048]{1,0:T(8,128)} %reduce-scatter.13.cloned.1.call-done) | copy-start | bytes 3145732
Sparse Core Ops, SparseCore 0:
  9.7 45.7 all-gather.8
  57.1 44.5 all-gather.14
  103.5 37.0 all-gather.12
  142.4 54.3 all-gather.10
  212.5 38.0 all-reduce.19
  356.3 35.7 reduce-scatter.24
  394.5 77.1 reduce-scatter.12
  474.0 77.0 reduce-scatter.10
  555.0 31.9 reduce-scatter.20
  590.5 34.1 reduce-scatter.18
  628.7 34.5 reduce-scatter.16
  667.6 71.2 reduce-scatter.22
  743.0 115.9 reduce-scatter.14

commit v2 on v1

v2 whole, which is shorter than its diff:
```python
import functools
import math

import jax
import jax.numpy as jnp
from jax import lax
from jax.experimental import pallas as pl
from jax.experimental.pallas import tpu as pltpu
from jax.sharding import PartitionSpec as P

EPSILON = 1e-05
f32 = jnp.float32
bf16 = jnp.bfloat16
BIG = 1e30
LANES = 128
SUB = 8


def cost(micros):
    return pl.CostEstimate(flops=int(micros * 1e9), transcendentals=0, bytes_accessed=int(micros * 1e6))


def tile_rows(ti, j, subs):
    return pl.ds((ti * subs + j) * SUB, SUB)


def put_tiles(ref, value, subs):
    for ti in range(value.shape[0] // SUB):
        for j in range(subs):
            ref[tile_rows(ti, j, subs), :] = value[ti * SUB : (ti + 1) * SUB, j * LANES : (j + 1) * LANES]


def get_tiles(ref, rows, subs):
    lines = []
    for ti in range(rows // SUB):
        lines.append(jnp.concatenate([ref[tile_rows(ti, j, subs), :] for j in range(subs)], axis=1))
    return jnp.concatenate(lines, axis=0)


def put_spread(ref, value, count):
    for ti in range(value.shape[0] // SUB):
        for n in range(count):
            ref[pl.ds((ti * count + n) * SUB, SUB), :] = jnp.broadcast_to(
                value[ti * SUB : (ti + 1) * SUB, n : n + 1], (SUB, LANES)
            )


def fwd_body(
    states, subs, keep_ref, step_ref, bc_ref, wdt_ref, db_ref, ds_ref, dec_ref, inner_ref, gate_ref, h0_ref,
    hs_ref, dl_ref, ys_ref, gated_ref, h_ref, du_sc, bb_sc, y_sc,
):
    chunk = pl.program_id(0)
    rows = step_ref.shape[0]
    span = states * subs

    @pl.when(chunk == 0)
    def _():
        h_ref[...] = h0_ref[...]

    raw = jnp.dot(step_ref[...], wdt_ref[...], preferred_element_type=f32) + db_ref[...]
    delta = jnp.maximum(raw, 0.0) + jnp.log1p(jnp.exp(-jnp.abs(raw)))
    inner = inner_ref[...].astype(f32)
    put_tiles(dl_ref, delta, subs)
    put_tiles(du_sc, delta * inner, subs)
    put_spread(bb_sc, bc_ref[...], 2 * states)
    hs_ref[pl.ds(0, span), :] = h_ref[...]
    decs = [dec_ref[pl.ds(n * subs, subs), :] for n in range(states)]

    def step(ti, hs):
        hs = list(hs)
        for s in range(SUB):
            t = ti * SUB + s
            row = ti * (subs * SUB) + s
            d = dl_ref[pl.ds(row, subs, stride=SUB), :]
            u = du_sc[pl.ds(row, subs, stride=SUB), :]
            d = jnp.where(keep_ref[chunk * rows + t] > 0, d, BIG)
            y = None
            for n in range(states):
                b = bb_sc[pl.ds((ti * 2 * states + n) * SUB + s, subs, stride=0), :]
                c = bb_sc[pl.ds((ti * 2 * states + states + n) * SUB + s, subs, stride=0), :]
                hs[n] = jnp.exp2(d * decs[n]) * hs[n] + u * b
                hs_ref[pl.ds(pl.multiple_of((t + 1) * span + n * subs, subs), subs), :] = hs[n]
                y = c * hs[n] if y is None else y + c * hs[n]
            y_sc[pl.ds(row, subs, stride=SUB), :] = y
        return tuple(hs)

    start = tuple(h_ref[pl.ds(n * subs, subs), :] for n in range(states))
    hs = lax.fori_loop(0, rows // SUB, step, start)
    for n in range(states):
        h_ref[pl.ds(n * subs, subs), :] = hs[n]
    total = get_tiles(y_sc, rows, subs) + ds_ref[...] * inner
    ys_ref[...] = total
    gate = gate_ref[...]
    gated_ref[...] = (total * gate / (1.0 + jnp.exp(-gate))).astype(bf16)


def scan_forward(keep, step_in, bc, wdt, dt_bias, d_skip, dec, inner, gate, h0, chunk_rows=64):
    rows, channels = inner.shape
    subs = channels // LANES
    states = bc.shape[1] // 2
    rank = step_in.shape[1]
    chunks = rows // chunk_rows
    span = states * subs

    def row_block(width):
        return pl.BlockSpec((chunk_rows, width), lambda i, *_: (i, 0))

    def whole(a):
        return pl.BlockSpec(a.shape, lambda i, *_: (0, 0))

    grid_spec = pltpu.PrefetchScalarGridSpec(
        num_scalar_prefetch=1,
        grid=(chunks,),
        in_specs=[
            row_block(rank), row_block(2 * states), whole(wdt), whole(dt_bias), whole(d_skip), whole(dec),
            row_block(channels), row_block(channels), whole(h0),
        ],
        out_specs=[
            pl.BlockSpec(((chunk_rows + 1) * span, LANES), lambda i, *_: (i, 0)),
            pl.BlockSpec((chunk_rows * subs, LANES), lambda i, *_: (i, 0)),
            row_block(channels), row_block(channels), whole(h0),
        ],
        scratch_shapes=[
            pltpu.VMEM((chunk_rows * subs, LANES), f32),
            pltpu.VMEM((chunk_rows * 2 * states, LANES), f32),
            pltpu.VMEM((chunk_rows * subs, LANES), f32),
        ],
    )
    made = jax.ShapeDtypeStruct
    return pl.pallas_call(
        functools.partial(fwd_body, states, subs),
        grid_spec=grid_spec,
        out_shape=[
            made((chunks * (chunk_rows + 1) * span, LANES), f32), made((rows * subs, LANES), f32),
            made((rows, channels), f32), made((rows, channels), bf16), made((span, LANES), f32),
        ],
        compiler_params=pltpu.CompilerParams(vmem_limit_bytes=58 << 20),
        cost_estimate=cost(1.0 * rows * channels / (512 * 1024)),
        name="scan_forward",
    )(keep, step_in, bc, wdt, dt_bias, d_skip, dec, inner, gate, h0)


def fold_rows(parts, sub_iota):
    if parts[0].shape[0] != SUB:
        return jnp.concatenate([jnp.sum(p, axis=0, keepdims=True) for p in parts], axis=0)
    upper = sub_iota < 4
    xs = [
        jnp.where(upper, parts[n], parts[n + 4]) + pltpu.roll(jnp.where(upper, parts[n + 4], parts[n]), 4, 0)
        for n in range(4)
    ]
    pair = (sub_iota & 3) < 2
    ys = [
        jnp.where(pair, xs[n] + pltpu.roll(xs[n], 6, 0), xs[n + 2] + pltpu.roll(xs[n + 2], 2, 0))
        for n in range(2)
    ]
    even = (sub_iota & 1) == 0
    return jnp.where(even, ys[0] + pltpu.roll(ys[0], 7, 0), ys[1] + pltpu.roll(ys[1], 1, 0))


def bwd_body(
    states, subs, keep_ref, bc_ref, wdt_ref, ds_ref, dst_ref, dec_ref, inner_ref, gate_ref, gg_ref, ys_ref, hs_ref,
    dl_ref, gh0_ref, gi_ref, gx_ref, gp_ref, mixed_ref, red_ref, acc_ref, gh_ref, in_sc, gy_sc, bb_sc, gd_sc, go_sc,
    r_sc,
):
    i = pl.program_id(0)
    last = pl.num_programs(0) - 1
    chunk = last - i
    rows = inner_ref.shape[0]
    all_rows = r_sc.shape[0] // (2 * states)
    span = states * subs
    rank = wdt_ref.shape[0]

    @pl.when(i == 0)
    def _():
        gh_ref[...] = gh0_ref[...]
        acc_ref[...] = jnp.zeros_like(acc_ref)
        red_ref[...] = jnp.zeros_like(red_ref)

    gate = gate_ref[...]
    sig = 1.0 / (1.0 + jnp.exp(-gate))
    gg = gg_ref[...].astype(f32)
    gy_all = gg * (gate * sig)
    gx_ref[...] = (gg * ys_ref[...] * (sig * (1.0 + gate * (1.0 - sig)))).astype(bf16)
    inner_all = inner_ref[...].astype(f32)
    red_ref[pl.ds(0, 1), :] += jnp.sum(gy_all * inner_all, axis=0, keepdims=True)
    put_tiles(gy_sc, gy_all, subs)
    put_tiles(in_sc, inner_all, subs)
    put_spread(bb_sc, bc_ref[...], 2 * states)
    sub_iota = lax.broadcasted_iota(jnp.int32, (SUB, LANES), 0)
    skip = dst_ref[...]
    order = (0, 4, 2, 6, 1, 5, 3, 7)

    def step(k, carried):
        ghs = list(carried[:states])
        accs = list(carried[states:])
        ti = rows // SUB - 1 - k
        for s in reversed(range(SUB)):
            t = ti * SUB + s
            row = ti * (subs * SUB) + s
            d = dl_ref[pl.ds(row, subs, stride=SUB), :]
            v = in_sc[pl.ds(row, subs, stride=SUB), :]
            gy = gy_sc[pl.ds(row, subs, stride=SUB), :]
            u = d * v
            da = jnp.where(keep_ref[chunk * rows + t] > 0, d, BIG)
            gd = gs = None
            for g in range(states // SUB):
                pb = [None] * SUB
                pc = [None] * SUB
                for o in order:
                    n = g * SUB + o
                    b = bb_sc[pl.ds((ti * 2 * states + n) * SUB + s, subs, stride=0), :]
                    c = bb_sc[pl.ds((ti * 2 * states + states + n) * SUB + s, subs, stride=0), :]
                    dec = dec_ref[pl.ds(n * subs, subs), :]
                    before = hs_ref[pl.ds(pl.multiple_of(t * span + n * subs, subs), subs), :]
                    after = hs_ref[pl.ds(pl.multiple_of((t + 1) * span + n * subs, subs), subs), :]
                    gh = c * gy + ghs[n]
                    ghs[n] = jnp.exp2(da * dec) * gh
                    q = ghs[n] * before
                    gd = dec * q if gd is None else gd + dec * q
                    accs[n] = accs[n] + q * d
                    gs = gh * b if gs is None else gs + gh * b
                    pb[o] = gh * u
                    pc[o] = after * gy
                at = chunk * rows + t
                r_sc[pl.ds(g * SUB * all_rows + at, SUB, stride=all_rows), :] = fold_rows(pb, sub_iota)
                r_sc[pl.ds((states + g * SUB) * all_rows + at, SUB, stride=all_rows), :] = fold_rows(pc, sub_iota)
            gd_sc[pl.ds(row, subs, stride=SUB), :] = gd * math.log(2.0) + gs * v
            go_sc[pl.ds(row, subs, stride=SUB), :] = gy * skip + gs * d
        return tuple(ghs + accs)

    init = tuple(gh_ref[pl.ds(n * subs, subs), :] for n in range(states))
    init = init + tuple(acc_ref[pl.ds(n * subs, subs), :] for n in range(states))
    out = lax.fori_loop(0, rows // SUB, step, init)
    for n in range(states):
        gh_ref[pl.ds(n * subs, subs), :] = out[n]
        acc_ref[pl.ds(n * subs, subs), :] = out[states + n]
    gi_ref[...] = get_tiles(go_sc, rows, subs)
    d_all = get_tiles(dl_ref, rows, subs)
    series = d_all * (1.0 - d_all * (0.5 - d_all * (1.0 / 6 - d_all * (1.0 / 24))))
    slope = jnp.where(d_all < 0.03125, series, 1.0 - jnp.exp(-d_all))
    gp = get_tiles(gd_sc, rows, subs) * slope
    red_ref[pl.ds(1, 1), :] += jnp.sum(gp, axis=0, keepdims=True)
    low = gp.astype(bf16)
    gp_ref[...] = low
    mixed_ref[pl.ds(pl.multiple_of(chunk * rows, rows), rows), pl.ds(0, rank)] = lax.dot_general(
        low, wdt_ref[...], (((1,), (1,)), ((), ())), preferred_element_type=f32
    ).astype(bf16)

    @pl.when(i == last)
    def _():
        lane = lax.broadcasted_iota(jnp.int32, (LANES, LANES), 1)
        total = jnp.zeros((all_rows, LANES), f32)
        for n in range(2 * states):
            pick = jnp.where(lane == n, 1.0, 0.0).astype(bf16)
            part = r_sc[pl.ds(n * all_rows, all_rows), :].astype(bf16)
            total = total + jnp.dot(part, pick, preferred_element_type=f32)
        mixed_ref[:, pl.ds(rank, 2 * states)] = total[:, : 2 * states].astype(bf16)


def scan_backward(h, keep, bc, wdt, d_skip, dec, inner, gate, gg, ysum, hs, delta_tm, gh0, chunk_rows=64):
    rows, channels = inner.shape
    subs = channels // LANES
    states = bc.shape[1] // 2
    rank = wdt.shape[0]
    chunks = rows // chunk_rows
    span = states * subs
    skip_tm = d_skip.reshape(subs, LANES)

    def back(i, *_):
        return (chunks - 1 - i, 0)

    def row_block(width):
        return pl.BlockSpec((chunk_rows, width), back)

    def fixed(shape):
        return pl.BlockSpec(shape, lambda i, *_: (0, 0))

    tile = pltpu.VMEM((chunk_rows * subs, LANES), f32)
    grid_spec = pltpu.PrefetchScalarGridSpec(
        num_scalar_prefetch=1,
        grid=(chunks,),
        in_specs=[
            row_block(2 * states), fixed(wdt.shape), fixed(d_skip.shape), fixed(skip_tm.shape), fixed(dec.shape),
            row_block(channels), row_block(channels),
            pl.BlockSpec((chunk_rows, channels), lambda i, *_: (h * chunks + chunks - 1 - i, 0)), row_block(channels),
            pl.BlockSpec(((chunk_rows + 1) * span, LANES), back),
            pl.BlockSpec((chunk_rows * subs, LANES), back), fixed(gh0.shape),
        ],
        out_specs=[
            row_block(channels), row_block(channels), row_block(channels), fixed((rows, rank + 2 * states)),
            fixed((8, channels)), fixed((span, LANES)), fixed((span, LANES)),
        ],
        scratch_shapes=[
            tile, tile, pltpu.VMEM((chunk_rows * 2 * states, LANES), f32), tile, tile,
            pltpu.VMEM((2 * states * rows, LANES), f32),
        ],
    )
    made = jax.ShapeDtypeStruct
    return pl.pallas_call(
        functools.partial(bwd_body, states, subs),
        grid_spec=grid_spec,
        out_shape=[
            made((rows, channels), f32), made((rows, channels), bf16), made((rows, channels), bf16),
            made((rows, rank + 2 * states), bf16), made((8, channels), f32), made((span, LANES), f32),
            made((span, LANES), f32),
        ],
        compiler_params=pltpu.CompilerParams(vmem_limit_bytes=58 << 20),
        cost_estimate=cost(45.0 * rows * channels / (512 * 1024)),
        name="scan_backward",
    )(keep, bc, wdt, d_skip, skip_tm, dec, inner, gate, gg, ysum, hs, delta_tm, gh0)


def norm_body(gain_ref, rows_ref, out_ref):
    value = rows_ref[...].astype(f32)
    factor = lax.rsqrt(jnp.mean(value * value, axis=1, keepdims=True) + EPSILON)
    out_ref[...] = (value * factor * gain_ref[...]).astype(bf16)


def norm_rows(rows_all, gain, parts):
    rows, width = rows_all.shape
    block = pl.BlockSpec((rows // parts, width), lambda i: (i, 0))
    return pl.pallas_call(
        norm_body,
        grid=(parts,),
        in_specs=[pl.BlockSpec(gain.shape, lambda i: (0, 0)), block],
        out_specs=block,
        out_shape=jax.ShapeDtypeStruct((rows, width), bf16),
        compiler_params=pltpu.CompilerParams(vmem_limit_bytes=24 << 20),
        cost_estimate=cost(3.0),
        name="norm_rows",
    )(gain, rows_all)


def split_specs(channels, width):
    chunk = min(256, channels // 2)
    half = channels // 2 // chunk
    first = pl.BlockSpec((chunk, width), lambda i, *_: (jnp.minimum(i, half - 1), 0))
    second = pl.BlockSpec((chunk, width), lambda i, *_: (jnp.maximum(i - half, 0), 0))
    return chunk, half, [first, second]


def front_body(
    half, normed_ref, xa_ref, xb_ref, ga_ref, gb_ref, taps_ref, bias_ref, wxp_ref, dist_ref, halo_ref, sig_ref, gate_ref,
    inner_ref, mixed_ref, ext_sc, acc_sc,
):
    i = pl.program_id(0)
    rows = normed_ref.shape[0]
    dims = (((1,), (1,)), ((), ()))

    def project(x_ref, g_ref):
        normed = normed_ref[...]
        ext_sc[pl.ds(SUB, rows), :] = lax.dot_general(normed, x_ref[...], dims, preferred_element_type=f32)
        gate_ref[...] = lax.dot_general(normed, g_ref[...], dims, preferred_element_type=f32)

    @pl.when(i < half)
    def _():
        project(xa_ref, ga_ref)

    @pl.when(i >= half)
    def _():
        project(xb_ref, gb_ref)

    ext_sc[pl.ds(0, SUB), :] = halo_ref[...]
    taps = taps_ref.shape[0]
    signal = ext_sc[pl.ds(SUB, rows), :]
    sig_ref[...] = signal
    dist = dist_ref[...]
    pre = bias_ref[...] + taps_ref[pl.ds(taps - 1, 1), :] * signal
    for lag in range(1, taps):
        shifted = ext_sc[pl.ds(SUB - lag, rows), :]
        pre = pre + jnp.where(dist >= lag, taps_ref[pl.ds(taps - 1 - lag, 1), :] * shifted, 0.0)
    inner = (pre / (1.0 + jnp.exp(-pre))).astype(bf16)
    inner_ref[...] = inner
    part = lax.dot_general(inner, wxp_ref[...], dims, preferred_element_type=f32)

    @pl.when(i == 0)
    def _():
        acc_sc[...] = part

    @pl.when(i > 0)
    def _():
        acc_sc[...] += part

    mixed_ref[...] = acc_sc[...].astype(bf16)


def front(h, rows, normed, w_x, w_g, taps, bias, w_xp, dist, halo):
    width = normed.shape[1]
    channels = taps.shape[1]
    chunk, half, pair = split_specs(channels, width)
    xw = w_xp.shape[0]

    def columns(height):
        return pl.BlockSpec((height, chunk), lambda i: (0, i))

    made = jax.ShapeDtypeStruct
    return pl.pallas_call(
        functools.partial(front_body, half),
        grid=(2 * half,),
        in_specs=[pl.BlockSpec((rows, width), lambda i: (h, 0))]
        + pair
        + pair
        + [
            columns(taps.shape[0]), columns(1), columns(xw), pl.BlockSpec((rows, 1), lambda i: (h, 0)), columns(SUB),
        ],
        out_specs=[columns(rows), columns(rows), columns(rows), pl.BlockSpec((rows, xw), lambda i: (0, 0))],
        out_shape=[
            made((rows, channels), f32), made((rows, channels), f32), made((rows, channels), bf16),
            made((rows, xw), bf16),
        ],
        scratch_shapes=[pltpu.VMEM((rows + SUB, chunk), f32), pltpu.VMEM((rows, xw), f32)],
        compiler_params=pltpu.CompilerParams(vmem_limit_bytes=40 << 20),
        cost_estimate=cost(7.0),
        name="front",
    )(normed, *w_x, *w_g, taps, bias, w_xp, dist, halo)


def turn_body(
    mixed_ref, gis_ref, sig_ref, halo_ref, taps_ref, bias_ref, wxp_ref, dist_ref, next_ref, dnext_ref, gsig_ref, head_ref,
    sums_ref, ext_sc, late_sc,
):
    rows = gis_ref.shape[0]
    taps = taps_ref.shape[0]
    ext_sc[pl.ds(0, SUB), :] = halo_ref[...]
    ext_sc[pl.ds(SUB, rows), :] = sig_ref[...]
    dist = dist_ref[...]
    signal = sig_ref[...]
    pre = bias_ref[...] + taps_ref[pl.ds(taps - 1, 1), :] * signal
    for lag in range(1, taps):
        shifted = ext_sc[pl.ds(SUB - lag, rows), :]
        pre = pre + jnp.where(dist >= lag, taps_ref[pl.ds(taps - 1 - lag, 1), :] * shifted, 0.0)
    sig = 1.0 / (1.0 + jnp.exp(-pre))
    g_inner = gis_ref[...] + jnp.dot(mixed_ref[...], wxp_ref[...], preferred_element_type=f32)
    g_pre = g_inner * (sig * (1.0 + pre * (1.0 - sig)))
    head_ref[...] = g_pre[:SUB, :]
    lines = [None] * taps
    lines[taps - 1] = jnp.sum(g_pre * signal, axis=0, keepdims=True)
    g_signal = taps_ref[pl.ds(taps - 1, 1), :] * g_pre
    for lag in range(1, taps):
        masked = jnp.where(dist >= lag, g_pre, 0.0)
        lines[taps - 1 - lag] = jnp.sum(masked * ext_sc[pl.ds(SUB - lag, rows), :], axis=0, keepdims=True)
        late_sc[pl.ds(0, rows), :] = masked
        late_sc[pl.ds(rows, SUB), :] = jnp.where(dnext_ref[...] >= lag, next_ref[...], 0.0)
        g_signal = g_signal + taps_ref[pl.ds(taps - 1 - lag, 1), :] * late_sc[pl.ds(lag, rows), :]
    lines.append(jnp.sum(g_pre, axis=0, keepdims=True))
    sums_ref[...] = jnp.zeros_like(sums_ref)
    for k, value in enumerate(lines):
        sums_ref[pl.ds(k, 1), :] = value
    gsig_ref[...] = g_signal.astype(bf16)


def turn(h, mixed, gis, signal, halo, taps, bias, w_xp, dist, late, dist_late):
    rows, channels = gis.shape
    chunk = min(256, channels // 2)
    xw = w_xp.shape[0]

    def columns(height):
        return pl.BlockSpec((height, chunk), lambda i: (0, i))

    def fixed(a):
        return pl.BlockSpec(a.shape, lambda i: (0, 0))

    made = jax.ShapeDtypeStruct
    return pl.pallas_call(
        turn_body,
        grid=(channels // chunk,),
        in_specs=[
            fixed(mixed), columns(rows), columns(rows), columns(SUB), columns(taps.shape[0]), columns(1), columns(xw),
            pl.BlockSpec((rows, 1), lambda i: (h, 0)), columns(SUB), fixed(dist_late),
        ],
        out_specs=[columns(rows), columns(SUB), columns(SUB)],
        out_shape=[made((rows, channels), bf16), made((SUB, channels), f32), made((SUB, channels), f32)],
        scratch_shapes=[pltpu.VMEM((rows + SUB, chunk), f32), pltpu.VMEM((rows + SUB, chunk), f32)],
        compiler_params=pltpu.CompilerParams(vmem_limit_bytes=32 << 20),
        cost_estimate=cost(3.0),
        name="turn",
    )(mixed, gis, signal, halo, taps, bias, w_xp, dist, late, dist_late)


def rear_body(half, gs_ref, gx_ref, xa_ref, xb_ref, ga_ref, gb_ref, normed_ref, out_ref, gain_ref, acc_sc):
    i = pl.program_id(0)

    def product(x_ref, g_ref):
        return jnp.dot(gs_ref[...], x_ref[...], preferred_element_type=f32) + jnp.dot(
            gx_ref[...], g_ref[...], preferred_element_type=f32
        )

    @pl.when(i == 0)
    def _():
        acc_sc[...] = product(xa_ref, ga_ref)

    @pl.when(jnp.logical_and(i > 0, i < half))
    def _():
        acc_sc[...] += product(xa_ref, ga_ref)

    @pl.when(i >= half)
    def _():
        acc_sc[...] += product(xb_ref, gb_ref)

    @pl.when(i == pl.num_programs(0) - 1)
    def _():
        total = acc_sc[...]
        out_ref[...] = total.astype(bf16)
        gain_ref[...] = jnp.sum(total * normed_ref[...].astype(f32), axis=0, keepdims=True)


def rear(h, g_signal, g_gate, w_x, w_g, normed):
    width = normed.shape[1]
    rows, channels = g_signal.shape
    chunk, half, pair = split_specs(channels, width)
    columns = pl.BlockSpec((rows, chunk), lambda i: (0, i))
    made = jax.ShapeDtypeStruct
    return pl.pallas_call(
        functools.partial(rear_body, half),
        grid=(2 * half,),
        in_specs=[columns, columns] + pair + pair + [pl.BlockSpec((rows, width), lambda i: (h, 0))],
        out_specs=[pl.BlockSpec((rows, width), lambda i: (0, 0)), pl.BlockSpec((1, width), lambda i: (0, 0))],
        out_shape=[made((rows, width), bf16), made((1, width), f32)],
        scratch_shapes=[pltpu.VMEM((rows, width), f32)],
        compiler_params=pltpu.CompilerParams(vmem_limit_bytes=40 << 20),
        cost_estimate=cost(5.0),
        name="rear",
    )(g_signal, g_gate, *w_x, *w_g, normed)


def distances(lengths, pack_rows, row_count):
    slot_count = lengths.shape[0]
    picks = pack_rows[:, None] == jnp.arange(slot_count, dtype=jnp.int32)[None, :]
    packed = jnp.sum(jnp.where(picks, lengths[None, :], 0), axis=1)
    starts = jnp.cumsum(packed) - packed
    positions = jnp.arange(row_count, dtype=jnp.int32)
    latest = jnp.max(jnp.where(starts[None, :] <= positions[:, None], starts[None, :], 0), axis=1)
    return positions - latest


def after(value, *others):
    return lax.optimization_barrier((value,) + others)[0]


def swap(value, bit):
    count = lax.axis_size("fsdp")
    return lax.ppermute(value, "fsdp", [(i, i ^ bit) for i in range(count)])


def gather_wide(value, order, *waits):
    pieces = {0: value}
    size = value.shape[0]
    axis = 0
    for bit in order:
        keys = sorted(pieces)
        sent = jnp.concatenate([pieces[k] for k in keys], axis=axis) if len(keys) > 1 else value
        if len(keys) > 1 and waits:
            sent = after(sent, *waits)
        got = swap(sent, bit)
        for i, k in enumerate(keys):
            pieces[k | bit] = lax.slice_in_dim(got, i * size, (i + 1) * size, axis=axis)
    return jnp.concatenate([pieces[k] for k in sorted(pieces)], axis=axis)


def halves(blocks, order, axis):
    bit, rest = order[0], order[1:]
    leave = sorted(k for k in blocks if k & bit)
    stay = sorted(k for k in blocks if not k & bit)
    width = blocks[leave[0]].shape[axis]
    lows = [blocks[k].astype(bf16) for k in leave]
    sent = jnp.concatenate(lows, axis=axis) if len(lows) > 1 else lows[0]

    def back(got):
        cut = [lax.slice_in_dim(got, i * width, (i + 1) * width, axis=axis) for i in range(len(leave))]
        return {k: blocks[k].astype(f32) + cut[i].astype(f32) for i, k in enumerate(stay)}, rest

    return sent, back, bit


def reduce_bits(blocks, order, axis):
    while order:
        sent, back, bit = halves(blocks, order, axis)
        blocks, order = back(swap(sent, bit))
    return blocks[0]


class LineSum:
    def __init__(self, parts, low, high):
        self.parts, self.low, self.high = parts, low, high
        self.count = lax.axis_size("tensor")
        self.place = lax.axis_index("tensor")
        self.up = self.down = None
        self.step = 0

    def block(self, index):
        rows = self.parts.shape[0] // (self.high - self.low)
        start = (jnp.clip(index, self.low, self.high - 1) - self.low) * rows
        return lax.dynamic_slice_in_dim(self.parts, start, rows, 0).astype(f32)

    def go(self, *waits):
        self.step += 1
        step, count, sent = self.step, self.count, []
        self.parts = after(self.parts, *waits)
        pairs = [(i, i + 1) for i in range(step) if i + 1 < count and self.low <= count - step + i < self.high]
        if pairs:
            part = self.block(count - step + self.place)
            part = (part if self.up is None else part + self.up.astype(f32)).astype(bf16)
            sent.append(part)
            self.up = lax.ppermute(part, "tensor", pairs)
        pairs = [(i, i - 1) for i in range(count - step, count) if self.low <= i - count + step < self.high]
        if pairs:
            part = self.block(self.place - count + step)
            part = (part if self.down is None else part + self.down.astype(f32)).astype(bf16)
            sent.append(part)
            self.down = lax.ppermute(part, "tensor", pairs)
        return tuple(sent)

    def finish(self):
        while self.step < self.count - 1:
            self.go()
        return self.block(self.place) + self.up.astype(f32) + self.down.astype(f32)


class WeightGrad:
    def __init__(self, lows, other, kept, orders, own_channels):
        self.kept, self.orders, self.own = kept, orders, own_channels
        middle = lows.shape[1] // 2
        self.leave = matmul(lows[:, middle:], other, (0, 0), bf16)
        self.got = swap(self.leave, 1)
        self.lows, self.other = lows[:, :middle], other

    def rest(self, *waits):
        self.stay = matmul(after(self.lows, self.leave, *waits), self.other, (0, 0), bf16)
        return self.stay

    def split(self):
        columns = self.stay.shape[1] // len(self.orders)
        self.streams = []
        for part, order in enumerate(self.orders):
            blocks = {}
            for i, k in enumerate(self.kept):
                cut = (slice(i * self.own, (i + 1) * self.own), slice(part * columns, (part + 1) * columns))
                blocks[k] = self.stay[cut].astype(f32) + self.got[cut].astype(f32)
            self.streams.append((blocks, order))
        return self.go()

    def go(self):
        sents, streams = [], []
        for blocks, order in self.streams:
            sent, back, bit = halves(blocks, order, 0)
            sents.append(sent)
            streams.append((back, swap(sent, bit)))
        self.waiting = streams
        self.streams = streams
        return tuple(sents)

    def take(self, *waits):
        self.streams = [back(after(got, *waits)) for back, got in self.waiting]

    def finish(self):
        if not isinstance(self.streams[0][0], dict):
            self.take()
        while self.streams[0][1]:
            self.go()
            self.take()
        return jnp.concatenate([blocks[0] for blocks, _ in self.streams], axis=1)


def ring_sum(part):
    count = lax.axis_size("tensor")
    total = part.astype(f32)
    for step in range(1, count):
        total = total + lax.ppermute(part, "tensor", [(i, (i + step) % count) for i in range(count)]).astype(f32)
    return total


def pair_sum(part):
    count = lax.axis_size("tensor")
    total, sents = part.astype(f32), []
    bit = 1
    while bit < count:
        sents.append(total.astype(bf16))
        total = total + lax.ppermute(sents[-1], "tensor", [(i, i ^ bit) for i in range(count)]).astype(f32)
        bit *= 2
    return total, sents


def placed(places):
    count = len(places)
    own = lax.axis_index("fsdp")
    owners = jnp.bitwise_xor(jnp.asarray(places, jnp.int32), own.astype(jnp.int32))
    return lax.broadcasted_iota(jnp.int32, (count, count), 0) == owners[None, :]


def matmul(left, right, dims, kind=f32):
    return lax.dot_general(left, right, ((dims[:1], dims[1:]), ((), ())), preferred_element_type=f32).astype(kind)


def shards(
    hidden,
    cotangent,
    seq_lengths,
    pack_order,
    norm_gain,
    w_in,
    conv_weight,
    conv_bias,
    w_xproj,
    w_dt,
    dt_bias,
    a_log,
    d_skip,
    w_out,
):
    n_fsdp = lax.axis_size("fsdp")
    n_tensor = lax.axis_size("tensor")
    place = lax.axis_index("tensor")
    own_channels = w_in.shape[1]
    width = hidden.shape[1]
    group_rows = hidden.shape[0] * n_tensor
    rank = w_dt.shape[1]
    states = a_log.shape[1]
    taps = conv_weight.shape[1]
    wide = [1 << i for i in range(1, n_fsdp.bit_length() - 1)]
    narrow = wide[::-1]
    kept = [k for k in range(n_fsdp) if not k & 1]
    places = kept + [k + 1 for k in kept]
    channels = own_channels * n_fsdp
    middle = channels // 2
    part_rows = group_rows // 2

    rows_all = lax.all_gather(hidden, "tensor", axis=0, tiled=True)
    gain_own = norm_gain.reshape(1, -1)
    lines = lax.broadcasted_iota(jnp.int32, (n_tensor, 1), 0)
    gain_line = jnp.where(lines == place, gain_own, 0)
    for step in range(1, n_tensor):
        got = lax.ppermute(gain_own, "tensor", [(i, (i + step) % n_tensor) for i in range(n_tensor)])
        gain_line = jnp.where(lines == lax.rem(place - step + n_tensor, n_tensor), got, gain_line)
    gain_rows = width // n_fsdp // own_channels
    small = jnp.concatenate(
        [
            w_xproj.T,
            w_dt.T,
            a_log.T,
            conv_weight.T,
            conv_bias[None],
            dt_bias[None],
            d_skip[None],
            gain_line.reshape(gain_rows, own_channels),
        ],
        axis=0,
    )
    small_got = [swap(small, k) for k in kept[1:]]
    w_xa = gather_wide(w_in[0], wide, *small_got)
    w_ga = gather_wide(w_in[1], narrow, *small_got)
    w_xb = swap(w_xa, 1)
    w_gb = swap(w_ga, 1)
    small_a = jnp.concatenate([small] + small_got, axis=1)
    small_all = jnp.concatenate([small_a, swap(small_a, 1)], axis=1)
    w_out_all = lax.all_gather(after(w_out, small), "fsdp", axis=0, tiled=True)
    cot_all = lax.all_gather(after(cotangent, w_xa, w_ga), "tensor", axis=0, tiled=True)
    own = lax.axis_index("fsdp").astype(jnp.int32)

    xw = rank + 2 * states
    w_xp = small_all[:xw]
    w_dt_rows = small_all[xw : xw + rank]
    at = xw + rank
    a_rows = small_all[at : at + states].astype(f32)
    at = at + states
    conv_rows = small_all[at : at + taps].astype(f32)
    at = at + taps
    conv_b = small_all[at : at + 1].astype(f32)
    dt_b = small_all[at + 1 : at + 2].astype(f32)
    skip_row = small_all[at + 2 : at + 3].astype(f32)
    gain_all = small_all[at + 3 :].astype(f32).reshape(1, gain_rows, n_fsdp, own_channels)
    owners = placed(places)
    gain = jnp.sum(jnp.where(owners[:, None, :, None], gain_all, 0.0), axis=2).reshape(1, width)
    decays = -jnp.exp(a_rows)
    rates = (decays * math.log2(math.e)).reshape(-1, LANES)

    offsets = distances(seq_lengths[0], pack_order[0], group_rows)
    keep = (offsets > 0).astype(jnp.int32)
    dist = offsets[:, None]
    normed = norm_rows(rows_all, gain, n_tensor)

    cuts = [slice(0, part_rows), slice(part_rows, group_rows)]
    halo = jnp.zeros((SUB, channels), f32)
    weights = ((w_xa, w_xb), (w_ga, w_gb))
    front_0 = front(0, part_rows, normed, *weights, conv_rows, conv_b, w_xp, dist, halo)
    halo_1 = front_0[0][part_rows - SUB :]
    front_1 = front(1, part_rows, normed, *weights, conv_rows, conv_b, w_xp, dist, halo_1)
    mixed_0 = ring_sum(front_0[3])
    mixed_1 = ring_sum(after(front_1[3], mixed_0))
    fronts, mixes, halos = [front_0, front_1], [mixed_0, mixed_1], [halo, halo_1]
    steps = [mixed[:, :rank].astype(bf16) for mixed in mixes]
    bcs = [mixed[:, rank:] for mixed in mixes]
    carried = jnp.zeros(rates.shape, f32)
    runs = []
    for h in (0, 1):
        bc = after(bcs[h], w_out_all) if h == 0 else bcs[h]
        made = scan_forward(
            keep[cuts[h]], steps[h], bc, w_dt_rows, dt_b, skip_row, rates, fronts[h][2], fronts[h][1], carried
        )
        carried = made[4]
        runs.append(made)
    gated = jnp.concatenate([runs[0][3], runs[1][3]], axis=0)
    step_all = jnp.concatenate(steps, axis=0)
    w_o = [lax.dynamic_slice_in_dim(w_out_all, (own ^ k) * own_channels, own_channels, 0) for k in places]
    w_o = jnp.concatenate(w_o, axis=0)
    grad_gated = matmul(after(cot_all, gated), w_o, (1, 1), bf16)
    gated_late = after(gated, grad_gated)
    branch = matmul(gated_late, w_o, (1, 0), bf16)
    branch_own = lax.psum_scatter(branch, "tensor", scatter_dimension=0, tiled=True)
    output = (hidden.astype(f32) + branch_own.astype(f32)).astype(bf16)
    orders = (wide, narrow)
    out_grad = WeightGrad(after(gated_late, branch), cot_all, kept, orders, own_channels)
    out_grad.rest()

    def backward(h, carried, *waits):
        return scan_backward(
            h, keep[cuts[h]], after(bcs[h], *waits), w_dt_rows, skip_row, rates, fronts[h][2], fronts[h][1],
            grad_gated, runs[h][2], runs[h][0], runs[h][1], carried,
        )

    back_1 = backward(1, jnp.zeros(rates.shape, f32), out_grad.stay)
    back_0 = backward(0, back_1[6])
    low_1 = ring_sum(back_1[3]).astype(bf16)
    low_0, low_sents = pair_sum(after(back_0[3], low_1))
    low_0 = low_0.astype(bf16)
    g_gate = jnp.concatenate([back_0[1], back_1[1]], axis=0)
    sent = out_grad.split()
    gate_grad = WeightGrad(after(g_gate, low_1, *sent), normed, kept, orders, own_channels)
    gate_grad.rest()
    late = jnp.zeros((SUB, channels), f32)
    dist_late = jnp.zeros((SUB, 1), jnp.int32)
    sig_1, late, sums_1 = turn(
        1, after(low_1, gate_grad.stay, *low_sents), back_1[0], fronts[1][0], halos[1], conv_rows, conv_b, w_xp,
        dist, late, dist_late,
    )
    out_grad.take(sig_1)
    sent = out_grad.go() + gate_grad.split()
    part_1, gain_1 = rear(1, after(sig_1, *sent), back_1[1], *weights, normed)
    line_1 = LineSum(part_1, n_tensor // 2, n_tensor)
    sent = line_1.go()
    sig_0, _, sums_0 = turn(
        0, after(low_0, *sent), back_0[0], fronts[0][0], halos[0], conv_rows, conv_b, w_xp, dist, late,
        dist[cuts[1]][:SUB],
    )
    out_grad.take()
    grad_w_out = out_grad.finish()
    gate_grad.take()
    sent = gate_grad.go()
    part_0, gain_0 = rear(0, after(sig_0, *sent), back_0[1], *weights, normed)
    line_0 = LineSum(part_0, 0, n_tensor // 2)
    sent = line_1.go(part_0) + line_0.go()
    g_signal = jnp.concatenate([sig_0, sig_1], axis=0)
    sig_grad = WeightGrad(after(g_signal, *sent), normed, kept, orders, own_channels)
    sig_grad.rest()
    gate_grad.take(sig_grad.stay)
    grad_w_gate = gate_grad.finish()
    sent = sig_grad.split()
    sent = line_1.go(*sent) + line_0.go(*sent)
    sig_grad.take(*sent)
    sent = sig_grad.go()
    line_0.go(*sent)
    sig_grad.take()
    grad_w_sig = sig_grad.finish()

    reds = back_0[4] + back_1[4]
    acc = back_0[5] + back_1[5]
    gain_sum = ((gain_0 + gain_1) / gain).reshape(n_fsdp, gain_rows, 1, own_channels)
    gain_sum = jnp.sum(jnp.where(owners[:, None, :, None], gain_sum, 0.0), axis=0).reshape(gain_rows, channels)
    gain_pad = -gain_rows % SUB
    small_grad = jnp.concatenate(
        [
            matmul(jnp.concatenate([low_0, low_1], axis=0), jnp.concatenate([fronts[0][2], fronts[1][2]], axis=0), (0, 0)),
            matmul(step_all, jnp.concatenate([back_0[2], back_1[2]], axis=0), (0, 0)),
            acc.reshape(states, channels) * decays,
            sums_0 + sums_1,
            reds,
            jnp.concatenate([gain_sum, jnp.zeros((gain_pad, channels), f32)], axis=0),
        ],
        axis=0,
    )
    small_half = small_grad[:, :middle] + swap(small_grad[:, middle:].astype(bf16), 1).astype(f32)
    small_own = small_half[:, :own_channels]
    for i, k in enumerate(kept[1:]):
        cut = small_half[:, (i + 1) * own_channels : (i + 2) * own_channels]
        small_own = small_own + swap(cut.astype(bf16), k).astype(f32)
    at = xw + rank + states
    gain_own = small_own[at + 2 * SUB : at + 2 * SUB + gain_rows].reshape(n_tensor, -1)
    grad_gain = lax.dynamic_slice_in_dim(gain_own, place, 1, 0)
    gain_low = gain_own.astype(bf16)
    for step in range(1, n_tensor):
        sent = lax.dynamic_slice_in_dim(gain_low, lax.rem(place + step, n_tensor), 1, 0)
        got = lax.ppermute(sent, "tensor", [(i, (i + step) % n_tensor) for i in range(n_tensor)])
        grad_gain = grad_gain + got.astype(f32)
    g_norm_own = jnp.where(place >= n_tensor // 2, line_1.finish(), line_0.finish())
    values = hidden.astype(f32)
    factor = lax.rsqrt(jnp.mean(values * values, axis=1, keepdims=True) + EPSILON)
    scaled = g_norm_own * gain
    xhat = values * factor
    grad_hidden = cotangent.astype(f32) + factor * (scaled - xhat * jnp.mean(scaled * xhat, axis=1, keepdims=True))
    columns = small_own.T
    return (
        output,
        grad_hidden,
        grad_gain.reshape(norm_gain.shape),
        jnp.stack([grad_w_sig, grad_w_gate], axis=0),
        columns[:, at : at + taps],
        small_own[at + taps],
        columns[:, :xw],
        columns[:, xw : xw + rank],
        small_own[at + SUB + 1],
        columns[:, at - states : at],
        small_own[at + SUB],
        grad_w_out,
    )


def solution(mesh):
    every = ("fsdp", "tensor")
    rows = P(every, None)
    line = P(every)
    planes = P(None, every, None)
    return jax.shard_map(
        shards,
        mesh=mesh,
        in_specs=(rows, rows, P("fsdp", None), P("fsdp", None), line, planes, rows, line, rows, rows, line, rows, line, rows),
        out_specs=(rows, rows, line, planes, rows, line, rows, rows, line, rows, line, rows),
        check_vma=False,
    )
```

time: 868 us -> 393 us (0.45)
  waiting for transfers between devices: 542 us -> 78.1 us
  blocking collectives: 146 us -> 0 us
  starting transfers between devices: 0.93 us -> 72.9 us
  Pallas kernels: 63.7 us -> 109 us
  matrix products: 56.9 us -> 27.1 us
  local copies, waits for them, and re-layouts: 23.1 us -> 45.5 us
  other arithmetic: 16.5 us -> 37.8 us
    reduce_scatter x7 -> x1, waiting for transfers between devices: 414 us -> 0.01 us  [shards(): lax.psum_scatter(branch, 'tensor', scatter_dimension=0, tiled=True)]
    all_gather x4 -> x3, waiting for transfers between devices: 90.3 us -> 0.01 us  [the longest x1 0.01 us: shards(): rows_all = lax.all_gather(hidden, 'tensor', axis=0, tiled=True)]
    ppermute x0 -> x54, waiting for transfers between devices: none -> 77.3 us  [the longest x29 47.3 us: swap(): return lax.ppermute(value, 'fsdp', [(i, i ^ bit) for i in range(count)])]
    ppermute x0 -> x54, starting transfers between devices: none -> 72.8 us  [the longest x29 25.6 us: swap(): return lax.ppermute(value, 'fsdp', [(i, i ^ bit) for i in range(count)])]
    all_gather x8 -> x0, blocking collectives: 71.4 us -> none  [the longest x1 12.7 us: shards(): lax.all_gather(gain_fsdp, 'tensor', axis=0, tiled=True)]
    unnamed x3 -> x0, blocking collectives: 48.7 us -> none
    pallas_call x0 -> x7, Pallas kernels: none -> 34.8 us  [the longest x2 15.3 us: front(): pl.pallas_call(functools.partial(front_body, half), grid=(2 * half,), in_...]
    psum x1 -> x0, waiting for transfers between devices: 34.8 us -> none  [shards(): mixed = lax.psum(pieces_x, 'tensor')]
  transfers between devices with their start and end apart: 13 -> 58, of which waited for: 11 -> 20; matrix products, arithmetic and copies ran while one was open for 7% -> 21% of each run, Pallas kernels for 0% -> 28%
where the time goes in v2:
time: 393 us; the launch traced here: 386 us
  Pallas kernels  109 us (28%)
  waiting for transfers between devices  78.1 us (20%)
  starting transfers between devices  72.9 us (19%)
  local copies, waits for them, and re-layouts  45.5 us (12%)
  other arithmetic  37.8 us (10%)
  matrix products  27.1 us (7%)
  between operations  15.7 us (4%)
    pallas_call x2, Pallas kernels, scan_backward(): pl.pallas_call(functools.partial(bwd_body, states, subs), grid_spec=grid_...  51 us
    ppermute x29, waiting for transfers between devices, swap(): return lax.ppermute(value, 'fsdp', [(i, i ^ bit) for i in range(count)])  47.3 us
    dot_general x10, matrix products, matmul(): lax.dot_general(left, right, ((dims[:1], dims[1:]), ((), ())), preferred_...  27.1 us
    ppermute x29, starting transfers between devices, swap(): return lax.ppermute(value, 'fsdp', [(i, i ^ bit) for i in range(count)])  25.6 us
    pallas_call x2, Pallas kernels, scan_forward(): pl.pallas_call(functools.partial(fwd_body, states, subs), grid_spec=grid_...  23.2 us
    unnamed x144, local copies, waits for them, and re-layouts  21.1 us
    ppermute x9, waiting for transfers between devices, ring_sum(): lax.ppermute(part, 'tensor', [(i, (i + step) % count) for i in range(coun...  15.6 us
    pallas_call x2, Pallas kernels, front(): pl.pallas_call(functools.partial(front_body, half), grid=(2 * half,), in_...  15.3 us
  transfers between devices with their start and end apart: 58, of which 20 were waited for; matrix products, arithmetic and copies ran while one was open for 21% of the time, Pallas kernels for 28%

profile of v2, /device:TPU:8, one launch (start us, length us, event | category | flops | bytes accessed | tf_op | source)
XLA Modules:
  0.0 386.2 jit_solution(3504335118821967620)
XLA Ops:
  8.0 1.6 collective-permute-start.2
  10.7 1.9 collective-permute-start
  15.3 2.3 concatenate.76
  17.8 1.6 collective-permute-start.10
  19.4 1.5 collective-permute-start.7
  22.5 1.5 collective-permute-start.4
  24.0 1.5 collective-permute-start.3
  25.5 8.2 %collective-permute-done.7 = bf16[128,2048]{1,0:T(8,128)(2,1)S(1)} collective-permute-done((bf16[128,2048]{1,0:T(8,128)(2,1)S(1)}, bf16[128,2048]{1,0:T(8,128)(2,1)S(1)}, u32[]{:S(2)}, u32[]{:S(2)}) %collective-permute-start.7) | collective-permute-done | bytes 524320 | tf_op jit(solution)/shard_map/ppermute | solution.py:542
  36.2 1.6 collective-permute-start.11
  38.5 19.8 %collective-permute-done.8 = bf16[256,2048]{1,0:T(8,128)(2,1)S(1)} collective-permute-done((bf16[256,2048]{1,0:T(8,128)(2,1)S(1)}, bf16[256,2048]{1,0:T(8,128)(2,1)S(1)}, u32[]{:S(2)}, u32[]{:S(2)}) %collective-permute-start.8) | collective-permute-done | bytes 1048608 | tf_op jit(solution)/shard_map/ppermute | solution.py:542
  61.1 1.5 pad_maximum_fusion.1.ga_ref
  69.6 1.6 copy-done.17
  72.1 8.0 %front.2 = (f32[256,1024]{1,0:T(8,128)S(1)}, f32[256,1024]{1,0:T(8,128)S(1)}, bf16[256,1024]{1,0:T(8,128)(2,1)S(1)}, bf16[256,160]{1,0:T(8,128)(2,1)S(1)}) custom-call(bf16[512,2048]{1,0:T(8,128)(2,1)S(1)} %norm_rows.1.normed_ref, bf16[512,2048]{1,0:T(8,128)(2,1)S(1)} %pad_maximum_fusion.xa_ref, bf16[512,2048]{1,0:T(8,128)(2,1)} %collective-permute-done.9.xb_ref, ...), custom_call_target="tpu_custom_call" | custom-call | flops 7000000000 | bytes 7000000 | tf_op jit(solution)/shard_map/front/pallas_call | solution.py:397
  82.0 1.6 collective-permute-start.15
  83.6 2.3 collective-permute-start.13
  86.9 7.3 %front.3 = (f32[256,1024]{1,0:T(8,128)S(1)}, f32[256,1024]{1,0:T(8,128)S(1)}, bf16[256,1024]{1,0:T(8,128)(2,1)S(1)}, bf16[256,160]{1,0:T(8,128)(2,1)S(1)}) custom-call(bf16[512,2048]{1,0:T(8,128)(2,1)S(1)} %norm_rows.1.normed_ref, bf16[512,2048]{1,0:T(8,128)(2,1)S(1)} %pad_maximum_fusion.xa_ref, bf16[512,2048]{1,0:T(8,128)(2,1)} %collective-permute-done.9.xb_ref, ...), custom_call_target="tpu_custom_call" | custom-call | flops 7000000000 | bytes 7000000 | tf_op jit(solution)/shard_map/front/pallas_call | solution.py:397
  97.4 2.3 collective-permute-start.17
  99.7 2.3 collective-permute-start.16
  102.8 1.7 slice.426.wdt_ref
  106.4 6.2 %collective-permute-done.18 = bf16[256,160]{1,0:T(8,128)(2,1)S(1)} collective-permute-done((bf16[256,160]{1,0:T(8,128)(2,1)S(1)}, bf16[256,160]{1,0:T(8,128)(2,1)S(1)}, u32[]{:S(2)}, u32[]{:S(2)}) %collective-permute-start.18) | collective-permute-done | bytes 81952 | tf_op jit(solution)/shard_map/ppermute | solution.py:668
  112.8 9.2 %collective-permute-done.16 = bf16[256,160]{1,0:T(8,128)(2,1)} collective-permute-done((bf16[256,160]{1,0:T(8,128)(2,1)S(1)}, bf16[256,160]{1,0:T(8,128)(2,1)}, u32[]{:S(2)}, u32[]{:S(2)}) %collective-permute-start.16) | collective-permute-done | bytes 81952 | tf_op jit(solution)/shard_map/ppermute | solution.py:668
  124.9 11.5 %scan_forward.2 = (f32[33280,128]{1,0:T(8,128)}, f32[2048,128]{1,0:T(8,128)}, f32[256,1024]{1,0:T(8,128)}, bf16[256,1024]{1,0:T(8,128)(2,1)}, f32[128,128]{1,0:T(8,128)}) custom-call(s32[256]{0:T(256)} %get-tuple-element.230.keep_ref, bf16[256,128]{1,0:T(8,128)(2,1)} %slice.588.step_ref, f32[256,32]{1,0:T(8,128)} %slice.425.bc_ref, ...), custom_call_target="tpu_custom_call" | custom-call | flops 500000000 | bytes 500000 | tf_op jit(solution)/shard_map/scan_forward/pallas_call | solution.py:130
  136.3 11.8 %scan_forward.3 = (f32[33280,128]{1,0:T(8,128)}, f32[2048,128]{1,0:T(8,128)}, f32[256,1024]{1,0:T(8,128)}, bf16[256,1024]{1,0:T(8,128)(2,1)}, f32[128,128]{1,0:T(8,128)}) custom-call(s32[256]{0:T(256)} %get-tuple-element.229.keep_ref, bf16[256,128]{1,0:T(8,128)(2,1)} %slice.587.step_ref, f32[256,32]{1,0:T(8,128)} %slice.431.bc_ref, ...), custom_call_target="tpu_custom_call" | custom-call | flops 500000000 | bytes 500000 | tf_op jit(solution)/shard_map/scan_forward/pallas_call | solution.py:130
  149.0 1.9 constant_dynamic-update-slice_fusion.5
  157.1 3.3 convolution_convert_fusion.7.gg_ref
  160.5 4.9 %convolution_convert_fusion = bf16[512,2048]{1,0:T(8,128)(2,1)} fusion(bf16[512,1024]{1,0:T(8,128)(2,1)} %constant_dynamic-update-slice_fusion.5, bf16[1024,2048]{1,0:T(8,128)(2,1)S(1)} %dynamic-slice_dynamic-update-slice_fusion), kind=kOutput, calls=%fused_computation | convolution fusion | flops 2148532224 | bytes 7340032 | tf_op jit(solution)/shard_map/dot_general | solution.py:691
  166.5 4.5 %convolution_convert_fusion.6 = bf16[512,2048]{1,0:T(8,128)(2,1)} fusion(bf16[512,2048]{1,0:T(8,128)(2,1)} %all-gather.8.cloned.1.call-done, bf16[512,1024]{1,0:T(8,128)(2,1)} %constant_dynamic-update-slice_fusion.5), kind=kOutput, calls=%fused_computation.6 | convolution fusion | flops 1074790400 | bytes 4718592 | tf_op jit(solution)/shard_map/dot_general | solution.py:691
  171.0 2.7 convolution_convert_fusion.5
  173.6 25.5 %scan_backward.2 = (f32[256,1024]{1,0:T(8,128)}, bf16[256,1024]{1,0:T(8,128)(2,1)}, bf16[256,1024]{1,0:T(8,128)(2,1)}, bf16[256,160]{1,0:T(8,128)(2,1)}, f32[8,1...) custom-call(s32[256]{0:T(256)} %get-tuple-element.229.keep_ref, f32[256,32]{1,0:T(8,128)} %slice.431.bc_ref, ...), custom_call_target="tpu_custom_call" | custom-call | flops 22499999744 | bytes 22500000 | tf_op jit(solution)/shard_map/scan_backward/pallas_call | solution.py:299
  200.1 4.5 %collective-permute-start.20 = (bf16[256,160]{1,0:T(8,128)(2,1)}, bf16[256,160]{1,0:T(8,128)(2,1)}, u32[]{:S(2)}, u32[]{:S(2)}) collective-permute-start(bf16[256,160]{1,0:T(8,128)(2,1)} %get-tuple-element.105), channel_id=1, source_target_pairs={{0,2},{1,3},{2,0},{3,1},{4,6},{5,7},{6,4},{7,5},{8,10},{9,11},{10,... | collective-permute-start | bytes 245768 | tf_op jit(solution)/shard_map/ppermute | solution.py:668
  204.9 25.6 %scan_backward.3 = (f32[256,1024]{1,0:T(8,128)}, bf16[256,1024]{1,0:T(8,128)(2,1)}, bf16[256,1024]{1,0:T(8,128)(2,1)}, bf16[256,160]{1,0:T(8,128)(2,1)}, f32[8,1...) custom-call(s32[256]{0:T(256)} %get-tuple-element.230.keep_ref, f32[256,32]{1,0:T(8,128)} %slice.425.bc_ref, ...), custom_call_target="tpu_custom_call" | custom-call | flops 22499999744 | bytes 22500000 | tf_op jit(solution)/shard_map/scan_backward/pallas_call | solution.py:299
  231.4 1.5 add.425
  236.7 2.0 collective-permute-start.23
  238.6 1.6 add_convert_fusion.19
  243.2 1.9 collective-permute-start.27
  246.6 2.9 turn.2
  249.6 9.0 %collective-permute-done.25 = bf16[256,1024]{1,0:T(8,128)(2,1)S(1)} collective-permute-done((bf16[256,1024]{1,0:T(8,128)(2,1)S(1)}, bf16[256,1024]{1,0:T(8,128)(2,1)S(1)}, u32[]{:S(2)}, u32[]{:S(2)}) %collective-permute-start.25) | collective-permute-done | bytes 524320 | tf_op jit(solution)/shard_map/ppermute | solution.py:542
  259.8 1.7 collective-permute-start.53
  263.1 3.5 collective-permute-done.53
  272.1 6.0 %rear.2 = (bf16[256,2048]{1,0:T(8,128)(2,1)S(1)}, f32[1,2048]{1,0:T(1,128)S(1)}) custom-call(bf16[256,1024]{1,0:T(8,128)(2,1)S(1)} %get-tuple-element.122.gs_ref, bf16[256,1024]{1,0:T(8,128)(2,1)S(1)} %copy-done.10, bf16[512,2048]{1,0:T(8,128)(2,1)S(1)} %pad_maximum_fusion.xa_ref, bf16[512,2048]{1,0:T(8,128)(2,1)} %collective-permute-done.9.xb_ref, ...), custom_call_target="tpu_custom_call" | custom-call | flops 5000000000 | bytes 5000000 | tf_op jit(solution)/shard_map/rear/pallas_call | solution.py:513
  278.2 1.5 collective-permute-start.30
  279.7 3.6 turn.3
  286.0 6.0 %rear.3 = (bf16[256,2048]{1,0:T(8,128)(2,1)S(1)}, f32[1,2048]{1,0:T(1,128)S(1)}) custom-call(bf16[256,1024]{1,0:T(8,128)(2,1)S(1)} %get-tuple-element.128.gs_ref, bf16[256,1024]{1,0:T(8,128)(2,1)S(1)} %copy-done.8, bf16[512,2048]{1,0:T(8,128)(2,1)S(1)} %copy-done.1, bf16[512,2048]{1,0:T(8,128)(2,1)} %collective-permute-done.9.xb_ref, ...), custom_call_target="tpu_custom_call" | custom-call | flops 5000000000 | bytes 5000000 | tf_op jit(solution)/shard_map/rear/pallas_call | solution.py:513
  292.0 1.6 collective-permute-start.51
  293.6 1.5 collective-permute-start.50
  298.4 2.6 convolution_convert_fusion.2
  301.1 6.2 %concatenate.97 = f32[328,1024]{1,0:T(8,128)} concatenate(f32[160,1024]{1,0:T(8,128)} %fusion.8, f32[128,1024]{1,0:T(8,128)S(1)} %copy-done.41, f32[16,1024]{1,0:T(8,128)S(1)} %copy-done.50, f32[8,1024]{1,0:T(8,128)S(1)} %add.424, f32[8,1024]{1,0:T(8,128)S(1)} %copy-done.51, f32[2,1024]{1,0:T(2,128)S(1)} %bitcast.73, f32[6,1024]{1,0:T(8,128)S(1)} %broadcast_in_dim.213), dimensions={0} | concatenate | bytes 2686976 | tf_op jit(solution)/shard_map/concatenate | solution.py:869
  309.0 4.2 %convolution_convert_fusion.1 = bf16[512,2048]{1,0:T(8,128)(2,1)} fusion(bf16[512,512]{1,0:T(8,128)(2,1)S(1)} %slice-done, bf16[512,2048]{1,0:T(8,128)(2,1)} %copy-done.18), kind=kOutput, calls=%fused_computation.1 | convolution fusion | flops 1074790400 | bytes 4718592 | tf_op jit(solution)/shard_map/dot_general | solution.py:691
  314.0 1.6 collective-permute-start.44
  315.6 1.5 collective-permute-start.43
  317.0 1.7 convert_add_fusion.4
  323.5 2.4 collective-permute-start.47
  326.4 2.5 collective-permute-start.46
  329.6 4.6 %collective-permute-start.32 = (bf16[128,2048]{1,0:T(8,128)(2,1)}, bf16[128,2048]{1,0:T(8,128)(2,1)S(1)}, u32[]{:S(2)}, u32[]{:S(2)}) collective-permute-start(bf16[128,2048]{1,0:T(8,128)(2,1)} %add_convert_fusion.3), channel_id=1, source_target_pairs={{0,1},{1,2},{4,5},{5,6},{8,9},{9,10},{12,13},{13,14},{16,17},{17,1... | collective-permute-start | bytes 1572872 | tf_op jit(solution)/shard_map/ppermute | solution.py:604
  334.8 1.9 add_convert_fusion.7
  342.1 2.3 collective-permute-done.32
  344.6 4.3 %collective-permute-start.33 = (bf16[128,2048]{1,0:T(8,128)(2,1)S(1)}, bf16[128,2048]{1,0:T(8,128)(2,1)S(1)}, u32[]{:S(2)}, u32[]{:S(2)}) collective-permute-start(bf16[128,2048]{1,0:T(8,128)(2,1)S(1)} %add_convert_fusion.2), channel_id=1, source_target_pairs={{1,2},{2,3},{5,6},{6,7},{9,10},{10,11},{13,14},{14,15},{17,18},{18... | collective-permute-start | bytes 1572872 | tf_op jit(solution)/shard_map/ppermute | solution.py:604
  350.4 1.8 collective-permute-start.49
  356.8 3.6 collective-permute-start.40
  362.0 1.5 pad_maximum_fusion.2
  363.5 3.5 collective-permute-done.38
  367.0 7.8 %collective-permute-done.40 = bf16[128,2048]{1,0:T(8,128)(2,1)S(1)} collective-permute-done((bf16[128,2048]{1,0:T(8,128)(2,1)S(1)}, bf16[128,2048]{1,0:T(8,128)(2,1)S(1)}, u32[]{:S(2)}, u32[]{:S(2)}) %collective-permute-start.40) | collective-permute-done | bytes 524320 | tf_op jit(solution)/shard_map/ppermute | solution.py:610
  374.8 1.5 fusion.2
  376.3 2.9 fusion.5
  (347 shorter events, 86.2 us)
Async XLA Ops:
  7.2 62.4 %all-gather.4.cloned.1.call-start = ((), (), s32[]{:S(2)}) async-start(), calls=%async_computation.1 | async-start | bytes 2621440 | tf_op jit(solution)/shard_map/all_gather | solution.py:727
  8.0 116.3 %all-gather.6.cloned.1.call-start = ((), (), s32[]{:S(2)}) async-start(), calls=%async_computation.2 | async-start | bytes 4718592 | tf_op jit(solution)/shard_map/all_gather | solution.py:755
  8.0 7.0 %collective-permute-start.2 = (bf16[1,64]{1,0:T(2,128)(2,1)}, bf16[1,64]{1,0:T(2,128)(2,1)S(1)}, u32[]{:S(2)}, u32[]{:S(2)}) collective-permute-start(bf16[1,64]{1,0:T(2,128)(2,1)} %bitcast.83), channel_id=1, source_target_pairs={{0,1},{1,2},{2,3},{3,0},{4,5},{5,6},{6,7},{7,4},{8,9},{9,10},{10,1... | collective-permute-start | bytes 392 | tf_op jit(solution)/shard_map/ppermute | solution.py:732
  9.6 5.5 %collective-permute-start.1 = (bf16[1,64]{1,0:T(2,128)(2,1)}, bf16[1,64]{1,0:T(2,128)(2,1)S(1)}, u32[]{:S(2)}, u32[]{:S(2)}) collective-permute-start(bf16[1,64]{1,0:T(2,128)(2,1)} %bitcast.84), channel_id=1, source_target_pairs={{0,2},{1,3},{2,0},{3,1},{4,6},{5,7},{6,4},{7,5},{8,10},{9,11},{10,... | collective-permute-start | bytes 392 | tf_op jit(solution)/shard_map/ppermute | solution.py:732
  10.7 4.5 %collective-permute-start = (bf16[1,64]{1,0:T(2,128)(2,1)}, bf16[1,64]{1,0:T(2,128)(2,1)S(1)}, u32[]{:S(2)}, u32[]{:S(2)}) collective-permute-start(bf16[1,64]{1,0:T(2,128)(2,1)} %bitcast.85), channel_id=1, source_target_pairs={{0,3},{1,0},{2,1},{3,2},{4,7},{5,4},{6,5},{7,6},{8,11},{9,8},{10,9... | collective-permute-start | bytes 392 | tf_op jit(solution)/shard_map/ppermute | solution.py:732
  17.6 133.2 %all-gather.8.cloned.1.call-start = ((), (), s32[]{:S(2)}) async-start(), calls=%async_computation.3 | async-start | bytes 2621440 | tf_op jit(solution)/shard_map/all_gather | solution.py:756
  17.8 18.3 %collective-permute-start.10 = (bf16[128,2048]{1,0:T(8,128)(2,1)S(1)}, bf16[128,2048]{1,0:T(8,128)(2,1)S(1)}, u32[]{:S(2)}, u32[]{:S(2)}) collective-permute-start(bf16[128,2048]{1,0:T(8,128)(2,1)S(1)} %get-tuple-element.216), channel_id=1, source_target_pairs={{0,16},{4,20},{8,24},{12,28},{16,0},{20,4},{24,8},{28,12},{1,17},{... | collective-permute-start | bytes 1572872 | tf_op jit(solution)/shard_map/ppermute | solution.py:542
  19.4 14.3 %collective-permute-start.7 = (bf16[128,2048]{1,0:T(8,128)(2,1)S(1)}, bf16[128,2048]{1,0:T(8,128)(2,1)S(1)}, u32[]{:S(2)}, u32[]{:S(2)}) collective-permute-start(bf16[128,2048]{1,0:T(8,128)(2,1)S(1)} %get-tuple-element.217), channel_id=1, source_target_pairs={{0,8},{4,12},{8,0},{12,4},{16,24},{20,28},{24,16},{28,20},{1,9},{5... | collective-permute-start | bytes 1572872 | tf_op jit(solution)/shard_map/ppermute | solution.py:542
  21.9 12.6 %collective-permute-start.5 = (bf16[313,128]{1,0:T(8,128)(2,1)S(1)}, bf16[313,128]{1,0:T(8,128)(2,1)S(1)}, u32[]{:S(2)}, u32[]{:S(2)}) collective-permute-start(bf16[313,128]{1,0:T(8,128)(2,1)S(1)} %concatenate.76), channel_id=1, source_target_pairs={{0,24},{4,28},{8,16},{12,20},{16,8},{20,12},{24,0},{28,4},{1,25},{... | collective-permute-start | bytes 240392 | tf_op jit(solution)/shard_map/ppermute | solution.py:542
  22.5 12.0 %collective-permute-start.4 = (bf16[313,128]{1,0:T(8,128)(2,1)S(1)}, bf16[313,128]{1,0:T(8,128)(2,1)S(1)}, u32[]{:S(2)}, u32[]{:S(2)}) collective-permute-start(bf16[313,128]{1,0:T(8,128)(2,1)S(1)} %concatenate.76), channel_id=1, source_target_pairs={{0,16},{4,20},{8,24},{12,28},{16,0},{20,4},{24,8},{28,12},{1,17},{... | collective-permute-start | bytes 240392 | tf_op jit(solution)/shard_map/ppermute | solution.py:542
  24.0 11.4 %collective-permute-start.3 = (bf16[313,128]{1,0:T(8,128)(2,1)S(1)}, bf16[313,128]{1,0:T(8,128)(2,1)S(1)}, u32[]{:S(2)}, u32[]{:S(2)}) collective-permute-start(bf16[313,128]{1,0:T(8,128)(2,1)S(1)} %concatenate.76), channel_id=1, source_target_pairs={{0,8},{4,12},{8,0},{12,4},{16,24},{20,28},{24,16},{28,20},{1,9},{5... | collective-permute-start | bytes 240392 | tf_op jit(solution)/shard_map/ppermute | solution.py:542
  34.5 25.2 %copy-start.46 = (bf16[313,128]{1,0:T(8,128)(2,1)}, bf16[313,128]{1,0:T(8,128)(2,1)S(1)}, u32[]{:S(2)}) copy-start(bf16[313,128]{1,0:T(8,128)(2,1)S(1)} %collective-permute-done.4) | copy-start | bytes 240388
  35.4 22.9 %collective-permute-start.8 = (bf16[256,2048]{1,0:T(8,128)(2,1)S(1)}, bf16[256,2048]{1,0:T(8,128)(2,1)S(1)}, u32[]{:S(2)}, u32[]{:S(2)}) collective-permute-start(bf16[256,2048]{1,0:T(8,128)(2,1)S(1)} %pad_maximum_fusion.3), channel_id=1, source_target_pairs={{0,16},{4,20},{8,24},{12,28},{16,0},{20,4},{24,8},{28,12},{1,17},{... | collective-permute-start | bytes 3145736 | tf_op jit(solution)/shard_map/ppermute | solution.py:542
  36.2 23.6 %collective-permute-start.11 = (bf16[256,2048]{1,0:T(8,128)(2,1)S(1)}, bf16[256,2048]{1,0:T(8,128)(2,1)S(1)}, u32[]{:S(2)}, u32[]{:S(2)}) collective-permute-start(bf16[256,2048]{1,0:T(8,128)(2,1)S(1)} %pad_maximum_fusion.4), channel_id=1, source_target_pairs={{0,8},{4,12},{8,0},{12,4},{16,24},{20,28},{24,16},{28,20},{1,9},{5... | collective-permute-start | bytes 3145736 | tf_op jit(solution)/shard_map/ppermute | solution.py:542
  59.6 212.4 %copy-start = (bf16[512,2048]{1,0:T(8,128)(2,1)}, bf16[512,2048]{1,0:T(8,128)(2,1)S(1)}, u32[]{:S(2)}) copy-start(bf16[512,2048]{1,0:T(8,128)(2,1)S(1)} %pad_maximum_fusion.xa_ref) | copy-start | bytes 6291460
  59.7 12.5 %collective-permute-start.9 = (bf16[512,2048]{1,0:T(8,128)(2,1)S(1)}, bf16[512,2048]{1,0:T(8,128)(2,1)}, u32[]{:S(2)}, u32[]{:S(2)}) collective-permute-start(bf16[512,2048]{1,0:T(8,128)(2,1)S(1)} %pad_maximum_fusion.xa_ref), channel_id=1, source_target_pairs={{0,4},{4,0},{8,12},{12,8},{16,20},{20,16},{24,28},{28,24},{1,5},{5... | collective-permute-start | bytes 6291464 | tf_op jit(solution)/shard_map/ppermute | solution.py:542
  62.6 9.5 %collective-permute-start.12 = (bf16[512,2048]{1,0:T(8,128)(2,1)}, bf16[512,2048]{1,0:T(8,128)(2,1)}, u32[]{:S(2)}, u32[]{:S(2)}) collective-permute-start(bf16[512,2048]{1,0:T(8,128)(2,1)} %pad_maximum_fusion.1.ga_ref), channel_id=1, source_target_pairs={{0,4},{4,0},{8,12},{12,8},{16,20},{20,16},{24,28},{28,24},{1,5},{5... | collective-permute-start | bytes 6291464 | tf_op jit(solution)/shard_map/ppermute | solution.py:542
  63.5 183.0 %copy-start.11 = (s32[512,1]{1,0:T(8,128)}, s32[512,1]{1,0:T(8,128)S(1)}, u32[]{:S(2)}) copy-start(s32[512,1]{1,0:T(8,128)S(1)} %iota_subtract_fusion.dist_ref) | copy-start | bytes 6148
  64.6 2.7 collective-permute-start.6
  67.5 308.9 %reduce-scatter.2.cloned.1.call-start = ((), (), s32[]{:S(2)}) async-start(), calls=%async_computation.4 | async-start | bytes 2621440 | tf_op jit(solution)/shard_map/reduce_scatter | solution.py:808
  82.0 14.9 %collective-permute-start.15 = (bf16[256,160]{1,0:T(8,128)(2,1)S(1)}, bf16[256,160]{1,0:T(8,128)(2,1)S(1)}, u32[]{:S(2)}, u32[]{:S(2)}) collective-permute-start(bf16[256,160]{1,0:T(8,128)(2,1)S(1)} %get-tuple-element.83), channel_id=1, source_target_pairs={{0,3},{1,0},{2,1},{3,2},{4,7},{5,4},{6,5},{7,6},{8,11},{9,8},{10,9... | collective-permute-start | bytes 245768 | tf_op jit(solution)/shard_map/ppermute | solution.py:668
  83.6 13.4 %collective-permute-start.14 = (bf16[256,160]{1,0:T(8,128)(2,1)S(1)}, bf16[256,160]{1,0:T(8,128)(2,1)S(1)}, u32[]{:S(2)}, u32[]{:S(2)}) collective-permute-start(bf16[256,160]{1,0:T(8,128)(2,1)S(1)} %get-tuple-element.83), channel_id=1, source_target_pairs={{0,2},{1,3},{2,0},{3,1},{4,6},{5,7},{6,4},{7,5},{8,10},{9,11},{10,... | collective-permute-start | bytes 245768 | tf_op jit(solution)/shard_map/ppermute | solution.py:668
  83.6 13.4 %collective-permute-start.13 = (bf16[256,160]{1,0:T(8,128)(2,1)S(1)}, bf16[256,160]{1,0:T(8,128)(2,1)S(1)}, u32[]{:S(2)}, u32[]{:S(2)}) collective-permute-start(bf16[256,160]{1,0:T(8,128)(2,1)S(1)} %get-tuple-element.83), channel_id=1, source_target_pairs={{0,1},{1,2},{2,3},{3,0},{4,5},{5,6},{6,7},{7,4},{8,9},{9,10},{10,1... | collective-permute-start | bytes 245768 | tf_op jit(solution)/shard_map/ppermute | solution.py:668
  97.0 15.6 %collective-permute-start.18 = (bf16[256,160]{1,0:T(8,128)(2,1)S(1)}, bf16[256,160]{1,0:T(8,128)(2,1)S(1)}, u32[]{:S(2)}, u32[]{:S(2)}) collective-permute-start(bf16[256,160]{1,0:T(8,128)(2,1)S(1)} %get-tuple-element.91), channel_id=1, source_target_pairs={{0,3},{1,0},{2,1},{3,2},{4,7},{5,4},{6,5},{7,6},{8,11},{9,8},{10,9... | collective-permute-start | bytes 245768 | tf_op jit(solution)/shard_map/ppermute | solution.py:668
  97.4 15.4 %collective-permute-start.17 = (bf16[256,160]{1,0:T(8,128)(2,1)S(1)}, bf16[256,160]{1,0:T(8,128)(2,1)S(1)}, u32[]{:S(2)}, u32[]{:S(2)}) collective-permute-start(bf16[256,160]{1,0:T(8,128)(2,1)S(1)} %get-tuple-element.91), channel_id=1, source_target_pairs={{0,2},{1,3},{2,0},{3,1},{4,6},{5,7},{6,4},{7,5},{8,10},{9,11},{10,... | collective-permute-start | bytes 245768 | tf_op jit(solution)/shard_map/ppermute | solution.py:668
  99.7 22.3 %collective-permute-start.16 = (bf16[256,160]{1,0:T(8,128)(2,1)S(1)}, bf16[256,160]{1,0:T(8,128)(2,1)}, u32[]{:S(2)}, u32[]{:S(2)}) collective-permute-start(bf16[256,160]{1,0:T(8,128)(2,1)S(1)} %get-tuple-element.91), channel_id=1, source_target_pairs={{0,1},{1,2},{2,3},{3,0},{4,5},{5,6},{6,7},{7,4},{8,9},{9,10},{10,1... | collective-permute-start | bytes 245768 | tf_op jit(solution)/shard_map/ppermute | solution.py:668
  199.1 36.4 %collective-permute-start.21 = (bf16[256,160]{1,0:T(8,128)(2,1)}, bf16[256,160]{1,0:T(8,128)(2,1)}, u32[]{:S(2)}, u32[]{:S(2)}) collective-permute-start(bf16[256,160]{1,0:T(8,128)(2,1)} %get-tuple-element.105), channel_id=1, source_target_pairs={{0,3},{1,0},{2,1},{3,2},{4,7},{5,4},{6,5},{7,6},{8,11},{9,8},{10,9... | collective-permute-start | bytes 245768 | tf_op jit(solution)/shard_map/ppermute | solution.py:668
  200.1 35.4 %collective-permute-start.20 = (bf16[256,160]{1,0:T(8,128)(2,1)}, bf16[256,160]{1,0:T(8,128)(2,1)}, u32[]{:S(2)}, u32[]{:S(2)}) collective-permute-start(bf16[256,160]{1,0:T(8,128)(2,1)} %get-tuple-element.105), channel_id=1, source_target_pairs={{0,2},{1,3},{2,0},{3,1},{4,6},{5,7},{6,4},{7,5},{8,10},{9,11},{10,... | collective-permute-start | bytes 245768 | tf_op jit(solution)/shard_map/ppermute | solution.py:668
  204.6 30.9 %collective-permute-start.19 = (bf16[256,160]{1,0:T(8,128)(2,1)}, bf16[256,160]{1,0:T(8,128)(2,1)}, u32[]{:S(2)}, u32[]{:S(2)}) collective-permute-start(bf16[256,160]{1,0:T(8,128)(2,1)} %get-tuple-element.105), channel_id=1, source_target_pairs={{0,1},{1,2},{2,3},{3,0},{4,5},{5,6},{6,7},{7,4},{8,9},{9,10},{10,1... | collective-permute-start | bytes 245768 | tf_op jit(solution)/shard_map/ppermute | solution.py:668
  204.8 33.8 %collective-permute-start.22 = (bf16[512,2048]{1,0:T(8,128)(2,1)}, bf16[512,2048]{1,0:T(8,128)(2,1)}, u32[]{:S(2)}, u32[]{:S(2)}) collective-permute-start(bf16[512,2048]{1,0:T(8,128)(2,1)} %convolution_convert_fusion.6), channel_id=1, source_target_pairs={{0,4},{4,0},{8,12},{12,8},{16,20},{20,16},{24,28},{28,24},{1,5},{5... | collective-permute-start | bytes 6291464 | tf_op jit(solution)/shard_map/ppermute | solution.py:542
  204.9 25.6 %copy-start.53 = (f32[128,128]{1,0:T(8,128)S(1)}, f32[128,128]{1,0:T(8,128)}, u32[]{:S(2)}) copy-start(f32[128,128]{1,0:T(8,128)} %get-tuple-element.141) | copy-start | bytes 196612
  204.9 29.5 %copy-start.9 = (bf16[256,1024]{1,0:T(8,128)(2,1)S(1)}, bf16[256,1024]{1,0:T(8,128)(2,1)}, u32[]{:S(2)}) copy-start(bf16[256,1024]{1,0:T(8,128)(2,1)} %get-tuple-element.111.gx_ref) | copy-start | bytes 1572868
  236.7 6.5 %collective-permute-start.23 = (bf16[256,160]{1,0:T(8,128)(2,1)S(1)}, bf16[256,160]{1,0:T(8,128)(2,1)S(1)}, u32[]{:S(2)}, u32[]{:S(2)}) collective-permute-start(bf16[256,160]{1,0:T(8,128)(2,1)S(1)} %copy-done.40), channel_id=1, source_target_pairs={{0,1},{1,0},{2,3},{3,2},{4,5},{5,4},{6,7},{7,6},{8,9},{9,8},{10,11... | collective-permute-start | bytes 245768 | tf_op jit(solution)/shard_map/ppermute | solution.py:678
  241.7 28.7 %collective-permute-start.26 = (bf16[512,2048]{1,0:T(8,128)(2,1)S(1)}, bf16[512,2048]{1,0:T(8,128)(2,1)S(1)}, u32[]{:S(2)}, u32[]{:S(2)}) collective-permute-start(bf16[512,2048]{1,0:T(8,128)(2,1)S(1)} %convolution_convert_fusion.4), channel_id=1, source_target_pairs={{0,4},{4,0},{8,12},{12,8},{16,20},{20,16},{24,28},{28,24},{1,5},{5... | collective-permute-start | bytes 6291464 | tf_op jit(solution)/shard_map/ppermute | solution.py:542
  243.2 18.7 %collective-permute-start.27 = (bf16[256,160]{1,0:T(8,128)(2,1)S(1)}, bf16[256,160]{1,0:T(8,128)(2,1)S(1)}, u32[]{:S(2)}, u32[]{:S(2)}) collective-permute-start(bf16[256,160]{1,0:T(8,128)(2,1)S(1)} %fusion.22), channel_id=1, source_target_pairs={{0,2},{1,3},{2,0},{3,1},{4,6},{5,7},{6,4},{7,5},{8,10},{9,11},{10,... | collective-permute-start | bytes 245768 | tf_op jit(solution)/shard_map/ppermute | solution.py:678
  245.1 13.4 %collective-permute-start.24 = (bf16[256,1024]{1,0:T(8,128)(2,1)S(1)}, bf16[256,1024]{1,0:T(8,128)(2,1)S(1)}, u32[]{:S(2)}, u32[]{:S(2)}) collective-permute-start(bf16[256,1024]{1,0:T(8,128)(2,1)S(1)} %pad_maximum_fusion.8), channel_id=1, source_target_pairs={{0,8},{4,12},{8,0},{12,4},{16,24},{20,28},{24,16},{28,20},{1,9},{5... | collective-permute-start | bytes 1572872 | tf_op jit(solution)/shard_map/ppermute | solution.py:542
  245.2 13.3 %collective-permute-start.25 = (bf16[256,1024]{1,0:T(8,128)(2,1)S(1)}, bf16[256,1024]{1,0:T(8,128)(2,1)S(1)}, u32[]{:S(2)}, u32[]{:S(2)}) collective-permute-start(bf16[256,1024]{1,0:T(8,128)(2,1)S(1)} %pad_maximum_fusion.9), channel_id=1, source_target_pairs={{0,16},{4,20},{8,24},{12,28},{16,0},{20,4},{24,8},{28,12},{1,17},{... | collective-permute-start | bytes 1572872 | tf_op jit(solution)/shard_map/ppermute | solution.py:542
  246.5 36.9 %copy-start.31 = (bf16[512,2048]{1,0:T(8,128)(2,1)}, bf16[512,2048]{1,0:T(8,128)(2,1)S(1)}, u32[]{:S(2)}) copy-start(bf16[512,2048]{1,0:T(8,128)(2,1)S(1)} %convolution_convert_fusion.3) | copy-start | bytes 6291460
  259.8 6.8 %collective-permute-start.53 = (bf16[128,1024]{1,0:T(8,128)(2,1)S(1)}, bf16[128,1024]{1,0:T(8,128)(2,1)S(1)}, u32[]{:S(2)}, u32[]{:S(2)}) collective-permute-start(bf16[128,1024]{1,0:T(8,128)(2,1)S(1)} %get-tuple-element.208), channel_id=1, source_target_pairs={{0,8},{4,12},{8,0},{12,4},{16,24},{20,28},{24,16},{28,20},{1,9},{5... | collective-permute-start | bytes 786440 | tf_op jit(solution)/shard_map/ppermute | solution.py:542
  261.6 6.4 %collective-permute-start.52 = (bf16[128,1024]{1,0:T(8,128)(2,1)S(1)}, bf16[128,1024]{1,0:T(8,128)(2,1)S(1)}, u32[]{:S(2)}, u32[]{:S(2)}) collective-permute-start(bf16[128,1024]{1,0:T(8,128)(2,1)S(1)} %get-tuple-element.209), channel_id=1, source_target_pairs={{0,16},{4,20},{8,24},{12,28},{16,0},{20,4},{24,8},{28,12},{1,17},{... | collective-permute-start | bytes 786440 | tf_op jit(solution)/shard_map/ppermute | solution.py:542
  270.8 12.6 %collective-permute-start.28 = (bf16[256,1024]{1,0:T(8,128)(2,1)S(1)}, bf16[256,1024]{1,0:T(8,128)(2,1)S(1)}, u32[]{:S(2)}, u32[]{:S(2)}) collective-permute-start(bf16[256,1024]{1,0:T(8,128)(2,1)S(1)} %pad_maximum_fusion.10), channel_id=1, source_target_pairs={{0,8},{4,12},{8,0},{12,4},{16,24},{20,28},{24,16},{28,20},{1,9},{5... | collective-permute-start | bytes 1572872 | tf_op jit(solution)/shard_map/ppermute | solution.py:542
  271.4 12.1 %collective-permute-start.29 = (bf16[256,1024]{1,0:T(8,128)(2,1)S(1)}, bf16[256,1024]{1,0:T(8,128)(2,1)S(1)}, u32[]{:S(2)}, u32[]{:S(2)}) collective-permute-start(bf16[256,1024]{1,0:T(8,128)(2,1)S(1)} %pad_maximum_fusion.11), channel_id=1, source_target_pairs={{0,16},{4,20},{8,24},{12,28},{16,0},{20,4},{24,8},{28,12},{1,17},{... | collective-permute-start | bytes 1572872 | tf_op jit(solution)/shard_map/ppermute | solution.py:542
  278.2 19.2 %collective-permute-start.30 = (bf16[128,2048]{1,0:T(8,128)(2,1)S(1)}, bf16[128,2048]{1,0:T(8,128)(2,1)S(1)}, u32[]{:S(2)}, u32[]{:S(2)}) collective-permute-start(bf16[128,2048]{1,0:T(8,128)(2,1)S(1)} %constant_dynamic-slice_fusion.7), channel_id=1, source_target_pairs={{0,1},{4,5},{8,9},{12,13},{16,17},{20,21},{24,25},{28,29}} | collective-permute-start | bytes 1572872 | tf_op jit(solution)/shard_map/ppermute | solution.py:604
  292.0 21.2 %collective-permute-start.51 = (bf16[128,1024]{1,0:T(8,128)(2,1)}, bf16[128,1024]{1,0:T(8,128)(2,1)}, u32[]{:S(2)}, u32[]{:S(2)}) collective-permute-start(bf16[128,1024]{1,0:T(8,128)(2,1)} %get-tuple-element.202), channel_id=1, source_target_pairs={{0,8},{4,12},{8,0},{12,4},{16,24},{20,28},{24,16},{28,20},{1,9},{5... | collective-permute-start | bytes 786440 | tf_op jit(solution)/shard_map/ppermute | solution.py:542
  293.6 19.6 %collective-permute-start.50 = (bf16[128,1024]{1,0:T(8,128)(2,1)}, bf16[128,1024]{1,0:T(8,128)(2,1)}, u32[]{:S(2)}, u32[]{:S(2)}) collective-permute-start(bf16[128,1024]{1,0:T(8,128)(2,1)} %get-tuple-element.203), channel_id=1, source_target_pairs={{0,16},{4,20},{8,24},{12,28},{16,0},{20,4},{24,8},{28,12},{1,17},{... | collective-permute-start | bytes 786440 | tf_op jit(solution)/shard_map/ppermute | solution.py:542
  295.9 43.7 %collective-permute-start.36 = (bf16[128,2048]{1,0:T(8,128)(2,1)}, bf16[128,2048]{1,0:T(8,128)(2,1)}, u32[]{:S(2)}, u32[]{:S(2)}) collective-permute-start(bf16[128,2048]{1,0:T(8,128)(2,1)} %constant_dynamic-slice_fusion.6), channel_id=1, source_target_pairs={{3,2},{7,6},{11,10},{15,14},{19,18},{23,22},{27,26},{31,30}} | collective-permute-start | bytes 1572872 | tf_op jit(solution)/shard_map/ppermute | solution.py:610
  301.0 33.8 %collective-permute-start.31 = (bf16[512,2048]{1,0:T(8,128)(2,1)}, bf16[512,2048]{1,0:T(8,128)(2,1)}, u32[]{:S(2)}, u32[]{:S(2)}) collective-permute-start(bf16[512,2048]{1,0:T(8,128)(2,1)} %convolution_convert_fusion.2), channel_id=1, source_target_pairs={{0,4},{4,0},{8,12},{12,8},{16,20},{20,16},{24,28},{28,24},{1,5},{5... | collective-permute-start | bytes 6291464 | tf_op jit(solution)/shard_map/ppermute | solution.py:542
  308.5 4.8 %collective-permute-start.41 = (bf16[328,512]{1,0:T(8,128)(2,1)S(1)}, bf16[328,512]{1,0:T(8,128)(2,1)S(1)}, u32[]{:S(2)}, u32[]{:S(2)}) collective-permute-start(bf16[328,512]{1,0:T(8,128)(2,1)S(1)} %slice.586), channel_id=1, source_target_pairs={{0,4},{4,0},{8,12},{12,8},{16,20},{20,16},{24,28},{28,24},{1,5},{5... | collective-permute-start | bytes 1007624 | tf_op jit(solution)/shard_map/ppermute | solution.py:542
  313.5 5.4 %collective-permute-start.42 = (bf16[328,128]{1,0:T(8,128)(2,1)S(1)}, bf16[328,128]{1,0:T(8,128)(2,1)S(1)}, u32[]{:S(2)}, u32[]{:S(2)}) collective-permute-start(bf16[328,128]{1,0:T(8,128)(2,1)S(1)} %get-tuple-element.223), channel_id=1, source_target_pairs={{0,8},{4,12},{8,0},{12,4},{16,24},{20,28},{24,16},{28,20},{1,9},{5... | collective-permute-start | bytes 251912 | tf_op jit(solution)/shard_map/ppermute | solution.py:542
  314.0 6.0 %collective-permute-start.44 = (bf16[328,128]{1,0:T(8,128)(2,1)S(1)}, bf16[328,128]{1,0:T(8,128)(2,1)S(1)}, u32[]{:S(2)}, u32[]{:S(2)}) collective-permute-start(bf16[328,128]{1,0:T(8,128)(2,1)S(1)} %get-tuple-element.224), channel_id=1, source_target_pairs={{0,24},{4,28},{8,16},{12,20},{16,8},{20,12},{24,0},{28,4},{1,25},{... | collective-permute-start | bytes 251912 | tf_op jit(solution)/shard_map/ppermute | solution.py:542
  315.6 5.5 %collective-permute-start.43 = (bf16[328,128]{1,0:T(8,128)(2,1)S(1)}, bf16[328,128]{1,0:T(8,128)(2,1)S(1)}, u32[]{:S(2)}, u32[]{:S(2)}) collective-permute-start(bf16[328,128]{1,0:T(8,128)(2,1)S(1)} %get-tuple-element.225), channel_id=1, source_target_pairs={{0,16},{4,20},{8,24},{12,28},{16,0},{20,4},{24,8},{28,12},{1,17},{... | collective-permute-start | bytes 251912 | tf_op jit(solution)/shard_map/ppermute | solution.py:542
  323.1 6.5 %collective-permute-start.45 = (bf16[1,64]{1,0:T(2,128)(2,1)S(1)}, bf16[1,64]{1,0:T(2,128)(2,1)S(1)}, u32[]{:S(2)}, u32[]{:S(2)}) collective-permute-start(bf16[1,64]{1,0:T(2,128)(2,1)S(1)} %get-tuple-element.231), channel_id=1, source_target_pairs={{0,1},{1,2},{2,3},{3,0},{4,5},{5,6},{6,7},{7,4},{8,9},{9,10},{10,1... | collective-permute-start | bytes 392 | tf_op jit(solution)/shard_map/ppermute | solution.py:891
  323.5 10.8 %collective-permute-start.47 = (bf16[1,64]{1,0:T(2,128)(2,1)S(1)}, bf16[1,64]{1,0:T(2,128)(2,1)S(1)}, u32[]{:S(2)}, u32[]{:S(2)}) collective-permute-start(bf16[1,64]{1,0:T(2,128)(2,1)S(1)} %get-tuple-element.232), channel_id=1, source_target_pairs={{0,3},{1,0},{2,1},{3,2},{4,7},{5,4},{6,5},{7,6},{8,11},{9,8},{10,9... | collective-permute-start | bytes 392 | tf_op jit(solution)/shard_map/ppermute | solution.py:891
  326.4 7.9 %collective-permute-start.46 = (bf16[1,64]{1,0:T(2,128)(2,1)S(1)}, bf16[1,64]{1,0:T(2,128)(2,1)S(1)}, u32[]{:S(2)}, u32[]{:S(2)}) collective-permute-start(bf16[1,64]{1,0:T(2,128)(2,1)S(1)} %get-tuple-element.233), channel_id=1, source_target_pairs={{0,2},{1,3},{2,0},{3,1},{4,6},{5,7},{6,4},{7,5},{8,10},{9,11},{10,... | collective-permute-start | bytes 392 | tf_op jit(solution)/shard_map/ppermute | solution.py:891
  329.6 14.9 %collective-permute-start.32 = (bf16[128,2048]{1,0:T(8,128)(2,1)}, bf16[128,2048]{1,0:T(8,128)(2,1)S(1)}, u32[]{:S(2)}, u32[]{:S(2)}) collective-permute-start(bf16[128,2048]{1,0:T(8,128)(2,1)} %add_convert_fusion.3), channel_id=1, source_target_pairs={{0,1},{1,2},{4,5},{5,6},{8,9},{9,10},{12,13},{13,14},{16,17},{17,1... | collective-permute-start | bytes 1572872 | tf_op jit(solution)/shard_map/ppermute | solution.py:604
  336.7 12.2 %collective-permute-start.35 = (bf16[256,1024]{1,0:T(8,128)(2,1)S(1)}, bf16[256,1024]{1,0:T(8,128)(2,1)S(1)}, u32[]{:S(2)}, u32[]{:S(2)}) collective-permute-start(bf16[256,1024]{1,0:T(8,128)(2,1)S(1)} %pad_maximum_fusion.12), channel_id=1, source_target_pairs={{0,8},{4,12},{8,0},{12,4},{16,24},{20,28},{24,16},{28,20},{1,9},{5... | collective-permute-start | bytes 1572872 | tf_op jit(solution)/shard_map/ppermute | solution.py:542
  337.5 11.6 %collective-permute-start.37 = (bf16[256,1024]{1,0:T(8,128)(2,1)S(1)}, bf16[256,1024]{1,0:T(8,128)(2,1)S(1)}, u32[]{:S(2)}, u32[]{:S(2)}) collective-permute-start(bf16[256,1024]{1,0:T(8,128)(2,1)S(1)} %pad_maximum_fusion.13), channel_id=1, source_target_pairs={{0,16},{4,20},{8,24},{12,28},{16,0},{20,4},{24,8},{28,12},{1,17},{... | collective-permute-start | bytes 1572872 | tf_op jit(solution)/shard_map/ppermute | solution.py:542
  338.9 24.5 %collective-permute-start.34 = (bf16[128,2048]{1,0:T(8,128)(2,1)S(1)}, bf16[128,2048]{1,0:T(8,128)(2,1)S(1)}, u32[]{:S(2)}, u32[]{:S(2)}) collective-permute-start(bf16[128,2048]{1,0:T(8,128)(2,1)S(1)} %constant_dynamic-slice_fusion.4), channel_id=1, source_target_pairs={{3,2},{7,6},{11,10},{15,14},{19,18},{23,22},{27,26},{31,30}} | collective-permute-start | bytes 1572872 | tf_op jit(solution)/shard_map/ppermute | solution.py:610
  340.8 13.5 %collective-permute-start.39 = (bf16[128,2048]{1,0:T(8,128)(2,1)S(1)}, bf16[128,2048]{1,0:T(8,128)(2,1)S(1)}, u32[]{:S(2)}, u32[]{:S(2)}) collective-permute-start(bf16[128,2048]{1,0:T(8,128)(2,1)S(1)} %add_convert_fusion.1), channel_id=1, source_target_pairs={{2,1},{3,2},{6,5},{7,6},{10,9},{11,10},{14,13},{15,14},{18,17},{19... | collective-permute-start | bytes 1572872 | tf_op jit(solution)/shard_map/ppermute | solution.py:610
  344.6 18.8 %collective-permute-start.33 = (bf16[128,2048]{1,0:T(8,128)(2,1)S(1)}, bf16[128,2048]{1,0:T(8,128)(2,1)S(1)}, u32[]{:S(2)}, u32[]{:S(2)}) collective-permute-start(bf16[128,2048]{1,0:T(8,128)(2,1)S(1)} %add_convert_fusion.2), channel_id=1, source_target_pairs={{1,2},{2,3},{5,6},{6,7},{9,10},{10,11},{13,14},{14,15},{17,18},{18... | collective-permute-start | bytes 1572872 | tf_op jit(solution)/shard_map/ppermute | solution.py:604
  350.4 6.4 %collective-permute-start.49 = (bf16[128,1024]{1,0:T(8,128)(2,1)S(1)}, bf16[128,1024]{1,0:T(8,128)(2,1)S(1)}, u32[]{:S(2)}, u32[]{:S(2)}) collective-permute-start(bf16[128,1024]{1,0:T(8,128)(2,1)S(1)} %get-tuple-element.196), channel_id=1, source_target_pairs={{0,8},{4,12},{8,0},{12,4},{16,24},{20,28},{24,16},{28,20},{1,9},{5... | collective-permute-start | bytes 786440 | tf_op jit(solution)/shard_map/ppermute | solution.py:542
  352.2 8.2 %collective-permute-start.48 = (bf16[128,1024]{1,0:T(8,128)(2,1)S(1)}, bf16[128,1024]{1,0:T(8,128)(2,1)S(1)}, u32[]{:S(2)}, u32[]{:S(2)}) collective-permute-start(bf16[128,1024]{1,0:T(8,128)(2,1)S(1)} %get-tuple-element.197), channel_id=1, source_target_pairs={{0,16},{4,20},{8,24},{12,28},{16,0},{20,4},{24,8},{28,12},{1,17},{... | collective-permute-start | bytes 786440 | tf_op jit(solution)/shard_map/ppermute | solution.py:542
  354.4 12.6 %collective-permute-start.38 = (bf16[128,2048]{1,0:T(8,128)(2,1)S(1)}, bf16[128,2048]{1,0:T(8,128)(2,1)S(1)}, u32[]{:S(2)}, u32[]{:S(2)}) collective-permute-start(bf16[128,2048]{1,0:T(8,128)(2,1)S(1)} %constant_dynamic-slice_fusion.3), channel_id=1, source_target_pairs={{0,1},{4,5},{8,9},{12,13},{16,17},{20,21},{24,25},{28,29}} | collective-permute-start | bytes 1572872 | tf_op jit(solution)/shard_map/ppermute | solution.py:604
  356.8 17.9 %collective-permute-start.40 = (bf16[128,2048]{1,0:T(8,128)(2,1)S(1)}, bf16[128,2048]{1,0:T(8,128)(2,1)S(1)}, u32[]{:S(2)}, u32[]{:S(2)}) collective-permute-start(bf16[128,2048]{1,0:T(8,128)(2,1)S(1)} %add_convert_fusion), channel_id=1, source_target_pairs={{1,0},{2,1},{5,4},{6,5},{9,8},{10,9},{13,12},{14,13},{17,16},{18,1... | collective-permute-start | bytes 1572872 | tf_op jit(solution)/shard_map/ppermute | solution.py:610
  (59 other events, 367.9 us)
Sparse Core Ops, SparseCore 0:
  9.6 45.5 all-gather.3
  57.1 37.0 all-gather.5
  95.7 48.0 all-gather.7
  165.5 48.7 reduce-scatter.1

commit v3 on v2

v3 whole, which is shorter than its diff:
```python
import functools
import math

import jax
import jax.numpy as jnp
from jax import lax
from jax.experimental import pallas as pl
from jax.experimental.pallas import tpu as pltpu
from jax.sharding import PartitionSpec as P

EPSILON = 1e-05
f32 = jnp.float32
bf16 = jnp.bfloat16
BIG = 1e30
LANES = 128
SUB = 8


def cost(micros):
    return pl.CostEstimate(flops=int(micros * 1e9), transcendentals=0, bytes_accessed=int(micros * 1e6))


def tile_rows(ti, j, subs):
    return pl.ds((ti * subs + j) * SUB, SUB)


def put_tiles(ref, value, subs):
    for ti in range(value.shape[0] // SUB):
        for j in range(subs):
            ref[tile_rows(ti, j, subs), :] = value[ti * SUB : (ti + 1) * SUB, j * LANES : (j + 1) * LANES]


def get_tiles(ref, rows, subs):
    lines = []
    for ti in range(rows // SUB):
        lines.append(jnp.concatenate([ref[tile_rows(ti, j, subs), :] for j in range(subs)], axis=1))
    return jnp.concatenate(lines, axis=0)


def put_spread(ref, value, count):
    for ti in range(value.shape[0] // SUB):
        for n in range(count):
            ref[pl.ds((ti * count + n) * SUB, SUB), :] = jnp.broadcast_to(
                value[ti * SUB : (ti + 1) * SUB, n : n + 1], (SUB, LANES)
            )


def fwd_body(
    states, subs, first_row, count, keep_ref, *refs
):
    part_refs, refs = refs[:count], refs[count:]
    wdt_ref, db_ref, ds_ref, dec_ref, inner_ref, gate_ref, h0_ref = refs[:7]
    hs_ref, dl_ref, ys_ref, gated_ref, mixed_ref, h_ref, du_sc, bb_sc, y_sc = refs[-9:]
    chunk = pl.program_id(0)
    rows = inner_ref.shape[0]
    span = states * subs
    rank = wdt_ref.shape[0]

    @pl.when(chunk == 0)
    def _():
        h_ref[...] = h0_ref[...]

    mixed = part_refs[0][...].astype(f32)
    for part_ref in part_refs[1:]:
        mixed = mixed + part_ref[...].astype(f32)
    mixed_ref[...] = mixed
    step_in = mixed[:, :rank].astype(bf16)
    raw = jnp.dot(step_in, wdt_ref[...], preferred_element_type=f32) + db_ref[...]
    delta = jnp.maximum(raw, 0.0) + jnp.log1p(jnp.exp(-jnp.abs(raw)))
    inner = inner_ref[...].astype(f32)
    put_tiles(dl_ref, delta, subs)
    put_tiles(du_sc, delta * inner, subs)
    put_spread(bb_sc, mixed[:, rank:], 2 * states)
    hs_ref[pl.ds(0, span), :] = h_ref[...]
    decs = [dec_ref[pl.ds(n * subs, subs), :] for n in range(states)]

    def step(ti, hs):
        hs = list(hs)
        for s in range(SUB):
            t = ti * SUB + s
            row = ti * (subs * SUB) + s
            d = dl_ref[pl.ds(row, subs, stride=SUB), :]
            u = du_sc[pl.ds(row, subs, stride=SUB), :]
            d = jnp.where(keep_ref[first_row + chunk * rows + t] > 0, d, BIG)
            y = None
            for n in range(states):
                b = bb_sc[pl.ds((ti * 2 * states + n) * SUB + s, subs, stride=0), :]
                c = bb_sc[pl.ds((ti * 2 * states + states + n) * SUB + s, subs, stride=0), :]
                hs[n] = jnp.exp2(d * decs[n]) * hs[n] + u * b
                hs_ref[pl.ds(pl.multiple_of((t + 1) * span + n * subs, subs), subs), :] = hs[n]
                y = c * hs[n] if y is None else y + c * hs[n]
            y_sc[pl.ds(row, subs, stride=SUB), :] = y
        return tuple(hs)

    start = tuple(h_ref[pl.ds(n * subs, subs), :] for n in range(states))
    hs = lax.fori_loop(0, rows // SUB, step, start)
    for n in range(states):
        h_ref[pl.ds(n * subs, subs), :] = hs[n]
    total = get_tiles(y_sc, rows, subs) + ds_ref[...] * inner
    ys_ref[...] = total
    gate = gate_ref[...]
    gated_ref[...] = (total * gate / (1.0 + jnp.exp(-gate))).astype(bf16)


def scan_forward(h, keep, parts, wdt, dt_bias, d_skip, dec, inner, gate, h0, into=None, chunk_rows=64):
    rows, channels = gate.shape
    subs = channels // LANES
    rank = wdt.shape[0]
    mix = parts[0].shape[1]
    states = (mix - rank) // 2
    chunks = rows // chunk_rows
    span = states * subs

    def row_block(width, start=0):
        return pl.BlockSpec((chunk_rows, width), lambda i, *_: (start + i, 0))

    def whole(a):
        return pl.BlockSpec(a.shape, lambda i, *_: (0, 0))

    extra = [] if into is None else [into]
    grid_spec = pltpu.PrefetchScalarGridSpec(
        num_scalar_prefetch=1,
        grid=(chunks,),
        in_specs=[row_block(mix) for _ in parts]
        + [whole(wdt), whole(dt_bias), whole(d_skip), whole(dec), row_block(channels, h * chunks), row_block(channels), whole(h0)]
        + [pl.BlockSpec(memory_space=pl.ANY) for _ in extra],
        out_specs=[
            pl.BlockSpec(((chunk_rows + 1) * span, LANES), lambda i, *_: (i, 0)),
            pl.BlockSpec((chunk_rows * subs, LANES), lambda i, *_: (i, 0)),
            row_block(channels), row_block(channels, h * chunks), row_block(mix), whole(h0),
        ],
        scratch_shapes=[
            pltpu.VMEM((chunk_rows * subs, LANES), f32),
            pltpu.VMEM((chunk_rows * 2 * states, LANES), f32),
            pltpu.VMEM((chunk_rows * subs, LANES), f32),
        ],
    )
    made = jax.ShapeDtypeStruct
    return pl.pallas_call(
        functools.partial(fwd_body, states, subs, h * rows, len(parts)),
        grid_spec=grid_spec,
        out_shape=[
            made((chunks * (chunk_rows + 1) * span, LANES), f32), made((rows * subs, LANES), f32),
            made((rows, channels), f32), made(inner.shape, bf16), made((rows, mix), f32), made((span, LANES), f32),
        ],
        input_output_aliases={} if into is None else {len(parts) + 8: 3},
        compiler_params=pltpu.CompilerParams(vmem_limit_bytes=58 << 20),
        cost_estimate=cost(0.02),
        name="scan_forward",
    )(keep, *parts, wdt, dt_bias, d_skip, dec, inner, gate, h0, *extra)


def fold_rows(parts, sub_iota):
    if parts[0].shape[0] != SUB:
        return jnp.concatenate([jnp.sum(p, axis=0, keepdims=True) for p in parts], axis=0)
    upper = sub_iota < 4
    xs = [
        jnp.where(upper, parts[n], parts[n + 4]) + pltpu.roll(jnp.where(upper, parts[n + 4], parts[n]), 4, 0)
        for n in range(4)
    ]
    pair = (sub_iota & 3) < 2
    ys = [
        jnp.where(pair, xs[n] + pltpu.roll(xs[n], 6, 0), xs[n + 2] + pltpu.roll(xs[n + 2], 2, 0))
        for n in range(2)
    ]
    even = (sub_iota & 1) == 0
    return jnp.where(even, ys[0] + pltpu.roll(ys[0], 7, 0), ys[1] + pltpu.roll(ys[1], 1, 0))


def bwd_body(
    states, subs, first_row, keep_ref, fwd_ref, wdt_ref, dst_ref, dec_ref, inner_ref, gate_ref, gg_ref, ys_ref, hs_ref,
    dl_ref, gh0_ref, *refs
):
    gi_ref, gx_ref, gp_ref, mixed_ref, red_ref, acc_ref, gh_ref, in_sc, gy_sc, bb_sc, gd_sc, go_sc, r_sc = refs[-13:]
    i = pl.program_id(0)
    last = pl.num_programs(0) - 1
    chunk = last - i
    rows = inner_ref.shape[0]
    all_rows = r_sc.shape[0] // (2 * states)
    span = states * subs
    rank = wdt_ref.shape[0]

    @pl.when(i == 0)
    def _():
        gh_ref[...] = gh0_ref[...]
        acc_ref[...] = jnp.zeros_like(acc_ref)
        red_ref[...] = jnp.zeros_like(red_ref)

    gate = gate_ref[...]
    sig = 1.0 / (1.0 + jnp.exp(-gate))
    gg = gg_ref[...].astype(f32)
    gy_all = gg * (gate * sig)
    gx_ref[...] = (gg * ys_ref[...] * (sig * (1.0 + gate * (1.0 - sig)))).astype(bf16)
    inner_all = inner_ref[...].astype(f32)
    red_ref[pl.ds(0, 1), :] += jnp.sum(gy_all * inner_all, axis=0, keepdims=True)
    put_tiles(gy_sc, gy_all, subs)
    put_tiles(in_sc, inner_all, subs)
    put_spread(bb_sc, fwd_ref[...][:, rank:], 2 * states)
    sub_iota = lax.broadcasted_iota(jnp.int32, (SUB, LANES), 0)
    skip = dst_ref[...]
    order = (0, 4, 2, 6, 1, 5, 3, 7)

    def step(k, carried):
        ghs = list(carried[:states])
        accs = list(carried[states:])
        ti = rows // SUB - 1 - k
        for s in reversed(range(SUB)):
            t = ti * SUB + s
            row = ti * (subs * SUB) + s
            d = dl_ref[pl.ds(row, subs, stride=SUB), :]
            v = in_sc[pl.ds(row, subs, stride=SUB), :]
            gy = gy_sc[pl.ds(row, subs, stride=SUB), :]
            u = d * v
            da = jnp.where(keep_ref[first_row + chunk * rows + t] > 0, d, BIG)
            gd = gs = None
            for g in range(states // SUB):
                pb = [None] * SUB
                pc = [None] * SUB
                for o in order:
                    n = g * SUB + o
                    b = bb_sc[pl.ds((ti * 2 * states + n) * SUB + s, subs, stride=0), :]
                    c = bb_sc[pl.ds((ti * 2 * states + states + n) * SUB + s, subs, stride=0), :]
                    dec = dec_ref[pl.ds(n * subs, subs), :]
                    before = hs_ref[pl.ds(pl.multiple_of(t * span + n * subs, subs), subs), :]
                    after = hs_ref[pl.ds(pl.multiple_of((t + 1) * span + n * subs, subs), subs), :]
                    gh = c * gy + ghs[n]
                    ghs[n] = jnp.exp2(da * dec) * gh
                    q = ghs[n] * before
                    gd = dec * q if gd is None else gd + dec * q
                    accs[n] = accs[n] + q * d
                    gs = gh * b if gs is None else gs + gh * b
                    pb[o] = gh * u
                    pc[o] = after * gy
                at = chunk * rows + t
                r_sc[pl.ds(g * SUB * all_rows + at, SUB, stride=all_rows), :] = fold_rows(pb, sub_iota)
                r_sc[pl.ds((states + g * SUB) * all_rows + at, SUB, stride=all_rows), :] = fold_rows(pc, sub_iota)
            gd_sc[pl.ds(row, subs, stride=SUB), :] = gd * math.log(2.0) + gs * v
            go_sc[pl.ds(row, subs, stride=SUB), :] = gy * skip + gs * d
        return tuple(ghs + accs)

    init = tuple(gh_ref[pl.ds(n * subs, subs), :] for n in range(states))
    init = init + tuple(acc_ref[pl.ds(n * subs, subs), :] for n in range(states))
    out = lax.fori_loop(0, rows // SUB, step, init)
    for n in range(states):
        gh_ref[pl.ds(n * subs, subs), :] = out[n]
        acc_ref[pl.ds(n * subs, subs), :] = out[states + n]
    gi_ref[...] = get_tiles(go_sc, rows, subs)
    d_all = get_tiles(dl_ref, rows, subs)
    series = d_all * (1.0 - d_all * (0.5 - d_all * (1.0 / 6 - d_all * (1.0 / 24))))
    slope = jnp.where(d_all < 0.03125, series, 1.0 - jnp.exp(-d_all))
    gp = get_tiles(gd_sc, rows, subs) * slope
    red_ref[pl.ds(1, 1), :] += jnp.sum(gp, axis=0, keepdims=True)
    low = gp.astype(bf16)
    gp_ref[...] = low
    mixed_ref[pl.ds(pl.multiple_of(chunk * rows, rows), rows), pl.ds(0, rank)] = lax.dot_general(
        low, wdt_ref[...], (((1,), (1,)), ((), ())), preferred_element_type=f32
    ).astype(bf16)

    @pl.when(i == last)
    def _():
        lane = lax.broadcasted_iota(jnp.int32, (LANES, LANES), 1)
        total = jnp.zeros((all_rows, LANES), f32)
        for n in range(2 * states):
            pick = jnp.where(lane == n, 1.0, 0.0).astype(bf16)
            part = r_sc[pl.ds(n * all_rows, all_rows), :].astype(bf16)
            total = total + jnp.dot(part, pick, preferred_element_type=f32)
        mixed_ref[:, pl.ds(rank, 2 * states)] = total[:, : 2 * states].astype(bf16)


def scan_backward(h, keep, mixed, wdt, d_skip, dec, inner, gate, gg, ysum, hs, delta_tm, gh0, into=(), chunk_rows=64):
    rows, channels = gate.shape
    subs = channels // LANES
    rank = wdt.shape[0]
    mix = mixed.shape[1]
    states = (mix - rank) // 2
    chunks = rows // chunk_rows
    span = states * subs
    skip_tm = d_skip.reshape(subs, LANES)

    def row_block(width, start=0):
        return pl.BlockSpec((chunk_rows, width), lambda i, *_: (start + chunks - 1 - i, 0))

    def fixed(shape):
        return pl.BlockSpec(shape, lambda i, *_: (0, 0))

    tile = pltpu.VMEM((chunk_rows * subs, LANES), f32)
    first = h * chunks
    grid_spec = pltpu.PrefetchScalarGridSpec(
        num_scalar_prefetch=1,
        grid=(chunks,),
        in_specs=[
            row_block(mix), fixed(wdt.shape), fixed(skip_tm.shape), fixed(dec.shape),
            row_block(channels, first), row_block(channels), row_block(channels, first), row_block(channels),
            pl.BlockSpec(((chunk_rows + 1) * span, LANES), lambda i, *_: (chunks - 1 - i, 0)),
            pl.BlockSpec((chunk_rows * subs, LANES), lambda i, *_: (chunks - 1 - i, 0)), fixed(gh0.shape),
        ]
        + [pl.BlockSpec(memory_space=pl.ANY) for _ in into],
        out_specs=[
            row_block(channels), row_block(channels, first), row_block(channels, first), fixed((rows, mix)),
            fixed((8, channels)), fixed((span, LANES)), fixed((span, LANES)),
        ],
        scratch_shapes=[
            tile, tile, pltpu.VMEM((chunk_rows * 2 * states, LANES), f32), tile, tile,
            pltpu.VMEM((2 * states * rows, LANES), f32),
        ],
    )
    made = jax.ShapeDtypeStruct
    return pl.pallas_call(
        functools.partial(bwd_body, states, subs, h * rows),
        grid_spec=grid_spec,
        out_shape=[
            made((rows, channels), f32), made(inner.shape, bf16), made(inner.shape, bf16),
            made((rows, mix), bf16), made((8, channels), f32), made((span, LANES), f32),
            made((span, LANES), f32),
        ],
        input_output_aliases={12 + i: 1 + i for i in range(len(into))},
        compiler_params=pltpu.CompilerParams(vmem_limit_bytes=58 << 20),
        cost_estimate=cost(0.02),
        name="scan_backward",
    )(keep, mixed, wdt, skip_tm, dec, inner, gate, gg, ysum, hs, delta_tm, gh0, *into)


def norm_body(gain_ref, rows_ref, out_ref):
    value = rows_ref[...].astype(f32)
    factor = lax.rsqrt(jnp.mean(value * value, axis=1, keepdims=True) + EPSILON)
    out_ref[...] = (value * factor * gain_ref[...]).astype(bf16)


def norm_rows(rows_all, gain, parts):
    rows, width = rows_all.shape
    block = pl.BlockSpec((rows // parts, width), lambda i: (i, 0))
    return pl.pallas_call(
        norm_body,
        grid=(parts,),
        in_specs=[pl.BlockSpec(gain.shape, lambda i: (0, 0)), block],
        out_specs=block,
        out_shape=jax.ShapeDtypeStruct((rows, width), bf16),
        compiler_params=pltpu.CompilerParams(vmem_limit_bytes=24 << 20),
        cost_estimate=cost(0.02),
        name="norm_rows",
    )(gain, rows_all)


def weave(one, two, own):
    pieces = []
    for at in range(0, one.shape[0], own):
        pieces += [one[at : at + own], two[at : at + own]]
    return jnp.concatenate(pieces, axis=0)


def weight_specs(chunk, width):
    whole = pl.BlockSpec((chunk, width), lambda i: (0, 0))
    first = pl.BlockSpec((chunk // 2, width), lambda i: (jnp.minimum(i, 1), 0))
    second = pl.BlockSpec((chunk // 2, width), lambda i: (jnp.maximum(i - 2, 0), 0))
    return [whole] * 4 + [first, first, second, second]


def front_body(
    own, normed_ref, *refs
):
    x_refs, g_refs, refs = refs[:4], refs[4:8], refs[8:]
    taps_ref, bias_ref, wxp_ref, dist_ref = refs[:4]
    refs = refs[4:]
    sig_ref, gate_ref, inner_ref, mixed_ref, ext_sc, acc_sc = refs[-6:]
    i = pl.program_id(0)
    rows = normed_ref.shape[0]
    dims = (((1,), (1,)), ((), ()))

    def project(x_ref, one_ref, two_ref):
        normed = normed_ref[...]
        ext_sc[pl.ds(SUB, rows), :] = lax.dot_general(normed, x_ref[...], dims, preferred_element_type=f32)
        gate = weave(one_ref[...], two_ref[...], own)
        gate_ref[...] = lax.dot_general(normed, gate, dims, preferred_element_type=f32)

    for block in range(4):

        @pl.when(i == block)
        def _(block=block):
            project(x_refs[block], *g_refs[block // 2 * 2 : block // 2 * 2 + 2])

    ext_sc[pl.ds(0, SUB), :] = jnp.zeros((SUB, ext_sc.shape[1]), f32)
    taps = taps_ref.shape[0]
    signal = ext_sc[pl.ds(SUB, rows), :]
    sig_ref[...] = signal
    dist = dist_ref[...]
    pre = bias_ref[...] + taps_ref[pl.ds(taps - 1, 1), :] * signal
    for lag in range(1, taps):
        shifted = ext_sc[pl.ds(SUB - lag, rows), :]
        pre = pre + jnp.where(dist >= lag, taps_ref[pl.ds(taps - 1 - lag, 1), :] * shifted, 0.0)
    inner = (pre / (1.0 + jnp.exp(-pre))).astype(bf16)
    inner_ref[...] = inner
    part = lax.dot_general(inner, wxp_ref[...], dims, preferred_element_type=f32)

    @pl.when(i == 0)
    def _():
        acc_sc[...] = part

    @pl.when(i > 0)
    def _():
        acc_sc[...] += part

    mixed_ref[...] = acc_sc[...].astype(bf16)


def front(normed, weights, taps, bias, w_xp, dist, own):
    rows, width = normed.shape
    channels = taps.shape[1]
    chunk = channels // 4
    xw = w_xp.shape[0]

    def columns(height):
        return pl.BlockSpec((height, chunk), lambda i: (0, i))

    made = jax.ShapeDtypeStruct
    return pl.pallas_call(
        functools.partial(front_body, own),
        grid=(4,),
        in_specs=[pl.BlockSpec((rows, width), lambda i: (0, 0))]
        + weight_specs(chunk, width)
        + [columns(taps.shape[0]), columns(1), columns(xw), pl.BlockSpec((rows, 1), lambda i: (0, 0))],
        out_specs=[columns(rows), columns(rows), columns(rows), pl.BlockSpec((rows, xw), lambda i: (0, 0))],
        out_shape=[
            made((rows, channels), f32), made((rows, channels), f32), made((rows, channels), bf16),
            made((rows, xw), bf16),
        ],
        scratch_shapes=[pltpu.VMEM((rows + SUB, chunk), f32), pltpu.VMEM((rows, xw), f32)],
        compiler_params=pltpu.CompilerParams(vmem_limit_bytes=44 << 20),
        cost_estimate=cost(0.02),
        name="front",
    )(normed, *weights, taps, bias, w_xp, dist)


def turn_body(count, begins, ends, *refs):
    part_refs, refs = refs[:count], refs[count:]
    gis_ref, sig_ref, taps_ref, bias_ref, wxp_ref, dist_ref = refs[:6]
    more = list(refs[6:-6])
    gsig_ref, low_ref, head_ref, sums_ref, ext_sc, late_sc = refs[-6:]
    rows, chunk = gis_ref.shape
    taps = taps_ref.shape[0]
    nothing = jnp.zeros((SUB, chunk), f32)
    ext_sc[pl.ds(0, SUB), :] = nothing if begins else more.pop(0)[...]
    ext_sc[pl.ds(SUB, rows), :] = sig_ref[...]
    dist = dist_ref[...]
    signal = sig_ref[...]
    pre = bias_ref[...] + taps_ref[pl.ds(taps - 1, 1), :] * signal
    for lag in range(1, taps):
        shifted = ext_sc[pl.ds(SUB - lag, rows), :]
        pre = pre + jnp.where(dist >= lag, taps_ref[pl.ds(taps - 1 - lag, 1), :] * shifted, 0.0)
    sig = 1.0 / (1.0 + jnp.exp(-pre))
    mixed = part_refs[0][...].astype(f32)
    for part_ref in part_refs[1:]:
        mixed = mixed + part_ref[...].astype(f32)
    low = mixed.astype(bf16)
    low_ref[...] = low
    g_inner = gis_ref[...] + jnp.dot(low, wxp_ref[...], preferred_element_type=f32)
    g_pre = g_inner * (sig * (1.0 + pre * (1.0 - sig)))
    head_ref[...] = g_pre[:SUB, :]
    lines = [None] * taps
    lines[taps - 1] = jnp.sum(g_pre * signal, axis=0, keepdims=True)
    g_signal = taps_ref[pl.ds(taps - 1, 1), :] * g_pre
    if not ends:
        next_ref, dnext_ref = more.pop(0), more.pop(0)
    for lag in range(1, taps):
        masked = jnp.where(dist >= lag, g_pre, 0.0)
        lines[taps - 1 - lag] = jnp.sum(masked * ext_sc[pl.ds(SUB - lag, rows), :], axis=0, keepdims=True)
        late_sc[pl.ds(0, rows), :] = masked
        late_sc[pl.ds(rows, SUB), :] = nothing if ends else jnp.where(dnext_ref[...] >= lag, next_ref[...], 0.0)
        g_signal = g_signal + taps_ref[pl.ds(taps - 1 - lag, 1), :] * late_sc[pl.ds(lag, rows), :]
    lines.append(jnp.sum(g_pre, axis=0, keepdims=True))
    sums_ref[...] = jnp.zeros_like(sums_ref)
    for k, value in enumerate(lines):
        sums_ref[pl.ds(k, 1), :] = value
    gsig_ref[...] = g_signal.astype(bf16)


def turn(h, parts, gis, signal, taps, bias, w_xp, dist, before=None, later=None):
    rows, channels = gis.shape
    chunk = min(256, channels // 2)
    xw = w_xp.shape[0]

    def columns(height, start=0):
        return pl.BlockSpec((height, chunk), lambda i: (start, i))

    def fixed(a):
        return pl.BlockSpec(a.shape, lambda i: (0, 0))

    extra, extra_specs, alias = [], [], {}
    if before is not None:
        extra.append(before)
        extra_specs.append(columns(SUB, rows // SUB - 1))
    if later is not None:
        extra += [later[2], dist, later[0]]
        extra_specs += [
            columns(SUB), pl.BlockSpec((SUB, 1), lambda i: ((h + 1) * rows // SUB, 0)), pl.BlockSpec(memory_space=pl.ANY)
        ]
        alias = {len(parts) + 6 + len(extra) - 1: 0}
    made = jax.ShapeDtypeStruct
    return pl.pallas_call(
        functools.partial(turn_body, len(parts), before is None, later is None),
        grid=(channels // chunk,),
        in_specs=[fixed(part) for part in parts]
        + [
            columns(rows), columns(rows), columns(taps.shape[0]), columns(1), columns(xw),
            pl.BlockSpec((rows, 1), lambda i: (h, 0)),
        ]
        + extra_specs,
        out_specs=[columns(rows, h), pl.BlockSpec((rows, xw), lambda i: (0, 0)), columns(SUB), columns(SUB)],
        out_shape=[
            made((dist.shape[0], channels), bf16), made((rows, xw), bf16), made((SUB, channels), f32),
            made((SUB, channels), f32),
        ],
        scratch_shapes=[pltpu.VMEM((rows + SUB, chunk), f32), pltpu.VMEM((rows + SUB, chunk), f32)],
        input_output_aliases=alias,
        compiler_params=pltpu.CompilerParams(vmem_limit_bytes=32 << 20),
        cost_estimate=cost(0.02),
        name="turn",
    )(*parts, gis, signal, taps, bias, w_xp, dist, *extra)


def rear_body(own, gs_ref, gx_ref, *refs):
    x_refs, g_refs, (normed_ref, out_ref, gain_ref, acc_sc) = refs[:4], refs[4:8], refs[8:]
    i = pl.program_id(0)
    for block in range(4):

        @pl.when(i == block)
        def _(block=block):
            gate = weave(*[ref[...] for ref in g_refs[block // 2 * 2 : block // 2 * 2 + 2]], own)
            part = jnp.dot(gs_ref[...], x_refs[block][...], preferred_element_type=f32) + jnp.dot(
                gx_ref[...], gate, preferred_element_type=f32
            )
            if block == 0:
                acc_sc[...] = part
            elif block < 3:
                acc_sc[...] += part
            else:
                total = acc_sc[...] + part
                out_ref[...] = total.astype(bf16)
                gain_ref[...] = jnp.sum(total * normed_ref[...].astype(f32), axis=0, keepdims=True)


def rear(g_signal, g_gate, weights, normed, own):
    rows, width = normed.shape
    channels = g_signal.shape[1]
    chunk = channels // 4
    columns = pl.BlockSpec((rows, chunk), lambda i: (0, i))
    whole = pl.BlockSpec((rows, width), lambda i: (0, 0))
    made = jax.ShapeDtypeStruct
    return pl.pallas_call(
        functools.partial(rear_body, own),
        grid=(4,),
        in_specs=[columns, columns] + weight_specs(chunk, width) + [whole],
        out_specs=[whole, pl.BlockSpec((1, width), lambda i: (0, 0))],
        out_shape=[made((rows, width), bf16), made((1, width), f32)],
        scratch_shapes=[pltpu.VMEM((rows, width), f32)],
        compiler_params=pltpu.CompilerParams(vmem_limit_bytes=44 << 20),
        cost_estimate=cost(0.02),
        name="rear",
    )(g_signal, g_gate, *weights, normed)


def cross_body(left_ref, right_ref, gated_ref, *refs):
    quarters, (gg_ref, out_ref) = refs[:4], refs[4:]
    chunk = quarters[0].shape[0]
    half = left_ref.shape[1]
    dims = (((1,), (1,)), ((), ()))
    total = None
    for q in range(4):
        w = quarters[q][...]
        cut = pl.ds(q * chunk, chunk)
        part = lax.dot_general(left_ref[...], w[:, :half], dims, preferred_element_type=f32)
        part = part + lax.dot_general(right_ref[...], w[:, half:], dims, preferred_element_type=f32)
        gg_ref[:, cut] = part.astype(bf16)
        part = jnp.dot(gated_ref[:, cut], w, preferred_element_type=f32)
        total = part if total is None else total + part
    out_ref[...] = total.astype(bf16)


def cross(cots, gated, quarters, parts=2):
    tokens, half = cots[0].shape
    channels = gated.shape[1]
    rows = tokens // parts

    def row_block(columns):
        return pl.BlockSpec((rows, columns), lambda i: (i, 0))

    made = jax.ShapeDtypeStruct
    return pl.pallas_call(
        cross_body,
        grid=(parts,),
        in_specs=[row_block(half), row_block(half), row_block(channels)]
        + [pl.BlockSpec(quarter.shape, lambda i: (0, 0)) for quarter in quarters],
        out_specs=[row_block(channels), row_block(2 * half)],
        out_shape=[made((tokens, channels), bf16), made((tokens, 2 * half), bf16)],
        compiler_params=pltpu.CompilerParams(vmem_limit_bytes=40 << 20),
        cost_estimate=cost(0.02),
        name="cross",
    )(*cots, gated, *quarters)


def stage_body(plans, *refs):
    refs = list(refs)
    sums = []
    for _ in plans:
        base, got = refs.pop(0), refs.pop(0)
        sums.append([base[k].astype(f32) + got[k].astype(f32) for k in range(base.shape[0])])
    for (stay, leave), blocks in zip(plans, sums):
        kept = refs.pop(0)
        for i, k in enumerate(stay):
            kept[i] = blocks[k]
        if leave:
            sent = refs.pop(0)
            for i, k in enumerate(leave):
                sent[i] = blocks[k].astype(bf16)


def stage(streams, plans, steps=2):
    height = streams[0][0][0].shape[1] // steps
    ins, in_specs, outs, out_specs = [], [], [], []
    for (base, got), (stay, leave), column in streams_with(streams, plans):
        width = base.shape[2] if column is None else base.shape[2] // len(streams)
        for a in (base, got):
            ins.append(a)
            in_specs.append(
                pl.BlockSpec((a.shape[0], height, width), lambda i, column=column: (0, i, 0 if column is None else column))
            )
        for blocks, kind in ((stay, f32), (leave, bf16)):
            if blocks:
                outs.append(jax.ShapeDtypeStruct((len(blocks), height * steps, width), kind))
                out_specs.append(pl.BlockSpec((len(blocks), height, width), lambda i: (0, i, 0)))
    return pl.pallas_call(
        functools.partial(stage_body, plans),
        grid=(steps,),
        in_specs=in_specs,
        out_specs=out_specs,
        out_shape=outs,
        compiler_params=pltpu.CompilerParams(vmem_limit_bytes=40 << 20),
        cost_estimate=cost(0.02),
        name="stage",
    )(*ins)


def streams_with(streams, plans):
    for (pair, column), plan in zip(streams, plans):
        yield pair, plan, column


def join_body(*refs):
    out_ref = refs[-1]
    pairs = [(refs[2 * i], refs[2 * i + 1]) for i in range((len(refs) - 1) // 2)]
    width = pairs[0][0].shape[2]
    for i, (base, got) in enumerate(pairs):
        out_ref[0, :, pl.ds(i * width, width)] = base[0].astype(f32) + got[0].astype(f32)


def join(pairs, plane, planes, into=None, steps=2):
    _, rows, width = pairs[0][0].shape
    height = rows // steps
    ins = [a for pair in pairs for a in pair]
    extra = [] if into is None else [into]

    def body(*refs):
        join_body(*refs[: len(ins)], refs[-1])

    return pl.pallas_call(
        body,
        grid=(steps,),
        in_specs=[pl.BlockSpec((1, height, width), lambda i: (0, i, 0)) for _ in ins]
        + [pl.BlockSpec(memory_space=pl.ANY) for _ in extra],
        out_specs=pl.BlockSpec((1, height, width * len(pairs)), lambda i: (plane, i, 0)),
        out_shape=jax.ShapeDtypeStruct((planes, rows, width * len(pairs)), f32),
        input_output_aliases={} if into is None else {len(ins): 0},
        compiler_params=pltpu.CompilerParams(vmem_limit_bytes=24 << 20),
        cost_estimate=cost(0.02),
        name="join",
    )(*ins, *extra)


def grad_body(lows_ref, *refs):
    out_ref = refs[-1]
    at = 0
    for ref in refs[:-1]:
        part = lax.dot_general(lows_ref[...], ref[...], (((0,), (0,)), ((), ())), preferred_element_type=f32)
        out_ref[:, pl.ds(at, ref.shape[1])] = part.astype(bf16)
        at += ref.shape[1]


def grad_half(h, lows, others):
    tokens, channels = lows.shape
    width = sum(other.shape[1] for other in others)
    chunk = min(256, channels // 2)
    steps = channels // 2 // chunk
    return pl.pallas_call(
        grad_body,
        grid=(steps,),
        in_specs=[pl.BlockSpec((tokens, chunk), lambda i: (0, h * steps + i))]
        + [pl.BlockSpec(other.shape, lambda i: (0, 0)) for other in others],
        out_specs=pl.BlockSpec((chunk, width), lambda i: (i, 0)),
        out_shape=jax.ShapeDtypeStruct((channels // 2, width), bf16),
        compiler_params=pltpu.CompilerParams(vmem_limit_bytes=24 << 20),
        cost_estimate=cost(0.02),
        name="grad_half",
    )(lows, *others)


def pack_body(half, rank, states, low_ref, mix_ref, inner_ref, gp_ref, acc_ref, dec_ref, sum_ref, red_ref, gain_ref,
              stay_ref, leave_ref, all_sc):
    i = pl.program_id(0)
    dims = (((0,), (0,)), ((), ()))
    chunk, xw = inner_ref.shape[1], low_ref.shape[1]
    all_sc[pl.ds(0, xw), :] = lax.dot_general(low_ref[...], inner_ref[...], dims, preferred_element_type=f32)
    step_in = mix_ref[...][:, :rank].astype(bf16)
    all_sc[pl.ds(xw, rank), :] = lax.dot_general(step_in, gp_ref[...], dims, preferred_element_type=f32)
    subs = dec_ref.shape[0] // states
    wide = chunk // LANES
    for j in range(wide):
        cut = pl.ds(i * wide + j, states, stride=subs)
        all_sc[pl.ds(xw + rank, states), pl.ds(j * LANES, LANES)] = acc_ref[cut, :] * (dec_ref[cut, :] * math.log(2.0))
    at = xw + rank + states
    all_sc[pl.ds(at, SUB), :] = sum_ref[...]
    all_sc[pl.ds(at + SUB, SUB), :] = red_ref[...]
    all_sc[pl.ds(at + 2 * SUB, SUB), :] = gain_ref[...]

    @pl.when(i < half)
    def _():
        stay_ref[...] = all_sc[...].astype(bf16)

    @pl.when(i >= half)
    def _():
        leave_ref[...] = all_sc[...].astype(bf16)


def pack(rank, states, low, mix, inner, gp, acc, dec, sums, reds, gain_rows):
    tokens, channels = inner.shape
    chunk = min(256, channels // 2)
    half = channels // 2 // chunk
    height = low.shape[1] + rank + states + 3 * SUB

    def columns(rows):
        return pl.BlockSpec((rows, chunk), lambda i: (0, i))

    def fixed(a):
        return pl.BlockSpec(a.shape, lambda i: (0, 0))

    made = jax.ShapeDtypeStruct((height, channels // 2), bf16)
    return pl.pallas_call(
        functools.partial(pack_body, half, rank, states),
        grid=(2 * half,),
        in_specs=[fixed(low), fixed(mix), columns(tokens), columns(tokens), fixed(acc), fixed(dec)] + [columns(SUB)] * 3,
        out_specs=[
            pl.BlockSpec((height, chunk), lambda i: (0, jnp.minimum(i, half - 1))),
            pl.BlockSpec((height, chunk), lambda i: (0, jnp.maximum(i - half, 0))),
        ],
        out_shape=[made, made],
        scratch_shapes=[pltpu.VMEM((height, chunk), f32)],
        compiler_params=pltpu.CompilerParams(vmem_limit_bytes=24 << 20),
        cost_estimate=cost(0.02),
        name="pack",
    )(low, mix, inner, gp, acc, dec, sums, reds, gain_rows)


def last_body(gn_ref, hidden_ref, cot_ref, gain_ref, out_ref):
    value = hidden_ref[...].astype(f32)
    factor = lax.rsqrt(jnp.mean(value * value, axis=1, keepdims=True) + EPSILON)
    xhat = value * factor
    scaled = gn_ref[...].astype(f32) * gain_ref[...]
    out_ref[...] = cot_ref[...].astype(f32) + factor * (scaled - xhat * jnp.mean(scaled * xhat, axis=1, keepdims=True))


def last(gn, hidden, cotangent, gain, parts=2):
    rows, width = hidden.shape
    block = pl.BlockSpec((rows // parts, width), lambda i: (i, 0))
    return pl.pallas_call(
        last_body,
        grid=(parts,),
        in_specs=[block, block, block, pl.BlockSpec(gain.shape, lambda i: (0, 0))],
        out_specs=block,
        out_shape=jax.ShapeDtypeStruct(hidden.shape, f32),
        cost_estimate=cost(0.02),
        name="last",
    )(gn, hidden, cotangent, gain)


def distances(lengths, pack_rows, row_count):
    slot_count = lengths.shape[0]
    picks = pack_rows[:, None] == jnp.arange(slot_count, dtype=jnp.int32)[None, :]
    packed = jnp.sum(jnp.where(picks, lengths[None, :], 0), axis=1)
    starts = jnp.cumsum(packed) - packed
    positions = jnp.arange(row_count, dtype=jnp.int32)
    latest = jnp.max(jnp.where(starts[None, :] <= positions[:, None], starts[None, :], 0), axis=1)
    return positions - latest


def after(value, *others):
    return lax.optimization_barrier((value,) + others)[0]


def swap(value, bit):
    count = lax.axis_size("fsdp")
    return lax.ppermute(value, "fsdp", [(i, i ^ bit) for i in range(count)])


class Gather:
    def __init__(self, value, order):
        self.pieces, self.order, self.size = {0: value}, list(order), value.shape[0]

    def send(self, *waits):
        bit = self.order.pop(0)
        self.keys, self.bit = sorted(self.pieces), bit
        sent = [self.pieces[k] for k in self.keys]
        sent = jnp.concatenate(sent, axis=0) if len(sent) > 1 else sent[0]
        self.sent = after(sent, *waits) if waits else sent
        self.got = swap(self.sent, bit)
        return self.got

    def take(self, *waits):
        got = after(self.got, *waits) if waits else self.got
        for i, k in enumerate(self.keys):
            self.pieces[k | self.bit] = lax.slice_in_dim(got, i * self.size, (i + 1) * self.size, axis=0)


class WeightGrad:
    def __init__(self, lows, other, kept, orders):
        self.orders = [list(order) for order in orders]
        self.keys = [list(kept) for _ in orders]
        self.leave = grad_half(1, lows, other)
        self.lows, self.other = lows, other
        self.columns = True

    def exchange(self, *waits):
        self.gots = [swap(after(self.leave, *waits) if waits else self.leave, 1)] * len(self.orders)

    def rest(self, *waits):
        self.bases = [grad_half(0, after(self.lows, self.leave, *waits), self.other)] * len(self.orders)
        return self.bases[0]

    def go(self, *waits):
        streams, plans, bits = [], [], []
        gots = [after(self.gots[0], *waits)] + self.gots[1:] if waits else self.gots
        if waits and self.columns:
            gots = [gots[0]] * len(gots)
        for s, keys in enumerate(self.keys):
            bit = self.orders[s].pop(0)
            shape = (len(keys), -1, self.bases[s].shape[-1])
            pair = (self.bases[s].reshape(shape), gots[s].reshape(shape))
            streams.append((pair, s if self.columns else None))
            leave = [i for i, k in enumerate(keys) if k & bit]
            stay = [i for i, k in enumerate(keys) if not k & bit]
            plans.append((stay, leave))
            bits.append(bit)
            self.keys[s] = [keys[i] for i in stay]
        made = stage(streams, plans)
        self.bases, sents = made[0::2], made[1::2]
        self.gots = [swap(sent, bit) for sent, bit in zip(sents, bits)]
        self.columns = False
        return tuple(sents)

    def finish(self, plane=0, planes=1, into=None):
        while self.orders[0]:
            self.go()
        return join(list(zip(self.bases, self.gots)), plane, planes, into)


def ring_parts(part):
    count = lax.axis_size("tensor")
    parts = [part]
    for step in range(1, count):
        parts.append(lax.ppermute(part, "tensor", [(i, (i + step) % count) for i in range(count)]))
    return parts


def placed(places):
    count = len(places)
    own = lax.axis_index("fsdp")
    owners = jnp.bitwise_xor(jnp.asarray(places, jnp.int32), own.astype(jnp.int32))
    return lax.broadcasted_iota(jnp.int32, (count, count), 0) == owners[None, :]


def shards(
    hidden,
    cotangent,
    seq_lengths,
    pack_order,
    norm_gain,
    w_in,
    conv_weight,
    conv_bias,
    w_xproj,
    w_dt,
    dt_bias,
    a_log,
    d_skip,
    w_out,
):
    n_fsdp = lax.axis_size("fsdp")
    n_tensor = lax.axis_size("tensor")
    place = lax.axis_index("tensor")
    own_channels = w_in.shape[1]
    width = hidden.shape[1]
    group_rows = hidden.shape[0] * n_tensor
    rank = w_dt.shape[1]
    states = a_log.shape[1]
    taps = conv_weight.shape[1]
    wide = [1 << i for i in range(1, n_fsdp.bit_length() - 1)]
    narrow = wide[::-1]
    kept = [k for k in range(n_fsdp) if not k & 1]
    places = kept + [k + 1 for k in kept]
    channels = own_channels * n_fsdp
    middle = channels // 2

    rows_all = lax.all_gather(hidden, "tensor", axis=0, tiled=True)
    gather_x, gather_g = Gather(w_in[0], wide), Gather(w_in[1], narrow)
    first_x, first_g = gather_x.send(), gather_g.send()
    first_x, first_g = lax.optimization_barrier((first_x, first_g))
    gather_x.got, gather_g.got = first_x, first_g
    gather_x.take()
    gather_g.take()
    for _ in wide[1:]:
        gather_x.send()
        gather_g.send()
        if gather_x.order:
            gather_x.take()
            gather_g.take()
    gain_own = after(norm_gain.reshape(1, -1), first_x, first_g)
    lines = lax.broadcasted_iota(jnp.int32, (n_tensor, 1), 0)
    gain_line = jnp.where(lines == place, gain_own, 0)
    for step in range(1, n_tensor):
        got = lax.ppermute(gain_own, "tensor", [(i, (i + step) % n_tensor) for i in range(n_tensor)])
        gain_line = jnp.where(lines == lax.rem(place - step + n_tensor, n_tensor), got, gain_line)
    gain_rows = width // n_fsdp // own_channels
    small = jnp.concatenate(
        [
            w_xproj.T,
            w_dt.T,
            a_log.T,
            conv_weight.T,
            conv_bias[None],
            dt_bias[None],
            d_skip[None],
            gain_line.reshape(gain_rows, own_channels),
        ],
        axis=0,
    )
    small_a = jnp.concatenate([small] + [swap(small, k) for k in kept[1:]], axis=1)
    small_all = jnp.concatenate([small_a, swap(small_a, 1)], axis=1)
    got_x, got_g = after(gather_x.got, small_a), after(gather_g.got, small_a)
    weights = (
        gather_x.sent, got_x, swap(gather_x.sent, 1), swap(got_x, 1),
        gather_g.sent, got_g, swap(gather_g.sent, 1), swap(got_g, 1),
    )
    half_width = width // 2
    cot_l = lax.all_gather(after(cotangent[:, :half_width], first_x), "tensor", axis=0, tiled=True)
    gather_o = Gather(after(w_out, got_x, got_g), wide)
    gather_o.send()

    xw = rank + 2 * states
    w_xp = small_all[:xw]
    w_dt_rows = small_all[xw : xw + rank]
    at = xw + rank
    a_rows = small_all[at : at + states].astype(f32)
    at = at + states
    conv_rows = small_all[at : at + taps].astype(f32)
    at = at + taps
    conv_b = small_all[at : at + 1].astype(f32)
    dt_b = small_all[at + 1 : at + 2].astype(f32)
    skip_row = small_all[at + 2 : at + 3].astype(f32)
    gain_all = small_all[at + 3 :].astype(f32).reshape(1, gain_rows, n_fsdp, own_channels)
    owners = placed(places)
    gain = jnp.sum(jnp.where(owners[:, None, :, None], gain_all, 0.0), axis=2).reshape(1, width)
    rates = (-jnp.exp(a_rows) * math.log2(math.e)).reshape(-1, LANES)

    offsets = distances(seq_lengths[0], pack_order[0], group_rows)
    keep = (offsets > 0).astype(jnp.int32)
    dist = offsets[:, None]
    normed = norm_rows(rows_all, gain, n_tensor)

    signal, gate, inner, mixed_own = front(normed, weights, conv_rows, conv_b, w_xp, dist, own_channels)
    parts = ring_parts(mixed_own)
    for _ in wide[1:]:
        gather_o.take(mixed_own)
        gather_o.send()
    none = jnp.zeros(rates.shape, f32)
    states_all, deltas, sums, gated, mixed, _ = scan_forward(
        0, keep, parts, w_dt_rows, dt_b, skip_row, rates, inner, gate, none
    )
    cot_r = lax.all_gather(after(cotangent[:, half_width:], *parts), "tensor", axis=0, tiled=True)
    got_o, sent_o = after(gather_o.got, mixed), after(gather_o.sent, mixed)
    quarters = (sent_o, got_o, swap(sent_o, 1), swap(got_o, 1))
    grad_gated, branch = cross((cot_l, cot_r), gated, quarters)
    branch_own = lax.psum_scatter(branch, "tensor", scatter_dimension=0, tiled=True)
    output = (hidden.astype(f32) + branch_own.astype(f32)).astype(bf16)
    orders = (wide, narrow)

    out_grad = WeightGrad(after(gated, branch), (cot_l, cot_r), kept, orders)
    out_grad.exchange()
    out_grad.rest()
    g_scan, g_gate, g_proj, g_mixed, reds, acc, _ = scan_backward(
        0, keep, after(mixed, out_grad.bases[0]), w_dt_rows, skip_row, rates, inner, gate, grad_gated, sums, states_all,
        deltas, none,
    )
    backs = ring_parts(g_mixed)
    gate_grad = WeightGrad(g_gate, (normed,), kept, orders)
    gate_grad.rest()
    sent = out_grad.go(gate_grad.bases[0])
    backs[0] = after(backs[0], *sent)
    gate_grad.exchange(*backs[1:])
    g_signal, low, _, conv_sums = turn(0, backs, g_scan, signal, conv_rows, conv_b, w_xp, dist)
    sent = gate_grad.go(low)
    g_norm, gain_term = rear(
        after(g_signal, branch_own, *sent, *out_grad.gots), g_gate, weights, normed, own_channels
    )
    g_norm = after(g_norm, *gate_grad.gots)
    g_norm_own = lax.psum_scatter(g_norm, "tensor", scatter_dimension=0, tiled=True)
    gain_sum = sum(part.astype(f32) for part in ring_parts((gain_term / gain).astype(bf16)))
    gain_sum = lax.dynamic_index_in_dim(gain_sum.reshape(n_fsdp, n_tensor, -1), place, 1, False)
    gain_sum = jnp.sum(jnp.where(owners[:, :, None], gain_sum[:, None, :], 0.0), axis=0)
    gain_sum = jnp.pad(gain_sum, ((0, 0), (0, own_channels - gain_sum.shape[1]))).reshape(1, channels)
    gain_sum = jnp.concatenate([gain_sum, jnp.zeros((SUB - 1, channels), f32)], axis=0)
    sent = out_grad.go(g_norm)
    sig_grad = WeightGrad(after(g_signal, *sent), (normed,), kept, orders)
    sig_grad.exchange()
    sent = gate_grad.go(sig_grad.leave)
    sig_grad.rest(*sent)
    small_stay, small_leave = pack(
        rank, states, low, mixed, inner, g_proj, acc, rates, conv_sums, reds, after(gain_sum, sig_grad.bases[0])
    )
    small_got = swap(small_leave, 1)
    sent = sig_grad.go(small_leave, *out_grad.gots)
    small_half = small_stay.astype(f32) + after(small_got, *sent).astype(f32)
    small_cuts = [small_half[:, i * own_channels : (i + 1) * own_channels] for i in range(len(kept))]
    small_lows = [cut.astype(bf16) for cut in small_cuts[1:]]
    small_gots = [swap(low, k) for low, k in zip(small_lows, kept[1:])]
    out_grad.gots[0] = after(out_grad.gots[0], *small_lows)
    grad_w_out = out_grad.finish()[0]
    gate_grad.gots[0] = after(gate_grad.gots[0], grad_w_out)
    grad_w_in = gate_grad.finish(1, 2)
    sig_grad.go(grad_w_in)
    small_gots[0] = after(small_gots[0], sig_grad.bases[0])
    small_own = small_cuts[0]
    for got in small_gots:
        small_own = small_own + got.astype(f32)
    grad_hidden = last(after(g_norm_own, small_own), hidden, cotangent, gain)
    grad_w_in = sig_grad.finish(0, 2, grad_w_in)
    at = xw + rank + states
    grad_gain = small_own[at + 2 * SUB, : norm_gain.shape[0]]
    columns = small_own.T
    return (
        output,
        grad_hidden,
        grad_gain,
        grad_w_in,
        columns[:, at : at + taps],
        small_own[at + taps],
        columns[:, :xw],
        columns[:, xw : xw + rank],
        small_own[at + SUB + 1],
        columns[:, at - states : at],
        small_own[at + SUB],
        grad_w_out,
    )


def solution(mesh):
    every = ("fsdp", "tensor")
    rows = P(every, None)
    line = P(every)
    planes = P(None, every, None)
    return jax.shard_map(
        shards,
        mesh=mesh,
        in_specs=(rows, rows, P("fsdp", None), P("fsdp", None), line, planes, rows, line, rows, rows, line, rows, line, rows),
        out_specs=(rows, rows, line, planes, rows, line, rows, rows, line, rows, line, rows),
        check_vma=False,
    )
```

time: 393 us -> 338 us (0.86)
  other arithmetic: 37.8 us -> 4.84 us
  matrix products: 27.1 us -> 0 us
  starting transfers between devices: 72.9 us -> 48 us
  Pallas kernels: 109 us -> 125 us
  local copies, waits for them, and re-layouts: 45.5 us -> 54.6 us
  waiting for transfers between devices: 78.1 us -> 86 us
    ppermute x22 -> x9, starting transfers between devices: 42.5 us -> 13.5 us  [ring_parts(): lax.ppermute(part, 'tensor', [(i, (i + step) % count) for i in range(coun...]
    dot_general x10 -> x0, matrix products: 27.1 us -> none  [matmul(): lax.dot_general(left, right, ((dims[:1], dims[1:]), ((), ())), preferred_...]
    unnamed x144 -> x188, local copies, waits for them, and re-layouts: 21.1 us -> 42.1 us
    pallas_call x10 -> x23, Pallas kernels: 108 us -> 124 us  [the longest x1 45.9 us: scan_backward(): pl.pallas_call(functools.partial(bwd_body, states, subs, h * rows), grid_...]
    add x10 -> x2, other arithmetic: 10.8 us -> 0.08 us  [the longest x1 0.04 us: shards(): small_own = small_own + got.astype(f32)]
    convert_element_type x14 -> x2, other arithmetic: 11.1 us -> 0.94 us  [the longest x1 0.92 us: shards(): output = (hidden.astype(f32) + branch_own.astype(f32)).astype(bf16)]
    ppermute x22 -> x9, waiting for transfers between devices: 30.1 us -> 37.3 us  [ring_parts(): lax.ppermute(part, 'tensor', [(i, (i + step) % count) for i in range(coun...]
    concatenate x14 -> x3, other arithmetic: 6.48 us -> 0.21 us  [the longest x2 0.17 us: send(): sent = jnp.concatenate(sent, axis=0) if len(sent) > 1 else sent[0]]
  transfers between devices with their start and end apart: 58 -> 52, of which waited for: 20 -> 20; matrix products, arithmetic and copies ran while one was open for 21% -> 6% of each run, Pallas kernels for 28% -> 35%
where the time goes in v3:
time: 338 us; the launch traced here: 334 us
  Pallas kernels  125 us (37%)
  waiting for transfers between devices  86 us (25%)
  local copies, waits for them, and re-layouts  54.6 us (16%)
  starting transfers between devices  48 us (14%)
  between operations  14.8 us (4%)
  other arithmetic  4.84 us (1%)
    pallas_call x1, Pallas kernels, scan_backward(): pl.pallas_call(functools.partial(bwd_body, states, subs, h * rows), grid_...  45.9 us
    ppermute x35, waiting for transfers between devices, swap(): return lax.ppermute(value, 'fsdp', [(i, i ^ bit) for i in range(count)])  45.3 us
    unnamed x188, local copies, waits for them, and re-layouts  42.1 us
    ppermute x9, waiting for transfers between devices, ring_parts(): lax.ppermute(part, 'tensor', [(i, (i + step) % count) for i in range(coun...  37.3 us
    ppermute x35, starting transfers between devices, swap(): return lax.ppermute(value, 'fsdp', [(i, i ^ bit) for i in range(count)])  29.6 us
    pallas_call x1, Pallas kernels, scan_forward(): pl.pallas_call(functools.partial(fwd_body, states, subs, h * rows, len(pa...  19.3 us
    ppermute x9, starting transfers between devices, ring_parts(): lax.ppermute(part, 'tensor', [(i, (i + step) % count) for i in range(coun...  13.5 us
    pallas_call x1, Pallas kernels, front(): pl.pallas_call(functools.partial(front_body, own), grid=(4,), in_specs=[p...  12.2 us
  transfers between devices with their start and end apart: 52, of which 20 were waited for; matrix products, arithmetic and copies ran while one was open for 6% of the time, Pallas kernels for 35%

profile of v3, /device:TPU:8, one launch (start us, length us, event | category | flops | bytes accessed | tf_op | source)
XLA Modules:
  0.0 333.7 jit_solution(14646257956526318877)
XLA Ops:
  8.0 1.3 slice_bitcast_fusion
  9.3 1.6 collective-permute-start.1
  10.9 1.5 collective-permute-start
  13.8 9.2 %collective-permute-done.1 = bf16[128,2048]{1,0:T(8,128)(2,1)S(1)} collective-permute-done((bf16[128,2048]{1,0:T(8,128)(2,1)S(1)}, bf16[128,2048]{1,0:T(8,128)(2,1)S(1)}, u32[]{:S(2)}, u32[]{:S(2)}) %collective-permute-start.1) | collective-permute-done | bytes 524320 | tf_op jit(solution)/shard_map/ppermute | solution.py:799
  25.9 1.6 collective-permute-start.12
  28.3 1.9 fusion.8
  30.2 1.6 collective-permute-start.4
  31.7 1.2 collective-permute-start.3
  33.0 1.8 collective-permute-start.2
  38.9 1.6 collective-permute-start.5
  40.5 12.6 %collective-permute-done.7 = bf16[313,128]{1,0:T(8,128)(2,1)S(1)} collective-permute-done((bf16[313,128]{1,0:T(8,128)(2,1)S(1)}, bf16[313,128]{1,0:T(8,128)(2,1)S(1)}, u32[]{:S(2)}, u32[]{:S(2)}) %collective-permute-start.7) | collective-permute-done | bytes 80160 | tf_op jit(solution)/shard_map/ppermute | solution.py:799
  54.5 2.7 collective-permute-done.8
  58.0 1.5 collective-permute-start.18
  59.7 1.9 constant_dynamic-update-slice_fusion.6
  61.5 1.6 copy-done.24
  64.1 1.3 copy-done
  65.4 12.2 %front.1 = (f32[512,1024]{1,0:T(8,128)}, f32[512,1024]{1,0:T(8,128)}, bf16[512,1024]{1,0:T(8,128)(2,1)S(1)}, bf16[512,160]{1,0:T(8,128)(2,1)S(1)}) custom-call(bf16[512,2048]{1,0:T(8,128)(2,1)} %copy-done, bf16[256,2048]{1,0:T(8,128)(2,1)S(1)} %pad_maximum_fusion.refs_0_, bf16[256,2048]{1,0:T(8,128)(2,1)S(1)} %collective-permute-done.9.refs_1_, ...), custom_call_target="tpu_custom_call" | custom-call | flops 20000000 | bytes 20000 | tf_op jit(solution)/shard_map/front/pallas_call | solution.py:415
  78.6 2.0 constant_dynamic-update-slice_fusion.5.refs_0_
  81.4 2.5 collective-permute-start.16
  83.9 2.6 collective-permute-start.15
  86.4 3.8 %collective-permute-done.17.refs_3_ = bf16[512,160]{1,0:T(8,128)(2,1)S(1)} collective-permute-done((bf16[512,160]{1,0:T(8,128)(2,1)S(1)}, bf16[512,160]{1,0:T(8,128)(2,1)S(1)}, u32[]{:S(2)}, u32[]{:S(2)}) %collective-permute-start.17) | collective-permute-done | bytes 163872 | tf_op jit(solution)/shard_map/ppermute | solution.py:867
  90.2 10.9 %collective-permute-done.16.refs_2_ = bf16[512,160]{1,0:T(8,128)(2,1)S(1)} collective-permute-done((bf16[512,160]{1,0:T(8,128)(2,1)S(1)}, bf16[512,160]{1,0:T(8,128)(2,1)S(1)}, u32[]{:S(2)}, u32[]{:S(2)}) %collective-permute-start.16) | collective-permute-done | bytes 163872 | tf_op jit(solution)/shard_map/ppermute | solution.py:867
  101.2 4.6 %collective-permute-done.15.refs_1_ = bf16[512,160]{1,0:T(8,128)(2,1)S(1)} collective-permute-done((bf16[512,160]{1,0:T(8,128)(2,1)S(1)}, bf16[512,160]{1,0:T(8,128)(2,1)S(1)}, u32[]{:S(2)}, u32[]{:S(2)}) %collective-permute-start.15) | collective-permute-done | bytes 163872 | tf_op jit(solution)/shard_map/ppermute | solution.py:867
  106.5 1.7 slice.103.refs_4_.wdt_ref
  110.3 19.3 %scan_forward.1 = (f32[66560,128]{1,0:T(8,128)}, f32[4096,128]{1,0:T(8,128)}, f32[512,1024]{1,0:T(8,128)}, bf16[512,1024]{1,0:T(8,128)(2,1)}, f32[512,160]{1,0:T(8,128)}, /*index=5*/f32[128,128]{1,0:T(8,128)}) custom-call(s32[512]{0:T(512)} %fusion.2.keep_ref, bf16[512,160]{1,0:T(8,128)(2,1)} %copy-done.57, bf16[512,160]{1,0:T(8,128)(2,1)} %copy-done.78, ...), custom_call_target="tpu_custom_call" | custom-call | flops 20000000 | bytes 20000 | tf_op jit(solution)/shard_map/scan_forward/pallas_call | solution.py:139
  130.2 3.0 collective-permute-done.20.refs_2_
  140.2 6.1 %cross.1 = (bf16[512,1024]{1,0:T(8,128)(2,1)S(1)}, bf16[512,2048]{1,0:T(8,128)(2,1)S(1)}) custom-call(bf16[512,1024]{1,0:T(8,128)(2,1)S(1)} %copy-done.5, bf16[512,1024]{1,0:T(8,128)(2,1)S(1)} %copy-done.9, bf16[512,1024]{1,0:T(8,128)(2,1)S(1)} %copy-done.11, bf16[256,2048]{1,0:T(8,128)(2,1)} %constant_dynamic-update-slice_fusion.5.refs_0_, ...), custom_call_target="tpu_custom_call" | custom-call | flops 20000000 | bytes 20000 | tf_op jit(solution)/shard_map/cross/pallas_call | solution.py:587
  146.3 1.4 copy-done.26
  150.2 1.6 grad_half.6
  151.8 1.6 grad_half.7
  153.4 45.9 %scan_backward.1 = (f32[512,1024]{1,0:T(8,128)}, bf16[512,1024]{1,0:T(8,128)(2,1)}, bf16[512,1024]{1,0:T(8,128)(2,1)}, bf16[512,160]{1,0:T(8,128)(2,1)}, f32[8,1...) custom-call(s32[512]{0:T(512)} %fusion.2.keep_ref, f32[512,160]{1,0:T(8,128)} %get-tuple-element.112.fwd_ref.mix_ref, ...), custom_call_target="tpu_custom_call" | custom-call | flops 20000000 | bytes 20000 | tf_op jit(solution)/shard_map/scan_backward/pallas_call | solution.py:308
  199.3 1.7 collective-permute-start.25
  201.1 1.6 collective-permute-start.24
  203.4 1.2 copy-done.7
  204.6 1.6 grad_half.8
  206.2 2.9 collective-permute-done.25.refs_3_
  209.1 9.5 %collective-permute-done.24.refs_2_ = bf16[512,160]{1,0:T(8,128)(2,1)S(1)} collective-permute-done((bf16[512,160]{1,0:T(8,128)(2,1)}, bf16[512,160]{1,0:T(8,128)(2,1)S(1)}, u32[]{:S(2)}, u32[]{:S(2)}) %collective-permute-start.24) | collective-permute-done | bytes 163872 | tf_op jit(solution)/shard_map/ppermute | solution.py:867
  218.5 5.5 %collective-permute-done.23.refs_1_ = bf16[512,160]{1,0:T(8,128)(2,1)S(1)} collective-permute-done((bf16[512,160]{1,0:T(8,128)(2,1)}, bf16[512,160]{1,0:T(8,128)(2,1)S(1)}, u32[]{:S(2)}, u32[]{:S(2)}) %collective-permute-start.23) | collective-permute-done | bytes 163872 | tf_op jit(solution)/shard_map/ppermute | solution.py:867
  224.1 1.6 grad_half.9
  226.7 1.8 collective-permute-start.27
  228.5 1.5 collective-permute-start.28
  230.0 6.6 %turn.1 = (bf16[512,1024]{1,0:T(8,128)(2,1)S(1)}, bf16[512,160]{1,0:T(8,128)(2,1)S(1)}, f32[8,1024]{1,0:T(8,128)}, f32[8,1024]{1,0:T(8,128)S(1)}) custom-call(bf16[512,160]{1,0:T(8,128)(2,1)S(1)} %copy-done.56, bf16[512,160]{1,0:T(8,128)(2,1)S(1)} %collective-permute-done.23.refs_1_, bf16[512,160]{1,0:T(8,128)(2,1)S(1)} %collective-permute-done.24.refs_2_, ...), custom_call_target="tpu_custom_call" | custom-call | flops 20000000 | bytes 20000 | tf_op jit(solution)/shard_map/turn/pallas_call | solution.py:498
  237.3 1.7 stage.7
  241.5 1.3 collective-permute-start.30
  246.9 9.8 %rear.1 = (bf16[512,2048]{1,0:T(8,128)(2,1)}, f32[1,2048]{1,0:T(1,128)S(1)}) custom-call(bf16[512,1024]{1,0:T(8,128)(2,1)S(1)} %get-tuple-element.151.gs_ref.lows_ref, bf16[512,1024]{1,0:T(8,128)(2,1)S(1)} %copy-done.8, bf16[256,2048]{1,0:T(8,128)(2,1)S(1)} %copy-done.14, bf16[256,2048]{1,0:T(8,128)(2,1)S(1)} %copy-done.20, ...), custom_call_target="tpu_custom_call" | custom-call | flops 20000000 | bytes 20000 | tf_op jit(solution)/shard_map/rear/pallas_call | solution.py:548
  256.8 1.4 copy-done.36
  263.3 2.6 grad_half.10
  265.9 1.7 collective-permute-start.33
  267.6 2.2 collective-permute-start.32
  272.2 1.4 stage.9
  273.7 1.6 grad_half.11
  275.3 1.3 copy-done.3
  276.9 1.4 copy-done.18
  283.9 1.7 pack.1
  286.4 1.5 collective-permute-start.37
  288.5 6.6 %collective-permute-done.36.refs_1_ = bf16[1,128,1024]{2,1,0:T(8,128)(2,1)S(1)} collective-permute-done((bf16[1,128,1024]{2,1,0:T(8,128)(2,1)}, bf16[1,128,1024]{2,1,0:T(8,128)(2,1)S(1)}, u32[]{:S(2)}, u32[]{:S(2)}) %collective-permute-start.36) | collective-permute-done | bytes 262176 | tf_op jit(solution)/shard_map/ppermute | solution.py:799
  295.8 2.0 stage.10
  297.8 1.4 collective-permute-start.39
  300.0 1.5 collective-permute-start.38
  301.6 1.3 collective-permute-start.44
  302.9 1.4 collective-permute-done.41.refs_3_
  308.0 7.5 %collective-permute-done.39.refs_1_ = bf16[2,128,1024]{2,1,0:T(8,128)(2,1)S(1)} collective-permute-done((bf16[2,128,1024]{2,1,0:T(8,128)(2,1)S(1)}, bf16[2,128,1024]{2,1,0:T(8,128)(2,1)S(1)}, u32[]{:S(2)}, u32[]{:S(2)}) %collective-permute-start.39) | collective-permute-done | bytes 524320 | tf_op jit(solution)/shard_map/ppermute | solution.py:799
  317.2 1.5 collective-permute-start.46
  324.6 2.5 last.1
  (321 shorter events, 64.6 us)
Async XLA Ops:
  7.2 54.3 %all-gather.6.cloned.1.call-start = ((), (), s32[]{:S(2)}) async-start(), calls=%async_computation.3 | async-start | bytes 2621440 | tf_op jit(solution)/shard_map/all_gather | solution.py:910
  7.9 122.2 %all-gather.4.cloned.1.call-start = ((), (), s32[]{:S(2)}) async-start(), calls=%async_computation.2 | async-start | bytes 1310720 | tf_op jit(solution)/shard_map/all_gather | solution.py:951
  9.3 13.7 %copy-start.70 = (bf16[128,2048]{1,0:T(8,128)(2,1)}, bf16[128,2048]{1,0:T(8,128)(2,1)S(1)}, u32[]{:S(2)}) copy-start(bf16[128,2048]{1,0:T(8,128)(2,1)S(1)} %get-tuple-element.210) | copy-start | bytes 1572868
  9.3 13.7 %collective-permute-start.1 = (bf16[128,2048]{1,0:T(8,128)(2,1)S(1)}, bf16[128,2048]{1,0:T(8,128)(2,1)S(1)}, u32[]{:S(2)}, u32[]{:S(2)}) collective-permute-start(bf16[128,2048]{1,0:T(8,128)(2,1)S(1)} %get-tuple-element.210), channel_id=1, source_target_pairs={{0,16},{4,20},{8,24},{12,28},{16,0},{20,4},{24,8},{28,12},{1,17},{... | collective-permute-start | bytes 1572872 | tf_op jit(solution)/shard_map/ppermute | solution.py:799
  10.9 13.4 %collective-permute-start = (bf16[128,2048]{1,0:T(8,128)(2,1)S(1)}, bf16[128,2048]{1,0:T(8,128)(2,1)S(1)}, u32[]{:S(2)}, u32[]{:S(2)}) collective-permute-start(bf16[128,2048]{1,0:T(8,128)(2,1)S(1)} %get-tuple-element.211), channel_id=1, source_target_pairs={{0,8},{4,12},{8,0},{12,4},{16,24},{20,28},{24,16},{28,20},{1,9},{5... | collective-permute-start | bytes 1572872 | tf_op jit(solution)/shard_map/ppermute | solution.py:799
  13.8 14.4 %copy-start.80 = (bf16[128,128]{1,0:T(8,128)(2,1)S(1)}, bf16[128,128]{1,0:T(8,128)(2,1)}, u32[]{:S(2)}) copy-start(bf16[128,128]{1,0:T(8,128)(2,1)} %param.24) | copy-start | bytes 98308
  24.4 41.0 %copy-start.13 = (bf16[256,2048]{1,0:T(8,128)(2,1)}, bf16[256,2048]{1,0:T(8,128)(2,1)S(1)}, u32[]{:S(2)}) copy-start(bf16[256,2048]{1,0:T(8,128)(2,1)S(1)} %pad_maximum_fusion.refs_0_) | copy-start | bytes 3145732
  24.4 12.4 %copy-start.79 = (bf16[128,160]{0,1:T(8,128)(2,1)S(1)}, bf16[128,160]{0,1:T(8,128)(2,1)}, u32[]{:S(2)}) copy-start(bf16[128,160]{0,1:T(8,128)(2,1)} %param.23) | copy-start | bytes 122884
  24.4 12.4 %copy-start.81 = (bf16[128,16]{0,1:T(8,128)(2,1)S(1)}, bf16[128,16]{0,1:T(8,128)(2,1)}, u32[]{:S(2)}) copy-start(bf16[128,16]{0,1:T(8,128)(2,1)} %param.26) | copy-start | bytes 12292
  24.4 12.4 %copy-start.82 = (bf16[128,4]{0,1:T(4,128)(2,1)S(1)}, bf16[128,4]{0,1:T(4,128)(2,1)}, u32[]{:S(2)}) copy-start(bf16[128,4]{0,1:T(4,128)(2,1)} %param.21) | copy-start | bytes 3076
  24.4 12.4 %copy-start.83 = (bf16[128]{0:T(256)(128)(2,1)S(1)}, bf16[128]{0:T(256)(128)(2,1)}, u32[]{:S(2)}) copy-start(bf16[128]{0:T(256)(128)(2,1)} %param.22) | copy-start | bytes 772
  24.5 29.4 %collective-permute-start.9 = (bf16[256,2048]{1,0:T(8,128)(2,1)S(1)}, bf16[256,2048]{1,0:T(8,128)(2,1)S(1)}, u32[]{:S(2)}, u32[]{:S(2)}) collective-permute-start(bf16[256,2048]{1,0:T(8,128)(2,1)S(1)} %pad_maximum_fusion.refs_0_), channel_id=1, source_target_pairs={{0,16},{4,20},{8,24},{12,28},{16,0},{20,4},{24,8},{28,12},{1,17},{... | collective-permute-start | bytes 3145736 | tf_op jit(solution)/shard_map/ppermute | solution.py:799
  25.9 39.5 %copy-start.15 = (bf16[256,2048]{1,0:T(8,128)(2,1)}, bf16[256,2048]{1,0:T(8,128)(2,1)S(1)}, u32[]{:S(2)}) copy-start(bf16[256,2048]{1,0:T(8,128)(2,1)S(1)} %pad_maximum_fusion.1.refs_4_) | copy-start | bytes 3145732
  25.9 28.5 %collective-permute-start.12 = (bf16[256,2048]{1,0:T(8,128)(2,1)S(1)}, bf16[256,2048]{1,0:T(8,128)(2,1)}, u32[]{:S(2)}, u32[]{:S(2)}) collective-permute-start(bf16[256,2048]{1,0:T(8,128)(2,1)S(1)} %pad_maximum_fusion.1.refs_4_), channel_id=1, source_target_pairs={{0,8},{4,12},{8,0},{12,4},{16,24},{20,28},{24,16},{28,20},{1,9},{5... | collective-permute-start | bytes 3145736 | tf_op jit(solution)/shard_map/ppermute | solution.py:799
  30.2 4.8 %collective-permute-start.4 = (bf16[1,64]{1,0:T(2,128)(2,1)S(1)}, bf16[1,64]{1,0:T(2,128)(2,1)S(1)}, u32[]{:S(2)}, u32[]{:S(2)}) collective-permute-start(bf16[1,64]{1,0:T(2,128)(2,1)S(1)} %bitcast.79), channel_id=1, source_target_pairs={{0,1},{1,2},{2,3},{3,0},{4,5},{5,6},{6,7},{7,4},{8,9},{9,10},{10,1... | collective-permute-start | bytes 392 | tf_op jit(solution)/shard_map/ppermute | solution.py:927
  31.7 4.5 %collective-permute-start.3 = (bf16[1,64]{1,0:T(2,128)(2,1)S(1)}, bf16[1,64]{1,0:T(2,128)(2,1)S(1)}, u32[]{:S(2)}, u32[]{:S(2)}) collective-permute-start(bf16[1,64]{1,0:T(2,128)(2,1)S(1)} %bitcast.80), channel_id=1, source_target_pairs={{0,2},{1,3},{2,0},{3,1},{4,6},{5,7},{6,4},{7,5},{8,10},{9,11},{10,... | collective-permute-start | bytes 392 | tf_op jit(solution)/shard_map/ppermute | solution.py:927
  33.0 3.7 %collective-permute-start.2 = (bf16[1,64]{1,0:T(2,128)(2,1)S(1)}, bf16[1,64]{1,0:T(2,128)(2,1)S(1)}, u32[]{:S(2)}, u32[]{:S(2)}) collective-permute-start(bf16[1,64]{1,0:T(2,128)(2,1)S(1)} %bitcast.81), channel_id=1, source_target_pairs={{0,3},{1,0},{2,1},{3,2},{4,7},{5,4},{6,5},{7,6},{8,11},{9,8},{10,9... | collective-permute-start | bytes 392 | tf_op jit(solution)/shard_map/ppermute | solution.py:927
  34.9 99.5 %all-gather.8.cloned.1.call-start = ((), (), s32[]{:S(2)}) async-start(), calls=%async_computation.4 | async-start | bytes 1310720 | tf_op jit(solution)/shard_map/all_gather | solution.py:985
  37.0 16.2 %collective-permute-start.7 = (bf16[313,128]{1,0:T(8,128)(2,1)S(1)}, bf16[313,128]{1,0:T(8,128)(2,1)S(1)}, u32[]{:S(2)}, u32[]{:S(2)}) collective-permute-start(bf16[313,128]{1,0:T(8,128)(2,1)S(1)} %concatenate.22), channel_id=1, source_target_pairs={{0,24},{4,28},{8,16},{12,20},{16,8},{20,12},{24,0},{28,4},{1,25},{... | collective-permute-start | bytes 240392 | tf_op jit(solution)/shard_map/ppermute | solution.py:799
  38.0 15.2 %collective-permute-start.6 = (bf16[313,128]{1,0:T(8,128)(2,1)S(1)}, bf16[313,128]{1,0:T(8,128)(2,1)S(1)}, u32[]{:S(2)}, u32[]{:S(2)}) collective-permute-start(bf16[313,128]{1,0:T(8,128)(2,1)S(1)} %concatenate.22), channel_id=1, source_target_pairs={{0,16},{4,20},{8,24},{12,28},{16,0},{20,4},{24,8},{28,12},{1,17},{... | collective-permute-start | bytes 240392 | tf_op jit(solution)/shard_map/ppermute | solution.py:799
  38.9 14.8 %collective-permute-start.5 = (bf16[313,128]{1,0:T(8,128)(2,1)S(1)}, bf16[313,128]{1,0:T(8,128)(2,1)S(1)}, u32[]{:S(2)}, u32[]{:S(2)}) collective-permute-start(bf16[313,128]{1,0:T(8,128)(2,1)S(1)} %concatenate.22), channel_id=1, source_target_pairs={{0,8},{4,12},{8,0},{12,4},{16,24},{20,28},{24,16},{28,20},{1,9},{5... | collective-permute-start | bytes 240392 | tf_op jit(solution)/shard_map/ppermute | solution.py:799
  53.1 12.2 %collective-permute-start.10 = (bf16[256,2048]{1,0:T(8,128)(2,1)S(1)}, bf16[256,2048]{1,0:T(8,128)(2,1)}, u32[]{:S(2)}, u32[]{:S(2)}) collective-permute-start(bf16[256,2048]{1,0:T(8,128)(2,1)S(1)} %pad_maximum_fusion.refs_0_), channel_id=1, source_target_pairs={{0,4},{4,0},{8,12},{12,8},{16,20},{20,16},{24,28},{28,24},{1,5},{5... | collective-permute-start | bytes 3145736 | tf_op jit(solution)/shard_map/ppermute | solution.py:799
  53.2 12.2 %collective-permute-start.13 = (bf16[256,2048]{1,0:T(8,128)(2,1)S(1)}, bf16[256,2048]{1,0:T(8,128)(2,1)}, u32[]{:S(2)}, u32[]{:S(2)}) collective-permute-start(bf16[256,2048]{1,0:T(8,128)(2,1)S(1)} %pad_maximum_fusion.1.refs_4_), channel_id=1, source_target_pairs={{0,4},{4,0},{8,12},{12,8},{16,20},{20,16},{24,28},{28,24},{1,5},{5... | collective-permute-start | bytes 3145736 | tf_op jit(solution)/shard_map/ppermute | solution.py:799
  53.7 3.5 %collective-permute-start.8 = (bf16[313,512]{1,0:T(8,128)(2,1)S(1)}, bf16[313,512]{1,0:T(8,128)(2,1)S(1)}, u32[]{:S(2)}, u32[]{:S(2)}) collective-permute-start(bf16[313,512]{1,0:T(8,128)(2,1)S(1)} %pad_maximum_fusion.2), channel_id=1, source_target_pairs={{0,4},{4,0},{8,12},{12,8},{16,20},{20,16},{24,28},{28,24},{1,5},{5... | collective-permute-start | bytes 961544 | tf_op jit(solution)/shard_map/ppermute | solution.py:799
  53.9 11.5 %collective-permute-start.11 = (bf16[256,2048]{1,0:T(8,128)(2,1)S(1)}, bf16[256,2048]{1,0:T(8,128)(2,1)}, u32[]{:S(2)}, u32[]{:S(2)}) collective-permute-start(bf16[256,2048]{1,0:T(8,128)(2,1)S(1)} %collective-permute-done.9.refs_1_), channel_id=1, source_target_pairs={{0,4},{4,0},{8,12},{12,8},{16,20},{20,16},{24,28},{28,24},{1,5},{5... | collective-permute-start | bytes 3145736 | tf_op jit(solution)/shard_map/ppermute | solution.py:799
  54.5 10.9 %collective-permute-start.14 = (bf16[256,2048]{1,0:T(8,128)(2,1)}, bf16[256,2048]{1,0:T(8,128)(2,1)}, u32[]{:S(2)}, u32[]{:S(2)}) collective-permute-start(bf16[256,2048]{1,0:T(8,128)(2,1)} %collective-permute-done.12.refs_5_), channel_id=1, source_target_pairs={{0,4},{4,0},{8,12},{12,8},{16,20},{20,16},{24,28},{28,24},{1,5},{5... | collective-permute-start | bytes 3145736 | tf_op jit(solution)/shard_map/ppermute | solution.py:799
  58.0 20.5 %collective-permute-start.18 = (bf16[128,2048]{1,0:T(8,128)(2,1)}, bf16[128,2048]{1,0:T(8,128)(2,1)}, u32[]{:S(2)}, u32[]{:S(2)}) collective-permute-start(bf16[128,2048]{1,0:T(8,128)(2,1)} %param.28), channel_id=1, source_target_pairs={{0,8},{4,12},{8,0},{12,4},{16,24},{20,28},{24,16},{28,20},{1,9},{5... | collective-permute-start | bytes 1572872 | tf_op jit(solution)/shard_map/ppermute | solution.py:799
  59.6 206.2 %copy-start.58 = (f32[8,2,128]{2,1,0:T(2,128)}, f32[8,2,128]{2,1,0:T(2,128)S(1)}, u32[]{:S(2)}) copy-start(f32[8,2,128]{2,1,0:T(2,128)S(1)} %select_reduce_fusion) | copy-start | bytes 24580
  80.6 49.1 %collective-permute-start.19 = (bf16[256,2048]{1,0:T(8,128)(2,1)}, bf16[256,2048]{1,0:T(8,128)(2,1)S(1)}, u32[]{:S(2)}, u32[]{:S(2)}) collective-permute-start(bf16[256,2048]{1,0:T(8,128)(2,1)} %constant_dynamic-update-slice_fusion.5.refs_0_), channel_id=1, source_target_pairs={{0,16},{4,20},{8,24},{12,28},{16,0},{20,4},{24,8},{28,12},{1,17},{... | collective-permute-start | bytes 3145736 | tf_op jit(solution)/shard_map/ppermute | solution.py:799
  80.9 9.3 %collective-permute-start.17 = (bf16[512,160]{1,0:T(8,128)(2,1)S(1)}, bf16[512,160]{1,0:T(8,128)(2,1)S(1)}, u32[]{:S(2)}, u32[]{:S(2)}) collective-permute-start(bf16[512,160]{1,0:T(8,128)(2,1)S(1)} %get-tuple-element.99.refs_0_), channel_id=1, source_target_pairs={{0,3},{1,0},{2,1},{3,2},{4,7},{5,4},{6,5},{7,6},{8,11},{9,8},{10,9... | collective-permute-start | bytes 491528 | tf_op jit(solution)/shard_map/ppermute | solution.py:867
  81.4 19.8 %collective-permute-start.16 = (bf16[512,160]{1,0:T(8,128)(2,1)S(1)}, bf16[512,160]{1,0:T(8,128)(2,1)S(1)}, u32[]{:S(2)}, u32[]{:S(2)}) collective-permute-start(bf16[512,160]{1,0:T(8,128)(2,1)S(1)} %get-tuple-element.99.refs_0_), channel_id=1, source_target_pairs={{0,2},{1,3},{2,0},{3,1},{4,6},{5,7},{6,4},{7,5},{8,10},{9,11},{10,... | collective-permute-start | bytes 491528 | tf_op jit(solution)/shard_map/ppermute | solution.py:867
  83.9 22.0 %collective-permute-start.15 = (bf16[512,160]{1,0:T(8,128)(2,1)S(1)}, bf16[512,160]{1,0:T(8,128)(2,1)S(1)}, u32[]{:S(2)}, u32[]{:S(2)}) collective-permute-start(bf16[512,160]{1,0:T(8,128)(2,1)S(1)} %get-tuple-element.99.refs_0_), channel_id=1, source_target_pairs={{0,1},{1,2},{2,3},{3,0},{4,5},{5,6},{6,7},{7,4},{8,9},{9,10},{10,1... | collective-permute-start | bytes 491528 | tf_op jit(solution)/shard_map/ppermute | solution.py:867
  90.2 20.0 %copy-start.76 = (bf16[512,160]{1,0:T(8,128)(2,1)}, bf16[512,160]{1,0:T(8,128)(2,1)S(1)}, u32[]{:S(2)}) copy-start(bf16[512,160]{1,0:T(8,128)(2,1)S(1)} %collective-permute-done.17.refs_3_) | copy-start | bytes 491524
  105.9 138.6 %reduce-scatter.3.cloned.1.call-start = ((), (), s32[]{:S(2)}) async-start(), calls=%async_computation.5 | async-start | bytes 2621440 | tf_op jit(solution)/shard_map/reduce_scatter | solution.py:989
  129.6 3.5 %collective-permute-start.20 = (bf16[256,2048]{1,0:T(8,128)(2,1)}, bf16[256,2048]{1,0:T(8,128)(2,1)S(1)}, u32[]{:S(2)}, u32[]{:S(2)}) collective-permute-start(bf16[256,2048]{1,0:T(8,128)(2,1)} %constant_dynamic-update-slice_fusion.5.refs_0_), channel_id=1, source_target_pairs={{0,4},{4,0},{8,12},{12,8},{16,20},{20,16},{24,28},{28,24},{1,5},{5... | collective-permute-start | bytes 3145736 | tf_op jit(solution)/shard_map/ppermute | solution.py:799
  129.7 4.7 %collective-permute-start.21 = (bf16[256,2048]{1,0:T(8,128)(2,1)S(1)}, bf16[256,2048]{1,0:T(8,128)(2,1)S(1)}, u32[]{:S(2)}, u32[]{:S(2)}) collective-permute-start(bf16[256,2048]{1,0:T(8,128)(2,1)S(1)} %collective-permute-done.19.refs_1_), channel_id=1, source_target_pairs={{0,4},{4,0},{8,12},{12,8},{16,20},{20,16},{24,28},{28,24},{1,5},{5... | collective-permute-start | bytes 3145736 | tf_op jit(solution)/shard_map/ppermute | solution.py:799
  148.7 175.9 %reduce-scatter.5.cloned.1.call-start = ((), (), s32[]{:S(2)}) async-start(), calls=%async_computation.6 | async-start | bytes 2621440 | tf_op jit(solution)/shard_map/reduce_scatter | solution.py:1012
  153.4 50.0 %copy-start.1 = (bf16[512,2048]{1,0:T(8,128)(2,1)S(1)}, bf16[512,2048]{1,0:T(8,128)(2,1)}, u32[]{:S(2)}) copy-start(bf16[512,2048]{1,0:T(8,128)(2,1)} %copy-done) | copy-start | bytes 6291460
  199.3 9.8 %collective-permute-start.25 = (bf16[512,160]{1,0:T(8,128)(2,1)}, bf16[512,160]{1,0:T(8,128)(2,1)S(1)}, u32[]{:S(2)}, u32[]{:S(2)}) collective-permute-start(bf16[512,160]{1,0:T(8,128)(2,1)} %get-tuple-element.123.refs_0_), channel_id=1, source_target_pairs={{0,3},{1,0},{2,1},{3,2},{4,7},{5,4},{6,5},{7,6},{8,11},{9,8},{10,9... | collective-permute-start | bytes 491528 | tf_op jit(solution)/shard_map/ppermute | solution.py:867
  201.1 17.5 %collective-permute-start.24 = (bf16[512,160]{1,0:T(8,128)(2,1)}, bf16[512,160]{1,0:T(8,128)(2,1)S(1)}, u32[]{:S(2)}, u32[]{:S(2)}) collective-permute-start(bf16[512,160]{1,0:T(8,128)(2,1)} %get-tuple-element.123.refs_0_), channel_id=1, source_target_pairs={{0,2},{1,3},{2,0},{3,1},{4,6},{5,7},{6,4},{7,5},{8,10},{9,11},{10,... | collective-permute-start | bytes 491528 | tf_op jit(solution)/shard_map/ppermute | solution.py:867
  202.6 21.4 %collective-permute-start.23 = (bf16[512,160]{1,0:T(8,128)(2,1)}, bf16[512,160]{1,0:T(8,128)(2,1)S(1)}, u32[]{:S(2)}, u32[]{:S(2)}) collective-permute-start(bf16[512,160]{1,0:T(8,128)(2,1)} %get-tuple-element.123.refs_0_), channel_id=1, source_target_pairs={{0,1},{1,2},{2,3},{3,0},{4,5},{5,6},{6,7},{7,4},{8,9},{9,10},{10,1... | collective-permute-start | bytes 491528 | tf_op jit(solution)/shard_map/ppermute | solution.py:867
  203.4 22.3 %collective-permute-start.22 = (bf16[512,2048]{1,0:T(8,128)(2,1)}, bf16[512,2048]{1,0:T(8,128)(2,1)S(1)}, u32[]{:S(2)}, u32[]{:S(2)}) collective-permute-start(bf16[512,2048]{1,0:T(8,128)(2,1)} %copy-done.28), channel_id=1, source_target_pairs={{0,4},{4,0},{8,12},{12,8},{16,20},{20,16},{24,28},{28,24},{1,5},{5... | collective-permute-start | bytes 6291464 | tf_op jit(solution)/shard_map/ppermute | solution.py:799
  224.1 13.2 %collective-permute-start.26 = (bf16[512,2048]{1,0:T(8,128)(2,1)S(1)}, bf16[512,2048]{1,0:T(8,128)(2,1)S(1)}, u32[]{:S(2)}, u32[]{:S(2)}) collective-permute-start(bf16[512,2048]{1,0:T(8,128)(2,1)S(1)} %grad_half.8), channel_id=1, source_target_pairs={{0,4},{4,0},{8,12},{12,8},{16,20},{20,16},{24,28},{28,24},{1,5},{5... | collective-permute-start | bytes 6291464 | tf_op jit(solution)/shard_map/ppermute | solution.py:799
  226.7 16.1 %collective-permute-start.27 = (bf16[2,128,1024]{2,1,0:T(8,128)(2,1)S(1)}, bf16[2,128,1024]{2,1,0:T(8,128)(2,1)S(1)}, u32[]{:S(2)}, u32[]{:S(2)}) collective-permute-start(bf16[2,128,1024]{2,1,0:T(8,128)(2,1)S(1)} %get-tuple-element.121), channel_id=1, source_target_pairs={{0,8},{4,12},{8,0},{12,4},{16,24},{20,28},{24,16},{28,20},{1,9},{5... | collective-permute-start | bytes 1572872 | tf_op jit(solution)/shard_map/ppermute | solution.py:799
  228.5 15.1 %collective-permute-start.28 = (bf16[2,128,1024]{2,1,0:T(8,128)(2,1)S(1)}, bf16[2,128,1024]{2,1,0:T(8,128)(2,1)S(1)}, u32[]{:S(2)}, u32[]{:S(2)}) collective-permute-start(bf16[2,128,1024]{2,1,0:T(8,128)(2,1)S(1)} %get-tuple-element.122), channel_id=1, source_target_pairs={{0,16},{4,20},{8,24},{12,28},{16,0},{20,4},{24,8},{28,12},{1,17},{... | collective-permute-start | bytes 1572872 | tf_op jit(solution)/shard_map/ppermute | solution.py:799
  241.0 15.7 %collective-permute-start.29 = (bf16[2,128,1024]{2,1,0:T(8,128)(2,1)}, bf16[2,128,1024]{2,1,0:T(8,128)(2,1)}, u32[]{:S(2)}, u32[]{:S(2)}) collective-permute-start(bf16[2,128,1024]{2,1,0:T(8,128)(2,1)} %get-tuple-element.130), channel_id=1, source_target_pairs={{0,8},{4,12},{8,0},{12,4},{16,24},{20,28},{24,16},{28,20},{1,9},{5... | collective-permute-start | bytes 1572872 | tf_op jit(solution)/shard_map/ppermute | solution.py:799
  241.5 15.2 %collective-permute-start.30 = (bf16[2,128,1024]{2,1,0:T(8,128)(2,1)}, bf16[2,128,1024]{2,1,0:T(8,128)(2,1)}, u32[]{:S(2)}, u32[]{:S(2)}) collective-permute-start(bf16[2,128,1024]{2,1,0:T(8,128)(2,1)} %get-tuple-element.131), channel_id=1, source_target_pairs={{0,16},{4,20},{8,24},{12,28},{16,0},{20,4},{24,8},{28,12},{1,17},{... | collective-permute-start | bytes 1572872 | tf_op jit(solution)/shard_map/ppermute | solution.py:799
  265.9 29.9 %collective-permute-start.35 = (bf16[512,2048]{1,0:T(8,128)(2,1)}, bf16[512,2048]{1,0:T(8,128)(2,1)}, u32[]{:S(2)}, u32[]{:S(2)}) collective-permute-start(bf16[512,2048]{1,0:T(8,128)(2,1)} %grad_half.10), channel_id=1, source_target_pairs={{0,4},{4,0},{8,12},{12,8},{16,20},{20,16},{24,28},{28,24},{1,5},{5... | collective-permute-start | bytes 6291464 | tf_op jit(solution)/shard_map/ppermute | solution.py:799
  265.9 10.7 %collective-permute-start.33 = (bf16[1,2048]{1,0:T(2,128)(2,1)S(1)}, bf16[1,2048]{1,0:T(2,128)(2,1)S(1)}, u32[]{:S(2)}, u32[]{:S(2)}) collective-permute-start(bf16[1,2048]{1,0:T(2,128)(2,1)S(1)} %divide_convert_fusion), channel_id=1, source_target_pairs={{0,3},{1,0},{2,1},{3,2},{4,7},{5,4},{6,5},{7,6},{8,11},{9,8},{10,9... | collective-permute-start | bytes 12296 | tf_op jit(solution)/shard_map/ppermute | solution.py:867
  267.6 9.0 %collective-permute-start.32 = (bf16[1,2048]{1,0:T(2,128)(2,1)S(1)}, bf16[1,2048]{1,0:T(2,128)(2,1)S(1)}, u32[]{:S(2)}, u32[]{:S(2)}) collective-permute-start(bf16[1,2048]{1,0:T(2,128)(2,1)S(1)} %divide_convert_fusion), channel_id=1, source_target_pairs={{0,2},{1,3},{2,0},{3,1},{4,6},{5,7},{6,4},{7,5},{8,10},{9,11},{10,... | collective-permute-start | bytes 12296 | tf_op jit(solution)/shard_map/ppermute | solution.py:867
  269.8 6.9 %collective-permute-start.31 = (bf16[1,2048]{1,0:T(2,128)(2,1)S(1)}, bf16[1,2048]{1,0:T(2,128)(2,1)S(1)}, u32[]{:S(2)}, u32[]{:S(2)}) collective-permute-start(bf16[1,2048]{1,0:T(2,128)(2,1)S(1)} %divide_convert_fusion), channel_id=1, source_target_pairs={{0,1},{1,2},{2,3},{3,0},{4,5},{5,6},{6,7},{7,4},{8,9},{9,10},{10,1... | collective-permute-start | bytes 12296 | tf_op jit(solution)/shard_map/ppermute | solution.py:867
  276.6 19.1 %copy-start.4 = (bf16[512,2048]{1,0:T(8,128)(2,1)S(1)}, bf16[512,2048]{1,0:T(8,128)(2,1)}, u32[]{:S(2)}) copy-start(bf16[512,2048]{1,0:T(8,128)(2,1)} %copy-done.3) | copy-start | bytes 6291460
  285.6 14.3 %collective-permute-start.34 = (bf16[328,512]{1,0:T(8,128)(2,1)S(1)}, bf16[328,512]{1,0:T(8,128)(2,1)S(1)}, u32[]{:S(2)}, u32[]{:S(2)}) collective-permute-start(bf16[328,512]{1,0:T(8,128)(2,1)S(1)} %get-tuple-element.154), channel_id=1, source_target_pairs={{0,4},{4,0},{8,12},{12,8},{16,20},{20,16},{24,28},{28,24},{1,5},{5... | collective-permute-start | bytes 1007624 | tf_op jit(solution)/shard_map/ppermute | solution.py:799
  285.7 9.4 %collective-permute-start.36 = (bf16[1,128,1024]{2,1,0:T(8,128)(2,1)}, bf16[1,128,1024]{2,1,0:T(8,128)(2,1)S(1)}, u32[]{:S(2)}, u32[]{:S(2)}) collective-permute-start(bf16[1,128,1024]{2,1,0:T(8,128)(2,1)} %copy-done.68), channel_id=1, source_target_pairs={{0,16},{4,20},{8,24},{12,28},{16,0},{20,4},{24,8},{28,12},{1,17},{... | collective-permute-start | bytes 786440 | tf_op jit(solution)/shard_map/ppermute | solution.py:799
  286.4 9.3 %collective-permute-start.37 = (bf16[1,128,1024]{2,1,0:T(8,128)(2,1)}, bf16[1,128,1024]{2,1,0:T(8,128)(2,1)S(1)}, u32[]{:S(2)}, u32[]{:S(2)}) collective-permute-start(bf16[1,128,1024]{2,1,0:T(8,128)(2,1)} %copy-done.67), channel_id=1, source_target_pairs={{0,8},{4,12},{8,0},{12,4},{16,24},{20,28},{24,16},{28,20},{1,9},{5... | collective-permute-start | bytes 786440 | tf_op jit(solution)/shard_map/ppermute | solution.py:799
  287.9 13.7 %collective-permute-start.40 = (bf16[1,128,1024]{2,1,0:T(8,128)(2,1)S(1)}, bf16[1,128,1024]{2,1,0:T(8,128)(2,1)S(1)}, u32[]{:S(2)}, u32[]{:S(2)}) collective-permute-start(bf16[1,128,1024]{2,1,0:T(8,128)(2,1)S(1)} %copy-done.66), channel_id=1, source_target_pairs={{0,16},{4,20},{8,24},{12,28},{16,0},{20,4},{24,8},{28,12},{1,17},{... | collective-permute-start | bytes 786440 | tf_op jit(solution)/shard_map/ppermute | solution.py:799
  295.0 9.2 %collective-permute-start.41 = (bf16[1,128,1024]{2,1,0:T(8,128)(2,1)S(1)}, bf16[1,128,1024]{2,1,0:T(8,128)(2,1)S(1)}, u32[]{:S(2)}, u32[]{:S(2)}) collective-permute-start(bf16[1,128,1024]{2,1,0:T(8,128)(2,1)S(1)} %copy-done.64), channel_id=1, source_target_pairs={{0,8},{4,12},{8,0},{12,4},{16,24},{20,28},{24,16},{28,20},{1,9},{5... | collective-permute-start | bytes 786440 | tf_op jit(solution)/shard_map/ppermute | solution.py:799
  297.8 17.7 %collective-permute-start.39 = (bf16[2,128,1024]{2,1,0:T(8,128)(2,1)S(1)}, bf16[2,128,1024]{2,1,0:T(8,128)(2,1)S(1)}, u32[]{:S(2)}, u32[]{:S(2)}) collective-permute-start(bf16[2,128,1024]{2,1,0:T(8,128)(2,1)S(1)} %get-tuple-element.156), channel_id=1, source_target_pairs={{0,8},{4,12},{8,0},{12,4},{16,24},{20,28},{24,16},{28,20},{1,9},{5... | collective-permute-start | bytes 1572872 | tf_op jit(solution)/shard_map/ppermute | solution.py:799
  299.1 16.4 %collective-permute-start.42 = (bf16[2,128,1024]{2,1,0:T(8,128)(2,1)S(1)}, bf16[2,128,1024]{2,1,0:T(8,128)(2,1)S(1)}, u32[]{:S(2)}, u32[]{:S(2)}) collective-permute-start(bf16[2,128,1024]{2,1,0:T(8,128)(2,1)S(1)} %get-tuple-element.157), channel_id=1, source_target_pairs={{0,16},{4,20},{8,24},{12,28},{16,0},{20,4},{24,8},{28,12},{1,17},{... | collective-permute-start | bytes 1572872 | tf_op jit(solution)/shard_map/ppermute | solution.py:799
  300.0 16.5 %collective-permute-start.38 = (bf16[328,128]{1,0:T(8,128)(2,1)S(1)}, bf16[328,128]{1,0:T(8,128)(2,1)S(1)}, u32[]{:S(2)}, u32[]{:S(2)}) collective-permute-start(bf16[328,128]{1,0:T(8,128)(2,1)S(1)} %get-tuple-element.219), channel_id=1, source_target_pairs={{0,8},{4,12},{8,0},{12,4},{16,24},{20,28},{24,16},{28,20},{1,9},{5... | collective-permute-start | bytes 251912 | tf_op jit(solution)/shard_map/ppermute | solution.py:799
  301.6 17.1 %collective-permute-start.44 = (bf16[328,128]{1,0:T(8,128)(2,1)S(1)}, bf16[328,128]{1,0:T(8,128)(2,1)S(1)}, u32[]{:S(2)}, u32[]{:S(2)}) collective-permute-start(bf16[328,128]{1,0:T(8,128)(2,1)S(1)} %get-tuple-element.220), channel_id=1, source_target_pairs={{0,24},{4,28},{8,16},{12,20},{16,8},{20,12},{24,0},{28,4},{1,25},{... | collective-permute-start | bytes 251912 | tf_op jit(solution)/shard_map/ppermute | solution.py:799
  304.3 14.4 %collective-permute-start.43 = (bf16[328,128]{1,0:T(8,128)(2,1)S(1)}, bf16[328,128]{1,0:T(8,128)(2,1)S(1)}, u32[]{:S(2)}, u32[]{:S(2)}) collective-permute-start(bf16[328,128]{1,0:T(8,128)(2,1)S(1)} %get-tuple-element.221), channel_id=1, source_target_pairs={{0,16},{4,20},{8,24},{12,28},{16,0},{20,4},{24,8},{28,12},{1,17},{... | collective-permute-start | bytes 251912 | tf_op jit(solution)/shard_map/ppermute | solution.py:799
  316.5 6.6 %collective-permute-start.45 = (bf16[1,128,1024]{2,1,0:T(8,128)(2,1)S(1)}, bf16[1,128,1024]{2,1,0:T(8,128)(2,1)S(1)}, u32[]{:S(2)}, u32[]{:S(2)}) collective-permute-start(bf16[1,128,1024]{2,1,0:T(8,128)(2,1)S(1)} %get-tuple-element.171), channel_id=1, source_target_pairs={{0,16},{4,20},{8,24},{12,28},{16,0},{20,4},{24,8},{28,12},{1,17},{... | collective-permute-start | bytes 786440 | tf_op jit(solution)/shard_map/ppermute | solution.py:799
  317.2 6.4 %collective-permute-start.46 = (bf16[1,128,1024]{2,1,0:T(8,128)(2,1)S(1)}, bf16[1,128,1024]{2,1,0:T(8,128)(2,1)S(1)}, u32[]{:S(2)}, u32[]{:S(2)}) collective-permute-start(bf16[1,128,1024]{2,1,0:T(8,128)(2,1)S(1)} %get-tuple-element.173), channel_id=1, source_target_pairs={{0,8},{4,12},{8,0},{12,4},{16,24},{20,28},{24,16},{28,20},{1,9},{5... | collective-permute-start | bytes 786440 | tf_op jit(solution)/shard_map/ppermute | solution.py:799
  (78 other events, 262.6 us)
Sparse Core Ops, SparseCore 0:
  9.6 45.5 all-gather.5
  56.7 28.4 all-gather.3
  106.0 28.3 all-gather.7
  148.8 41.4 reduce-scatter.2
  256.9 43.5 reduce-scatter.4

commit v4 on v3

--- a/solution.py
+++ b/solution.py
@@ -59,18 +59,21 @@
     @pl.when(chunk == 0)
     def _():
         h_ref[...] = h0_ref[...]
-
-    mixed = part_refs[0][...].astype(f32)
-    for part_ref in part_refs[1:]:
-        mixed = mixed + part_ref[...].astype(f32)
-    mixed_ref[...] = mixed
-    step_in = mixed[:, :rank].astype(bf16)
+        total = part_refs[0][...].astype(f32)
+        for part_ref in part_refs[1:]:
+            total = total + part_ref[...].astype(f32)
+        mixed_ref[:, pl.ds(0, rank)] = total[:rank].T
+        blank = jnp.zeros((LANES - 2 * states, total.shape[1]), f32)
+        mixed_ref[:, pl.ds(rank, LANES)] = jnp.concatenate([total[rank:], blank], axis=0).T
+
+    own_rows = pl.ds(pl.multiple_of(chunk * rows, rows), rows)
+    step_in = mixed_ref[own_rows, pl.ds(0, rank)].astype(bf16)
     raw = jnp.dot(step_in, wdt_ref[...], preferred_element_type=f32) + db_ref[...]
     delta = jnp.maximum(raw, 0.0) + jnp.log1p(jnp.exp(-jnp.abs(raw)))
     inner = inner_ref[...].astype(f32)
     put_tiles(dl_ref, delta, subs)
     put_tiles(du_sc, delta * inner, subs)
-    put_spread(bb_sc, mixed[:, rank:], 2 * states)
+    put_spread(bb_sc, mixed_ref[own_rows, pl.ds(rank, LANES)], 2 * states)
     hs_ref[pl.ds(0, span), :] = h_ref[...]
     decs = [dec_ref[pl.ds(n * subs, subs), :] for n in range(states)]
 
@@ -106,8 +109,8 @@
     rows, channels = gate.shape
     subs = channels // LANES
     rank = wdt.shape[0]
-    mix = parts[0].shape[1]
-    states = (mix - rank) // 2
+    states = (parts[0].shape[0] - rank) // 2
+    mix = rank + LANES
     chunks = rows // chunk_rows
     span = states * subs
 
@@ -121,13 +124,13 @@
     grid_spec = pltpu.PrefetchScalarGridSpec(
         num_scalar_prefetch=1,
         grid=(chunks,),
-        in_specs=[row_block(mix) for _ in parts]
+        in_specs=[whole(part) for part in parts]
         + [whole(wdt), whole(dt_bias), whole(d_skip), whole(dec), row_block(channels, h * chunks), row_block(channels), whole(h0)]
         + [pl.BlockSpec(memory_space=pl.ANY) for _ in extra],
         out_specs=[
             pl.BlockSpec(((chunk_rows + 1) * span, LANES), lambda i, *_: (i, 0)),
             pl.BlockSpec((chunk_rows * subs, LANES), lambda i, *_: (i, 0)),
-            row_block(channels), row_block(channels, h * chunks), row_block(mix), whole(h0),
+            row_block(channels), row_block(channels, h * chunks), pl.BlockSpec((rows, mix), lambda i, *_: (0, 0)), whole(h0),
         ],
         scratch_shapes=[
             pltpu.VMEM((chunk_rows * subs, LANES), f32),
@@ -145,7 +148,7 @@
         ],
         input_output_aliases={} if into is None else {len(parts) + 8: 3},
         compiler_params=pltpu.CompilerParams(vmem_limit_bytes=58 << 20),
-        cost_estimate=cost(0.02),
+        cost_estimate=cost(40.0),
         name="scan_forward",
     )(keep, *parts, wdt, dt_bias, d_skip, dec, inner, gate, h0, *extra)
 
@@ -250,11 +253,7 @@
     slope = jnp.where(d_all < 0.03125, series, 1.0 - jnp.exp(-d_all))
     gp = get_tiles(gd_sc, rows, subs) * slope
     red_ref[pl.ds(1, 1), :] += jnp.sum(gp, axis=0, keepdims=True)
-    low = gp.astype(bf16)
-    gp_ref[...] = low
-    mixed_ref[pl.ds(pl.multiple_of(chunk * rows, rows), rows), pl.ds(0, rank)] = lax.dot_general(
-        low, wdt_ref[...], (((1,), (1,)), ((), ())), preferred_element_type=f32
-    ).astype(bf16)
+    gp_ref[pl.ds(pl.multiple_of(chunk * rows, rows), rows), :] = gp.astype(bf16)
 
     @pl.when(i == last)
     def _():
@@ -264,7 +263,9 @@
             pick = jnp.where(lane == n, 1.0, 0.0).astype(bf16)
             part = r_sc[pl.ds(n * all_rows, all_rows), :].astype(bf16)
             total = total + jnp.dot(part, pick, preferred_element_type=f32)
-        mixed_ref[:, pl.ds(rank, 2 * states)] = total[:, : 2 * states].astype(bf16)
+        step = lax.dot_general(wdt_ref[...], gp_ref[...], (((1,), (1,)), ((), ())), preferred_element_type=f32)
+        mixed_ref[pl.ds(0, rank), :] = step.astype(bf16)
+        mixed_ref[pl.ds(rank, 2 * states), :] = total.T[: 2 * states].astype(bf16)
 
 
 def scan_backward(h, keep, mixed, wdt, d_skip, dec, inner, gate, gg, ysum, hs, delta_tm, gh0, into=(), chunk_rows=64):
@@ -272,7 +273,7 @@
     subs = channels // LANES
     rank = wdt.shape[0]
     mix = mixed.shape[1]
-    states = (mix - rank) // 2
+    states = dec.shape[0] // subs
     chunks = rows // chunk_rows
     span = states * subs
     skip_tm = d_skip.reshape(subs, LANES)
@@ -296,7 +297,7 @@
         ]
         + [pl.BlockSpec(memory_space=pl.ANY) for _ in into],
         out_specs=[
-            row_block(channels), row_block(channels, first), row_block(channels, first), fixed((rows, mix)),
+            row_block(channels), row_block(channels, first), fixed((rows, channels)), fixed((rank + 2 * states, rows)),
             fixed((8, channels)), fixed((span, LANES)), fixed((span, LANES)),
         ],
         scratch_shapes=[
@@ -310,12 +311,12 @@
         grid_spec=grid_spec,
         out_shape=[
             made((rows, channels), f32), made(inner.shape, bf16), made(inner.shape, bf16),
-            made((rows, mix), bf16), made((8, channels), f32), made((span, LANES), f32),
+            made((rank + 2 * states, rows), bf16), made((8, channels), f32), made((span, LANES), f32),
             made((span, LANES), f32),
         ],
         input_output_aliases={12 + i: 1 + i for i in range(len(into))},
         compiler_params=pltpu.CompilerParams(vmem_limit_bytes=58 << 20),
-        cost_estimate=cost(0.02),
+        cost_estimate=cost(100.0),
         name="scan_backward",
     )(keep, mixed, wdt, skip_tm, dec, inner, gate, gg, ysum, hs, delta_tm, gh0, *into)
 
@@ -389,7 +390,7 @@
         pre = pre + jnp.where(dist >= lag, taps_ref[pl.ds(taps - 1 - lag, 1), :] * shifted, 0.0)
     inner = (pre / (1.0 + jnp.exp(-pre))).astype(bf16)
     inner_ref[...] = inner
-    part = lax.dot_general(inner, wxp_ref[...], dims, preferred_element_type=f32)
+    part = lax.dot_general(wxp_ref[...], inner, dims, preferred_element_type=f32)
 
     @pl.when(i == 0)
     def _():
@@ -418,12 +419,12 @@
         in_specs=[pl.BlockSpec((rows, width), lambda i: (0, 0))]
         + weight_specs(chunk, width)
         + [columns(taps.shape[0]), columns(1), columns(xw), pl.BlockSpec((rows, 1), lambda i: (0, 0))],
-        out_specs=[columns(rows), columns(rows), columns(rows), pl.BlockSpec((rows, xw), lambda i: (0, 0))],
+        out_specs=[columns(rows), columns(rows), columns(rows), pl.BlockSpec((xw, rows), lambda i: (0, 0))],
         out_shape=[
             made((rows, channels), f32), made((rows, channels), f32), made((rows, channels), bf16),
-            made((rows, xw), bf16),
+            made((xw, rows), bf16),
         ],
-        scratch_shapes=[pltpu.VMEM((rows + SUB, chunk), f32), pltpu.VMEM((rows, xw), f32)],
+        scratch_shapes=[pltpu.VMEM((rows + SUB, chunk), f32), pltpu.VMEM((xw, rows), f32)],
         compiler_params=pltpu.CompilerParams(vmem_limit_bytes=44 << 20),
         cost_estimate=cost(0.02),
         name="front",
@@ -443,16 +444,19 @@
     dist = dist_ref[...]
     signal = sig_ref[...]
     pre = bias_ref[...] + taps_ref[pl.ds(taps - 1, 1), :] * signal
+    earlier = {}
     for lag in range(1, taps):
-        shifted = ext_sc[pl.ds(SUB - lag, rows), :]
-        pre = pre + jnp.where(dist >= lag, taps_ref[pl.ds(taps - 1 - lag, 1), :] * shifted, 0.0)
+        earlier[lag] = jnp.where(dist >= lag, ext_sc[pl.ds(SUB - lag, rows), :], 0.0)
+        pre = pre + taps_ref[pl.ds(taps - 1 - lag, 1), :] * earlier[lag]
     sig = 1.0 / (1.0 + jnp.exp(-pre))
     mixed = part_refs[0][...].astype(f32)
     for part_ref in part_refs[1:]:
         mixed = mixed + part_ref[...].astype(f32)
     low = mixed.astype(bf16)
     low_ref[...] = low
-    g_inner = gis_ref[...] + jnp.dot(low, wxp_ref[...], preferred_element_type=f32)
+    g_inner = gis_ref[...] + lax.dot_general(
+        low, wxp_ref[...], (((0,), (0,)), ((), ())), preferred_element_type=f32
+    )
     g_pre = g_inner * (sig * (1.0 + pre * (1.0 - sig)))
     head_ref[...] = g_pre[:SUB, :]
     lines = [None] * taps
@@ -462,7 +466,7 @@
         next_ref, dnext_ref = more.pop(0), more.pop(0)
     for lag in range(1, taps):
         masked = jnp.where(dist >= lag, g_pre, 0.0)
-        lines[taps - 1 - lag] = jnp.sum(masked * ext_sc[pl.ds(SUB - lag, rows), :], axis=0, keepdims=True)
+        lines[taps - 1 - lag] = jnp.sum(g_pre * earlier[lag], axis=0, keepdims=True)
         late_sc[pl.ds(0, rows), :] = masked
         late_sc[pl.ds(rows, SUB), :] = nothing if ends else jnp.where(dnext_ref[...] >= lag, next_ref[...], 0.0)
         g_signal = g_signal + taps_ref[pl.ds(taps - 1 - lag, 1), :] * late_sc[pl.ds(lag, rows), :]
@@ -504,15 +508,15 @@
             pl.BlockSpec((rows, 1), lambda i: (h, 0)),
         ]
         + extra_specs,
-        out_specs=[columns(rows, h), pl.BlockSpec((rows, xw), lambda i: (0, 0)), columns(SUB), columns(SUB)],
+        out_specs=[columns(rows, h), pl.BlockSpec((xw, rows), lambda i: (0, 0)), columns(SUB), columns(SUB)],
         out_shape=[
-            made((dist.shape[0], channels), bf16), made((rows, xw), bf16), made((SUB, channels), f32),
+            made((dist.shape[0], channels), bf16), made((xw, rows), bf16), made((SUB, channels), f32),
             made((SUB, channels), f32),
         ],
         scratch_shapes=[pltpu.VMEM((rows + SUB, chunk), f32), pltpu.VMEM((rows + SUB, chunk), f32)],
         input_output_aliases=alias,
         compiler_params=pltpu.CompilerParams(vmem_limit_bytes=32 << 20),
-        cost_estimate=cost(0.02),
+        cost_estimate=cost(40.0),
         name="turn",
     )(*parts, gis, signal, taps, bias, w_xp, dist, *extra)
 
@@ -552,8 +556,8 @@
         out_specs=[whole, pl.BlockSpec((1, width), lambda i: (0, 0))],
         out_shape=[made((rows, width), bf16), made((1, width), f32)],
         scratch_shapes=[pltpu.VMEM((rows, width), f32)],
-        compiler_params=pltpu.CompilerParams(vmem_limit_bytes=44 << 20),
-        cost_estimate=cost(0.02),
+        compiler_params=pltpu.CompilerParams(vmem_limit_bytes=60 << 20),
+        cost_estimate=cost(40.0),
         name="rear",
     )(g_signal, g_gate, *weights, normed)
 
@@ -591,7 +595,7 @@
         + [pl.BlockSpec(quarter.shape, lambda i: (0, 0)) for quarter in quarters],
         out_specs=[row_block(channels), row_block(2 * half)],
         out_shape=[made((tokens, channels), bf16), made((tokens, 2 * half), bf16)],
-        compiler_params=pltpu.CompilerParams(vmem_limit_bytes=40 << 20),
+        compiler_params=pltpu.CompilerParams(vmem_limit_bytes=60 << 20),
         cost_estimate=cost(0.02),
         name="cross",
     )(*cots, gated, *quarters)
@@ -706,8 +710,8 @@
               stay_ref, leave_ref, all_sc):
     i = pl.program_id(0)
     dims = (((0,), (0,)), ((), ()))
-    chunk, xw = inner_ref.shape[1], low_ref.shape[1]
-    all_sc[pl.ds(0, xw), :] = lax.dot_general(low_ref[...], inner_ref[...], dims, preferred_element_type=f32)
+    chunk, xw = inner_ref.shape[1], low_ref.shape[0]
+    all_sc[pl.ds(0, xw), :] = jnp.dot(low_ref[...], inner_ref[...], preferred_element_type=f32)
     step_in = mix_ref[...][:, :rank].astype(bf16)
     all_sc[pl.ds(xw, rank), :] = lax.dot_general(step_in, gp_ref[...], dims, preferred_element_type=f32)
     subs = dec_ref.shape[0] // states
@@ -733,7 +737,7 @@
     tokens, channels = inner.shape
     chunk = min(256, channels // 2)
     half = channels // 2 // chunk
-    height = low.shape[1] + rank + states + 3 * SUB
+    height = low.shape[0] + rank + states + 3 * SUB
 
     def columns(rows):
         return pl.BlockSpec((rows, chunk), lambda i: (0, i))
@@ -978,13 +982,14 @@
     for _ in wide[1:]:
         gather_o.take(mixed_own)
         gather_o.send()
+    cot_r = lax.all_gather(after(cotangent[:, half_width:], *parts), "tensor", axis=0, tiled=True)
+    got_o, sent_o = after(gather_o.got, *parts[1:]), after(gather_o.sent, *parts[1:])
+    quarters = (sent_o, got_o, swap(sent_o, 1), swap(got_o, 1))
     none = jnp.zeros(rates.shape, f32)
     states_all, deltas, sums, gated, mixed, _ = scan_forward(
         0, keep, parts, w_dt_rows, dt_b, skip_row, rates, inner, gate, none
     )
-    cot_r = lax.all_gather(after(cotangent[:, half_width:], *parts), "tensor", axis=0, tiled=True)
-    got_o, sent_o = after(gather_o.got, mixed), after(gather_o.sent, mixed)
-    quarters = (sent_o, got_o, swap(sent_o, 1), swap(got_o, 1))
+    quarters = tuple(after(quarter, mixed) for quarter in quarters)
     grad_gated, branch = cross((cot_l, cot_r), gated, quarters)
     branch_own = lax.psum_scatter(branch, "tensor", scatter_dimension=0, tiled=True)
     output = (hidden.astype(f32) + branch_own.astype(f32)).astype(bf16)
@@ -1002,7 +1007,7 @@
     gate_grad.rest()
     sent = out_grad.go(gate_grad.bases[0])
     backs[0] = after(backs[0], *sent)
-    gate_grad.exchange(*backs[1:])
+    gate_grad.exchange()
     g_signal, low, _, conv_sums = turn(0, backs, g_scan, signal, conv_rows, conv_b, w_xp, dist)
     sent = gate_grad.go(low)
     g_norm, gain_term = rear(
@@ -1015,30 +1020,31 @@
     gain_sum = jnp.sum(jnp.where(owners[:, :, None], gain_sum[:, None, :], 0.0), axis=0)
     gain_sum = jnp.pad(gain_sum, ((0, 0), (0, own_channels - gain_sum.shape[1]))).reshape(1, channels)
     gain_sum = jnp.concatenate([gain_sum, jnp.zeros((SUB - 1, channels), f32)], axis=0)
-    sent = out_grad.go(g_norm)
-    sig_grad = WeightGrad(after(g_signal, *sent), (normed,), kept, orders)
+    sig_grad = WeightGrad(after(g_signal, g_norm), (normed,), kept, orders)
     sig_grad.exchange()
-    sent = gate_grad.go(sig_grad.leave)
+    sent = out_grad.go(sig_grad.leave)
     sig_grad.rest(*sent)
+    sent = gate_grad.go(sig_grad.bases[0])
+    sent = sig_grad.go(*sent)
     small_stay, small_leave = pack(
-        rank, states, low, mixed, inner, g_proj, acc, rates, conv_sums, reds, after(gain_sum, sig_grad.bases[0])
+        rank, states, low, mixed, inner, g_proj, acc, rates, conv_sums, reds, after(gain_sum, *sent)
     )
     small_got = swap(small_leave, 1)
-    sent = sig_grad.go(small_leave, *out_grad.gots)
-    small_half = small_stay.astype(f32) + after(small_got, *sent).astype(f32)
+    out_grad.gots[0] = after(out_grad.gots[0], small_leave)
+    grad_w_out = out_grad.finish()[0]
+    small_half = small_stay.astype(f32) + after(small_got, grad_w_out).astype(f32)
     small_cuts = [small_half[:, i * own_channels : (i + 1) * own_channels] for i in range(len(kept))]
     small_lows = [cut.astype(bf16) for cut in small_cuts[1:]]
     small_gots = [swap(low, k) for low, k in zip(small_lows, kept[1:])]
-    out_grad.gots[0] = after(out_grad.gots[0], *small_lows)
-    grad_w_out = out_grad.finish()[0]
-    gate_grad.gots[0] = after(gate_grad.gots[0], grad_w_out)
+    gate_grad.gots[0] = after(gate_grad.gots[0], *small_lows)
     grad_w_in = gate_grad.finish(1, 2)
     sig_grad.go(grad_w_in)
     small_gots[0] = after(small_gots[0], sig_grad.bases[0])
     small_own = small_cuts[0]
     for got in small_gots:
         small_own = small_own + got.astype(f32)
-    grad_hidden = last(after(g_norm_own, small_own), hidden, cotangent, gain)
+    grad_hidden = last(g_norm_own, hidden, cotangent, gain)
+    sig_grad.gots[0] = after(sig_grad.gots[0], grad_hidden)
     grad_w_in = sig_grad.finish(0, 2, grad_w_in)
     at = xw + rank + states
     grad_gain = small_own[at + 2 * SUB, : norm_gain.shape[0]]

time: 338 us -> 304 us (0.90)
  waiting for transfers between devices: 86 us -> 64.3 us
  local copies, waits for them, and re-layouts: 54.6 us -> 34.9 us
  Pallas kernels: 125 us -> 131 us
    ppermute x9, waiting for transfers between devices: 37.3 us -> 13 us  [ring_parts(): lax.ppermute(part, 'tensor', [(i, (i + step) % count) for i in range(coun...]
    unnamed x188 -> x170, local copies, waits for them, and re-layouts: 42.1 us -> 22.5 us
  transfers between devices with their start and end apart: 52 -> 52, of which waited for: 20 -> 16; matrix products, arithmetic and copies ran while one was open for 6% -> 7% of each run, Pallas kernels for 35% -> 40%
where the time goes in v4:
time: 304 us; the launch traced here: 300 us
  Pallas kernels  131 us (43%)
  waiting for transfers between devices  64.3 us (21%)
  starting transfers between devices  48.8 us (16%)
  local copies, waits for them, and re-layouts  34.9 us (11%)
  between operations  14.9 us (5%)
  other arithmetic  5.78 us (2%)
    ppermute x35, waiting for transfers between devices, swap(): return lax.ppermute(value, 'fsdp', [(i, i ^ bit) for i in range(count)])  46 us
    pallas_call x1, Pallas kernels, scan_backward(): pl.pallas_call(functools.partial(bwd_body, states, subs, h * rows), grid_...  45.7 us
    ppermute x35, starting transfers between devices, swap(): return lax.ppermute(value, 'fsdp', [(i, i ^ bit) for i in range(count)])  29.9 us
    unnamed x170, local copies, waits for them, and re-layouts  22.5 us
    pallas_call x1, Pallas kernels, scan_forward(): pl.pallas_call(functools.partial(fwd_body, states, subs, h * rows, len(pa...  19.6 us
    ppermute x9, starting transfers between devices, ring_parts(): lax.ppermute(part, 'tensor', [(i, (i + step) % count) for i in range(coun...  14 us
    ppermute x9, waiting for transfers between devices, ring_parts(): lax.ppermute(part, 'tensor', [(i, (i + step) % count) for i in range(coun...  13 us
    pallas_call x1, Pallas kernels, front(): pl.pallas_call(functools.partial(front_body, own), grid=(4,), in_specs=[p...  12.4 us
  transfers between devices with their start and end apart: 52, of which 16 were waited for; matrix products, arithmetic and copies ran while one was open for 7% of the time, Pallas kernels for 40%

profile of v4, /device:TPU:8, one launch (start us, length us, event | category | flops | bytes accessed | tf_op | source)
XLA Modules:
  0.0 299.9 jit_solution(18216954319853067412)
XLA Ops:
  8.0 1.3 slice_bitcast_fusion
  9.3 1.6 collective-permute-start.1
  10.9 1.5 collective-permute-start
  13.8 9.2 %collective-permute-done.1 = bf16[128,2048]{1,0:T(8,128)(2,1)S(1)} collective-permute-done((bf16[128,2048]{1,0:T(8,128)(2,1)S(1)}, bf16[128,2048]{1,0:T(8,128)(2,1)S(1)}, u32[]{:S(2)}, u32[]{:S(2)}) %collective-permute-start.1) | collective-permute-done | bytes 524320 | tf_op jit(solution)/shard_map/ppermute | solution.py:803
  23.0 1.2 collective-permute-done
  26.7 1.6 collective-permute-start.12
  29.1 1.9 fusion.8
  30.9 1.6 collective-permute-start.4
  32.5 1.2 collective-permute-start.3
  33.8 1.8 collective-permute-start.2
  39.7 1.6 collective-permute-start.5
  41.3 12.4 %collective-permute-done.7 = bf16[313,128]{1,0:T(8,128)(2,1)S(1)} collective-permute-done((bf16[313,128]{1,0:T(8,128)(2,1)S(1)}, bf16[313,128]{1,0:T(8,128)(2,1)S(1)}, u32[]{:S(2)}, u32[]{:S(2)}) %collective-permute-start.7) | collective-permute-done | bytes 80160 | tf_op jit(solution)/shard_map/ppermute | solution.py:803
  55.1 2.7 collective-permute-done.8
  57.9 1.6 collective-permute-start.18
  61.2 1.6 copy-done.13
  63.7 1.3 copy-done
  65.1 12.4 %front.1 = (f32[512,1024]{1,0:T(8,128)}, f32[512,1024]{1,0:T(8,128)}, bf16[512,1024]{1,0:T(8,128)(2,1)S(1)}, bf16[160,512]{1,0:T(8,128)(2,1)}) custom-call(bf16[512,2048]{1,0:T(8,128)(2,1)} %copy-done, bf16[256,2048]{1,0:T(8,128)(2,1)S(1)} %pad_maximum_fusion.refs_0_, bf16[256,2048]{1,0:T(8,128)(2,1)S(1)} %collective-permute-done.9.refs_1_, ...), custom_call_target="tpu_custom_call" | custom-call | flops 20000000 | bytes 20000 | tf_op jit(solution)/shard_map/front/pallas_call | solution.py:416
  78.4 1.9 constant_dynamic-update-slice_fusion.5.refs_0_
  81.9 1.7 slice.103.refs_4_.wdt_ref
  84.1 2.5 collective-permute-start.16
  86.6 2.5 collective-permute-start.15
  90.6 7.3 %collective-permute-done.16.refs_2_ = bf16[160,512]{1,0:T(8,128)(2,1)S(1)} collective-permute-done((bf16[160,512]{1,0:T(8,128)(2,1)}, bf16[160,512]{1,0:T(8,128)(2,1)S(1)}, u32[]{:S(2)}, u32[]{:S(2)}) %collective-permute-start.16) | collective-permute-done | bytes 163872 | tf_op jit(solution)/shard_map/ppermute | solution.py:871
  97.9 2.6 collective-permute-done.15.refs_1_
  101.2 4.3 %collective-permute-done.19.refs_1_ = bf16[256,2048]{1,0:T(8,128)(2,1)S(1)} collective-permute-done((bf16[256,2048]{1,0:T(8,128)(2,1)}, bf16[256,2048]{1,0:T(8,128)(2,1)S(1)}, u32[]{:S(2)}, u32[]{:S(2)}) %collective-permute-start.19) | collective-permute-done | bytes 1048608 | tf_op jit(solution)/shard_map/ppermute | solution.py:803
  106.2 19.6 %scan_forward.1 = (f32[66560,128]{1,0:T(8,128)}, f32[4096,128]{1,0:T(8,128)}, f32[512,1024]{1,0:T(8,128)}, bf16[512,1024]{1,0:T(8,128)(2,1)}, f32[512,256]{1,0:T(8,128)}, /*index=5*/f32[128,128]{1,0:T(8,128)}) custom-call(s32[512]{0:T(512)} %fusion.2.keep_ref, bf16[160,512]{1,0:T(8,128)(2,1)} %get-tuple-element.102.refs_0_, bf16[160,512]{1,0:T(8,128)(2,1)} %copy-done.76, ...), custom_call_target="tpu_custom_call" | custom-call | flops 40000000000 | bytes 40000000 | tf_op jit(solution)/shard_map/scan_forward/pallas_call | solution.py:142
  126.0 3.0 %all-gather.8.cloned.1.call-done.right_ref.refs_1_ = bf16[512,1024]{1,0:T(8,128)(2,1)} async-done(((bf16[128,1024]{1,0:T(8,128)(2,1)}), bf16[512,1024]{1,0:T(8,128)(2,1)}) %all-gather.8.cloned.1.call-update) | async-done | bytes 1048592 | tf_op jit(solution)/shard_map/all_gather | solution.py:985
  129.0 8.7 %cross.1 = (bf16[512,1024]{1,0:T(8,128)(2,1)}, bf16[512,2048]{1,0:T(8,128)(2,1)}) custom-call(bf16[512,1024]{1,0:T(8,128)(2,1)} %all-gather.4.cloned.1.call-done.left_ref.refs_0_, bf16[512,1024]{1,0:T(8,128)(2,1)} %all-gather.8.cloned.1.call-done.right_ref.refs_1_, bf16[512,1024]{1,0:T(8,128)(2,1)} %get-tuple-element.118.gated_ref.lows_ref, ...), custom_call_target="tpu_custom_call" | custom-call | flops 20000000 | bytes 20000 | tf_op jit(solution)/shard_map/cross/pallas_call | solution.py:591
  139.3 2.6 grad_half.6
  141.9 1.6 grad_half.7
  143.5 45.7 %scan_backward.1 = (f32[512,1024]{1,0:T(8,128)}, bf16[512,1024]{1,0:T(8,128)(2,1)}, bf16[512,1024]{1,0:T(8,128)(2,1)}, bf16[160,512]{1,0:T(8,128)(2,1)}, f32[8,1...) custom-call(s32[512]{0:T(512)} %fusion.2.keep_ref, f32[512,256]{1,0:T(8,128)} %get-tuple-element.119.fwd_ref.mix_ref, ...), custom_call_target="tpu_custom_call" | custom-call | flops 99999997952 | bytes 100000000 | tf_op jit(solution)/shard_map/scan_backward/pallas_call | solution.py:309
  189.8 1.9 collective-permute-start.24
  191.7 1.9 collective-permute-start.23
  193.7 1.2 copy-done.8
  194.9 1.6 grad_half.8
  196.6 1.6 grad_half.9
  198.2 2.1 stage.6
  200.4 1.4 collective-permute-start.27
  201.7 1.5 collective-permute-start.28
  203.2 3.1 %collective-permute-done.23.refs_1_ = bf16[160,512]{1,0:T(8,128)(2,1)S(1)} collective-permute-done((bf16[160,512]{1,0:T(8,128)(2,1)}, bf16[160,512]{1,0:T(8,128)(2,1)S(1)}, u32[]{:S(2)}, u32[]{:S(2)}) %collective-permute-start.23) | collective-permute-done | bytes 163872 | tf_op jit(solution)/shard_map/ppermute | solution.py:871
  206.4 6.0 %turn.1 = (bf16[512,1024]{1,0:T(8,128)(2,1)S(1)}, bf16[160,512]{1,0:T(8,128)(2,1)S(1)}, f32[8,1024]{1,0:T(8,128)}, f32[8,1024]{1,0:T(8,128)S(1)}) custom-call(bf16[160,512]{1,0:T(8,128)(2,1)S(1)} %copy-done.52, bf16[160,512]{1,0:T(8,128)(2,1)S(1)} %collective-permute-done.23.refs_1_, bf16[160,512]{1,0:T(8,128)(2,1)S(1)} %collective-permute-done.24.refs_2_, ...), custom_call_target="tpu_custom_call" | custom-call | flops 40000000000 | bytes 40000000 | tf_op jit(solution)/shard_map/turn/pallas_call | solution.py:502
  213.4 1.7 stage.7
  217.0 1.5 collective-permute-start.29
  218.5 1.5 collective-permute-start.30
  221.6 10.7 %rear.1 = (bf16[512,2048]{1,0:T(8,128)(2,1)}, f32[1,2048]{1,0:T(1,128)}) custom-call(bf16[512,1024]{1,0:T(8,128)(2,1)} %copy-done.9, bf16[512,1024]{1,0:T(8,128)(2,1)} %get-tuple-element.126.lows_ref.gx_ref, bf16[256,2048]{1,0:T(8,128)(2,1)} %copy-done.11, bf16[256,2048]{1,0:T(8,128)(2,1)} %copy-done.16, bf16[256,2048]{1,0:T(8,128)(2,1)} %collective-permute-done.10.refs_2_, ...), custom_call_target="tpu_custom_call" | custom-call | flops 40000000000 | bytes 40000000 | tf_op jit(solution)/shard_map/rear/pallas_call | solution.py:552
  232.5 1.5 copy-done.2
  233.9 2.6 grad_half.10
  236.6 1.8 collective-permute-start.33
  238.4 2.1 collective-permute-start.32
  240.5 1.2 copy-done.21
  245.5 1.6 grad_half.11
  247.2 1.3 copy-done.3
  248.5 1.5 stage.9
  251.7 2.1 stage.10
  254.0 1.6 pack.1
  257.0 1.3 collective-permute-start.40
  258.3 1.4 collective-permute-start.41
  259.8 5.0 %collective-permute-done.36.refs_1_ = bf16[1,128,1024]{2,1,0:T(8,128)(2,1)S(1)} collective-permute-done((bf16[1,128,1024]{2,1,0:T(8,128)(2,1)S(1)}, bf16[1,128,1024]{2,1,0:T(8,128)(2,1)S(1)}, u32[]{:S(2)}, u32[]{:S(2)}) %collective-permute-start.36) | collective-permute-done | bytes 262176 | tf_op jit(solution)/shard_map/ppermute | solution.py:803
  265.4 1.4 collective-permute-start.42
  268.8 1.7 collective-permute-done.40.refs_1_
  271.2 1.4 collective-permute-start.43
  274.5 7.8 %collective-permute-done.39.refs_1_ = bf16[2,128,1024]{2,1,0:T(8,128)(2,1)S(1)} collective-permute-done((bf16[2,128,1024]{2,1,0:T(8,128)(2,1)S(1)}, bf16[2,128,1024]{2,1,0:T(8,128)(2,1)S(1)}, u32[]{:S(2)}, u32[]{:S(2)}) %collective-permute-start.39) | collective-permute-done | bytes 524320 | tf_op jit(solution)/shard_map/ppermute | solution.py:803
  282.7 1.4 collective-permute-done.38
  284.1 1.4 collective-permute-start.45
  289.8 2.5 last.1
  (303 shorter events, 44.0 us)
Async XLA Ops:
  7.2 53.9 %all-gather.6.cloned.1.call-start = ((), (), s32[]{:S(2)}) async-start(), calls=%async_computation.3 | async-start | bytes 2621440 | tf_op jit(solution)/shard_map/all_gather | solution.py:914
  7.9 118.0 %all-gather.4.cloned.1.call-start = ((), (), s32[]{:S(2)}) async-start(), calls=%async_computation.2 | async-start | bytes 1310720 | tf_op jit(solution)/shard_map/all_gather | solution.py:955
  9.3 13.7 %copy-start.55 = (bf16[128,2048]{1,0:T(8,128)(2,1)}, bf16[128,2048]{1,0:T(8,128)(2,1)S(1)}, u32[]{:S(2)}) copy-start(bf16[128,2048]{1,0:T(8,128)(2,1)S(1)} %get-tuple-element.216) | copy-start | bytes 1572868
  9.3 13.7 %collective-permute-start.1 = (bf16[128,2048]{1,0:T(8,128)(2,1)S(1)}, bf16[128,2048]{1,0:T(8,128)(2,1)S(1)}, u32[]{:S(2)}, u32[]{:S(2)}) collective-permute-start(bf16[128,2048]{1,0:T(8,128)(2,1)S(1)} %get-tuple-element.216), channel_id=1, source_target_pairs={{0,16},{4,20},{8,24},{12,28},{16,0},{20,4},{24,8},{28,12},{1,17},{... | collective-permute-start | bytes 1572872 | tf_op jit(solution)/shard_map/ppermute | solution.py:803
  10.9 13.4 %collective-permute-start = (bf16[128,2048]{1,0:T(8,128)(2,1)S(1)}, bf16[128,2048]{1,0:T(8,128)(2,1)S(1)}, u32[]{:S(2)}, u32[]{:S(2)}) collective-permute-start(bf16[128,2048]{1,0:T(8,128)(2,1)S(1)} %get-tuple-element.217), channel_id=1, source_target_pairs={{0,8},{4,12},{8,0},{12,4},{16,24},{20,28},{24,16},{28,20},{1,9},{5... | collective-permute-start | bytes 1572872 | tf_op jit(solution)/shard_map/ppermute | solution.py:803
  13.1 47.0 %copy-start.68 = (pred[8,8]{1,0:T(8,128)(4,1)}, pred[8,8]{1,0:T(8,128)(4,1)S(1)}, u32[]{:S(2)}) copy-start(pred[8,8]{1,0:T(8,128)(4,1)S(1)} %iota_compare_fusion.1) | copy-start | bytes 196
  13.8 15.1 %copy-start.65 = (bf16[128,128]{1,0:T(8,128)(2,1)S(1)}, bf16[128,128]{1,0:T(8,128)(2,1)}, u32[]{:S(2)}) copy-start(bf16[128,128]{1,0:T(8,128)(2,1)} %param.24) | copy-start | bytes 98308
  24.4 40.7 %copy-start.11 = (bf16[256,2048]{1,0:T(8,128)(2,1)}, bf16[256,2048]{1,0:T(8,128)(2,1)S(1)}, u32[]{:S(2)}) copy-start(bf16[256,2048]{1,0:T(8,128)(2,1)S(1)} %pad_maximum_fusion.refs_0_) | copy-start | bytes 3145732
  24.4 13.1 %copy-start.64 = (bf16[128,160]{0,1:T(8,128)(2,1)S(1)}, bf16[128,160]{0,1:T(8,128)(2,1)}, u32[]{:S(2)}) copy-start(bf16[128,160]{0,1:T(8,128)(2,1)} %param.23) | copy-start | bytes 122884
  24.4 13.1 %copy-start.67 = (bf16[128,16]{0,1:T(8,128)(2,1)S(1)}, bf16[128,16]{0,1:T(8,128)(2,1)}, u32[]{:S(2)}) copy-start(bf16[128,16]{0,1:T(8,128)(2,1)} %param.26) | copy-start | bytes 12292
  24.5 30.0 %collective-permute-start.9 = (bf16[256,2048]{1,0:T(8,128)(2,1)S(1)}, bf16[256,2048]{1,0:T(8,128)(2,1)S(1)}, u32[]{:S(2)}, u32[]{:S(2)}) collective-permute-start(bf16[256,2048]{1,0:T(8,128)(2,1)S(1)} %pad_maximum_fusion.refs_0_), channel_id=1, source_target_pairs={{0,16},{4,20},{8,24},{12,28},{16,0},{20,4},{24,8},{28,12},{1,17},{... | collective-permute-start | bytes 3145736 | tf_op jit(solution)/shard_map/ppermute | solution.py:803
  26.7 38.3 %copy-start.12 = (bf16[256,2048]{1,0:T(8,128)(2,1)}, bf16[256,2048]{1,0:T(8,128)(2,1)S(1)}, u32[]{:S(2)}) copy-start(bf16[256,2048]{1,0:T(8,128)(2,1)S(1)} %pad_maximum_fusion.1.refs_4_) | copy-start | bytes 3145732
  26.7 28.3 %collective-permute-start.12 = (bf16[256,2048]{1,0:T(8,128)(2,1)S(1)}, bf16[256,2048]{1,0:T(8,128)(2,1)}, u32[]{:S(2)}, u32[]{:S(2)}) collective-permute-start(bf16[256,2048]{1,0:T(8,128)(2,1)S(1)} %pad_maximum_fusion.1.refs_4_), channel_id=1, source_target_pairs={{0,8},{4,12},{8,0},{12,4},{16,24},{20,28},{24,16},{28,20},{1,9},{5... | collective-permute-start | bytes 3145736 | tf_op jit(solution)/shard_map/ppermute | solution.py:803
  30.9 4.8 %collective-permute-start.4 = (bf16[1,64]{1,0:T(2,128)(2,1)S(1)}, bf16[1,64]{1,0:T(2,128)(2,1)S(1)}, u32[]{:S(2)}, u32[]{:S(2)}) collective-permute-start(bf16[1,64]{1,0:T(2,128)(2,1)S(1)} %bitcast.77), channel_id=1, source_target_pairs={{0,1},{1,2},{2,3},{3,0},{4,5},{5,6},{6,7},{7,4},{8,9},{9,10},{10,1... | collective-permute-start | bytes 392 | tf_op jit(solution)/shard_map/ppermute | solution.py:931
  32.5 4.4 %collective-permute-start.3 = (bf16[1,64]{1,0:T(2,128)(2,1)S(1)}, bf16[1,64]{1,0:T(2,128)(2,1)S(1)}, u32[]{:S(2)}, u32[]{:S(2)}) collective-permute-start(bf16[1,64]{1,0:T(2,128)(2,1)S(1)} %bitcast.78), channel_id=1, source_target_pairs={{0,2},{1,3},{2,0},{3,1},{4,6},{5,7},{6,4},{7,5},{8,10},{9,11},{10,... | collective-permute-start | bytes 392 | tf_op jit(solution)/shard_map/ppermute | solution.py:931
  33.8 3.7 %collective-permute-start.2 = (bf16[1,64]{1,0:T(2,128)(2,1)S(1)}, bf16[1,64]{1,0:T(2,128)(2,1)S(1)}, u32[]{:S(2)}, u32[]{:S(2)}) collective-permute-start(bf16[1,64]{1,0:T(2,128)(2,1)S(1)} %bitcast.79), channel_id=1, source_target_pairs={{0,3},{1,0},{2,1},{3,2},{4,7},{5,4},{6,5},{7,6},{8,11},{9,8},{10,9... | collective-permute-start | bytes 392 | tf_op jit(solution)/shard_map/ppermute | solution.py:931
  35.7 93.3 %all-gather.8.cloned.1.call-start = ((), (), s32[]{:S(2)}) async-start(), calls=%async_computation.4 | async-start | bytes 1310720 | tf_op jit(solution)/shard_map/all_gather | solution.py:985
  37.7 22.5 %copy-start.62 = (bf16[128,2048]{1,0:T(8,128)(2,1)S(1)}, bf16[128,2048]{1,0:T(8,128)(2,1)}, u32[]{:S(2)}) copy-start(bf16[128,2048]{1,0:T(8,128)(2,1)} %param.28) | copy-start | bytes 1572868
  37.8 16.0 %collective-permute-start.7 = (bf16[313,128]{1,0:T(8,128)(2,1)S(1)}, bf16[313,128]{1,0:T(8,128)(2,1)S(1)}, u32[]{:S(2)}, u32[]{:S(2)}) collective-permute-start(bf16[313,128]{1,0:T(8,128)(2,1)S(1)} %concatenate.22), channel_id=1, source_target_pairs={{0,24},{4,28},{8,16},{12,20},{16,8},{20,12},{24,0},{28,4},{1,25},{... | collective-permute-start | bytes 240392 | tf_op jit(solution)/shard_map/ppermute | solution.py:803
  38.6 15.1 %collective-permute-start.6 = (bf16[313,128]{1,0:T(8,128)(2,1)S(1)}, bf16[313,128]{1,0:T(8,128)(2,1)S(1)}, u32[]{:S(2)}, u32[]{:S(2)}) collective-permute-start(bf16[313,128]{1,0:T(8,128)(2,1)S(1)} %concatenate.22), channel_id=1, source_target_pairs={{0,16},{4,20},{8,24},{12,28},{16,0},{20,4},{24,8},{28,12},{1,17},{... | collective-permute-start | bytes 240392 | tf_op jit(solution)/shard_map/ppermute | solution.py:803
  39.7 14.5 %collective-permute-start.5 = (bf16[313,128]{1,0:T(8,128)(2,1)S(1)}, bf16[313,128]{1,0:T(8,128)(2,1)S(1)}, u32[]{:S(2)}, u32[]{:S(2)}) collective-permute-start(bf16[313,128]{1,0:T(8,128)(2,1)S(1)} %concatenate.22), channel_id=1, source_target_pairs={{0,8},{4,12},{8,0},{12,4},{16,24},{20,28},{24,16},{28,20},{1,9},{5... | collective-permute-start | bytes 240392 | tf_op jit(solution)/shard_map/ppermute | solution.py:803
  53.7 11.3 %collective-permute-start.10 = (bf16[256,2048]{1,0:T(8,128)(2,1)S(1)}, bf16[256,2048]{1,0:T(8,128)(2,1)}, u32[]{:S(2)}, u32[]{:S(2)}) collective-permute-start(bf16[256,2048]{1,0:T(8,128)(2,1)S(1)} %pad_maximum_fusion.refs_0_), channel_id=1, source_target_pairs={{0,4},{4,0},{8,12},{12,8},{16,20},{20,16},{24,28},{28,24},{1,5},{5... | collective-permute-start | bytes 3145736 | tf_op jit(solution)/shard_map/ppermute | solution.py:803
  53.7 11.3 %collective-permute-start.13 = (bf16[256,2048]{1,0:T(8,128)(2,1)S(1)}, bf16[256,2048]{1,0:T(8,128)(2,1)}, u32[]{:S(2)}, u32[]{:S(2)}) collective-permute-start(bf16[256,2048]{1,0:T(8,128)(2,1)S(1)} %pad_maximum_fusion.1.refs_4_), channel_id=1, source_target_pairs={{0,4},{4,0},{8,12},{12,8},{16,20},{20,16},{24,28},{28,24},{1,5},{5... | collective-permute-start | bytes 3145736 | tf_op jit(solution)/shard_map/ppermute | solution.py:803
  54.3 3.5 %collective-permute-start.8 = (bf16[313,512]{1,0:T(8,128)(2,1)S(1)}, bf16[313,512]{1,0:T(8,128)(2,1)S(1)}, u32[]{:S(2)}, u32[]{:S(2)}) collective-permute-start(bf16[313,512]{1,0:T(8,128)(2,1)S(1)} %pad_maximum_fusion.2), channel_id=1, source_target_pairs={{0,4},{4,0},{8,12},{12,8},{16,20},{20,16},{24,28},{28,24},{1,5},{5... | collective-permute-start | bytes 961544 | tf_op jit(solution)/shard_map/ppermute | solution.py:803
  54.5 10.5 %collective-permute-start.11 = (bf16[256,2048]{1,0:T(8,128)(2,1)S(1)}, bf16[256,2048]{1,0:T(8,128)(2,1)}, u32[]{:S(2)}, u32[]{:S(2)}) collective-permute-start(bf16[256,2048]{1,0:T(8,128)(2,1)S(1)} %collective-permute-done.9.refs_1_), channel_id=1, source_target_pairs={{0,4},{4,0},{8,12},{12,8},{16,20},{20,16},{24,28},{28,24},{1,5},{5... | collective-permute-start | bytes 3145736 | tf_op jit(solution)/shard_map/ppermute | solution.py:803
  55.1 10.0 %collective-permute-start.14 = (bf16[256,2048]{1,0:T(8,128)(2,1)}, bf16[256,2048]{1,0:T(8,128)(2,1)}, u32[]{:S(2)}, u32[]{:S(2)}) collective-permute-start(bf16[256,2048]{1,0:T(8,128)(2,1)} %collective-permute-done.12.refs_5_), channel_id=1, source_target_pairs={{0,4},{4,0},{8,12},{12,8},{16,20},{20,16},{24,28},{28,24},{1,5},{5... | collective-permute-start | bytes 3145736 | tf_op jit(solution)/shard_map/ppermute | solution.py:803
  57.9 20.5 %collective-permute-start.18 = (bf16[128,2048]{1,0:T(8,128)(2,1)}, bf16[128,2048]{1,0:T(8,128)(2,1)}, u32[]{:S(2)}, u32[]{:S(2)}) collective-permute-start(bf16[128,2048]{1,0:T(8,128)(2,1)} %param.28), channel_id=1, source_target_pairs={{0,8},{4,12},{8,0},{12,4},{16,24},{20,28},{24,16},{28,20},{1,9},{5... | collective-permute-start | bytes 1572872 | tf_op jit(solution)/shard_map/ppermute | solution.py:803
  60.2 176.3 %copy-start.40 = (f32[8,2,128]{2,1,0:T(2,128)}, f32[8,2,128]{2,1,0:T(2,128)S(1)}, u32[]{:S(2)}) copy-start(f32[8,2,128]{2,1,0:T(2,128)S(1)} %select_reduce_fusion) | copy-start | bytes 24580
  80.3 25.2 %collective-permute-start.19 = (bf16[256,2048]{1,0:T(8,128)(2,1)}, bf16[256,2048]{1,0:T(8,128)(2,1)S(1)}, u32[]{:S(2)}, u32[]{:S(2)}) collective-permute-start(bf16[256,2048]{1,0:T(8,128)(2,1)} %constant_dynamic-update-slice_fusion.5.refs_0_), channel_id=1, source_target_pairs={{0,16},{4,20},{8,24},{12,28},{16,0},{20,4},{24,8},{28,12},{1,17},{... | collective-permute-start | bytes 3145736 | tf_op jit(solution)/shard_map/ppermute | solution.py:803
  83.6 7.0 %collective-permute-start.17 = (bf16[160,512]{1,0:T(8,128)(2,1)}, bf16[160,512]{1,0:T(8,128)(2,1)S(1)}, u32[]{:S(2)}, u32[]{:S(2)}) collective-permute-start(bf16[160,512]{1,0:T(8,128)(2,1)} %get-tuple-element.102.refs_0_), channel_id=1, source_target_pairs={{0,3},{1,0},{2,1},{3,2},{4,7},{5,4},{6,5},{7,6},{8,11},{9,8},{10,9... | collective-permute-start | bytes 491528 | tf_op jit(solution)/shard_map/ppermute | solution.py:871
  84.1 13.8 %collective-permute-start.16 = (bf16[160,512]{1,0:T(8,128)(2,1)}, bf16[160,512]{1,0:T(8,128)(2,1)S(1)}, u32[]{:S(2)}, u32[]{:S(2)}) collective-permute-start(bf16[160,512]{1,0:T(8,128)(2,1)} %get-tuple-element.102.refs_0_), channel_id=1, source_target_pairs={{0,2},{1,3},{2,0},{3,1},{4,6},{5,7},{6,4},{7,5},{8,10},{9,11},{10,... | collective-permute-start | bytes 491528 | tf_op jit(solution)/shard_map/ppermute | solution.py:871
  86.6 13.8 %collective-permute-start.15 = (bf16[160,512]{1,0:T(8,128)(2,1)}, bf16[160,512]{1,0:T(8,128)(2,1)S(1)}, u32[]{:S(2)}, u32[]{:S(2)}) collective-permute-start(bf16[160,512]{1,0:T(8,128)(2,1)} %get-tuple-element.102.refs_0_), channel_id=1, source_target_pairs={{0,1},{1,2},{2,3},{3,0},{4,5},{5,6},{6,7},{7,4},{8,9},{9,10},{10,1... | collective-permute-start | bytes 491528 | tf_op jit(solution)/shard_map/ppermute | solution.py:871
  90.6 15.6 %copy-start.74 = (bf16[160,512]{1,0:T(8,128)(2,1)}, bf16[160,512]{1,0:T(8,128)(2,1)S(1)}, u32[]{:S(2)}) copy-start(bf16[160,512]{1,0:T(8,128)(2,1)S(1)} %collective-permute-done.17.refs_3_) | copy-start | bytes 491524
  101.1 24.8 %collective-permute-start.20 = (bf16[256,2048]{1,0:T(8,128)(2,1)}, bf16[256,2048]{1,0:T(8,128)(2,1)S(1)}, u32[]{:S(2)}, u32[]{:S(2)}) collective-permute-start(bf16[256,2048]{1,0:T(8,128)(2,1)} %constant_dynamic-update-slice_fusion.5.refs_0_), channel_id=1, source_target_pairs={{0,4},{4,0},{8,12},{12,8},{16,20},{20,16},{24,28},{28,24},{1,5},{5... | collective-permute-start | bytes 3145736 | tf_op jit(solution)/shard_map/ppermute | solution.py:803
  101.1 120.5 %reduce-scatter.3.cloned.1.call-start = ((), (), s32[]{:S(2)}) async-start(), calls=%async_computation.5 | async-start | bytes 2621440 | tf_op jit(solution)/shard_map/reduce_scatter | solution.py:994
  105.5 20.4 %copy-start.57 = (bf16[256,2048]{1,0:T(8,128)(2,1)}, bf16[256,2048]{1,0:T(8,128)(2,1)S(1)}, u32[]{:S(2)}) copy-start(bf16[256,2048]{1,0:T(8,128)(2,1)S(1)} %collective-permute-done.19.refs_1_) | copy-start | bytes 3145732
  105.5 20.4 %collective-permute-start.21 = (bf16[256,2048]{1,0:T(8,128)(2,1)S(1)}, bf16[256,2048]{1,0:T(8,128)(2,1)S(1)}, u32[]{:S(2)}, u32[]{:S(2)}) collective-permute-start(bf16[256,2048]{1,0:T(8,128)(2,1)S(1)} %collective-permute-done.19.refs_1_), channel_id=1, source_target_pairs={{0,4},{4,0},{8,12},{12,8},{16,20},{20,16},{24,28},{28,24},{1,5},{5... | collective-permute-start | bytes 3145736 | tf_op jit(solution)/shard_map/ppermute | solution.py:803
  137.8 152.0 %reduce-scatter.5.cloned.1.call-start = ((), (), s32[]{:S(2)}) async-start(), calls=%async_computation.6 | async-start | bytes 2621440 | tf_op jit(solution)/shard_map/reduce_scatter | solution.py:1017
  141.8 56.3 %collective-permute-start.22 = (bf16[512,2048]{1,0:T(8,128)(2,1)}, bf16[512,2048]{1,0:T(8,128)(2,1)}, u32[]{:S(2)}, u32[]{:S(2)}) collective-permute-start(bf16[512,2048]{1,0:T(8,128)(2,1)} %grad_half.6), channel_id=1, source_target_pairs={{0,4},{4,0},{8,12},{12,8},{16,20},{20,16},{24,28},{28,24},{1,5},{5... | collective-permute-start | bytes 6291464 | tf_op jit(solution)/shard_map/ppermute | solution.py:803
  143.5 50.2 %copy-start.1 = (bf16[512,2048]{1,0:T(8,128)(2,1)S(1)}, bf16[512,2048]{1,0:T(8,128)(2,1)}, u32[]{:S(2)}) copy-start(bf16[512,2048]{1,0:T(8,128)(2,1)} %copy-done) | copy-start | bytes 6291460
  189.2 12.5 %collective-permute-start.25 = (bf16[160,512]{1,0:T(8,128)(2,1)}, bf16[160,512]{1,0:T(8,128)(2,1)S(1)}, u32[]{:S(2)}, u32[]{:S(2)}) collective-permute-start(bf16[160,512]{1,0:T(8,128)(2,1)} %get-tuple-element.130.refs_0_), channel_id=1, source_target_pairs={{0,3},{1,0},{2,1},{3,2},{4,7},{5,4},{6,5},{7,6},{8,11},{9,8},{10,9... | collective-permute-start | bytes 491528 | tf_op jit(solution)/shard_map/ppermute | solution.py:871
  189.8 13.4 %collective-permute-start.24 = (bf16[160,512]{1,0:T(8,128)(2,1)}, bf16[160,512]{1,0:T(8,128)(2,1)S(1)}, u32[]{:S(2)}, u32[]{:S(2)}) collective-permute-start(bf16[160,512]{1,0:T(8,128)(2,1)} %get-tuple-element.130.refs_0_), channel_id=1, source_target_pairs={{0,2},{1,3},{2,0},{3,1},{4,6},{5,7},{6,4},{7,5},{8,10},{9,11},{10,... | collective-permute-start | bytes 491528 | tf_op jit(solution)/shard_map/ppermute | solution.py:871
  191.7 14.6 %collective-permute-start.23 = (bf16[160,512]{1,0:T(8,128)(2,1)}, bf16[160,512]{1,0:T(8,128)(2,1)S(1)}, u32[]{:S(2)}, u32[]{:S(2)}) collective-permute-start(bf16[160,512]{1,0:T(8,128)(2,1)} %get-tuple-element.130.refs_0_), channel_id=1, source_target_pairs={{0,1},{1,2},{2,3},{3,0},{4,5},{5,6},{6,7},{7,4},{8,9},{9,10},{10,1... | collective-permute-start | bytes 491528 | tf_op jit(solution)/shard_map/ppermute | solution.py:871
  196.5 16.9 %collective-permute-start.26 = (bf16[512,2048]{1,0:T(8,128)(2,1)S(1)}, bf16[512,2048]{1,0:T(8,128)(2,1)S(1)}, u32[]{:S(2)}, u32[]{:S(2)}) collective-permute-start(bf16[512,2048]{1,0:T(8,128)(2,1)S(1)} %grad_half.8), channel_id=1, source_target_pairs={{0,4},{4,0},{8,12},{12,8},{16,20},{20,16},{24,28},{28,24},{1,5},{5... | collective-permute-start | bytes 6291464 | tf_op jit(solution)/shard_map/ppermute | solution.py:803
  200.4 19.6 %collective-permute-start.27 = (bf16[2,128,1024]{2,1,0:T(8,128)(2,1)S(1)}, bf16[2,128,1024]{2,1,0:T(8,128)(2,1)S(1)}, u32[]{:S(2)}, u32[]{:S(2)}) collective-permute-start(bf16[2,128,1024]{2,1,0:T(8,128)(2,1)S(1)} %get-tuple-element.128), channel_id=1, source_target_pairs={{0,8},{4,12},{8,0},{12,4},{16,24},{20,28},{24,16},{28,20},{1,9},{5... | collective-permute-start | bytes 1572872 | tf_op jit(solution)/shard_map/ppermute | solution.py:803
  201.7 19.1 %collective-permute-start.28 = (bf16[2,128,1024]{2,1,0:T(8,128)(2,1)S(1)}, bf16[2,128,1024]{2,1,0:T(8,128)(2,1)S(1)}, u32[]{:S(2)}, u32[]{:S(2)}) collective-permute-start(bf16[2,128,1024]{2,1,0:T(8,128)(2,1)S(1)} %get-tuple-element.129), channel_id=1, source_target_pairs={{0,16},{4,20},{8,24},{12,28},{16,0},{20,4},{24,8},{28,12},{1,17},{... | collective-permute-start | bytes 1572872 | tf_op jit(solution)/shard_map/ppermute | solution.py:803
  217.0 15.3 %collective-permute-start.29 = (bf16[2,128,1024]{2,1,0:T(8,128)(2,1)}, bf16[2,128,1024]{2,1,0:T(8,128)(2,1)}, u32[]{:S(2)}, u32[]{:S(2)}) collective-permute-start(bf16[2,128,1024]{2,1,0:T(8,128)(2,1)} %get-tuple-element.136), channel_id=1, source_target_pairs={{0,8},{4,12},{8,0},{12,4},{16,24},{20,28},{24,16},{28,20},{1,9},{5... | collective-permute-start | bytes 1572872 | tf_op jit(solution)/shard_map/ppermute | solution.py:803
  218.5 13.9 %collective-permute-start.30 = (bf16[2,128,1024]{2,1,0:T(8,128)(2,1)}, bf16[2,128,1024]{2,1,0:T(8,128)(2,1)}, u32[]{:S(2)}, u32[]{:S(2)}) collective-permute-start(bf16[2,128,1024]{2,1,0:T(8,128)(2,1)} %get-tuple-element.137), channel_id=1, source_target_pairs={{0,16},{4,20},{8,24},{12,28},{16,0},{20,4},{24,8},{28,12},{1,17},{... | collective-permute-start | bytes 1572872 | tf_op jit(solution)/shard_map/ppermute | solution.py:803
  236.5 15.1 %collective-permute-start.34 = (bf16[512,2048]{1,0:T(8,128)(2,1)}, bf16[512,2048]{1,0:T(8,128)(2,1)}, u32[]{:S(2)}, u32[]{:S(2)}) collective-permute-start(bf16[512,2048]{1,0:T(8,128)(2,1)} %grad_half.10), channel_id=1, source_target_pairs={{0,4},{4,0},{8,12},{12,8},{16,20},{20,16},{24,28},{28,24},{1,5},{5... | collective-permute-start | bytes 6291464 | tf_op jit(solution)/shard_map/ppermute | solution.py:803
  236.6 14.8 %collective-permute-start.33 = (bf16[1,2048]{1,0:T(2,128)(2,1)S(1)}, bf16[1,2048]{1,0:T(2,128)(2,1)S(1)}, u32[]{:S(2)}, u32[]{:S(2)}) collective-permute-start(bf16[1,2048]{1,0:T(2,128)(2,1)S(1)} %divide_convert_fusion), channel_id=1, source_target_pairs={{0,3},{1,0},{2,1},{3,2},{4,7},{5,4},{6,5},{7,6},{8,11},{9,8},{10,9... | collective-permute-start | bytes 12296 | tf_op jit(solution)/shard_map/ppermute | solution.py:871
  238.4 13.0 %collective-permute-start.32 = (bf16[1,2048]{1,0:T(2,128)(2,1)S(1)}, bf16[1,2048]{1,0:T(2,128)(2,1)S(1)}, u32[]{:S(2)}, u32[]{:S(2)}) collective-permute-start(bf16[1,2048]{1,0:T(2,128)(2,1)S(1)} %divide_convert_fusion), channel_id=1, source_target_pairs={{0,2},{1,3},{2,0},{3,1},{4,6},{5,7},{6,4},{7,5},{8,10},{9,11},{10,... | collective-permute-start | bytes 12296 | tf_op jit(solution)/shard_map/ppermute | solution.py:871
  240.4 10.9 %collective-permute-start.31 = (bf16[1,2048]{1,0:T(2,128)(2,1)S(1)}, bf16[1,2048]{1,0:T(2,128)(2,1)S(1)}, u32[]{:S(2)}, u32[]{:S(2)}) collective-permute-start(bf16[1,2048]{1,0:T(2,128)(2,1)S(1)} %divide_convert_fusion), channel_id=1, source_target_pairs={{0,1},{1,2},{2,3},{3,0},{4,5},{5,6},{6,7},{7,4},{8,9},{9,10},{10,1... | collective-permute-start | bytes 12296 | tf_op jit(solution)/shard_map/ppermute | solution.py:871
  255.6 12.4 %collective-permute-start.35 = (bf16[328,512]{1,0:T(8,128)(2,1)S(1)}, bf16[328,512]{1,0:T(8,128)(2,1)S(1)}, u32[]{:S(2)}, u32[]{:S(2)}) collective-permute-start(bf16[328,512]{1,0:T(8,128)(2,1)S(1)} %get-tuple-element.163), channel_id=1, source_target_pairs={{0,4},{4,0},{8,12},{12,8},{16,20},{20,16},{24,28},{28,24},{1,5},{5... | collective-permute-start | bytes 1007624 | tf_op jit(solution)/shard_map/ppermute | solution.py:803
  255.7 9.2 %collective-permute-start.36 = (bf16[1,128,1024]{2,1,0:T(8,128)(2,1)S(1)}, bf16[1,128,1024]{2,1,0:T(8,128)(2,1)S(1)}, u32[]{:S(2)}, u32[]{:S(2)}) collective-permute-start(bf16[1,128,1024]{2,1,0:T(8,128)(2,1)S(1)} %copy-done.51), channel_id=1, source_target_pairs={{0,16},{4,20},{8,24},{12,28},{16,0},{20,4},{24,8},{28,12},{1,17},{... | collective-permute-start | bytes 786440 | tf_op jit(solution)/shard_map/ppermute | solution.py:803
  256.3 9.1 %collective-permute-start.37 = (bf16[1,128,1024]{2,1,0:T(8,128)(2,1)S(1)}, bf16[1,128,1024]{2,1,0:T(8,128)(2,1)S(1)}, u32[]{:S(2)}, u32[]{:S(2)}) collective-permute-start(bf16[1,128,1024]{2,1,0:T(8,128)(2,1)S(1)} %copy-done.49), channel_id=1, source_target_pairs={{0,8},{4,12},{8,0},{12,4},{16,24},{20,28},{24,16},{28,20},{1,9},{5... | collective-permute-start | bytes 786440 | tf_op jit(solution)/shard_map/ppermute | solution.py:803
  257.0 13.5 %collective-permute-start.40 = (bf16[1,128,1024]{2,1,0:T(8,128)(2,1)S(1)}, bf16[1,128,1024]{2,1,0:T(8,128)(2,1)S(1)}, u32[]{:S(2)}, u32[]{:S(2)}) collective-permute-start(bf16[1,128,1024]{2,1,0:T(8,128)(2,1)S(1)} %copy-done.47), channel_id=1, source_target_pairs={{0,16},{4,20},{8,24},{12,28},{16,0},{20,4},{24,8},{28,12},{1,17},{... | collective-permute-start | bytes 786440 | tf_op jit(solution)/shard_map/ppermute | solution.py:803
  258.3 12.8 %collective-permute-start.41 = (bf16[1,128,1024]{2,1,0:T(8,128)(2,1)S(1)}, bf16[1,128,1024]{2,1,0:T(8,128)(2,1)S(1)}, u32[]{:S(2)}, u32[]{:S(2)}) collective-permute-start(bf16[1,128,1024]{2,1,0:T(8,128)(2,1)S(1)} %copy-done.45), channel_id=1, source_target_pairs={{0,8},{4,12},{8,0},{12,4},{16,24},{20,28},{24,16},{28,20},{1,9},{5... | collective-permute-start | bytes 786440 | tf_op jit(solution)/shard_map/ppermute | solution.py:803
  264.8 17.5 %collective-permute-start.39 = (bf16[2,128,1024]{2,1,0:T(8,128)(2,1)S(1)}, bf16[2,128,1024]{2,1,0:T(8,128)(2,1)S(1)}, u32[]{:S(2)}, u32[]{:S(2)}) collective-permute-start(bf16[2,128,1024]{2,1,0:T(8,128)(2,1)S(1)} %get-tuple-element.159), channel_id=1, source_target_pairs={{0,8},{4,12},{8,0},{12,4},{16,24},{20,28},{24,16},{28,20},{1,9},{5... | collective-permute-start | bytes 1572872 | tf_op jit(solution)/shard_map/ppermute | solution.py:803
  265.4 16.9 %collective-permute-start.42 = (bf16[2,128,1024]{2,1,0:T(8,128)(2,1)S(1)}, bf16[2,128,1024]{2,1,0:T(8,128)(2,1)S(1)}, u32[]{:S(2)}, u32[]{:S(2)}) collective-permute-start(bf16[2,128,1024]{2,1,0:T(8,128)(2,1)S(1)} %get-tuple-element.160), channel_id=1, source_target_pairs={{0,16},{4,20},{8,24},{12,28},{16,0},{20,4},{24,8},{28,12},{1,17},{... | collective-permute-start | bytes 1572872 | tf_op jit(solution)/shard_map/ppermute | solution.py:803
  268.1 16.0 %collective-permute-start.38 = (bf16[328,128]{1,0:T(8,128)(2,1)S(1)}, bf16[328,128]{1,0:T(8,128)(2,1)S(1)}, u32[]{:S(2)}, u32[]{:S(2)}) collective-permute-start(bf16[328,128]{1,0:T(8,128)(2,1)S(1)} %get-tuple-element.225), channel_id=1, source_target_pairs={{0,8},{4,12},{8,0},{12,4},{16,24},{20,28},{24,16},{28,20},{1,9},{5... | collective-permute-start | bytes 251912 | tf_op jit(solution)/shard_map/ppermute | solution.py:803
  270.4 15.7 %collective-permute-start.44 = (bf16[328,128]{1,0:T(8,128)(2,1)S(1)}, bf16[328,128]{1,0:T(8,128)(2,1)S(1)}, u32[]{:S(2)}, u32[]{:S(2)}) collective-permute-start(bf16[328,128]{1,0:T(8,128)(2,1)S(1)} %get-tuple-element.226), channel_id=1, source_target_pairs={{0,24},{4,28},{8,16},{12,20},{16,8},{20,12},{24,0},{28,4},{1,25},{... | collective-permute-start | bytes 251912 | tf_op jit(solution)/shard_map/ppermute | solution.py:803
  271.2 15.0 %collective-permute-start.43 = (bf16[328,128]{1,0:T(8,128)(2,1)S(1)}, bf16[328,128]{1,0:T(8,128)(2,1)S(1)}, u32[]{:S(2)}, u32[]{:S(2)}) collective-permute-start(bf16[328,128]{1,0:T(8,128)(2,1)S(1)} %get-tuple-element.227), channel_id=1, source_target_pairs={{0,16},{4,20},{8,24},{12,28},{16,0},{20,4},{24,8},{28,12},{1,17},{... | collective-permute-start | bytes 251912 | tf_op jit(solution)/shard_map/ppermute | solution.py:803
  284.1 8.2 %collective-permute-start.45 = (bf16[1,128,1024]{2,1,0:T(8,128)(2,1)S(1)}, bf16[1,128,1024]{2,1,0:T(8,128)(2,1)S(1)}, u32[]{:S(2)}, u32[]{:S(2)}) collective-permute-start(bf16[1,128,1024]{2,1,0:T(8,128)(2,1)S(1)} %get-tuple-element.176), channel_id=1, source_target_pairs={{0,16},{4,20},{8,24},{12,28},{16,0},{20,4},{24,8},{28,12},{1,17},{... | collective-permute-start | bytes 786440 | tf_op jit(solution)/shard_map/ppermute | solution.py:803
  285.5 6.7 %collective-permute-start.46 = (bf16[1,128,1024]{2,1,0:T(8,128)(2,1)S(1)}, bf16[1,128,1024]{2,1,0:T(8,128)(2,1)S(1)}, u32[]{:S(2)}, u32[]{:S(2)}) collective-permute-start(bf16[1,128,1024]{2,1,0:T(8,128)(2,1)S(1)} %get-tuple-element.179), channel_id=1, source_target_pairs={{0,8},{4,12},{8,0},{12,4},{16,24},{20,28},{24,16},{28,20},{1,9},{5... | collective-permute-start | bytes 786440 | tf_op jit(solution)/shard_map/ppermute | solution.py:803
  (69 other events, 303.3 us)
Sparse Core Ops, SparseCore 0:
  9.6 45.5 all-gather.5
  56.7 28.2 all-gather.3
  101.3 27.7 all-gather.7
  137.9 41.1 reduce-scatter.2
  232.6 43.3 reduce-scatter.4

commit v5 on v4

--- a/solution.py
+++ b/solution.py
@@ -562,43 +562,50 @@
     )(g_signal, g_gate, *weights, normed)
 
 
-def cross_body(left_ref, right_ref, gated_ref, *refs):
-    quarters, (gg_ref, out_ref) = refs[:4], refs[4:]
-    chunk = quarters[0].shape[0]
+def quarters_of(pieces):
+    each = len(pieces) // 4
+    for q in range(4):
+        yield jnp.concatenate([piece[...] for piece in pieces[q * each : (q + 1) * each]], axis=0)
+
+
+def branch_body(gated_ref, *refs):
+    total, at = None, 0
+    for w in quarters_of(refs[:-1]):
+        part = jnp.dot(gated_ref[:, pl.ds(at, w.shape[0])], w, preferred_element_type=f32)
+        total = part if total is None else total + part
+        at += w.shape[0]
+    refs[-1][...] = total.astype(bf16)
+
+
+def cross_body(left_ref, right_ref, *refs):
     half = left_ref.shape[1]
     dims = (((1,), (1,)), ((), ()))
-    total = None
-    for q in range(4):
-        w = quarters[q][...]
-        cut = pl.ds(q * chunk, chunk)
+    at = 0
+    for w in quarters_of(refs[:-1]):
         part = lax.dot_general(left_ref[...], w[:, :half], dims, preferred_element_type=f32)
         part = part + lax.dot_general(right_ref[...], w[:, half:], dims, preferred_element_type=f32)
-        gg_ref[:, cut] = part.astype(bf16)
-        part = jnp.dot(gated_ref[:, cut], w, preferred_element_type=f32)
-        total = part if total is None else total + part
-    out_ref[...] = total.astype(bf16)
-
-
-def cross(cots, gated, quarters, parts=2):
-    tokens, half = cots[0].shape
-    channels = gated.shape[1]
+        refs[-1][:, pl.ds(at, w.shape[0])] = part.astype(bf16)
+        at += w.shape[0]
+
+
+def with_pieces(body, name, lefts, pieces, columns, parts=2):
+    tokens = lefts[0].shape[0]
     rows = tokens // parts
 
-    def row_block(columns):
-        return pl.BlockSpec((rows, columns), lambda i: (i, 0))
-
-    made = jax.ShapeDtypeStruct
-    return pl.pallas_call(
-        cross_body,
+    def row_block(width):
+        return pl.BlockSpec((rows, width), lambda i: (i, 0))
+
+    return pl.pallas_call(
+        body,
         grid=(parts,),
-        in_specs=[row_block(half), row_block(half), row_block(channels)]
-        + [pl.BlockSpec(quarter.shape, lambda i: (0, 0)) for quarter in quarters],
-        out_specs=[row_block(channels), row_block(2 * half)],
-        out_shape=[made((tokens, channels), bf16), made((tokens, 2 * half), bf16)],
+        in_specs=[row_block(left.shape[1]) for left in lefts]
+        + [pl.BlockSpec(piece.shape, lambda i: (0, 0)) for piece in pieces],
+        out_specs=row_block(columns),
+        out_shape=jax.ShapeDtypeStruct((tokens, columns), bf16),
         compiler_params=pltpu.CompilerParams(vmem_limit_bytes=60 << 20),
         cost_estimate=cost(0.02),
-        name="cross",
-    )(*cots, gated, *quarters)
+        name=name,
+    )(*lefts, *pieces)
 
 
 def stage_body(plans, *refs):
@@ -617,7 +624,7 @@
                 sent[i] = blocks[k].astype(bf16)
 
 
-def stage(streams, plans, steps=2):
+def stage(streams, plans, steps=1):
     height = streams[0][0][0].shape[1] // steps
     ins, in_specs, outs, out_specs = [], [], [], []
     for (base, got), (stay, leave), column in streams_with(streams, plans):
@@ -953,12 +960,12 @@
     )
     half_width = width // 2
     cot_l = lax.all_gather(after(cotangent[:, :half_width], first_x), "tensor", axis=0, tiled=True)
-    gather_o = Gather(after(w_out, got_x, got_g), wide)
-    gather_o.send()
+    outs = {0: after(w_out, got_x, got_g)}
+    for bit in wide:
+        outs[bit] = swap(outs[0], bit)
 
     xw = rank + 2 * states
     w_xp = small_all[:xw]
-    w_dt_rows = small_all[xw : xw + rank]
     at = xw + rank
     a_rows = small_all[at : at + states].astype(f32)
     at = at + states
@@ -979,39 +986,44 @@
 
     signal, gate, inner, mixed_own = front(normed, weights, conv_rows, conv_b, w_xp, dist, own_channels)
     parts = ring_parts(mixed_own)
-    for _ in wide[1:]:
-        gather_o.take(mixed_own)
-        gather_o.send()
+    for i, bit in enumerate(wide):
+        for k in kept[1 : 1 << i]:
+            near = after(outs[k], outs[bit], mixed_own)
+            outs[k | bit] = swap(near, bit)
     cot_r = lax.all_gather(after(cotangent[:, half_width:], *parts), "tensor", axis=0, tiled=True)
-    got_o, sent_o = after(gather_o.got, *parts[1:]), after(gather_o.sent, *parts[1:])
-    quarters = (sent_o, got_o, swap(sent_o, 1), swap(got_o, 1))
+    late = [after(outs[k], *parts[1:]) for k in kept]
+    quarters = late + [swap(piece, 1) for piece in late]
+    parts[0] = after(parts[0], *late)
+    w_dt_rows = after(small_all, *parts[1:])[xw : xw + rank]
     none = jnp.zeros(rates.shape, f32)
     states_all, deltas, sums, gated, mixed, _ = scan_forward(
         0, keep, parts, w_dt_rows, dt_b, skip_row, rates, inner, gate, none
     )
     quarters = tuple(after(quarter, mixed) for quarter in quarters)
-    grad_gated, branch = cross((cot_l, cot_r), gated, quarters)
+    branch = with_pieces(branch_body, "branch", (gated,), quarters, width)
+    grad_gated = with_pieces(cross_body, "cross", (after(cot_l, branch), after(cot_r, branch)), quarters, channels)
     branch_own = lax.psum_scatter(branch, "tensor", scatter_dimension=0, tiled=True)
     output = (hidden.astype(f32) + branch_own.astype(f32)).astype(bf16)
     orders = (wide, narrow)
 
-    out_grad = WeightGrad(after(gated, branch), (cot_l, cot_r), kept, orders)
+    out_grad = WeightGrad(after(gated, grad_gated), (cot_l, cot_r), kept, orders)
     out_grad.exchange()
-    out_grad.rest()
     g_scan, g_gate, g_proj, g_mixed, reds, acc, _ = scan_backward(
-        0, keep, after(mixed, out_grad.bases[0]), w_dt_rows, skip_row, rates, inner, gate, grad_gated, sums, states_all,
+        0, keep, after(mixed, out_grad.leave), w_dt_rows, skip_row, rates, inner, gate, grad_gated, sums, states_all,
         deltas, none,
     )
     backs = ring_parts(g_mixed)
     gate_grad = WeightGrad(g_gate, (normed,), kept, orders)
     gate_grad.rest()
-    sent = out_grad.go(gate_grad.bases[0])
+    out_grad.rest(gate_grad.bases[0])
+    sent = out_grad.go()
     backs[0] = after(backs[0], *sent)
     gate_grad.exchange()
     g_signal, low, _, conv_sums = turn(0, backs, g_scan, signal, conv_rows, conv_b, w_xp, dist)
-    sent = gate_grad.go(low)
+    sent_g = gate_grad.go(low)
+    sent = sent_g + out_grad.go(*sent_g)
     g_norm, gain_term = rear(
-        after(g_signal, branch_own, *sent, *out_grad.gots), g_gate, weights, normed, own_channels
+        after(g_signal, branch_own, *sent), g_gate, weights, normed, own_channels
     )
     g_norm = after(g_norm, *gate_grad.gots)
     g_norm_own = lax.psum_scatter(g_norm, "tensor", scatter_dimension=0, tiled=True)
@@ -1022,8 +1034,7 @@
     gain_sum = jnp.concatenate([gain_sum, jnp.zeros((SUB - 1, channels), f32)], axis=0)
     sig_grad = WeightGrad(after(g_signal, g_norm), (normed,), kept, orders)
     sig_grad.exchange()
-    sent = out_grad.go(sig_grad.leave)
-    sig_grad.rest(*sent)
+    sig_grad.rest(*out_grad.gots)
     sent = gate_grad.go(sig_grad.bases[0])
     sent = sig_grad.go(*sent)
     small_stay, small_leave = pack(

time: 304 us -> 294 us (0.967)
  local copies, waits for them, and re-layouts: 34.9 us -> 28.9 us
  waiting for transfers between devices: 64.3 us -> 59 us
    unnamed x170 -> x165, local copies, waits for them, and re-layouts: 22.5 us -> 18.4 us
    pallas_call x1 -> x2, Pallas kernels: 8.71 us -> 11.9 us  [with_pieces(): pl.pallas_call(body, grid=(parts,), in_specs=[row_block(left.shape[1]) fo...]
    ppermute x35 -> x38, waiting for transfers between devices: 46 us -> 43.8 us  [swap(): return lax.ppermute(value, 'fsdp', [(i, i ^ bit) for i in range(count)])]
    ppermute x35 -> x38, starting transfers between devices: 29.9 us -> 30.5 us  [swap(): return lax.ppermute(value, 'fsdp', [(i, i ^ bit) for i in range(count)])]
  transfers between devices with their start and end apart: 52 -> 55, of which waited for: 16 -> 15; matrix products, arithmetic and copies ran while one was open for 7% -> 6% of each run, Pallas kernels for 40% -> 45%
where the time goes in v5:
time: 294 us; the launch traced here: 292 us
  Pallas kernels  132 us (45%)
  waiting for transfers between devices  59 us (20%)
  starting transfers between devices  51.3 us (17%)
  local copies, waits for them, and re-layouts  28.9 us (10%)
  between operations  15 us (5%)
  other arithmetic  5.78 us (2%)
    pallas_call x1, Pallas kernels, scan_backward(): pl.pallas_call(functools.partial(bwd_body, states, subs, h * rows), grid_...  45.7 us
    ppermute x38, waiting for transfers between devices, swap(): return lax.ppermute(value, 'fsdp', [(i, i ^ bit) for i in range(count)])  43.8 us
    ppermute x38, starting transfers between devices, swap(): return lax.ppermute(value, 'fsdp', [(i, i ^ bit) for i in range(count)])  30.5 us
    pallas_call x1, Pallas kernels, scan_forward(): pl.pallas_call(functools.partial(fwd_body, states, subs, h * rows, len(pa...  19.6 us
    unnamed x165, local copies, waits for them, and re-layouts  18.4 us
    ppermute x9, starting transfers between devices, ring_parts(): lax.ppermute(part, 'tensor', [(i, (i + step) % count) for i in range(coun...  15.8 us
    ppermute x9, waiting for transfers between devices, ring_parts(): lax.ppermute(part, 'tensor', [(i, (i + step) % count) for i in range(coun...  12.9 us
    pallas_call x1, Pallas kernels, front(): pl.pallas_call(functools.partial(front_body, own), grid=(4,), in_specs=[p...  12.3 us
  transfers between devices with their start and end apart: 55, of which 15 were waited for; matrix products, arithmetic and copies ran while one was open for 6% of the time, Pallas kernels for 45%

profile of v5, /device:TPU:8, one launch (start us, length us, event | category | flops | bytes accessed | tf_op | source)
XLA Modules:
  0.0 291.9 jit_solution(13934636849738725523)
XLA Ops:
  8.0 1.3 slice_bitcast_fusion
  9.3 1.6 collective-permute-start.1
  10.9 1.5 collective-permute-start
  13.8 9.2 %collective-permute-done.1 = bf16[128,2048]{1,0:T(8,128)(2,1)S(1)} collective-permute-done((bf16[128,2048]{1,0:T(8,128)(2,1)S(1)}, bf16[128,2048]{1,0:T(8,128)(2,1)S(1)}, u32[]{:S(2)}, u32[]{:S(2)}) %collective-permute-start.1) | collective-permute-done | bytes 524320 | tf_op jit(solution)/shard_map/ppermute | solution.py:810
  23.0 1.2 collective-permute-done
  24.5 1.1 collective-permute-start.9
  25.6 1.1 pad_maximum_fusion.1.refs_4_
  26.7 1.6 collective-permute-start.12
  29.1 1.9 fusion.8
  30.9 1.6 collective-permute-start.4
  32.5 1.2 collective-permute-start.3
  33.7 1.8 collective-permute-start.2
  35.7 1.2 collective-permute-done.3
  38.7 1.1 collective-permute-start.6
  39.8 13.0 %collective-permute-done.7 = bf16[313,128]{1,0:T(8,128)(2,1)S(1)} collective-permute-done((bf16[313,128]{1,0:T(8,128)(2,1)S(1)}, bf16[313,128]{1,0:T(8,128)(2,1)S(1)}, u32[]{:S(2)}, u32[]{:S(2)}) %collective-permute-start.7) | collective-permute-done | bytes 80160 | tf_op jit(solution)/shard_map/ppermute | solution.py:810
  52.9 1.5 collective-permute-start.5
  54.5 2.8 collective-permute-done.5
  60.1 1.5 collective-permute-start.18
  62.4 1.6 copy-done.16
  65.0 1.3 copy-done
  66.3 12.3 %front.1 = (f32[512,1024]{1,0:T(8,128)}, f32[512,1024]{1,0:T(8,128)}, bf16[512,1024]{1,0:T(8,128)(2,1)S(1)}, bf16[160,512]{1,0:T(8,128)(2,1)}) custom-call(bf16[512,2048]{1,0:T(8,128)(2,1)} %copy-done, bf16[256,2048]{1,0:T(8,128)(2,1)S(1)} %pad_maximum_fusion.refs_0_, bf16[256,2048]{1,0:T(8,128)(2,1)S(1)} %collective-permute-done.9.refs_1_, ...), custom_call_target="tpu_custom_call" | custom-call | flops 20000000 | bytes 20000 | tf_op jit(solution)/shard_map/front/pallas_call | solution.py:416
  81.9 2.5 collective-permute-start.16
  84.4 2.6 collective-permute-start.15
  88.4 1.4 collective-permute-done.17.refs_3_
  89.8 5.6 %collective-permute-done.16.refs_2_ = bf16[160,512]{1,0:T(8,128)(2,1)S(1)} collective-permute-done((bf16[160,512]{1,0:T(8,128)(2,1)}, bf16[160,512]{1,0:T(8,128)(2,1)S(1)}, u32[]{:S(2)}, u32[]{:S(2)}) %collective-permute-start.16) | collective-permute-done | bytes 163872 | tf_op jit(solution)/shard_map/ppermute | solution.py:878
  95.3 2.5 collective-permute-done.15.refs_1_
  97.9 1.7 slice.81.refs_4_.wdt_ref
  101.4 19.6 %scan_forward.1 = (f32[66560,128]{1,0:T(8,128)}, f32[4096,128]{1,0:T(8,128)}, f32[512,1024]{1,0:T(8,128)}, bf16[512,1024]{1,0:T(8,128)(2,1)}, f32[512,256]{1,0:T(8,128)}, /*index=5*/f32[128,128]{1,0:T(8,128)}) custom-call(s32[512]{0:T(512)} %fusion.2.keep_ref, bf16[160,512]{1,0:T(8,128)(2,1)} %get-tuple-element.115.refs_0_, bf16[160,512]{1,0:T(8,128)(2,1)} %copy-done.74, ...), custom_call_target="tpu_custom_call" | custom-call | flops 40000000000 | bytes 40000000 | tf_op jit(solution)/shard_map/scan_forward/pallas_call | solution.py:142
  122.4 5.8 %branch.1 = bf16[512,2048]{1,0:T(8,128)(2,1)} custom-call(bf16[512,1024]{1,0:T(8,128)(2,1)} %get-tuple-element.141.gated_ref.lows_ref, bf16[128,2048]{1,0:T(8,128)(2,1)} %refs_0_.1, bf16[128,2048]{1,0:T(8,128)(2,1)} %collective-permute-done.18.refs_1_, bf16[128,2048]{1,0:T(8,128)(2,1)} %collective-permute-done.19.refs_2_, bf16[128,2048]{1,0:T(8,128)(2,1)} %copy-done.52, ...), custom_call_target="tpu_custom_call" | custom-call | flops 20000000 | bytes 20000 | tf_op jit(solution)/shard_map/branch/pallas_call | solution.py:598
  128.6 6.0 %cross.1.gg_ref = bf16[512,1024]{1,0:T(8,128)(2,1)} custom-call(bf16[512,1024]{1,0:T(8,128)(2,1)} %all-gather.6.cloned.1.call-done.left_ref.refs_0_, bf16[512,1024]{1,0:T(8,128)(2,1)} %all-gather.8.cloned.1.call-done.right_ref.refs_1_, bf16[128,2048]{1,0:T(8,128)(2,1)} %refs_0_.1, bf16[128,2048]{1,0:T(8,128)(2,1)} %collective-permute-done.18.refs_1_, ...), custom_call_target="tpu_custom_call" | custom-call | flops 20000000 | bytes 20000 | tf_op jit(solution)/shard_map/cross/pallas_call | solution.py:598
  134.6 2.6 grad_half.6
  137.3 45.7 %scan_backward.1 = (f32[512,1024]{1,0:T(8,128)}, bf16[512,1024]{1,0:T(8,128)(2,1)}, bf16[512,1024]{1,0:T(8,128)(2,1)}, bf16[160,512]{1,0:T(8,128)(2,1)}, f32[8,1...) custom-call(s32[512]{0:T(512)} %fusion.2.keep_ref, f32[512,256]{1,0:T(8,128)} %get-tuple-element.134.fwd_ref.mix_ref, ...), custom_call_target="tpu_custom_call" | custom-call | flops 99999997952 | bytes 100000000 | tf_op jit(solution)/shard_map/scan_backward/pallas_call | solution.py:309
  183.0 2.0 collective-permute-start.28
  185.1 1.9 collective-permute-start.27
  186.9 1.2 copy-done.10
  188.2 1.6 grad_half.7
  189.9 1.6 grad_half.8
  191.5 1.6 grad_half.9
  193.6 1.2 collective-permute-start.30
  194.8 1.5 collective-permute-start.31
  196.3 3.4 %collective-permute-done.26.refs_1_ = bf16[160,512]{1,0:T(8,128)(2,1)S(1)} collective-permute-done((bf16[160,512]{1,0:T(8,128)(2,1)}, bf16[160,512]{1,0:T(8,128)(2,1)S(1)}, u32[]{:S(2)}, u32[]{:S(2)}) %collective-permute-start.26) | collective-permute-done | bytes 163872 | tf_op jit(solution)/shard_map/ppermute | solution.py:878
  199.7 6.0 %turn.1 = (bf16[512,1024]{1,0:T(8,128)(2,1)S(1)}, bf16[160,512]{1,0:T(8,128)(2,1)S(1)}, f32[8,1024]{1,0:T(8,128)}, f32[8,1024]{1,0:T(8,128)S(1)}) custom-call(bf16[160,512]{1,0:T(8,128)(2,1)S(1)} %copy-done.49, bf16[160,512]{1,0:T(8,128)(2,1)S(1)} %collective-permute-done.26.refs_1_, bf16[160,512]{1,0:T(8,128)(2,1)S(1)} %collective-permute-done.27.refs_2_, ...), custom_call_target="tpu_custom_call" | custom-call | flops 40000000000 | bytes 40000000 | tf_op jit(solution)/shard_map/turn/pallas_call | solution.py:502
  207.4 1.4 stage.7
  210.7 1.5 collective-permute-start.32
  212.1 1.5 collective-permute-start.33
  216.8 10.7 %rear.1 = (bf16[512,2048]{1,0:T(8,128)(2,1)}, f32[1,2048]{1,0:T(1,128)}) custom-call(bf16[512,1024]{1,0:T(8,128)(2,1)} %copy-done.12, bf16[512,1024]{1,0:T(8,128)(2,1)} %get-tuple-element.140.lows_ref.gx_ref, bf16[256,2048]{1,0:T(8,128)(2,1)} %copy-done.14, bf16[256,2048]{1,0:T(8,128)(2,1)} %copy-done.19, bf16[256,2048]{1,0:T(8,128)(2,1)} %collective-permute-done.10.refs_2_, ...), custom_call_target="tpu_custom_call" | custom-call | flops 40000000000 | bytes 40000000 | tf_op jit(solution)/shard_map/rear/pallas_call | solution.py:552
  227.6 1.5 copy-done.2
  229.1 2.6 grad_half.10
  232.9 2.8 collective-permute-start.36
  236.8 3.9 %collective-permute-done.37.refs_1_ = bf16[1,128,1024]{2,1,0:T(8,128)(2,1)S(1)} collective-permute-done((bf16[1,128,1024]{2,1,0:T(8,128)(2,1)}, bf16[1,128,1024]{2,1,0:T(8,128)(2,1)S(1)}, u32[]{:S(2)}, u32[]{:S(2)}) %collective-permute-start.37) | collective-permute-done | bytes 262176 | tf_op jit(solution)/shard_map/ppermute | solution.py:810
  240.7 2.4 collective-permute-start.34
  243.0 1.6 grad_half.11
  244.7 1.3 copy-done.3
  246.0 1.5 stage.9
  249.3 2.2 stage.10
  251.6 1.6 pack.1
  254.5 1.4 collective-permute-start.42
  255.9 1.5 collective-permute-start.45
  259.3 3.2 %collective-permute-done.43.refs_1_ = bf16[1,128,1024]{2,1,0:T(8,128)(2,1)S(1)} collective-permute-done((bf16[1,128,1024]{2,1,0:T(8,128)(2,1)S(1)}, bf16[1,128,1024]{2,1,0:T(8,128)(2,1)S(1)}, u32[]{:S(2)}, u32[]{:S(2)}) %collective-permute-start.43) | collective-permute-done | bytes 262176 | tf_op jit(solution)/shard_map/ppermute | solution.py:810
  263.1 1.5 collective-permute-start.46
  266.5 7.8 %collective-permute-done.42.refs_1_ = bf16[2,128,1024]{2,1,0:T(8,128)(2,1)S(1)} collective-permute-done((bf16[2,128,1024]{2,1,0:T(8,128)(2,1)S(1)}, bf16[2,128,1024]{2,1,0:T(8,128)(2,1)S(1)}, u32[]{:S(2)}, u32[]{:S(2)}) %collective-permute-start.42) | collective-permute-done | bytes 524320 | tf_op jit(solution)/shard_map/ppermute | solution.py:810
  274.5 1.6 collective-permute-done.41
  276.1 1.5 collective-permute-start.48
  281.8 2.5 last.1
  (304 shorter events, 39.8 us)
Async XLA Ops:
  7.2 55.2 %all-gather.4.cloned.1.call-start = ((), (), s32[]{:S(2)}) async-start(), calls=%async_computation.2 | async-start | bytes 2621440 | tf_op jit(solution)/shard_map/all_gather | solution.py:921
  7.9 120.3 %all-gather.6.cloned.1.call-start = ((), (), s32[]{:S(2)}) async-start(), calls=%async_computation.4 | async-start | bytes 1310720 | tf_op jit(solution)/shard_map/all_gather | solution.py:962
  9.3 13.7 %copy-start.57 = (bf16[128,2048]{1,0:T(8,128)(2,1)}, bf16[128,2048]{1,0:T(8,128)(2,1)S(1)}, u32[]{:S(2)}) copy-start(bf16[128,2048]{1,0:T(8,128)(2,1)S(1)} %get-tuple-element.230) | copy-start | bytes 1572868
  9.3 13.7 %collective-permute-start.1 = (bf16[128,2048]{1,0:T(8,128)(2,1)S(1)}, bf16[128,2048]{1,0:T(8,128)(2,1)S(1)}, u32[]{:S(2)}, u32[]{:S(2)}) collective-permute-start(bf16[128,2048]{1,0:T(8,128)(2,1)S(1)} %get-tuple-element.230), channel_id=1, source_target_pairs={{0,16},{4,20},{8,24},{12,28},{16,0},{20,4},{24,8},{28,12},{1,17},{... | collective-permute-start | bytes 1572872 | tf_op jit(solution)/shard_map/ppermute | solution.py:810
  10.9 13.4 %collective-permute-start = (bf16[128,2048]{1,0:T(8,128)(2,1)S(1)}, bf16[128,2048]{1,0:T(8,128)(2,1)S(1)}, u32[]{:S(2)}, u32[]{:S(2)}) collective-permute-start(bf16[128,2048]{1,0:T(8,128)(2,1)S(1)} %get-tuple-element.231), channel_id=1, source_target_pairs={{0,8},{4,12},{8,0},{12,4},{16,24},{20,28},{24,16},{28,20},{1,9},{5... | collective-permute-start | bytes 1572872 | tf_op jit(solution)/shard_map/ppermute | solution.py:810
  13.8 15.2 %copy-start.63 = (bf16[128,128]{1,0:T(8,128)(2,1)S(1)}, bf16[128,128]{1,0:T(8,128)(2,1)}, u32[]{:S(2)}) copy-start(bf16[128,128]{1,0:T(8,128)(2,1)} %param.24) | copy-start | bytes 98308
  24.4 41.9 %copy-start.14 = (bf16[256,2048]{1,0:T(8,128)(2,1)}, bf16[256,2048]{1,0:T(8,128)(2,1)S(1)}, u32[]{:S(2)}) copy-start(bf16[256,2048]{1,0:T(8,128)(2,1)S(1)} %pad_maximum_fusion.refs_0_) | copy-start | bytes 3145732
  24.5 33.0 %collective-permute-start.9 = (bf16[256,2048]{1,0:T(8,128)(2,1)S(1)}, bf16[256,2048]{1,0:T(8,128)(2,1)S(1)}, u32[]{:S(2)}, u32[]{:S(2)}) collective-permute-start(bf16[256,2048]{1,0:T(8,128)(2,1)S(1)} %pad_maximum_fusion.refs_0_), channel_id=1, source_target_pairs={{0,16},{4,20},{8,24},{12,28},{16,0},{20,4},{24,8},{28,12},{1,17},{... | collective-permute-start | bytes 3145736 | tf_op jit(solution)/shard_map/ppermute | solution.py:810
  26.7 39.6 %copy-start.15 = (bf16[256,2048]{1,0:T(8,128)(2,1)}, bf16[256,2048]{1,0:T(8,128)(2,1)S(1)}, u32[]{:S(2)}) copy-start(bf16[256,2048]{1,0:T(8,128)(2,1)S(1)} %pad_maximum_fusion.1.refs_4_) | copy-start | bytes 3145732
  26.7 31.3 %collective-permute-start.12 = (bf16[256,2048]{1,0:T(8,128)(2,1)S(1)}, bf16[256,2048]{1,0:T(8,128)(2,1)}, u32[]{:S(2)}, u32[]{:S(2)}) collective-permute-start(bf16[256,2048]{1,0:T(8,128)(2,1)S(1)} %pad_maximum_fusion.1.refs_4_), channel_id=1, source_target_pairs={{0,8},{4,12},{8,0},{12,4},{16,24},{20,28},{24,16},{28,20},{1,9},{5... | collective-permute-start | bytes 3145736 | tf_op jit(solution)/shard_map/ppermute | solution.py:810
  30.9 4.7 %collective-permute-start.4 = (bf16[1,64]{1,0:T(2,128)(2,1)S(1)}, bf16[1,64]{1,0:T(2,128)(2,1)S(1)}, u32[]{:S(2)}, u32[]{:S(2)}) collective-permute-start(bf16[1,64]{1,0:T(2,128)(2,1)S(1)} %bitcast.79), channel_id=1, source_target_pairs={{0,1},{1,2},{2,3},{3,0},{4,5},{5,6},{6,7},{7,4},{8,9},{9,10},{10,1... | collective-permute-start | bytes 392 | tf_op jit(solution)/shard_map/ppermute | solution.py:938
  32.5 4.4 %collective-permute-start.3 = (bf16[1,64]{1,0:T(2,128)(2,1)S(1)}, bf16[1,64]{1,0:T(2,128)(2,1)S(1)}, u32[]{:S(2)}, u32[]{:S(2)}) collective-permute-start(bf16[1,64]{1,0:T(2,128)(2,1)S(1)} %bitcast.80), channel_id=1, source_target_pairs={{0,2},{1,3},{2,0},{3,1},{4,6},{5,7},{6,4},{7,5},{8,10},{9,11},{10,... | collective-permute-start | bytes 392 | tf_op jit(solution)/shard_map/ppermute | solution.py:938
  33.7 3.7 %collective-permute-start.2 = (bf16[1,64]{1,0:T(2,128)(2,1)S(1)}, bf16[1,64]{1,0:T(2,128)(2,1)S(1)}, u32[]{:S(2)}, u32[]{:S(2)}) collective-permute-start(bf16[1,64]{1,0:T(2,128)(2,1)S(1)} %bitcast.81), channel_id=1, source_target_pairs={{0,3},{1,0},{2,1},{3,2},{4,7},{5,4},{6,5},{7,6},{8,11},{9,8},{10,9... | collective-permute-start | bytes 392 | tf_op jit(solution)/shard_map/ppermute | solution.py:938
  35.6 24.5 %collective-permute-start.10 = (bf16[256,2048]{1,0:T(8,128)(2,1)S(1)}, bf16[256,2048]{1,0:T(8,128)(2,1)}, u32[]{:S(2)}, u32[]{:S(2)}) collective-permute-start(bf16[256,2048]{1,0:T(8,128)(2,1)S(1)} %pad_maximum_fusion.refs_0_), channel_id=1, source_target_pairs={{0,4},{4,0},{8,12},{12,8},{16,20},{20,16},{24,28},{28,24},{1,5},{5... | collective-permute-start | bytes 3145736 | tf_op jit(solution)/shard_map/ppermute | solution.py:810
  37.7 15.1 %collective-permute-start.7 = (bf16[313,128]{1,0:T(8,128)(2,1)S(1)}, bf16[313,128]{1,0:T(8,128)(2,1)S(1)}, u32[]{:S(2)}, u32[]{:S(2)}) collective-permute-start(bf16[313,128]{1,0:T(8,128)(2,1)S(1)} %concatenate.19), channel_id=1, source_target_pairs={{0,24},{4,28},{8,16},{12,20},{16,8},{20,12},{24,0},{28,4},{1,25},{... | collective-permute-start | bytes 240392 | tf_op jit(solution)/shard_map/ppermute | solution.py:810
  38.6 23.1 %copy-start.66 = (pred[8,8]{1,0:T(8,128)(4,1)}, pred[8,8]{1,0:T(8,128)(4,1)S(1)}, u32[]{:S(2)}) copy-start(pred[8,8]{1,0:T(8,128)(4,1)S(1)} %iota_compare_fusion.1) | copy-start | bytes 196
  38.6 89.9 %all-gather.8.cloned.1.call-start = ((), (), s32[]{:S(2)}) async-start(), calls=%async_computation.5 | async-start | bytes 1310720 | tf_op jit(solution)/shard_map/all_gather | solution.py:993
  38.7 15.7 %collective-permute-start.6 = (bf16[313,128]{1,0:T(8,128)(2,1)S(1)}, bf16[313,128]{1,0:T(8,128)(2,1)S(1)}, u32[]{:S(2)}, u32[]{:S(2)}) collective-permute-start(bf16[313,128]{1,0:T(8,128)(2,1)S(1)} %concatenate.19), channel_id=1, source_target_pairs={{0,16},{4,20},{8,24},{12,28},{16,0},{20,4},{24,8},{28,12},{1,17},{... | collective-permute-start | bytes 240392 | tf_op jit(solution)/shard_map/ppermute | solution.py:810
  52.9 4.4 %collective-permute-start.5 = (bf16[313,128]{1,0:T(8,128)(2,1)S(1)}, bf16[313,128]{1,0:T(8,128)(2,1)S(1)}, u32[]{:S(2)}, u32[]{:S(2)}) collective-permute-start(bf16[313,128]{1,0:T(8,128)(2,1)S(1)} %concatenate.19), channel_id=1, source_target_pairs={{0,8},{4,12},{8,0},{12,4},{16,24},{20,28},{24,16},{28,20},{1,9},{5... | collective-permute-start | bytes 240392 | tf_op jit(solution)/shard_map/ppermute | solution.py:810
  54.4 11.9 %collective-permute-start.13 = (bf16[256,2048]{1,0:T(8,128)(2,1)S(1)}, bf16[256,2048]{1,0:T(8,128)(2,1)}, u32[]{:S(2)}, u32[]{:S(2)}) collective-permute-start(bf16[256,2048]{1,0:T(8,128)(2,1)S(1)} %pad_maximum_fusion.1.refs_4_), channel_id=1, source_target_pairs={{0,4},{4,0},{8,12},{12,8},{16,20},{20,16},{24,28},{28,24},{1,5},{5... | collective-permute-start | bytes 3145736 | tf_op jit(solution)/shard_map/ppermute | solution.py:810
  57.3 1.7 collective-permute-start.8
  57.5 8.8 %collective-permute-start.11 = (bf16[256,2048]{1,0:T(8,128)(2,1)S(1)}, bf16[256,2048]{1,0:T(8,128)(2,1)}, u32[]{:S(2)}, u32[]{:S(2)}) collective-permute-start(bf16[256,2048]{1,0:T(8,128)(2,1)S(1)} %collective-permute-done.9.refs_1_), channel_id=1, source_target_pairs={{0,4},{4,0},{8,12},{12,8},{16,20},{20,16},{24,28},{28,24},{1,5},{5... | collective-permute-start | bytes 3145736 | tf_op jit(solution)/shard_map/ppermute | solution.py:810
  58.0 8.2 %collective-permute-start.14 = (bf16[256,2048]{1,0:T(8,128)(2,1)}, bf16[256,2048]{1,0:T(8,128)(2,1)}, u32[]{:S(2)}, u32[]{:S(2)}) collective-permute-start(bf16[256,2048]{1,0:T(8,128)(2,1)} %collective-permute-done.12.refs_5_), channel_id=1, source_target_pairs={{0,4},{4,0},{8,12},{12,8},{16,20},{20,16},{24,28},{28,24},{1,5},{5... | collective-permute-start | bytes 3145736 | tf_op jit(solution)/shard_map/ppermute | solution.py:810
  59.2 20.5 %collective-permute-start.19 = (bf16[128,2048]{1,0:T(8,128)(2,1)}, bf16[128,2048]{1,0:T(8,128)(2,1)}, u32[]{:S(2)}, u32[]{:S(2)}) collective-permute-start(bf16[128,2048]{1,0:T(8,128)(2,1)} %refs_0_.1), channel_id=1, source_target_pairs={{0,16},{4,20},{8,24},{12,28},{16,0},{20,4},{24,8},{28,12},{1,17},{... | collective-permute-start | bytes 1572872 | tf_op jit(solution)/shard_map/ppermute | solution.py:810
  60.1 19.5 %collective-permute-start.18 = (bf16[128,2048]{1,0:T(8,128)(2,1)}, bf16[128,2048]{1,0:T(8,128)(2,1)}, u32[]{:S(2)}, u32[]{:S(2)}) collective-permute-start(bf16[128,2048]{1,0:T(8,128)(2,1)} %refs_0_.1), channel_id=1, source_target_pairs={{0,8},{4,12},{8,0},{12,4},{16,24},{20,28},{24,16},{28,20},{1,9},{5... | collective-permute-start | bytes 1572872 | tf_op jit(solution)/shard_map/ppermute | solution.py:810
  61.7 171.1 %copy-start.39 = (f32[8,2,128]{2,1,0:T(2,128)}, f32[8,2,128]{2,1,0:T(2,128)S(1)}, u32[]{:S(2)}) copy-start(f32[8,2,128]{2,1,0:T(2,128)S(1)} %select_reduce_fusion) | copy-start | bytes 24580
  79.6 20.6 %collective-permute-start.20 = (bf16[128,2048]{1,0:T(8,128)(2,1)}, bf16[128,2048]{1,0:T(8,128)(2,1)S(1)}, u32[]{:S(2)}, u32[]{:S(2)}) collective-permute-start(bf16[128,2048]{1,0:T(8,128)(2,1)} %collective-permute-done.18.refs_1_), channel_id=1, source_target_pairs={{0,16},{4,20},{8,24},{12,28},{16,0},{20,4},{24,8},{28,12},{1,17},{... | collective-permute-start | bytes 1572872 | tf_op jit(solution)/shard_map/ppermute | solution.py:810
  81.3 8.5 %collective-permute-start.17 = (bf16[160,512]{1,0:T(8,128)(2,1)}, bf16[160,512]{1,0:T(8,128)(2,1)S(1)}, u32[]{:S(2)}, u32[]{:S(2)}) collective-permute-start(bf16[160,512]{1,0:T(8,128)(2,1)} %get-tuple-element.115.refs_0_), channel_id=1, source_target_pairs={{0,3},{1,0},{2,1},{3,2},{4,7},{5,4},{6,5},{7,6},{8,11},{9,8},{10,9... | collective-permute-start | bytes 491528 | tf_op jit(solution)/shard_map/ppermute | solution.py:878
  81.9 13.5 %collective-permute-start.16 = (bf16[160,512]{1,0:T(8,128)(2,1)}, bf16[160,512]{1,0:T(8,128)(2,1)S(1)}, u32[]{:S(2)}, u32[]{:S(2)}) collective-permute-start(bf16[160,512]{1,0:T(8,128)(2,1)} %get-tuple-element.115.refs_0_), channel_id=1, source_target_pairs={{0,2},{1,3},{2,0},{3,1},{4,6},{5,7},{6,4},{7,5},{8,10},{9,11},{10,... | collective-permute-start | bytes 491528 | tf_op jit(solution)/shard_map/ppermute | solution.py:878
  84.4 13.5 %collective-permute-start.15 = (bf16[160,512]{1,0:T(8,128)(2,1)}, bf16[160,512]{1,0:T(8,128)(2,1)S(1)}, u32[]{:S(2)}, u32[]{:S(2)}) collective-permute-start(bf16[160,512]{1,0:T(8,128)(2,1)} %get-tuple-element.115.refs_0_), channel_id=1, source_target_pairs={{0,1},{1,2},{2,3},{3,0},{4,5},{5,6},{6,7},{7,4},{8,9},{9,10},{10,1... | collective-permute-start | bytes 491528 | tf_op jit(solution)/shard_map/ppermute | solution.py:878
  99.6 21.5 %collective-permute-start.21 = (bf16[128,2048]{1,0:T(8,128)(2,1)}, bf16[128,2048]{1,0:T(8,128)(2,1)S(1)}, u32[]{:S(2)}, u32[]{:S(2)}) collective-permute-start(bf16[128,2048]{1,0:T(8,128)(2,1)} %refs_0_.1), channel_id=1, source_target_pairs={{0,4},{4,0},{8,12},{12,8},{16,20},{20,16},{24,28},{28,24},{1,5},{5... | collective-permute-start | bytes 1572872 | tf_op jit(solution)/shard_map/ppermute | solution.py:810
  99.6 21.5 %collective-permute-start.22 = (bf16[128,2048]{1,0:T(8,128)(2,1)}, bf16[128,2048]{1,0:T(8,128)(2,1)S(1)}, u32[]{:S(2)}, u32[]{:S(2)}) collective-permute-start(bf16[128,2048]{1,0:T(8,128)(2,1)} %collective-permute-done.18.refs_1_), channel_id=1, source_target_pairs={{0,4},{4,0},{8,12},{12,8},{16,20},{20,16},{24,28},{28,24},{1,5},{5... | collective-permute-start | bytes 1572872 | tf_op jit(solution)/shard_map/ppermute | solution.py:810
  100.1 20.9 %collective-permute-start.23 = (bf16[128,2048]{1,0:T(8,128)(2,1)}, bf16[128,2048]{1,0:T(8,128)(2,1)S(1)}, u32[]{:S(2)}, u32[]{:S(2)}) collective-permute-start(bf16[128,2048]{1,0:T(8,128)(2,1)} %collective-permute-done.19.refs_2_), channel_id=1, source_target_pairs={{0,4},{4,0},{8,12},{12,8},{16,20},{20,16},{24,28},{28,24},{1,5},{5... | collective-permute-start | bytes 1572872 | tf_op jit(solution)/shard_map/ppermute | solution.py:810
  100.2 116.6 %reduce-scatter.3.cloned.1.call-start = ((), (), s32[]{:S(2)}) async-start(), calls=%async_computation.3 | async-start | bytes 2621440 | tf_op jit(solution)/shard_map/reduce_scatter | solution.py:1005
  100.2 20.8 %copy-start.52 = (bf16[128,2048]{1,0:T(8,128)(2,1)}, bf16[128,2048]{1,0:T(8,128)(2,1)S(1)}, u32[]{:S(2)}) copy-start(bf16[128,2048]{1,0:T(8,128)(2,1)S(1)} %collective-permute-done.20.refs_3_) | copy-start | bytes 1572868
  100.2 20.9 %collective-permute-start.24 = (bf16[128,2048]{1,0:T(8,128)(2,1)S(1)}, bf16[128,2048]{1,0:T(8,128)(2,1)S(1)}, u32[]{:S(2)}, u32[]{:S(2)}) collective-permute-start(bf16[128,2048]{1,0:T(8,128)(2,1)S(1)} %collective-permute-done.20.refs_3_), channel_id=1, source_target_pairs={{0,4},{4,0},{8,12},{12,8},{16,20},{20,16},{24,28},{28,24},{1,5},{5... | collective-permute-start | bytes 1572872 | tf_op jit(solution)/shard_map/ppermute | solution.py:810
  128.3 153.5 %reduce-scatter.5.cloned.1.call-start = ((), (), s32[]{:S(2)}) async-start(), calls=%async_computation.6 | async-start | bytes 2621440 | tf_op jit(solution)/shard_map/reduce_scatter | solution.py:1029
  137.2 55.9 %collective-permute-start.25 = (bf16[512,2048]{1,0:T(8,128)(2,1)}, bf16[512,2048]{1,0:T(8,128)(2,1)S(1)}, u32[]{:S(2)}, u32[]{:S(2)}) collective-permute-start(bf16[512,2048]{1,0:T(8,128)(2,1)} %grad_half.6), channel_id=1, source_target_pairs={{0,4},{4,0},{8,12},{12,8},{16,20},{20,16},{24,28},{28,24},{1,5},{5... | collective-permute-start | bytes 6291464 | tf_op jit(solution)/shard_map/ppermute | solution.py:810
  137.3 49.6 %copy-start.1 = (bf16[512,2048]{1,0:T(8,128)(2,1)S(1)}, bf16[512,2048]{1,0:T(8,128)(2,1)}, u32[]{:S(2)}) copy-start(bf16[512,2048]{1,0:T(8,128)(2,1)} %copy-done) | copy-start | bytes 6291460
  183.0 11.8 %collective-permute-start.28 = (bf16[160,512]{1,0:T(8,128)(2,1)}, bf16[160,512]{1,0:T(8,128)(2,1)S(1)}, u32[]{:S(2)}, u32[]{:S(2)}) collective-permute-start(bf16[160,512]{1,0:T(8,128)(2,1)} %get-tuple-element.144.refs_0_), channel_id=1, source_target_pairs={{0,3},{1,0},{2,1},{3,2},{4,7},{5,4},{6,5},{7,6},{8,11},{9,8},{10,9... | collective-permute-start | bytes 491528 | tf_op jit(solution)/shard_map/ppermute | solution.py:878
  185.1 11.3 %collective-permute-start.27 = (bf16[160,512]{1,0:T(8,128)(2,1)}, bf16[160,512]{1,0:T(8,128)(2,1)S(1)}, u32[]{:S(2)}, u32[]{:S(2)}) collective-permute-start(bf16[160,512]{1,0:T(8,128)(2,1)} %get-tuple-element.144.refs_0_), channel_id=1, source_target_pairs={{0,2},{1,3},{2,0},{3,1},{4,6},{5,7},{6,4},{7,5},{8,10},{9,11},{10,... | collective-permute-start | bytes 491528 | tf_op jit(solution)/shard_map/ppermute | solution.py:878
  186.9 12.8 %collective-permute-start.26 = (bf16[160,512]{1,0:T(8,128)(2,1)}, bf16[160,512]{1,0:T(8,128)(2,1)S(1)}, u32[]{:S(2)}, u32[]{:S(2)}) collective-permute-start(bf16[160,512]{1,0:T(8,128)(2,1)} %get-tuple-element.144.refs_0_), channel_id=1, source_target_pairs={{0,1},{1,2},{2,3},{3,0},{4,5},{5,6},{6,7},{7,4},{8,9},{9,10},{10,1... | collective-permute-start | bytes 491528 | tf_op jit(solution)/shard_map/ppermute | solution.py:878
  189.8 17.6 %collective-permute-start.29 = (bf16[512,2048]{1,0:T(8,128)(2,1)S(1)}, bf16[512,2048]{1,0:T(8,128)(2,1)S(1)}, u32[]{:S(2)}, u32[]{:S(2)}) collective-permute-start(bf16[512,2048]{1,0:T(8,128)(2,1)S(1)} %grad_half.7), channel_id=1, source_target_pairs={{0,4},{4,0},{8,12},{12,8},{16,20},{20,16},{24,28},{28,24},{1,5},{5... | collective-permute-start | bytes 6291464 | tf_op jit(solution)/shard_map/ppermute | solution.py:810
  193.6 20.0 %collective-permute-start.30 = (bf16[2,128,1024]{2,1,0:T(8,128)(2,1)S(1)}, bf16[2,128,1024]{2,1,0:T(8,128)(2,1)S(1)}, u32[]{:S(2)}, u32[]{:S(2)}) collective-permute-start(bf16[2,128,1024]{2,1,0:T(8,128)(2,1)S(1)} %get-tuple-element.142), channel_id=1, source_target_pairs={{0,8},{4,12},{8,0},{12,4},{16,24},{20,28},{24,16},{28,20},{1,9},{5... | collective-permute-start | bytes 1572872 | tf_op jit(solution)/shard_map/ppermute | solution.py:810
  194.8 18.8 %collective-permute-start.31 = (bf16[2,128,1024]{2,1,0:T(8,128)(2,1)S(1)}, bf16[2,128,1024]{2,1,0:T(8,128)(2,1)S(1)}, u32[]{:S(2)}, u32[]{:S(2)}) collective-permute-start(bf16[2,128,1024]{2,1,0:T(8,128)(2,1)S(1)} %get-tuple-element.143), channel_id=1, source_target_pairs={{0,16},{4,20},{8,24},{12,28},{16,0},{20,4},{24,8},{28,12},{1,17},{... | collective-permute-start | bytes 1572872 | tf_op jit(solution)/shard_map/ppermute | solution.py:810
  210.7 16.9 %collective-permute-start.32 = (bf16[2,128,1024]{2,1,0:T(8,128)(2,1)}, bf16[2,128,1024]{2,1,0:T(8,128)(2,1)}, u32[]{:S(2)}, u32[]{:S(2)}) collective-permute-start(bf16[2,128,1024]{2,1,0:T(8,128)(2,1)} %get-tuple-element.150), channel_id=1, source_target_pairs={{0,8},{4,12},{8,0},{12,4},{16,24},{20,28},{24,16},{28,20},{1,9},{5... | collective-permute-start | bytes 1572872 | tf_op jit(solution)/shard_map/ppermute | solution.py:810
  212.1 15.4 %collective-permute-start.33 = (bf16[2,128,1024]{2,1,0:T(8,128)(2,1)}, bf16[2,128,1024]{2,1,0:T(8,128)(2,1)}, u32[]{:S(2)}, u32[]{:S(2)}) collective-permute-start(bf16[2,128,1024]{2,1,0:T(8,128)(2,1)} %get-tuple-element.151), channel_id=1, source_target_pairs={{0,16},{4,20},{8,24},{12,28},{16,0},{20,4},{24,8},{28,12},{1,17},{... | collective-permute-start | bytes 1572872 | tf_op jit(solution)/shard_map/ppermute | solution.py:810
  231.7 17.5 %collective-permute-start.39 = (bf16[512,2048]{1,0:T(8,128)(2,1)}, bf16[512,2048]{1,0:T(8,128)(2,1)}, u32[]{:S(2)}, u32[]{:S(2)}) collective-permute-start(bf16[512,2048]{1,0:T(8,128)(2,1)} %grad_half.10), channel_id=1, source_target_pairs={{0,4},{4,0},{8,12},{12,8},{16,20},{20,16},{24,28},{28,24},{1,5},{5... | collective-permute-start | bytes 6291464 | tf_op jit(solution)/shard_map/ppermute | solution.py:810
  231.7 8.9 %collective-permute-start.37 = (bf16[1,128,1024]{2,1,0:T(8,128)(2,1)}, bf16[1,128,1024]{2,1,0:T(8,128)(2,1)S(1)}, u32[]{:S(2)}, u32[]{:S(2)}) collective-permute-start(bf16[1,128,1024]{2,1,0:T(8,128)(2,1)} %copy-done.48), channel_id=1, source_target_pairs={{0,16},{4,20},{8,24},{12,28},{16,0},{20,4},{24,8},{28,12},{1,17},{... | collective-permute-start | bytes 786440 | tf_op jit(solution)/shard_map/ppermute | solution.py:810
  232.3 10.8 %collective-permute-start.38 = (bf16[1,128,1024]{2,1,0:T(8,128)(2,1)}, bf16[1,128,1024]{2,1,0:T(8,128)(2,1)S(1)}, u32[]{:S(2)}, u32[]{:S(2)}) collective-permute-start(bf16[1,128,1024]{2,1,0:T(8,128)(2,1)} %copy-done.47), channel_id=1, source_target_pairs={{0,8},{4,12},{8,0},{12,4},{16,24},{20,28},{24,16},{28,20},{1,9},{5... | collective-permute-start | bytes 786440 | tf_op jit(solution)/shard_map/ppermute | solution.py:810
  232.9 13.1 %copy-start.24 = (f32[2,128,1024]{2,1,0:T(8,128)S(1)}, f32[2,128,1024]{2,1,0:T(8,128)}, u32[]{:S(2)}) copy-start(f32[2,128,1024]{2,1,0:T(8,128)} %copy-done.23) | copy-start | bytes 3145732
  232.9 16.1 %collective-permute-start.36 = (bf16[1,2048]{1,0:T(2,128)(2,1)S(1)}, bf16[1,2048]{1,0:T(2,128)(2,1)S(1)}, u32[]{:S(2)}, u32[]{:S(2)}) collective-permute-start(bf16[1,2048]{1,0:T(2,128)(2,1)S(1)} %divide_convert_fusion), channel_id=1, source_target_pairs={{0,3},{1,0},{2,1},{3,2},{4,7},{5,4},{6,5},{7,6},{8,11},{9,8},{10,9... | collective-permute-start | bytes 12296 | tf_op jit(solution)/shard_map/ppermute | solution.py:878
  235.7 13.2 %collective-permute-start.35 = (bf16[1,2048]{1,0:T(2,128)(2,1)S(1)}, bf16[1,2048]{1,0:T(2,128)(2,1)S(1)}, u32[]{:S(2)}, u32[]{:S(2)}) collective-permute-start(bf16[1,2048]{1,0:T(2,128)(2,1)S(1)} %divide_convert_fusion), channel_id=1, source_target_pairs={{0,2},{1,3},{2,0},{3,1},{4,6},{5,7},{6,4},{7,5},{8,10},{9,11},{10,... | collective-permute-start | bytes 12296 | tf_op jit(solution)/shard_map/ppermute | solution.py:878
  240.7 8.3 %collective-permute-start.34 = (bf16[1,2048]{1,0:T(2,128)(2,1)S(1)}, bf16[1,2048]{1,0:T(2,128)(2,1)S(1)}, u32[]{:S(2)}, u32[]{:S(2)}) collective-permute-start(bf16[1,2048]{1,0:T(2,128)(2,1)S(1)} %divide_convert_fusion), channel_id=1, source_target_pairs={{0,1},{1,2},{2,3},{3,0},{4,5},{5,6},{6,7},{7,4},{8,9},{9,10},{10,1... | collective-permute-start | bytes 12296 | tf_op jit(solution)/shard_map/ppermute | solution.py:878
  253.2 5.3 %collective-permute-start.40 = (bf16[328,512]{1,0:T(8,128)(2,1)S(1)}, bf16[328,512]{1,0:T(8,128)(2,1)S(1)}, u32[]{:S(2)}, u32[]{:S(2)}) collective-permute-start(bf16[328,512]{1,0:T(8,128)(2,1)S(1)} %get-tuple-element.177), channel_id=1, source_target_pairs={{0,4},{4,0},{8,12},{12,8},{16,20},{20,16},{24,28},{28,24},{1,5},{5... | collective-permute-start | bytes 1007624 | tf_op jit(solution)/shard_map/ppermute | solution.py:810
  253.3 9.2 %collective-permute-start.43 = (bf16[1,128,1024]{2,1,0:T(8,128)(2,1)S(1)}, bf16[1,128,1024]{2,1,0:T(8,128)(2,1)S(1)}, u32[]{:S(2)}, u32[]{:S(2)}) collective-permute-start(bf16[1,128,1024]{2,1,0:T(8,128)(2,1)S(1)} %copy-done.46), channel_id=1, source_target_pairs={{0,16},{4,20},{8,24},{12,28},{16,0},{20,4},{24,8},{28,12},{1,17},{... | collective-permute-start | bytes 786440 | tf_op jit(solution)/shard_map/ppermute | solution.py:810
  253.9 9.2 %collective-permute-start.44 = (bf16[1,128,1024]{2,1,0:T(8,128)(2,1)S(1)}, bf16[1,128,1024]{2,1,0:T(8,128)(2,1)S(1)}, u32[]{:S(2)}, u32[]{:S(2)}) collective-permute-start(bf16[1,128,1024]{2,1,0:T(8,128)(2,1)S(1)} %copy-done.44), channel_id=1, source_target_pairs={{0,8},{4,12},{8,0},{12,4},{16,24},{20,28},{24,16},{28,20},{1,9},{5... | collective-permute-start | bytes 786440 | tf_op jit(solution)/shard_map/ppermute | solution.py:810
  254.5 19.8 %collective-permute-start.42 = (bf16[2,128,1024]{2,1,0:T(8,128)(2,1)S(1)}, bf16[2,128,1024]{2,1,0:T(8,128)(2,1)S(1)}, u32[]{:S(2)}, u32[]{:S(2)}) collective-permute-start(bf16[2,128,1024]{2,1,0:T(8,128)(2,1)S(1)} %get-tuple-element.173), channel_id=1, source_target_pairs={{0,8},{4,12},{8,0},{12,4},{16,24},{20,28},{24,16},{28,20},{1,9},{5... | collective-permute-start | bytes 1572872 | tf_op jit(solution)/shard_map/ppermute | solution.py:810
  255.9 18.4 %collective-permute-start.45 = (bf16[2,128,1024]{2,1,0:T(8,128)(2,1)S(1)}, bf16[2,128,1024]{2,1,0:T(8,128)(2,1)S(1)}, u32[]{:S(2)}, u32[]{:S(2)}) collective-permute-start(bf16[2,128,1024]{2,1,0:T(8,128)(2,1)S(1)} %get-tuple-element.174), channel_id=1, source_target_pairs={{0,16},{4,20},{8,24},{12,28},{16,0},{20,4},{24,8},{28,12},{1,17},{... | collective-permute-start | bytes 1572872 | tf_op jit(solution)/shard_map/ppermute | solution.py:810
  258.7 17.4 %collective-permute-start.41 = (bf16[328,128]{1,0:T(8,128)(2,1)S(1)}, bf16[328,128]{1,0:T(8,128)(2,1)S(1)}, u32[]{:S(2)}, u32[]{:S(2)}) collective-permute-start(bf16[328,128]{1,0:T(8,128)(2,1)S(1)} %get-tuple-element.239), channel_id=1, source_target_pairs={{0,8},{4,12},{8,0},{12,4},{16,24},{20,28},{24,16},{28,20},{1,9},{5... | collective-permute-start | bytes 251912 | tf_op jit(solution)/shard_map/ppermute | solution.py:810
  262.5 15.7 %collective-permute-start.47 = (bf16[328,128]{1,0:T(8,128)(2,1)S(1)}, bf16[328,128]{1,0:T(8,128)(2,1)S(1)}, u32[]{:S(2)}, u32[]{:S(2)}) collective-permute-start(bf16[328,128]{1,0:T(8,128)(2,1)S(1)} %get-tuple-element.240), channel_id=1, source_target_pairs={{0,24},{4,28},{8,16},{12,20},{16,8},{20,12},{24,0},{28,4},{1,25},{... | collective-permute-start | bytes 251912 | tf_op jit(solution)/shard_map/ppermute | solution.py:810
  263.1 15.1 %collective-permute-start.46 = (bf16[328,128]{1,0:T(8,128)(2,1)S(1)}, bf16[328,128]{1,0:T(8,128)(2,1)S(1)}, u32[]{:S(2)}, u32[]{:S(2)}) collective-permute-start(bf16[328,128]{1,0:T(8,128)(2,1)S(1)} %get-tuple-element.241), channel_id=1, source_target_pairs={{0,16},{4,20},{8,24},{12,28},{16,0},{20,4},{24,8},{28,12},{1,17},{... | collective-permute-start | bytes 251912 | tf_op jit(solution)/shard_map/ppermute | solution.py:810
  276.1 8.2 %collective-permute-start.48 = (bf16[1,128,1024]{2,1,0:T(8,128)(2,1)S(1)}, bf16[1,128,1024]{2,1,0:T(8,128)(2,1)S(1)}, u32[]{:S(2)}, u32[]{:S(2)}) collective-permute-start(bf16[1,128,1024]{2,1,0:T(8,128)(2,1)S(1)} %get-tuple-element.190), channel_id=1, source_target_pairs={{0,16},{4,20},{8,24},{12,28},{16,0},{20,4},{24,8},{28,12},{1,17},{... | collective-permute-start | bytes 786440 | tf_op jit(solution)/shard_map/ppermute | solution.py:810
  277.6 6.7 %collective-permute-start.49 = (bf16[1,128,1024]{2,1,0:T(8,128)(2,1)S(1)}, bf16[1,128,1024]{2,1,0:T(8,128)(2,1)S(1)}, u32[]{:S(2)}, u32[]{:S(2)}) collective-permute-start(bf16[1,128,1024]{2,1,0:T(8,128)(2,1)S(1)} %get-tuple-element.193), channel_id=1, source_target_pairs={{0,8},{4,12},{8,0},{12,4},{16,24},{20,28},{24,16},{28,20},{1,9},{5... | collective-permute-start | bytes 786440 | tf_op jit(solution)/shard_map/ppermute | solution.py:810
  (70 other events, 311.6 us)
Sparse Core Ops, SparseCore 0:
  9.6 45.5 all-gather.3
  56.7 28.2 all-gather.5
  100.3 27.6 all-gather.7
  130.1 41.1 reduce-scatter.2
  227.7 42.5 reduce-scatter.4
